TPU v7x, 32 devices: a whole 2x2x4 slice. The times are simulated.
32 devices in a mesh: row: 2 (over y), col: 16 (over z, x, core).
Axes of the slice: x: 2, y: 2, z: 4, core: 2. Of those that a mesh axis runs over, the one named last changes fastest.
Arguments:
- right_side: float32 [2048, 4096], P('row', 'col'), may hold values from -8 to 8
- factor_panels: float32 [4, 256, 2048], P(None, 'col', 'row'), may hold values from -0.1875 to 0.1875
- inverses: float32 [4, 256, 256], P(None, 'col'), may hold values from -0.5 to 1.6, as said below
Outputs:
- solved: float32 [2048, 4096], P('row', 'col')
Inputs may be any that keep to these rules, and one draw needn't show every extreme that they name: inverses[k] is lower triangular with a diagonal between 0.6 and 1.6 and independent entries below it.
All inputs are finite; a program needn't handle non-finite values.
Results may differ from a plain program's by a relative error of at most 0.0001.
Values sent between devices are 32-bit elements; how exact they have to be, the bound alone decides.
No kernel may reach another device: no remote copies, remote signals or barrier semaphores. Data moves between devices by JAX's collectives and lax.ppermute only.
A program may use at most 64 MiB of HBM per device.

v0:
```python
import functools

import jax
import jax.numpy as jnp
from jax import lax
from jax.experimental import pallas as pl
from jax.experimental.pallas import tpu as pltpu
from jax.sharding import PartitionSpec as P


def ring_place(chip, chips):
    return jnp.where(chip % 2 == 0, chip // 2, chips - 1 - chip // 2)


def ring_chip(place, chips):
    up = 2 * place
    down = 2 * (chips - 1 - place) + 1
    if isinstance(place, int):
        return up if place < chips // 2 else down
    return jnp.where(place < chips // 2, up, down)


def split(value):
    high = value.astype(jnp.bfloat16)
    low = (value - high.astype(jnp.float32)).astype(jnp.bfloat16)
    return high, low


def dot3(left, right, dims):
    mult = functools.partial(
        lax.dot_general, dimension_numbers=(dims, ((), ())), preferred_element_type=jnp.float32
    )
    return mult(left[0], right[0]) + (mult(left[0], right[1]) + mult(left[1], right[0]))


def ring(first, half_core, chips):
    steps = chips // 2
    nearest = []
    for place in range(chips):
        here = ring_chip(place, chips)
        nearest.append((2 * here, 2 * ring_chip((place + 1) % chips, chips)))
        nearest.append((2 * here + 1, 2 * ring_chip((place - 1) % chips, chips) + 1))
    swap = [(i, i ^ 1) for i in range(2 * chips)]
    moving = first
    pieces = []
    for step in range(1, steps + 1):
        last = step == steps
        pairs = [p for p in nearest if not last or p[0] % 2 == half_core]
        moving = lax.ppermute(moving, "col", pairs)
        across = [p for p in swap if not last or p[0] % 2 == half_core]
        pieces.append((moving, lax.ppermute(moving, "col", across)))
    return pieces


def streams(chips):
    core = lax.axis_index("col") % 2
    here = ring_place(lax.axis_index("col") // 2, chips)
    found = [(lax.axis_index("col") // 2, core)]
    steps = chips // 2
    for step in range(1, steps + 1):
        turn = step * (1 - 2 * core)
        mine = ring_chip((here - turn + chips) % chips, chips)
        other = ring_chip((here + turn + chips) % chips, chips)
        if step < steps:
            found.append((mine, core))
            found.append((other, 1 - core))
        else:
            found.append((mine, None))
    return found


def assemble(piece_refs, mat_ref, chips, half_core):
    depth = piece_refs[0].shape[2]

    def put(row, value):
        mat_ref[:, pl.ds(pl.multiple_of(row, value.shape[1]), value.shape[1]), :] = value

    for at, (chip, core) in enumerate(streams(chips)):
        halves = []
        for half in range(2):
            if core is None:
                halves.append(piece_refs[at][half ^ half_core] + piece_refs[at + 1][half ^ half_core])
            elif depth % 8 == 0:
                halves.append(piece_refs[at][jnp.where(core == 0, half, 1 - half)])
            else:
                halves.append(jnp.where(core == 0, piece_refs[at][half], piece_refs[at][1 - half]))
        if depth % 8 == 0:
            for half in range(2):
                put((2 * chip + half) * depth, halves[half])
        else:
            put(2 * chip * depth, jnp.concatenate(halves, axis=1))


def solve_kernel(panels, group_count, locals_, chips, *refs):
    piece_refs, right_ref = refs[: chips + 1], refs[chips + 1]
    received = refs[chips + 2 : -3]
    x_ref, mat_ref, work_ref = refs[-3:]
    nb = right_ref.shape[0] // locals_
    me = lax.axis_index("row")
    assemble(piece_refs, mat_ref, chips, 0)
    for shift in range(group_count):
        owner = (me + shift) % group_count
        source = right_ref if shift == 0 else received[shift - 1]
        for local in range(locals_):
            rank = local * group_count + owner

            @pl.when(rank < panels)
            def _(rank=rank, local=local, source=source):
                work_ref[rank] = source[local * nb : (local + 1) * nb]

    solved = []
    for panel in range(panels):
        current = work_ref[panel]
        for before in range(panel):
            tri = panels + panel * (panel - 1) // 2 + before
            current = current - dot3(split(mat_ref[tri]), solved[before], ((0,), (0,)))
        answer = dot3(split(mat_ref[panel]), split(current), ((1,), (0,)))
        x_ref[panel] = answer
        solved.append(split(answer))


def update_kernel(panels, group_count, locals_, chips, *refs):
    *piece_refs, right_ref, x_ref, out_ref, mat_ref = refs
    nb = x_ref.shape[1]
    sure = panels // group_count
    me = lax.axis_index("row")
    assemble(piece_refs, mat_ref, chips, 1)
    total = right_ref[sure * nb :]
    for panel in range(panels):
        total = total - dot3(split(mat_ref[panel]), split(x_ref[panel]), ((0,), (0,)))
    out_ref[sure * nb :] = total
    for local in range(locals_):
        rank = local * group_count + me

        @pl.when(rank < panels)
        def _(rank=rank, local=local):
            out_ref[local * nb : (local + 1) * nb] = x_ref[rank]


def per_device(right_side, factor_panels, inverses):
    group_count = lax.axis_size("row")
    chips = lax.axis_size("col") // 2
    me = lax.axis_index("row")
    panels, _, rows = factor_panels.shape
    nb = inverses.shape[2]
    columns = right_side.shape[1]
    locals_ = -(-panels // group_count)
    swap = [(i, i ^ 1) for i in range(2 * chips)]
    shifts = [
        [((g + shift) % group_count, g) for g in range(group_count)] for shift in range(1, group_count)
    ]

    factor_other = lax.ppermute(factor_panels, "col", swap)
    wanted = [
        (local, panel)
        for local in range(locals_)
        for panel in range(min(local * group_count + group_count - 1, panels - 1))
    ]
    tri_own = jnp.stack([factor_panels[k, :, l * nb : (l + 1) * nb] for l, k in wanted])
    tri = [tri_own] + [lax.ppermute(tri_own, "row", pairs) for pairs in shifts]
    above = right_side[: locals_ * nb]
    received = [lax.ppermute(above, "row", pairs) for pairs in shifts]

    sure = panels // group_count * nb
    trail_first = jnp.stack([factor_panels[:, :, sure:], factor_other[:, :, sure:]])
    blocks = []
    for rank in range(1, panels):
        local, owner = divmod(rank, group_count)
        for panel in range(rank):
            at = wanted.index((local, panel))
            value = tri[0][at]
            for shift in range(1, group_count):
                value = jnp.where((me + shift) % group_count == owner, tri[shift][at], value)
            blocks.append(value)
    near_own = jnp.concatenate([inverses, jnp.stack(blocks)])
    near_first = jnp.stack([near_own, lax.ppermute(near_own, "col", swap)])

    near = ring(near_first, 0, chips)
    trail = ring(trail_first, 1, chips)

    near_pieces = [near_first] + [p for pair in near for p in pair]
    trail_pieces = [trail_first] + [p for pair in trail for p in pair]
    vmem = pl.BlockSpec(memory_space=pltpu.VMEM)
    sizes = (panels, group_count, locals_, chips)
    count = near_first.shape[1]
    solved = pl.pallas_call(
        functools.partial(solve_kernel, *sizes),
        out_shape=jax.ShapeDtypeStruct((panels, nb, columns), jnp.float32),
        in_specs=[vmem] * (len(near_pieces) + group_count),
        out_specs=vmem,
        scratch_shapes=[
            pltpu.VMEM((count, nb, nb), jnp.float32),
            pltpu.VMEM((panels, nb, columns), jnp.float32),
        ],
        cost_estimate=pl.CostEstimate(flops=6 * count * nb * nb * columns, bytes_accessed=6 << 20, transcendentals=0),
        compiler_params=pltpu.CompilerParams(vmem_limit_bytes=16 << 20),
        name="solve",
    )(*near_pieces, above, *received)
    return pl.pallas_call(
        functools.partial(update_kernel, *sizes),
        out_shape=jax.ShapeDtypeStruct(right_side.shape, jnp.float32),
        in_specs=[vmem] * (len(trail_pieces) + 2),
        out_specs=vmem,
        scratch_shapes=[pltpu.VMEM((panels, nb, rows - sure), jnp.float32)],
        cost_estimate=pl.CostEstimate(
            flops=6 * panels * nb * columns * (rows - sure), bytes_accessed=6 << 20, transcendentals=0
        ),
        compiler_params=pltpu.CompilerParams(vmem_limit_bytes=16 << 20),
        name="update",
    )(*trail_pieces, right_side, solved)


def solution(mesh):
    in_specs = (P("row", "col"), P(None, "col", "row"), P(None, "col", None))
    out_specs = P("row", "col")

    return jax.shard_map(per_device, mesh=mesh, in_specs=in_specs, out_specs=out_specs, check_vma=False)
```

profile of v0, /device:TPU:0, one launch (start us, length us, event | category | flops | bytes accessed | tf_op | source)
XLA Modules:
  0.0 52.4 jit_solution(9597226882441245824)
XLA Ops:
  0.0 0.9 %slice.41 = f32[3,16,256]{2,1,0:T(8,128)S(1)} slice(f32[4,16,1024]{2,1,0:T(8,128)} %param.4), slice={[0:3], [0:16], [256:512]} | slice | bytes 98304 | tf_op jit(solution)/shard_map/slice | solution.py:159
  0.9 0.7 %slice.40 = f32[1,16,256]{2,1,0:T(8,128)S(1)} slice(f32[4,16,1024]{2,1,0:T(8,128)} %param.4), slice={[0:1], [0:16], [0:256]} | slice | bytes 32768 | tf_op jit(solution)/shard_map/slice | solution.py:159
  1.6 3.0 %collective-permute-start.9 = (f32[4,16,256]{2,1,0:T(8,128)S(1)}, f32[4,16,256]{2,1,0:T(8,128)S(1)}, u32[]{:S(2)}, u32[]{:S(2)}) collective-permute-start(f32[4,16,256]{2,1,0:T(8,128)S(1)} %pad_maximum_fusion.2), channel_id=1, source_target_pairs={{16,0},{0,16},{17,1},{1,17},{18,2},{2,18},{19,3},{3,19},{20,4},{4,... | collective-permute-start | bytes 196616 | tf_op jit(solution)/shard_map/ppermute | solution.py:160
  4.6 0.9 %constant_dynamic-update-slice_fusion.4 = f32[10,16,256]{2,1,0:T(8,128)S(1)} fusion(f32[4,16,256]{2,1,0:T(8,128)} %param.5), kind=kLoop, calls=%fused_computation.13 | loop fusion | bytes 131072
  5.5 1.3 %collective-permute-done.9 = f32[4,16,256]{2,1,0:T(8,128)S(1)} collective-permute-done((f32[4,16,256]{2,1,0:T(8,128)S(1)}, f32[4,16,256]{2,1,0:T(8,128)S(1)}, u32[]{:S(2)}, u32[]{:S(2)}) %collective-permute-start.9) | collective-permute-done | bytes 65568 | tf_op jit(solution)/shard_map/ppermute | solution.py:160
  7.5 0.9 %collective-permute-done.10 = f32[10,16,256]{2,1,0:T(8,128)S(1)} collective-permute-done((f32[10,16,256]{2,1,0:T(8,128)S(1)}, f32[10,16,256]{2,1,0:T(8,128)S(1)}, u32[]{:S(2)}, u32[]{:S(2)}) %collective-permute-start.10) | collective-permute-done | bytes 163872 | tf_op jit(solution)/shard_map/ppermute | solution.py:176
  8.4 2.1 %collective-permute-start.11 = (f32[2,10,16,256]{3,2,1,0:T(8,128)S(1)}, f32[2,10,16,256]{3,2,1,0:T(8,128)S(1)}, u32[]{:S(2)}, u32[]{:S(2)}) collective-permute-start(f32[2,10,16,256]{3,2,1,0:T(8,128)S(1)} %pad_maximum_fusion.refs_0_), channel_id=1, source_target_pairs={{0,4},{1,3},{4,8},{5,1},{8,12},{9,5},{12,14},{13,9},{14,10},{15,13... | collective-permute-start | bytes 983048 | tf_op jit(solution)/shard_map/ppermute | solution.py:49
  10.6 5.0 %collective-permute-done.11.refs_1_ = f32[2,10,16,256]{3,2,1,0:T(8,128)S(1)} collective-permute-done((f32[2,10,16,256]{3,2,1,0:T(8,128)S(1)}, f32[2,10,16,256]{3,2,1,0:T(8,128)S(1)}, u32[]{:S(2)}, u32[]{:S(2)}) %collective-permute-start.11) | collective-permute-done | bytes 327712 | tf_op jit(solution)/shard_map/ppermute | solution.py:49
  15.5 2.1 %collective-permute-start.13 = (f32[2,10,16,256]{3,2,1,0:T(8,128)S(1)}, f32[2,10,16,256]{3,2,1,0:T(8,128)S(1)}, u32[]{:S(2)}, u32[]{:S(2)}) collective-permute-start(f32[2,10,16,256]{3,2,1,0:T(8,128)S(1)} %collective-permute-done.11.refs_1_), channel_id=1, source_target_pairs={{0,4},{1,3},{4,8},{5,1},{8,12},{9,5},{12,14},{13,9},{14,10},{15,13... | collective-permute-start | bytes 983048 | tf_op jit(solution)/shard_map/ppermute | solution.py:49
  17.6 1.6 %collective-permute-start.1 = (f32[2,4,16,512]{3,2,1,0:T(8,128)S(1)}, f32[2,4,16,512]{3,2,1,0:T(8,128)S(1)}, u32[]{:S(2)}, u32[]{:S(2)}) collective-permute-start(f32[2,4,16,512]{3,2,1,0:T(8,128)S(1)} %pad_maximum_fusion.1.refs_0_), channel_id=1, source_target_pairs={{0,4},{1,3},{4,8},{5,1},{8,12},{9,5},{12,14},{13,9},{14,10},{15,13... | collective-permute-start | bytes 786440 | tf_op jit(solution)/shard_map/ppermute | solution.py:49
  19.3 1.6 %collective-permute-start.19 = (f32[512,256]{1,0:T(8,128)S(1)}, f32[512,256]{1,0:T(8,128)S(1)}, u32[]{:S(2)}, u32[]{:S(2)}) collective-permute-start(f32[512,256]{1,0:T(8,128)S(1)} %slice.49.refs_9_), channel_id=1, source_target_pairs={{16,0},{0,16},{17,1},{1,17},{18,2},{2,18},{19,3},{3,19},{20,4},{4,... | collective-permute-start | bytes 1572872 | tf_op jit(solution)/shard_map/ppermute | solution.py:162
  20.9 1.7 %collective-permute-done.13.refs_3_ = f32[2,10,16,256]{3,2,1,0:T(8,128)S(1)} collective-permute-done((f32[2,10,16,256]{3,2,1,0:T(8,128)S(1)}, f32[2,10,16,256]{3,2,1,0:T(8,128)S(1)}, u32[]{:S(2)}, u32[]{:S(2)}) %collective-permute-start.13) | collective-permute-done | bytes 327712 | tf_op jit(solution)/shard_map/ppermute | solution.py:49
  22.6 2.1 %collective-permute-start.15 = (f32[2,10,16,256]{3,2,1,0:T(8,128)S(1)}, f32[2,10,16,256]{3,2,1,0:T(8,128)S(1)}, u32[]{:S(2)}, u32[]{:S(2)}) collective-permute-start(f32[2,10,16,256]{3,2,1,0:T(8,128)S(1)} %collective-permute-done.13.refs_3_), channel_id=1, source_target_pairs={{0,4},{1,3},{4,8},{5,1},{8,12},{9,5},{12,14},{13,9},{14,10},{15,13... | collective-permute-start | bytes 983048 | tf_op jit(solution)/shard_map/ppermute | solution.py:49
  24.7 0.7 %collective-permute-done.1.refs_1_ = f32[2,4,16,512]{3,2,1,0:T(8,128)S(1)} collective-permute-done((f32[2,4,16,512]{3,2,1,0:T(8,128)S(1)}, f32[2,4,16,512]{3,2,1,0:T(8,128)S(1)}, u32[]{:S(2)}, u32[]{:S(2)}) %collective-permute-start.1) | collective-permute-done | bytes 262176 | tf_op jit(solution)/shard_map/ppermute | solution.py:49
  25.4 2.1 %collective-permute-start.3 = (f32[2,4,16,512]{3,2,1,0:T(8,128)S(1)}, f32[2,4,16,512]{3,2,1,0:T(8,128)S(1)}, u32[]{:S(2)}, u32[]{:S(2)}) collective-permute-start(f32[2,4,16,512]{3,2,1,0:T(8,128)S(1)} %collective-permute-done.1.refs_1_), channel_id=1, source_target_pairs={{0,4},{1,3},{4,8},{5,1},{8,12},{9,5},{12,14},{13,9},{14,10},{15,13... | collective-permute-start | bytes 786440 | tf_op jit(solution)/shard_map/ppermute | solution.py:49
  27.5 5.0 %collective-permute-done.3.refs_3_ = f32[2,4,16,512]{3,2,1,0:T(8,128)S(1)} collective-permute-done((f32[2,4,16,512]{3,2,1,0:T(8,128)S(1)}, f32[2,4,16,512]{3,2,1,0:T(8,128)S(1)}, u32[]{:S(2)}, u32[]{:S(2)}) %collective-permute-start.3) | collective-permute-done | bytes 262176 | tf_op jit(solution)/shard_map/ppermute | solution.py:49
  32.5 2.1 %collective-permute-start.5 = (f32[2,4,16,512]{3,2,1,0:T(8,128)S(1)}, f32[2,4,16,512]{3,2,1,0:T(8,128)S(1)}, u32[]{:S(2)}, u32[]{:S(2)}) collective-permute-start(f32[2,4,16,512]{3,2,1,0:T(8,128)S(1)} %collective-permute-done.3.refs_3_), channel_id=1, source_target_pairs={{0,4},{1,3},{4,8},{5,1},{8,12},{9,5},{12,14},{13,9},{14,10},{15,13... | collective-permute-start | bytes 786440 | tf_op jit(solution)/shard_map/ppermute | solution.py:49
  34.6 3.5 %collective-permute-start.17 = (f32[2,10,16,256]{3,2,1,0:T(8,128)S(1)}, f32[2,10,16,256]{3,2,1,0:T(8,128)S(1)}, u32[]{:S(2)}, u32[]{:S(2)}) collective-permute-start(f32[2,10,16,256]{3,2,1,0:T(8,128)S(1)} %collective-permute-done.15.refs_5_), channel_id=1, source_target_pairs={{0,4},{4,8},{8,12},{12,14},{14,10},{10,6},{6,2},{2,0},{16,20},{20,... | collective-permute-start | bytes 983048 | tf_op jit(solution)/shard_map/ppermute | solution.py:49
  39.5 4.0 %collective-permute-done.17.refs_7_ = f32[2,10,16,256]{3,2,1,0:T(8,128)S(1)} collective-permute-done((f32[2,10,16,256]{3,2,1,0:T(8,128)S(1)}, f32[2,10,16,256]{3,2,1,0:T(8,128)S(1)}, u32[]{:S(2)}, u32[]{:S(2)}) %collective-permute-start.17) | collective-permute-done | bytes 327712 | tf_op jit(solution)/shard_map/ppermute | solution.py:49
  43.5 1.3 %collective-permute-start.18 = (f32[2,10,16,256]{3,2,1,0:T(8,128)S(1)}, f32[2,10,16,256]{3,2,1,0:T(8,128)S(1)}, u32[]{:S(2)}, u32[]{:S(2)}) collective-permute-start(f32[2,10,16,256]{3,2,1,0:T(8,128)S(1)} %collective-permute-done.17.refs_7_), channel_id=1, source_target_pairs={{0,1},{2,3},{4,5},{6,7},{8,9},{10,11},{12,13},{14,15},{16,17},{18,... | collective-permute-start | bytes 983048 | tf_op jit(solution)/shard_map/ppermute | solution.py:51
  45.4 0.8 %collective-permute-start.6 = (f32[2,4,16,512]{3,2,1,0:T(8,128)S(1)}, f32[2,4,16,512]{3,2,1,0:T(8,128)S(1)}, u32[]{:S(2)}, u32[]{:S(2)}) collective-permute-start(f32[2,4,16,512]{3,2,1,0:T(8,128)S(1)} %collective-permute-done.5.refs_5_), channel_id=1, source_target_pairs={{0,1},{1,0},{2,3},{3,2},{4,5},{5,4},{6,7},{7,6},{8,9},{9,8},{10,11... | collective-permute-start | bytes 786440 | tf_op jit(solution)/shard_map/ppermute | solution.py:51
  46.3 1.3 %collective-permute-start.8 = (f32[2,4,16,512]{3,2,1,0:T(8,128)S(1)}, f32[2,4,16,512]{3,2,1,0:T(8,128)S(1)}, u32[]{:S(2)}, u32[]{:S(2)}) collective-permute-start(f32[2,4,16,512]{3,2,1,0:T(8,128)S(1)} %collective-permute-done.7.refs_7_), channel_id=1, source_target_pairs={{1,0},{3,2},{5,4},{7,6},{9,8},{11,10},{13,12},{15,14},{17,16},{19,... | collective-permute-start | bytes 786440 | tf_op jit(solution)/shard_map/ppermute | solution.py:51
  47.6 2.6 %solve.1.refs_10_ = f32[4,256,256]{2,1,0:T(8,128)S(1)} custom-call(f32[2,10,16,256]{3,2,1,0:T(8,128)S(1)} %pad_maximum_fusion.refs_0_, f32[2,10,16,256]{3,2,1,0:T(8,128)S(1)} %collective-permute-done.11.refs_1_, f32[2,10,16,256]{3,2,1,0:T(8,128)S(1)} %collective-permute-done.12.refs_2_, f32[2,10,16,256]{3,2,1,0:T(8,128)S(1)} %collective-permute-done.13.refs_3_, ...), custom_call_target="tpu_custom_call" | custom-call | flops 1006632960 | bytes 6291456 | tf_op jit(solution)/shard_map/solve/pallas_call | solution.py:186
  50.2 2.2 %update.1 = f32[1024,256]{1,0:T(8,128)} custom-call(f32[2,4,16,512]{3,2,1,0:T(8,128)S(1)} %pad_maximum_fusion.1.refs_0_, f32[2,4,16,512]{3,2,1,0:T(8,128)S(1)} %collective-permute-done.1.refs_1_, f32[2,4,16,512]{3,2,1,0:T(8,128)S(1)} %collective-permute-done.2.refs_2_, f32[2,4,16,512]{3,2,1,0:T(8,128)S(1)} %collective-permute-done.3.refs_3_, ...), custom_call_target="tpu_custom_call" | custom-call | flops 805306368 | bytes 6291456 | tf_op jit(solution)/shard_map/update/pallas_call | solution.py:199
  (37 shorter events, 2.8 us)
Async XLA Ops:
  0.0 6.8 %copy-start.1 = (f32[4,16,1024]{2,1,0:T(8,128)S(1)}, f32[4,16,1024]{2,1,0:T(8,128)}, u32[]{:S(2)}) copy-start(f32[4,16,1024]{2,1,0:T(8,128)} %param.4) | copy-start | bytes 786436
  1.6 5.2 %collective-permute-start.9 = (f32[4,16,256]{2,1,0:T(8,128)S(1)}, f32[4,16,256]{2,1,0:T(8,128)S(1)}, u32[]{:S(2)}, u32[]{:S(2)}) collective-permute-start(f32[4,16,256]{2,1,0:T(8,128)S(1)} %pad_maximum_fusion.2), channel_id=1, source_target_pairs={{16,0},{0,16},{17,1},{1,17},{18,2},{2,18},{19,3},{3,19},{20,4},{4,... | collective-permute-start | bytes 196616 | tf_op jit(solution)/shard_map/ppermute | solution.py:160
  4.6 14.7 %copy-start = (f32[1024,256]{1,0:T(8,128)S(1)}, f32[1024,256]{1,0:T(8,128)}, u32[]{:S(2)}) copy-start(f32[1024,256]{1,0:T(8,128)} %refs_9_.1) | copy-start | bytes 3145732
  6.9 1.5 %collective-permute-start.10 = (f32[10,16,256]{2,1,0:T(8,128)S(1)}, f32[10,16,256]{2,1,0:T(8,128)S(1)}, u32[]{:S(2)}, u32[]{:S(2)}) collective-permute-start(f32[10,16,256]{2,1,0:T(8,128)S(1)} %fusion), channel_id=1, source_target_pairs={{0,1},{1,0},{2,3},{3,2},{4,5},{5,4},{6,7},{7,6},{8,9},{9,8},{10,11... | collective-permute-start | bytes 491528 | tf_op jit(solution)/shard_map/ppermute | solution.py:176
  7.0 3.6 %collective-permute-start = (f32[4,16,1024]{2,1,0:T(8,128)S(1)}, f32[4,16,1024]{2,1,0:T(8,128)S(1)}, u32[]{:S(2)}, u32[]{:S(2)}) collective-permute-start(f32[4,16,1024]{2,1,0:T(8,128)S(1)} %copy-done.1), channel_id=1, source_target_pairs={{0,1},{1,0},{2,3},{3,2},{4,5},{5,4},{6,7},{7,6},{8,9},{9,8},{10,11... | collective-permute-start | bytes 786440 | tf_op jit(solution)/shard_map/ppermute | solution.py:153
  8.4 7.1 %collective-permute-start.11 = (f32[2,10,16,256]{3,2,1,0:T(8,128)S(1)}, f32[2,10,16,256]{3,2,1,0:T(8,128)S(1)}, u32[]{:S(2)}, u32[]{:S(2)}) collective-permute-start(f32[2,10,16,256]{3,2,1,0:T(8,128)S(1)} %pad_maximum_fusion.refs_0_), channel_id=1, source_target_pairs={{0,4},{1,3},{4,8},{5,1},{8,12},{9,5},{12,14},{13,9},{14,10},{15,13... | collective-permute-start | bytes 983048 | tf_op jit(solution)/shard_map/ppermute | solution.py:49
  15.5 7.1 %collective-permute-start.13 = (f32[2,10,16,256]{3,2,1,0:T(8,128)S(1)}, f32[2,10,16,256]{3,2,1,0:T(8,128)S(1)}, u32[]{:S(2)}, u32[]{:S(2)}) collective-permute-start(f32[2,10,16,256]{3,2,1,0:T(8,128)S(1)} %collective-permute-done.11.refs_1_), channel_id=1, source_target_pairs={{0,4},{1,3},{4,8},{5,1},{8,12},{9,5},{12,14},{13,9},{14,10},{15,13... | collective-permute-start | bytes 983048 | tf_op jit(solution)/shard_map/ppermute | solution.py:49
  17.6 7.8 %collective-permute-start.1 = (f32[2,4,16,512]{3,2,1,0:T(8,128)S(1)}, f32[2,4,16,512]{3,2,1,0:T(8,128)S(1)}, u32[]{:S(2)}, u32[]{:S(2)}) collective-permute-start(f32[2,4,16,512]{3,2,1,0:T(8,128)S(1)} %pad_maximum_fusion.1.refs_0_), channel_id=1, source_target_pairs={{0,4},{1,3},{4,8},{5,1},{8,12},{9,5},{12,14},{13,9},{14,10},{15,13... | collective-permute-start | bytes 786440 | tf_op jit(solution)/shard_map/ppermute | solution.py:49
  19.3 19.3 %collective-permute-start.19 = (f32[512,256]{1,0:T(8,128)S(1)}, f32[512,256]{1,0:T(8,128)S(1)}, u32[]{:S(2)}, u32[]{:S(2)}) collective-permute-start(f32[512,256]{1,0:T(8,128)S(1)} %slice.49.refs_9_), channel_id=1, source_target_pairs={{16,0},{0,16},{17,1},{1,17},{18,2},{2,18},{19,3},{3,19},{20,4},{4,... | collective-permute-start | bytes 1572872 | tf_op jit(solution)/shard_map/ppermute | solution.py:162
  22.6 12.0 %collective-permute-start.15 = (f32[2,10,16,256]{3,2,1,0:T(8,128)S(1)}, f32[2,10,16,256]{3,2,1,0:T(8,128)S(1)}, u32[]{:S(2)}, u32[]{:S(2)}) collective-permute-start(f32[2,10,16,256]{3,2,1,0:T(8,128)S(1)} %collective-permute-done.13.refs_3_), channel_id=1, source_target_pairs={{0,4},{1,3},{4,8},{5,1},{8,12},{9,5},{12,14},{13,9},{14,10},{15,13... | collective-permute-start | bytes 983048 | tf_op jit(solution)/shard_map/ppermute | solution.py:49
  25.4 7.1 %collective-permute-start.3 = (f32[2,4,16,512]{3,2,1,0:T(8,128)S(1)}, f32[2,4,16,512]{3,2,1,0:T(8,128)S(1)}, u32[]{:S(2)}, u32[]{:S(2)}) collective-permute-start(f32[2,4,16,512]{3,2,1,0:T(8,128)S(1)} %collective-permute-done.1.refs_1_), channel_id=1, source_target_pairs={{0,4},{1,3},{4,8},{5,1},{8,12},{9,5},{12,14},{13,9},{14,10},{15,13... | collective-permute-start | bytes 786440 | tf_op jit(solution)/shard_map/ppermute | solution.py:49
  32.5 6.4 %collective-permute-start.5 = (f32[2,4,16,512]{3,2,1,0:T(8,128)S(1)}, f32[2,4,16,512]{3,2,1,0:T(8,128)S(1)}, u32[]{:S(2)}, u32[]{:S(2)}) collective-permute-start(f32[2,4,16,512]{3,2,1,0:T(8,128)S(1)} %collective-permute-done.3.refs_3_), channel_id=1, source_target_pairs={{0,4},{1,3},{4,8},{5,1},{8,12},{9,5},{12,14},{13,9},{14,10},{15,13... | collective-permute-start | bytes 786440 | tf_op jit(solution)/shard_map/ppermute | solution.py:49
  34.6 9.0 %collective-permute-start.17 = (f32[2,10,16,256]{3,2,1,0:T(8,128)S(1)}, f32[2,10,16,256]{3,2,1,0:T(8,128)S(1)}, u32[]{:S(2)}, u32[]{:S(2)}) collective-permute-start(f32[2,10,16,256]{3,2,1,0:T(8,128)S(1)} %collective-permute-done.15.refs_5_), channel_id=1, source_target_pairs={{0,4},{4,8},{8,12},{12,14},{14,10},{10,6},{6,2},{2,0},{16,20},{20,... | collective-permute-start | bytes 983048 | tf_op jit(solution)/shard_map/ppermute | solution.py:49
  38.1 6.8 %collective-permute-start.12 = (f32[2,10,16,256]{3,2,1,0:T(8,128)S(1)}, f32[2,10,16,256]{3,2,1,0:T(8,128)S(1)}, u32[]{:S(2)}, u32[]{:S(2)}) collective-permute-start(f32[2,10,16,256]{3,2,1,0:T(8,128)S(1)} %collective-permute-done.11.refs_1_), channel_id=1, source_target_pairs={{0,1},{1,0},{2,3},{3,2},{4,5},{5,4},{6,7},{7,6},{8,9},{9,8},{10,11... | collective-permute-start | bytes 983048 | tf_op jit(solution)/shard_map/ppermute | solution.py:51
  38.1 6.8 %collective-permute-start.14 = (f32[2,10,16,256]{3,2,1,0:T(8,128)S(1)}, f32[2,10,16,256]{3,2,1,0:T(8,128)S(1)}, u32[]{:S(2)}, u32[]{:S(2)}) collective-permute-start(f32[2,10,16,256]{3,2,1,0:T(8,128)S(1)} %collective-permute-done.13.refs_3_), channel_id=1, source_target_pairs={{0,1},{1,0},{2,3},{3,2},{4,5},{5,4},{6,7},{7,6},{8,9},{9,8},{10,11... | collective-permute-start | bytes 983048 | tf_op jit(solution)/shard_map/ppermute | solution.py:51
  38.6 7.6 %collective-permute-start.16 = (f32[2,10,16,256]{3,2,1,0:T(8,128)S(1)}, f32[2,10,16,256]{3,2,1,0:T(8,128)S(1)}, u32[]{:S(2)}, u32[]{:S(2)}) collective-permute-start(f32[2,10,16,256]{3,2,1,0:T(8,128)S(1)} %collective-permute-done.15.refs_5_), channel_id=1, source_target_pairs={{0,1},{1,0},{2,3},{3,2},{4,5},{5,4},{6,7},{7,6},{8,9},{9,8},{10,11... | collective-permute-start | bytes 983048 | tf_op jit(solution)/shard_map/ppermute | solution.py:51
  38.9 6.6 %collective-permute-start.7 = (f32[2,4,16,512]{3,2,1,0:T(8,128)S(1)}, f32[2,4,16,512]{3,2,1,0:T(8,128)S(1)}, u32[]{:S(2)}, u32[]{:S(2)}) collective-permute-start(f32[2,4,16,512]{3,2,1,0:T(8,128)S(1)} %collective-permute-done.5.refs_5_), channel_id=1, source_target_pairs={{1,3},{5,1},{9,5},{13,9},{15,13},{11,15},{7,11},{3,7},{17,19},{21,... | collective-permute-start | bytes 786440 | tf_op jit(solution)/shard_map/ppermute | solution.py:49
  43.5 4.0 %collective-permute-start.18 = (f32[2,10,16,256]{3,2,1,0:T(8,128)S(1)}, f32[2,10,16,256]{3,2,1,0:T(8,128)S(1)}, u32[]{:S(2)}, u32[]{:S(2)}) collective-permute-start(f32[2,10,16,256]{3,2,1,0:T(8,128)S(1)} %collective-permute-done.17.refs_7_), channel_id=1, source_target_pairs={{0,1},{2,3},{4,5},{6,7},{8,9},{10,11},{12,13},{14,15},{16,17},{18,... | collective-permute-start | bytes 983048 | tf_op jit(solution)/shard_map/ppermute | solution.py:51
  44.8 5.3 %collective-permute-start.2 = (f32[2,4,16,512]{3,2,1,0:T(8,128)S(1)}, f32[2,4,16,512]{3,2,1,0:T(8,128)S(1)}, u32[]{:S(2)}, u32[]{:S(2)}) collective-permute-start(f32[2,4,16,512]{3,2,1,0:T(8,128)S(1)} %collective-permute-done.1.refs_1_), channel_id=1, source_target_pairs={{0,1},{1,0},{2,3},{3,2},{4,5},{5,4},{6,7},{7,6},{8,9},{9,8},{10,11... | collective-permute-start | bytes 786440 | tf_op jit(solution)/shard_map/ppermute | solution.py:51
  44.9 5.2 %collective-permute-start.4 = (f32[2,4,16,512]{3,2,1,0:T(8,128)S(1)}, f32[2,4,16,512]{3,2,1,0:T(8,128)S(1)}, u32[]{:S(2)}, u32[]{:S(2)}) collective-permute-start(f32[2,4,16,512]{3,2,1,0:T(8,128)S(1)} %collective-permute-done.3.refs_3_), channel_id=1, source_target_pairs={{0,1},{1,0},{2,3},{3,2},{4,5},{5,4},{6,7},{7,6},{8,9},{9,8},{10,11... | collective-permute-start | bytes 786440 | tf_op jit(solution)/shard_map/ppermute | solution.py:51
  45.4 4.7 %collective-permute-start.6 = (f32[2,4,16,512]{3,2,1,0:T(8,128)S(1)}, f32[2,4,16,512]{3,2,1,0:T(8,128)S(1)}, u32[]{:S(2)}, u32[]{:S(2)}) collective-permute-start(f32[2,4,16,512]{3,2,1,0:T(8,128)S(1)} %collective-permute-done.5.refs_5_), channel_id=1, source_target_pairs={{0,1},{1,0},{2,3},{3,2},{4,5},{5,4},{6,7},{7,6},{8,9},{9,8},{10,11... | collective-permute-start | bytes 786440 | tf_op jit(solution)/shard_map/ppermute | solution.py:51
  46.3 3.9 %collective-permute-start.8 = (f32[2,4,16,512]{3,2,1,0:T(8,128)S(1)}, f32[2,4,16,512]{3,2,1,0:T(8,128)S(1)}, u32[]{:S(2)}, u32[]{:S(2)}) collective-permute-start(f32[2,4,16,512]{3,2,1,0:T(8,128)S(1)} %collective-permute-done.7.refs_7_), channel_id=1, source_target_pairs={{1,0},{3,2},{5,4},{7,6},{9,8},{11,10},{13,12},{15,14},{17,16},{19,... | collective-permute-start | bytes 786440 | tf_op jit(solution)/shard_map/ppermute | solution.py:51
where the time goes:
time: 53.3 us; the launch traced here: 52.4 us
  starting transfers between devices  26 us (49%)
  waiting for transfers between devices  18.8 us (35%)
  Pallas kernels  4.82 us (9%)
  local copies, waits for them, and re-layouts  2.59 us (5%)
    ppermute x8, waiting for transfers between devices, ring(): moving = lax.ppermute(moving, 'col', pairs)  16.5 us
    ppermute x8, starting transfers between devices, ring(): moving = lax.ppermute(moving, 'col', pairs)  16.2 us
    ppermute x8, starting transfers between devices, ring(): pieces.append((moving, lax.ppermute(moving, 'col', across)))  4.61 us
    ppermute x1, starting transfers between devices, per_device(): tri = [tri_own] + [lax.ppermute(tri_own, 'row', pairs) for pairs in shifts]  3 us
    pallas_call x1, Pallas kernels, per_device(): pl.pallas_call(functools.partial(solve_kernel, *sizes), out_shape=jax.Sha...  2.57 us
    pallas_call x1, Pallas kernels, per_device(): pl.pallas_call(functools.partial(update_kernel, *sizes), out_shape=jax.Sh...  2.24 us
    slice x2, local copies, waits for them, and re-layouts, per_device(): factor_panels[k, :, l * nb:(l + 1) * nb]  1.59 us
    ppermute x1, starting transfers between devices, per_device(): received = [lax.ppermute(above, 'row', pairs) for pairs in shifts]  1.58 us
  transfers between devices with their start and end apart: 20, of which 8 were waited for; matrix products, arithmetic and copies ran while one was open for 2% of the time, Pallas kernels for 5%

commit v1 on v0

v1 whole, which is shorter than its diff:
```python
import functools

import jax
import jax.numpy as jnp
from jax import lax
from jax.experimental import pallas as pl
from jax.experimental.pallas import tpu as pltpu
from jax.sharding import PartitionSpec as P


def ring_place(chip, chips):
    return jnp.where(chip % 2 == 0, chip // 2, chips - 1 - chip // 2)


def ring_chip(place, chips):
    up = 2 * place
    down = 2 * (chips - 1 - place) + 1
    if isinstance(place, int):
        return up if place < chips // 2 else down
    return jnp.where(place < chips // 2, up, down)


def split(value):
    high = value.astype(jnp.bfloat16)
    low = (value - high.astype(jnp.float32)).astype(jnp.bfloat16)
    return high, low


def dot3(left, right, dims):
    mult = functools.partial(
        lax.dot_general, dimension_numbers=(dims, ((), ())), preferred_element_type=jnp.float32
    )
    return mult(left[0], right[0]) + (mult(left[0], right[1]) + mult(left[1], right[0]))


def ring(first, chips):
    steps = chips // 2
    nearest = []
    for place in range(chips):
        here = ring_chip(place, chips)
        nearest.append((2 * here, 2 * ring_chip((place + 1) % chips, chips)))
        nearest.append((2 * here + 1, 2 * ring_chip((place - 1) % chips, chips) + 1))
    swap = [(i, i ^ 1) for i in range(2 * chips)]
    moving = first
    pieces = [first]
    for step in range(1, steps + 1):
        moving = lax.ppermute(moving if step < steps else moving[0], "col", nearest)
        pieces += [moving, lax.ppermute(moving, "col", swap)]
    return pieces


def streams(chips):
    core = lax.axis_index("col") % 2
    here = ring_place(lax.axis_index("col") // 2, chips)
    found = [(lax.axis_index("col") // 2, core)]
    for step in range(1, chips // 2 + 1):
        turn = step * (1 - 2 * core)
        found.append((ring_chip((here - turn + chips) % chips, chips), core))
        found.append((ring_chip((here + turn + chips) % chips, chips), 1 - core))
    return found


def assemble(piece_refs, mat_ref, chips):
    depth = piece_refs[0].shape[2]

    def put(row, value):
        mat_ref[:, pl.ds(pl.multiple_of(row, value.shape[1]), value.shape[1]), :] = value

    table = streams(chips)
    for at, (chip, core) in enumerate(table):
        ref = piece_refs[at]
        if at < chips - 1:
            if depth % 8 == 0:
                for half in range(2):
                    put((2 * chip + half) * depth, ref[jnp.where(core == 0, half, 1 - half)])
                continue
            pair = [ref[0], ref[1]]
        else:
            if depth % 8 == 0:
                put((2 * chip + core) * depth, ref[...])
                continue
            if at == chips:
                continue
            pair = [ref[...], piece_refs[at + 1][...]]
        low, high = jnp.where(core == 0, pair[0], pair[1]), jnp.where(core == 0, pair[1], pair[0])
        put(2 * chip * depth, jnp.concatenate([low, high], axis=1))


def solve_kernel(panels, group_count, locals_, chips, *refs):
    count = chips + 1
    inverse_refs, tri_refs, right_ref = refs[:count], refs[count : 2 * count], refs[2 * count]
    received = refs[2 * count + 1 : -4]
    x_ref, inv_ref, tri_ref, work_ref = refs[-4:]
    nb = right_ref.shape[0] // locals_
    me = lax.axis_index("row")
    assemble(inverse_refs, inv_ref, chips)
    assemble(tri_refs, tri_ref, chips)
    for shift in range(group_count):
        owner = (me + shift) % group_count
        source = right_ref if shift == 0 else received[shift - 1]
        for local in range(locals_):
            rank = local * group_count + owner

            @pl.when(rank < panels)
            def _(rank=rank, local=local, source=source):
                work_ref[rank] = source[local * nb : (local + 1) * nb]

    solved = []
    for panel in range(panels):
        current = work_ref[panel]
        for before in range(panel):
            tri = panel * (panel - 1) // 2 + before
            current = current - dot3(split(tri_ref[tri]), solved[before], ((0,), (0,)))
        answer = dot3(split(inv_ref[panel]), split(current), ((1,), (0,)))
        x_ref[panel] = answer
        solved.append(split(answer))


def update_kernel(panels, group_count, locals_, chips, *refs):
    *piece_refs, right_ref, x_ref, out_ref, mat_ref = refs
    nb = x_ref.shape[1]
    sure = panels // group_count
    me = lax.axis_index("row")
    assemble(piece_refs, mat_ref, chips)
    total = right_ref[sure * nb :]
    for panel in range(panels):
        total = total - dot3(split(mat_ref[panel]), split(x_ref[panel]), ((0,), (0,)))
    out_ref[sure * nb :] = total
    for local in range(locals_):
        rank = local * group_count + me

        @pl.when(rank < panels)
        def _(rank=rank, local=local):
            out_ref[local * nb : (local + 1) * nb] = x_ref[rank]


def per_device(right_side, factor_panels, inverses):
    group_count = lax.axis_size("row")
    chips = lax.axis_size("col") // 2
    me = lax.axis_index("row")
    panels, _, rows = factor_panels.shape
    nb = inverses.shape[2]
    columns = right_side.shape[1]
    locals_ = -(-panels // group_count)
    swap = [(i, i ^ 1) for i in range(2 * chips)]
    shifts = [
        [((g + shift) % group_count, g) for g in range(group_count)] for shift in range(1, group_count)
    ]

    inverse_pieces = jnp.stack([inverses, lax.ppermute(inverses, "col", swap)])
    factor_other = lax.ppermute(factor_panels, "col", swap)
    deep = min((locals_ - 1) * group_count + group_count - 1, panels - 1)
    tri_own = factor_panels[:deep, :, : locals_ * nb]
    tri = [tri_own] + [lax.ppermute(tri_own, "row", pairs) for pairs in shifts]
    above = right_side[: locals_ * nb]
    received = [lax.ppermute(above, "row", pairs) for pairs in shifts]

    sure = panels // group_count * nb
    trail_first = jnp.stack([factor_panels[:, :, sure:], factor_other[:, :, sure:]])
    blocks = []
    for rank in range(1, panels):
        local, owner = divmod(rank, group_count)
        for panel in range(rank):
            value = tri[0]
            for shift in range(1, group_count):
                value = jnp.where((me + shift) % group_count == owner, tri[shift], value)
            blocks.append(value[panel, :, local * nb : (local + 1) * nb])
    tri_half = jnp.stack(blocks)
    tri_first = jnp.stack([tri_half, lax.ppermute(tri_half, "col", swap)])

    inverse_pieces = ring(inverse_pieces, chips)
    tri_pieces = ring(tri_first, chips)
    trail_pieces = ring(trail_first, chips)
    vmem = pl.BlockSpec(memory_space=pltpu.VMEM)
    sizes = (panels, group_count, locals_, chips)
    count = panels + len(blocks)
    solved = pl.pallas_call(
        functools.partial(solve_kernel, *sizes),
        out_shape=jax.ShapeDtypeStruct((panels, nb, columns), jnp.float32),
        in_specs=[vmem] * (len(inverse_pieces) + len(tri_pieces) + group_count),
        out_specs=vmem,
        scratch_shapes=[
            pltpu.VMEM((panels, nb, nb), jnp.float32),
            pltpu.VMEM((len(blocks), nb, nb), jnp.float32),
            pltpu.VMEM((panels, nb, columns), jnp.float32),
        ],
        cost_estimate=pl.CostEstimate(flops=6 * count * nb * nb * columns, bytes_accessed=6 << 20, transcendentals=0),
        compiler_params=pltpu.CompilerParams(vmem_limit_bytes=16 << 20),
        name="solve",
    )(*inverse_pieces, *tri_pieces, above, *received)
    return pl.pallas_call(
        functools.partial(update_kernel, *sizes),
        out_shape=jax.ShapeDtypeStruct(right_side.shape, jnp.float32),
        in_specs=[vmem] * (len(trail_pieces) + 2),
        out_specs=vmem,
        scratch_shapes=[pltpu.VMEM((panels, nb, rows - sure), jnp.float32)],
        cost_estimate=pl.CostEstimate(
            flops=6 * panels * nb * columns * (rows - sure), bytes_accessed=6 << 20, transcendentals=0
        ),
        compiler_params=pltpu.CompilerParams(vmem_limit_bytes=16 << 20),
        name="update",
    )(*trail_pieces, right_side, solved)


def solution(mesh):
    in_specs = (P("row", "col"), P(None, "col", "row"), P(None, "col", None))
    out_specs = P("row", "col")

    return jax.shard_map(per_device, mesh=mesh, in_specs=in_specs, out_specs=out_specs, check_vma=False)
```

time: 53.3 us -> 49.5 us (0.929); the launches traced: 52.4 us -> 49.3 us
  waiting for transfers between devices: 18.8 us -> 15 us
  other arithmetic: 0.08 us -> 0.97 us
  local copies, waits for them, and re-layouts: 2.59 us -> 1.9 us
    ppermute x17 -> x26, waiting for transfers between devices: 17.4 us -> 11.2 us  [the longest x12 11.2 us: ring(): moving = lax.ppermute(moving if step < steps else moving[0], 'col', nearest)]
    ppermute x1, waiting for transfers between devices: 0.01 us -> 1.45 us  [per_device(): received = [lax.ppermute(above, 'row', pairs) for pairs in shifts]]
    ppermute x1, waiting for transfers between devices: 1.31 us -> 2.3 us  [per_device(): tri = [tri_own] + [lax.ppermute(tri_own, 'row', pairs) for pairs in shifts]]
    unnamed x5 -> x4, local copies, waits for them, and re-layouts: 0.94 us -> 0.01 us
    select_n x0 -> x2, other arithmetic: none -> 0.91 us  [per_device(): value = jnp.where((me + shift) % group_count == owner, tri[shift], value)]
    another operation x2, local copies, waits for them, and re-layouts: 0.02 us -> 0.92 us  [per_device(): jnp.stack([factor_panels[:, :, sure:], factor_other[:, :, sure:]])]
    ppermute x17 -> x26, starting transfers between devices: 20.9 us -> 21.7 us  [the longest x12 19 us: ring(): moving = lax.ppermute(moving if step < steps else moving[0], 'col', nearest)]
    slice x2 -> x3, local copies, waits for them, and re-layouts: 1.59 us -> 0.91 us  [the longest x1 0.9 us: per_device(): tri_own = factor_panels[:deep, :, :locals_ * nb]]
  transfers between devices with their start and end apart: 20 -> 29, of which waited for: 8 -> 9; matrix products, arithmetic and copies ran while one was open for 2% -> 6% of each run, Pallas kernels for 5% -> 5%
where the time goes in v1:
time: 49.5 us; the launch traced here: 49.3 us
  starting transfers between devices  26.3 us (53%)
  waiting for transfers between devices  15 us (30%)
  Pallas kernels  4.92 us (10%)
  local copies, waits for them, and re-layouts  1.9 us (4%)
  other arithmetic  0.97 us (2%)
    ppermute x12, starting transfers between devices, ring(): moving = lax.ppermute(moving if step < steps else moving[0], 'col', nearest)  19 us
    ppermute x12, waiting for transfers between devices, ring(): moving = lax.ppermute(moving if step < steps else moving[0], 'col', nearest)  11.2 us
    pallas_call x1, Pallas kernels, per_device(): pl.pallas_call(functools.partial(solve_kernel, *sizes), out_shape=jax.Sha...  2.68 us
    ppermute x1, starting transfers between devices, per_device(): tri = [tri_own] + [lax.ppermute(tri_own, 'row', pairs) for pairs in shifts]  2.54 us
    ppermute x12, starting transfers between devices, ring(): pieces += [moving, lax.ppermute(moving, 'col', swap)]  2.44 us
    ppermute x1, waiting for transfers between devices, per_device(): tri = [tri_own] + [lax.ppermute(tri_own, 'row', pairs) for pairs in shifts]  2.3 us
    pallas_call x1, Pallas kernels, per_device(): pl.pallas_call(functools.partial(update_kernel, *sizes), out_shape=jax.Sh...  2.24 us
    ppermute x1, starting transfers between devices, per_device(): received = [lax.ppermute(above, 'row', pairs) for pairs in shifts]  1.58 us
  transfers between devices with their start and end apart: 29, of which 9 were waited for; matrix products, arithmetic and copies ran while one was open for 6% of the time, Pallas kernels for 5%

profile of v1, /device:TPU:0, one launch (start us, length us, event | category | flops | bytes accessed | tf_op | source)
XLA Modules:
  0.0 49.3 jit_solution(681042465370479681)
XLA Ops:
  1.4 2.5 %collective-permute-start.18 = (f32[3,16,512]{2,1,0:T(8,128)S(1)}, f32[3,16,512]{2,1,0:T(8,128)S(1)}, u32[]{:S(2)}, u32[]{:S(2)}) collective-permute-start(f32[3,16,512]{2,1,0:T(8,128)S(1)} %slice.39), channel_id=1, source_target_pairs={{16,0},{0,16},{17,1},{1,17},{18,2},{2,18},{19,3},{3,19},{20,4},{4,... | collective-permute-start | bytes 294920 | tf_op jit(solution)/shard_map/ppermute | solution.py:154
  4.1 0.9 %slice_bitcast_fusion.2 = f32[1,4,16,512]{3,2,1,0:T(8,128)S(1)} fusion(f32[4,16,1024]{2,1,0:T(8,128)} %param.4), kind=kLoop, calls=%fused_computation.5 | loop fusion | bytes 262144 | tf_op jit(solution)/shard_map/stack | solution.py:159
  5.1 2.3 %collective-permute-done.18 = f32[3,16,512]{2,1,0:T(8,128)S(1)} collective-permute-done((f32[3,16,512]{2,1,0:T(8,128)S(1)}, f32[3,16,512]{2,1,0:T(8,128)S(1)}, u32[]{:S(2)}, u32[]{:S(2)}) %collective-permute-start.18) | collective-permute-done | bytes 98336 | tf_op jit(solution)/shard_map/ppermute | solution.py:154
  8.5 1.9 %collective-permute-start.10 = (f32[2,4,16,256]{3,2,1,0:T(8,128)S(1)}, f32[2,4,16,256]{3,2,1,0:T(8,128)S(1)}, u32[]{:S(2)}, u32[]{:S(2)}) collective-permute-start(f32[2,4,16,256]{3,2,1,0:T(8,128)S(1)} %pad_maximum_fusion.2.refs_0_), channel_id=1, source_target_pairs={{0,4},{1,3},{4,8},{5,1},{8,12},{9,5},{12,14},{13,9},{14,10},{15,13... | collective-permute-start | bytes 393224 | tf_op jit(solution)/shard_map/ppermute | solution.py:47
  10.3 1.6 %collective-permute-start.20 = (f32[2,6,16,256]{3,2,1,0:T(8,128)S(1)}, f32[2,6,16,256]{3,2,1,0:T(8,128)S(1)}, u32[]{:S(2)}, u32[]{:S(2)}) collective-permute-start(f32[2,6,16,256]{3,2,1,0:T(8,128)S(1)} %pad_maximum_fusion.1.refs_9_), channel_id=1, source_target_pairs={{0,4},{1,3},{4,8},{5,1},{8,12},{9,5},{12,14},{13,9},{14,10},{15,13... | collective-permute-start | bytes 589832 | tf_op jit(solution)/shard_map/ppermute | solution.py:47
  12.0 1.6 %collective-permute-start.1 = (f32[2,4,16,512]{3,2,1,0:T(8,128)S(1)}, f32[2,4,16,512]{3,2,1,0:T(8,128)S(1)}, u32[]{:S(2)}, u32[]{:S(2)}) collective-permute-start(f32[2,4,16,512]{3,2,1,0:T(8,128)S(1)} %pad_maximum_fusion.refs_0_), channel_id=1, source_target_pairs={{0,4},{1,3},{4,8},{5,1},{8,12},{9,5},{12,14},{13,9},{14,10},{15,13... | collective-permute-start | bytes 786440 | tf_op jit(solution)/shard_map/ppermute | solution.py:47
  13.6 1.6 %collective-permute-start.12 = (f32[2,4,16,256]{3,2,1,0:T(8,128)S(1)}, f32[2,4,16,256]{3,2,1,0:T(8,128)S(1)}, u32[]{:S(2)}, u32[]{:S(2)}) collective-permute-start(f32[2,4,16,256]{3,2,1,0:T(8,128)S(1)} %collective-permute-done.10.refs_1_), channel_id=1, source_target_pairs={{0,4},{1,3},{4,8},{5,1},{8,12},{9,5},{12,14},{13,9},{14,10},{15,13... | collective-permute-start | bytes 393224 | tf_op jit(solution)/shard_map/ppermute | solution.py:47
  16.1 1.6 %collective-permute-start.22 = (f32[2,6,16,256]{3,2,1,0:T(8,128)S(1)}, f32[2,6,16,256]{3,2,1,0:T(8,128)S(1)}, u32[]{:S(2)}, u32[]{:S(2)}) collective-permute-start(f32[2,6,16,256]{3,2,1,0:T(8,128)S(1)} %collective-permute-done.20.refs_10_), channel_id=1, source_target_pairs={{0,4},{1,3},{4,8},{5,1},{8,12},{9,5},{12,14},{13,9},{14,10},{15,13... | collective-permute-start | bytes 589832 | tf_op jit(solution)/shard_map/ppermute | solution.py:47
  17.6 2.6 %collective-permute-done.12.refs_3_ = f32[2,4,16,256]{3,2,1,0:T(8,128)S(1)} collective-permute-done((f32[2,4,16,256]{3,2,1,0:T(8,128)S(1)}, f32[2,4,16,256]{3,2,1,0:T(8,128)S(1)}, u32[]{:S(2)}, u32[]{:S(2)}) %collective-permute-start.12) | collective-permute-done | bytes 131104 | tf_op jit(solution)/shard_map/ppermute | solution.py:47
  20.3 1.6 %collective-permute-start.14 = (f32[2,4,16,256]{3,2,1,0:T(8,128)S(1)}, f32[2,4,16,256]{3,2,1,0:T(8,128)S(1)}, u32[]{:S(2)}, u32[]{:S(2)}) collective-permute-start(f32[2,4,16,256]{3,2,1,0:T(8,128)S(1)} %collective-permute-done.12.refs_3_), channel_id=1, source_target_pairs={{0,4},{1,3},{4,8},{5,1},{8,12},{9,5},{12,14},{13,9},{14,10},{15,13... | collective-permute-start | bytes 393224 | tf_op jit(solution)/shard_map/ppermute | solution.py:47
  21.8 1.6 %collective-permute-start.3 = (f32[2,4,16,512]{3,2,1,0:T(8,128)S(1)}, f32[2,4,16,512]{3,2,1,0:T(8,128)S(1)}, u32[]{:S(2)}, u32[]{:S(2)}) collective-permute-start(f32[2,4,16,512]{3,2,1,0:T(8,128)S(1)} %collective-permute-done.1.refs_1_), channel_id=1, source_target_pairs={{0,4},{1,3},{4,8},{5,1},{8,12},{9,5},{12,14},{13,9},{14,10},{15,13... | collective-permute-start | bytes 786440 | tf_op jit(solution)/shard_map/ppermute | solution.py:47
  23.5 1.6 %collective-permute-start.28 = (f32[512,256]{1,0:T(8,128)S(1)}, f32[512,256]{1,0:T(8,128)S(1)}, u32[]{:S(2)}, u32[]{:S(2)}) collective-permute-start(f32[512,256]{1,0:T(8,128)S(1)} %slice.44.refs_18_), channel_id=1, source_target_pairs={{16,0},{0,16},{17,1},{1,17},{18,2},{2,18},{19,3},{3,19},{20,4},{4,... | collective-permute-start | bytes 1572872 | tf_op jit(solution)/shard_map/ppermute | solution.py:156
  25.6 1.5 %collective-permute-start.24 = (f32[2,6,16,256]{3,2,1,0:T(8,128)S(1)}, f32[2,6,16,256]{3,2,1,0:T(8,128)S(1)}, u32[]{:S(2)}, u32[]{:S(2)}) collective-permute-start(f32[2,6,16,256]{3,2,1,0:T(8,128)S(1)} %collective-permute-done.22.refs_12_), channel_id=1, source_target_pairs={{0,4},{1,3},{4,8},{5,1},{8,12},{9,5},{12,14},{13,9},{14,10},{15,13... | collective-permute-start | bytes 589832 | tf_op jit(solution)/shard_map/ppermute | solution.py:47
  27.1 1.2 %collective-permute-done.3.refs_3_ = f32[2,4,16,512]{3,2,1,0:T(8,128)S(1)} collective-permute-done((f32[2,4,16,512]{3,2,1,0:T(8,128)S(1)}, f32[2,4,16,512]{3,2,1,0:T(8,128)S(1)}, u32[]{:S(2)}, u32[]{:S(2)}) %collective-permute-start.3) | collective-permute-done | bytes 262176 | tf_op jit(solution)/shard_map/ppermute | solution.py:47
  28.2 1.6 %collective-permute-start.16 = (f32[4,16,256]{2,1,0:T(8,128)S(1)}, f32[4,16,256]{2,1,0:T(8,128)S(1)}, u32[]{:S(2)}, u32[]{:S(2)}) collective-permute-start(f32[4,16,256]{2,1,0:T(8,128)S(1)} %slice_bitcast_fusion.4), channel_id=1, source_target_pairs={{0,4},{1,3},{4,8},{5,1},{8,12},{9,5},{12,14},{13,9},{14,10},{15,13... | collective-permute-start | bytes 196616 | tf_op jit(solution)/shard_map/ppermute | solution.py:47
  29.8 1.4 %collective-permute-done.24.refs_14_ = f32[2,6,16,256]{3,2,1,0:T(8,128)S(1)} collective-permute-done((f32[2,6,16,256]{3,2,1,0:T(8,128)S(1)}, f32[2,6,16,256]{3,2,1,0:T(8,128)S(1)}, u32[]{:S(2)}, u32[]{:S(2)}) %collective-permute-start.24) | collective-permute-done | bytes 196640 | tf_op jit(solution)/shard_map/ppermute | solution.py:47
  31.2 1.5 %collective-permute-start.5 = (f32[2,4,16,512]{3,2,1,0:T(8,128)S(1)}, f32[2,4,16,512]{3,2,1,0:T(8,128)S(1)}, u32[]{:S(2)}, u32[]{:S(2)}) collective-permute-start(f32[2,4,16,512]{3,2,1,0:T(8,128)S(1)} %collective-permute-done.3.refs_3_), channel_id=1, source_target_pairs={{0,4},{1,3},{4,8},{5,1},{8,12},{9,5},{12,14},{13,9},{14,10},{15,13... | collective-permute-start | bytes 786440 | tf_op jit(solution)/shard_map/ppermute | solution.py:47
  32.7 1.4 %collective-permute-start.26 = (f32[6,16,256]{2,1,0:T(8,128)S(1)}, f32[6,16,256]{2,1,0:T(8,128)S(1)}, u32[]{:S(2)}, u32[]{:S(2)}) collective-permute-start(f32[6,16,256]{2,1,0:T(8,128)S(1)} %slice_bitcast_fusion.3), channel_id=1, source_target_pairs={{0,4},{1,3},{4,8},{5,1},{8,12},{9,5},{12,14},{13,9},{14,10},{15,13... | collective-permute-start | bytes 294920 | tf_op jit(solution)/shard_map/ppermute | solution.py:47
  34.7 1.4 %collective-permute-done.28.refs_19_ = f32[512,256]{1,0:T(8,128)S(1)} collective-permute-done((f32[512,256]{1,0:T(8,128)S(1)}, f32[512,256]{1,0:T(8,128)S(1)}, u32[]{:S(2)}, u32[]{:S(2)}) %collective-permute-start.28) | collective-permute-done | bytes 524320 | tf_op jit(solution)/shard_map/ppermute | solution.py:156
  36.6 2.1 %collective-permute-done.26.refs_16_ = f32[6,16,256]{2,1,0:T(8,128)S(1)} collective-permute-done((f32[6,16,256]{2,1,0:T(8,128)S(1)}, f32[6,16,256]{2,1,0:T(8,128)S(1)}, u32[]{:S(2)}, u32[]{:S(2)}) %collective-permute-start.26) | collective-permute-done | bytes 98336 | tf_op jit(solution)/shard_map/ppermute | solution.py:47
  39.3 1.5 %collective-permute-start.7 = (f32[4,16,512]{2,1,0:T(8,128)S(1)}, f32[4,16,512]{2,1,0:T(8,128)S(1)}, u32[]{:S(2)}, u32[]{:S(2)}) collective-permute-start(f32[4,16,512]{2,1,0:T(8,128)S(1)} %slice_bitcast_fusion), channel_id=1, source_target_pairs={{0,4},{1,3},{4,8},{5,1},{8,12},{9,5},{12,14},{13,9},{14,10},{15,13... | collective-permute-start | bytes 393224 | tf_op jit(solution)/shard_map/ppermute | solution.py:47
  41.4 3.0 %collective-permute-done.7.refs_7_ = f32[4,16,512]{2,1,0:T(8,128)S(1)} collective-permute-done((f32[4,16,512]{2,1,0:T(8,128)S(1)}, f32[4,16,512]{2,1,0:T(8,128)S(1)}, u32[]{:S(2)}, u32[]{:S(2)}) %collective-permute-start.7) | collective-permute-done | bytes 131104 | tf_op jit(solution)/shard_map/ppermute | solution.py:47
  44.3 2.7 %solve.1.refs_10_ = f32[4,256,256]{2,1,0:T(8,128)S(1)} custom-call(f32[2,4,16,256]{3,2,1,0:T(8,128)S(1)} %pad_maximum_fusion.2.refs_0_, f32[2,4,16,256]{3,2,1,0:T(8,128)S(1)} %collective-permute-done.10.refs_1_, f32[2,4,16,256]{3,2,1,0:T(8,128)S(1)} %collective-permute-done.11.refs_2_, f32[2,4,16,256]{3,2,1,0:T(8,128)S(1)} %collective-permute-done.12.refs_3_, ...), custom_call_target="tpu_custom_call" | custom-call | flops 1006632960 | bytes 6291456 | tf_op jit(solution)/shard_map/solve/pallas_call | solution.py:177
  47.1 2.2 %update.1 = f32[1024,256]{1,0:T(8,128)} custom-call(f32[2,4,16,512]{3,2,1,0:T(8,128)S(1)} %pad_maximum_fusion.refs_0_, f32[2,4,16,512]{3,2,1,0:T(8,128)S(1)} %collective-permute-done.1.refs_1_, f32[2,4,16,512]{3,2,1,0:T(8,128)S(1)} %collective-permute-done.2.refs_2_, f32[2,4,16,512]{3,2,1,0:T(8,128)S(1)} %collective-permute-done.3.refs_3_, ...), custom_call_target="tpu_custom_call" | custom-call | flops 805306368 | bytes 6291456 | tf_op jit(solution)/shard_map/update/pallas_call | solution.py:191
  (55 shorter events, 6.2 us)
Async XLA Ops:
  0.0 12.0 %collective-permute-start = (f32[4,16,1024]{2,1,0:T(8,128)}, f32[4,16,1024]{2,1,0:T(8,128)S(1)}, u32[]{:S(2)}, u32[]{:S(2)}) collective-permute-start(f32[4,16,1024]{2,1,0:T(8,128)} %param.4), channel_id=1, source_target_pairs={{0,1},{1,0},{2,3},{3,2},{4,5},{5,4},{6,7},{7,6},{8,9},{9,8},{10,11... | collective-permute-start | bytes 786440 | tf_op jit(solution)/shard_map/ppermute | solution.py:151
  1.4 6.0 %collective-permute-start.18 = (f32[3,16,512]{2,1,0:T(8,128)S(1)}, f32[3,16,512]{2,1,0:T(8,128)S(1)}, u32[]{:S(2)}, u32[]{:S(2)}) collective-permute-start(f32[3,16,512]{2,1,0:T(8,128)S(1)} %slice.39), channel_id=1, source_target_pairs={{16,0},{0,16},{17,1},{1,17},{18,2},{2,18},{19,3},{3,19},{20,4},{4,... | collective-permute-start | bytes 294920 | tf_op jit(solution)/shard_map/ppermute | solution.py:154
  3.9 4.5 %collective-permute-start.9 = (f32[4,16,256]{2,1,0:T(8,128)S(1)}, f32[4,16,256]{2,1,0:T(8,128)S(1)}, u32[]{:S(2)}, u32[]{:S(2)}) collective-permute-start(f32[4,16,256]{2,1,0:T(8,128)S(1)} %copy-done.1), channel_id=1, source_target_pairs={{0,1},{1,0},{2,3},{3,2},{4,5},{5,4},{6,7},{7,6},{8,9},{9,8},{10,11... | collective-permute-start | bytes 196616 | tf_op jit(solution)/shard_map/ppermute | solution.py:150
  8.5 5.2 %collective-permute-start.10 = (f32[2,4,16,256]{3,2,1,0:T(8,128)S(1)}, f32[2,4,16,256]{3,2,1,0:T(8,128)S(1)}, u32[]{:S(2)}, u32[]{:S(2)}) collective-permute-start(f32[2,4,16,256]{3,2,1,0:T(8,128)S(1)} %pad_maximum_fusion.2.refs_0_), channel_id=1, source_target_pairs={{0,4},{1,3},{4,8},{5,1},{8,12},{9,5},{12,14},{13,9},{14,10},{15,13... | collective-permute-start | bytes 393224 | tf_op jit(solution)/shard_map/ppermute | solution.py:47
  10.3 5.7 %collective-permute-start.20 = (f32[2,6,16,256]{3,2,1,0:T(8,128)S(1)}, f32[2,6,16,256]{3,2,1,0:T(8,128)S(1)}, u32[]{:S(2)}, u32[]{:S(2)}) collective-permute-start(f32[2,6,16,256]{3,2,1,0:T(8,128)S(1)} %pad_maximum_fusion.1.refs_9_), channel_id=1, source_target_pairs={{0,4},{1,3},{4,8},{5,1},{8,12},{9,5},{12,14},{13,9},{14,10},{15,13... | collective-permute-start | bytes 589832 | tf_op jit(solution)/shard_map/ppermute | solution.py:47
  12.0 9.8 %collective-permute-start.1 = (f32[2,4,16,512]{3,2,1,0:T(8,128)S(1)}, f32[2,4,16,512]{3,2,1,0:T(8,128)S(1)}, u32[]{:S(2)}, u32[]{:S(2)}) collective-permute-start(f32[2,4,16,512]{3,2,1,0:T(8,128)S(1)} %pad_maximum_fusion.refs_0_), channel_id=1, source_target_pairs={{0,4},{1,3},{4,8},{5,1},{8,12},{9,5},{12,14},{13,9},{14,10},{15,13... | collective-permute-start | bytes 786440 | tf_op jit(solution)/shard_map/ppermute | solution.py:47
  13.6 6.6 %collective-permute-start.12 = (f32[2,4,16,256]{3,2,1,0:T(8,128)S(1)}, f32[2,4,16,256]{3,2,1,0:T(8,128)S(1)}, u32[]{:S(2)}, u32[]{:S(2)}) collective-permute-start(f32[2,4,16,256]{3,2,1,0:T(8,128)S(1)} %collective-permute-done.10.refs_1_), channel_id=1, source_target_pairs={{0,4},{1,3},{4,8},{5,1},{8,12},{9,5},{12,14},{13,9},{14,10},{15,13... | collective-permute-start | bytes 393224 | tf_op jit(solution)/shard_map/ppermute | solution.py:47
  16.1 9.5 %collective-permute-start.22 = (f32[2,6,16,256]{3,2,1,0:T(8,128)S(1)}, f32[2,6,16,256]{3,2,1,0:T(8,128)S(1)}, u32[]{:S(2)}, u32[]{:S(2)}) collective-permute-start(f32[2,6,16,256]{3,2,1,0:T(8,128)S(1)} %collective-permute-done.20.refs_10_), channel_id=1, source_target_pairs={{0,4},{1,3},{4,8},{5,1},{8,12},{9,5},{12,14},{13,9},{14,10},{15,13... | collective-permute-start | bytes 589832 | tf_op jit(solution)/shard_map/ppermute | solution.py:47
  20.3 5.0 %collective-permute-start.14 = (f32[2,4,16,256]{3,2,1,0:T(8,128)S(1)}, f32[2,4,16,256]{3,2,1,0:T(8,128)S(1)}, u32[]{:S(2)}, u32[]{:S(2)}) collective-permute-start(f32[2,4,16,256]{3,2,1,0:T(8,128)S(1)} %collective-permute-done.12.refs_3_), channel_id=1, source_target_pairs={{0,4},{1,3},{4,8},{5,1},{8,12},{9,5},{12,14},{13,9},{14,10},{15,13... | collective-permute-start | bytes 393224 | tf_op jit(solution)/shard_map/ppermute | solution.py:47
  21.8 6.4 %collective-permute-start.3 = (f32[2,4,16,512]{3,2,1,0:T(8,128)S(1)}, f32[2,4,16,512]{3,2,1,0:T(8,128)S(1)}, u32[]{:S(2)}, u32[]{:S(2)}) collective-permute-start(f32[2,4,16,512]{3,2,1,0:T(8,128)S(1)} %collective-permute-done.1.refs_1_), channel_id=1, source_target_pairs={{0,4},{1,3},{4,8},{5,1},{8,12},{9,5},{12,14},{13,9},{14,10},{15,13... | collective-permute-start | bytes 786440 | tf_op jit(solution)/shard_map/ppermute | solution.py:47
  23.5 12.6 %collective-permute-start.28 = (f32[512,256]{1,0:T(8,128)S(1)}, f32[512,256]{1,0:T(8,128)S(1)}, u32[]{:S(2)}, u32[]{:S(2)}) collective-permute-start(f32[512,256]{1,0:T(8,128)S(1)} %slice.44.refs_18_), channel_id=1, source_target_pairs={{16,0},{0,16},{17,1},{1,17},{18,2},{2,18},{19,3},{3,19},{20,4},{4,... | collective-permute-start | bytes 1572872 | tf_op jit(solution)/shard_map/ppermute | solution.py:156
  25.1 7.7 %collective-permute-start.11 = (f32[2,4,16,256]{3,2,1,0:T(8,128)S(1)}, f32[2,4,16,256]{3,2,1,0:T(8,128)S(1)}, u32[]{:S(2)}, u32[]{:S(2)}) collective-permute-start(f32[2,4,16,256]{3,2,1,0:T(8,128)S(1)} %collective-permute-done.10.refs_1_), channel_id=1, source_target_pairs={{0,1},{1,0},{2,3},{3,2},{4,5},{5,4},{6,7},{7,6},{8,9},{9,8},{10,11... | collective-permute-start | bytes 393224 | tf_op jit(solution)/shard_map/ppermute | solution.py:48
  25.2 8.9 %collective-permute-start.13 = (f32[2,4,16,256]{3,2,1,0:T(8,128)S(1)}, f32[2,4,16,256]{3,2,1,0:T(8,128)S(1)}, u32[]{:S(2)}, u32[]{:S(2)}) collective-permute-start(f32[2,4,16,256]{3,2,1,0:T(8,128)S(1)} %collective-permute-done.12.refs_3_), channel_id=1, source_target_pairs={{0,1},{1,0},{2,3},{3,2},{4,5},{5,4},{6,7},{7,6},{8,9},{9,8},{10,11... | collective-permute-start | bytes 393224 | tf_op jit(solution)/shard_map/ppermute | solution.py:48
  25.6 5.7 %collective-permute-start.24 = (f32[2,6,16,256]{3,2,1,0:T(8,128)S(1)}, f32[2,6,16,256]{3,2,1,0:T(8,128)S(1)}, u32[]{:S(2)}, u32[]{:S(2)}) collective-permute-start(f32[2,6,16,256]{3,2,1,0:T(8,128)S(1)} %collective-permute-done.22.refs_12_), channel_id=1, source_target_pairs={{0,4},{1,3},{4,8},{5,1},{8,12},{9,5},{12,14},{13,9},{14,10},{15,13... | collective-permute-start | bytes 589832 | tf_op jit(solution)/shard_map/ppermute | solution.py:47
  28.2 5.9 %collective-permute-start.16 = (f32[4,16,256]{2,1,0:T(8,128)S(1)}, f32[4,16,256]{2,1,0:T(8,128)S(1)}, u32[]{:S(2)}, u32[]{:S(2)}) collective-permute-start(f32[4,16,256]{2,1,0:T(8,128)S(1)} %slice_bitcast_fusion.4), channel_id=1, source_target_pairs={{0,4},{1,3},{4,8},{5,1},{8,12},{9,5},{12,14},{13,9},{14,10},{15,13... | collective-permute-start | bytes 196616 | tf_op jit(solution)/shard_map/ppermute | solution.py:47
  31.2 7.4 %collective-permute-start.5 = (f32[2,4,16,512]{3,2,1,0:T(8,128)S(1)}, f32[2,4,16,512]{3,2,1,0:T(8,128)S(1)}, u32[]{:S(2)}, u32[]{:S(2)}) collective-permute-start(f32[2,4,16,512]{3,2,1,0:T(8,128)S(1)} %collective-permute-done.3.refs_3_), channel_id=1, source_target_pairs={{0,4},{1,3},{4,8},{5,1},{8,12},{9,5},{12,14},{13,9},{14,10},{15,13... | collective-permute-start | bytes 786440 | tf_op jit(solution)/shard_map/ppermute | solution.py:47
  32.7 5.9 %collective-permute-start.26 = (f32[6,16,256]{2,1,0:T(8,128)S(1)}, f32[6,16,256]{2,1,0:T(8,128)S(1)}, u32[]{:S(2)}, u32[]{:S(2)}) collective-permute-start(f32[6,16,256]{2,1,0:T(8,128)S(1)} %slice_bitcast_fusion.3), channel_id=1, source_target_pairs={{0,4},{1,3},{4,8},{5,1},{8,12},{9,5},{12,14},{13,9},{14,10},{15,13... | collective-permute-start | bytes 294920 | tf_op jit(solution)/shard_map/ppermute | solution.py:47
  34.1 5.1 %collective-permute-start.21 = (f32[2,6,16,256]{3,2,1,0:T(8,128)S(1)}, f32[2,6,16,256]{3,2,1,0:T(8,128)S(1)}, u32[]{:S(2)}, u32[]{:S(2)}) collective-permute-start(f32[2,6,16,256]{3,2,1,0:T(8,128)S(1)} %collective-permute-done.20.refs_10_), channel_id=1, source_target_pairs={{0,1},{1,0},{2,3},{3,2},{4,5},{5,4},{6,7},{7,6},{8,9},{9,8},{10,11... | collective-permute-start | bytes 589832 | tf_op jit(solution)/shard_map/ppermute | solution.py:48
  36.1 4.7 %collective-permute-start.23 = (f32[2,6,16,256]{3,2,1,0:T(8,128)S(1)}, f32[2,6,16,256]{3,2,1,0:T(8,128)S(1)}, u32[]{:S(2)}, u32[]{:S(2)}) collective-permute-start(f32[2,6,16,256]{3,2,1,0:T(8,128)S(1)} %collective-permute-done.22.refs_12_), channel_id=1, source_target_pairs={{0,1},{1,0},{2,3},{3,2},{4,5},{5,4},{6,7},{7,6},{8,9},{9,8},{10,11... | collective-permute-start | bytes 589832 | tf_op jit(solution)/shard_map/ppermute | solution.py:48
  38.7 5.7 %collective-permute-start.25 = (f32[2,6,16,256]{3,2,1,0:T(8,128)S(1)}, f32[2,6,16,256]{3,2,1,0:T(8,128)S(1)}, u32[]{:S(2)}, u32[]{:S(2)}) collective-permute-start(f32[2,6,16,256]{3,2,1,0:T(8,128)S(1)} %collective-permute-done.24.refs_14_), channel_id=1, source_target_pairs={{0,1},{1,0},{2,3},{3,2},{4,5},{5,4},{6,7},{7,6},{8,9},{9,8},{10,11... | collective-permute-start | bytes 589832 | tf_op jit(solution)/shard_map/ppermute | solution.py:48
  39.2 7.8 %collective-permute-start.2 = (f32[2,4,16,512]{3,2,1,0:T(8,128)S(1)}, f32[2,4,16,512]{3,2,1,0:T(8,128)S(1)}, u32[]{:S(2)}, u32[]{:S(2)}) collective-permute-start(f32[2,4,16,512]{3,2,1,0:T(8,128)S(1)} %collective-permute-done.1.refs_1_), channel_id=1, source_target_pairs={{0,1},{1,0},{2,3},{3,2},{4,5},{5,4},{6,7},{7,6},{8,9},{9,8},{10,11... | collective-permute-start | bytes 786440 | tf_op jit(solution)/shard_map/ppermute | solution.py:48
  39.3 5.0 %collective-permute-start.7 = (f32[4,16,512]{2,1,0:T(8,128)S(1)}, f32[4,16,512]{2,1,0:T(8,128)S(1)}, u32[]{:S(2)}, u32[]{:S(2)}) collective-permute-start(f32[4,16,512]{2,1,0:T(8,128)S(1)} %slice_bitcast_fusion), channel_id=1, source_target_pairs={{0,4},{1,3},{4,8},{5,1},{8,12},{9,5},{12,14},{13,9},{14,10},{15,13... | collective-permute-start | bytes 393224 | tf_op jit(solution)/shard_map/ppermute | solution.py:47
  40.8 6.2 %collective-permute-start.4 = (f32[2,4,16,512]{3,2,1,0:T(8,128)S(1)}, f32[2,4,16,512]{3,2,1,0:T(8,128)S(1)}, u32[]{:S(2)}, u32[]{:S(2)}) collective-permute-start(f32[2,4,16,512]{3,2,1,0:T(8,128)S(1)} %collective-permute-done.3.refs_3_), channel_id=1, source_target_pairs={{0,1},{1,0},{2,3},{3,2},{4,5},{5,4},{6,7},{7,6},{8,9},{9,8},{10,11... | collective-permute-start | bytes 786440 | tf_op jit(solution)/shard_map/ppermute | solution.py:48
  40.9 6.2 %collective-permute-start.6 = (f32[2,4,16,512]{3,2,1,0:T(8,128)S(1)}, f32[2,4,16,512]{3,2,1,0:T(8,128)S(1)}, u32[]{:S(2)}, u32[]{:S(2)}) collective-permute-start(f32[2,4,16,512]{3,2,1,0:T(8,128)S(1)} %collective-permute-done.5.refs_5_), channel_id=1, source_target_pairs={{0,1},{1,0},{2,3},{3,2},{4,5},{5,4},{6,7},{7,6},{8,9},{9,8},{10,11... | collective-permute-start | bytes 786440 | tf_op jit(solution)/shard_map/ppermute | solution.py:48
  (7 other events, 31.1 us)

commit v2 on v1

v2 whole, which is shorter than its diff:
```python
import functools

import jax
import jax.numpy as jnp
from jax import lax
from jax.experimental import pallas as pl
from jax.experimental.pallas import tpu as pltpu
from jax.sharding import PartitionSpec as P

ROWS = ((0,), (0,))
PLAIN = ((1,), (0,))


def ring_place(chip, chips):
    return jnp.where(chip % 2 == 0, chip // 2, chips - 1 - chip // 2)


def ring_chip(place, chips):
    up = 2 * place
    down = 2 * (chips - 1 - place) + 1
    if isinstance(place, int):
        return up if place < chips // 2 else down
    return jnp.where(place < chips // 2, up, down)


def split(value):
    high = value.astype(jnp.bfloat16)
    low = (value - high.astype(jnp.float32)).astype(jnp.bfloat16)
    return high, low


def dot3(left, right, dims):
    mult = functools.partial(
        lax.dot_general, dimension_numbers=(dims, ((), ())), preferred_element_type=jnp.float32
    )
    return mult(left[0], right[0]) + (mult(left[0], right[1]) + mult(left[1], right[0]))


def kernel_call(body, out_shapes, scratch, operands, flops=0):
    vmem = pl.BlockSpec(memory_space=pltpu.VMEM)
    return pl.pallas_call(
        body,
        out_shape=out_shapes,
        in_specs=[vmem] * len(operands),
        out_specs=jax.tree.map(lambda _: vmem, out_shapes),
        scratch_shapes=scratch,
        cost_estimate=pl.CostEstimate(flops=flops, bytes_accessed=4 << 20, transcendentals=0),
        compiler_params=pltpu.CompilerParams(vmem_limit_bytes=20 << 20),
    )(*operands)


def ring(first, chips):
    steps = chips // 2
    nearest = []
    for place in range(chips):
        here = ring_chip(place, chips)
        nearest.append((2 * here, 2 * ring_chip((place + 1) % chips, chips)))
        nearest.append((2 * here + 1, 2 * ring_chip((place - 1) % chips, chips) + 1))
    swap = [(i, i ^ 1) for i in range(2 * chips)]
    moving = first
    pieces = [first]
    for step in range(1, steps + 1):
        moving = lax.ppermute(moving if step < steps else moving[0], "col", nearest)
        pieces += [moving, lax.ppermute(moving, "col", swap)]
    return pieces


def streams(chips):
    core = lax.axis_index("col") % 2
    here = ring_place(lax.axis_index("col") // 2, chips)
    found = [(lax.axis_index("col") // 2, core)]
    for step in range(1, chips // 2 + 1):
        turn = step * (1 - 2 * core)
        found.append((ring_chip((here - turn + chips) % chips, chips), core))
        found.append((ring_chip((here + turn + chips) % chips, chips), 1 - core))
    return found


def assemble(piece_refs, high_ref, low_ref, whole_ref, chips):
    depth = piece_refs[0].shape[2]

    def put(row, value):
        rows = pl.ds(pl.multiple_of(row, value.shape[1]), value.shape[1])
        if depth % 16 == 0:
            high_ref[:, rows, :], low_ref[:, rows, :] = split(value)
        else:
            whole_ref[:, rows, :] = value

    for at, (chip, core) in enumerate(streams(chips)):
        ref = piece_refs[at]
        if depth % 16 == 0:
            if at < chips - 1:
                for half in range(2):
                    put((2 * chip + half) * depth, ref[jnp.where(core == 0, half, 1 - half)])
            else:
                put((2 * chip + core) * depth, ref[...])
            continue
        if at == chips:
            continue
        pair = [ref[0], ref[1]] if at < chips - 1 else [ref[...], piece_refs[at + 1][...]]
        low, high = jnp.where(core == 0, pair[0], pair[1]), jnp.where(core == 0, pair[1], pair[0])
        put(2 * chip * depth, jnp.concatenate([low, high], axis=1))
    if depth % 16 != 0:
        high_ref[...], low_ref[...] = split(whole_ref[...])


def split_scratch(count, nb, depth):
    whole = (count, nb, nb) if depth % 16 != 0 else (1, 8, nb)
    return [
        pltpu.VMEM((count, nb, nb), jnp.bfloat16),
        pltpu.VMEM((count, nb, nb), jnp.bfloat16),
        pltpu.VMEM(whole, jnp.float32),
    ]


class Plan:
    def __init__(self, group_count, chips, panels, nb, rows):
        self.group_count, self.chips, self.panels, self.nb = group_count, chips, panels, nb
        self.held = -(-panels // group_count)
        self.sure = panels // group_count
        self.wide = rows // nb - self.sure
        self.tri = [(rank, panel) for rank in range(1, panels) for panel in range(rank)]
        self.deep = max(
            min(rank, panels - 1) for rank in range((self.held - 1) * group_count, self.held * group_count)
        )
        sizes = [
            max(panels + self.wide * s, len(self.tri) + self.wide * (panels - s)) for s in range(panels + 1)
        ]
        self.early = panels - sizes[::-1].index(min(sizes))
        self.first = panels + self.wide * self.early
        self.second = len(self.tri) + self.wide * (panels - self.early)

    def chosen(self, owner, sources):
        me = lax.axis_index("row")
        value = sources[0]
        for shift in range(1, self.group_count):
            value = jnp.where((me + shift) % self.group_count == owner, sources[shift], value)
        return value

    def panel_rows(self, rank, right_ref, received):
        local, owner = divmod(rank, self.group_count)
        rows = slice(local * self.nb, (local + 1) * self.nb)
        return self.chosen(owner, [right_ref[rows]] + [r[rows] for r in received])


def first_kernel(plan, inv_ref, inv_other, factor_ref, factor_other, out_ref):
    for side, (inv, factor) in enumerate(((inv_ref, factor_ref), (inv_other, factor_other))):
        out_ref[side, : plan.panels] = inv[...]
        for panel in range(plan.early):
            for block in range(plan.wide):
                at = (plan.sure + block) * plan.nb
                to = plan.panels + panel * plan.wide + block
                out_ref[side, to] = factor[panel, :, at : at + plan.nb]


def tri_kernel(plan, *refs):
    *sources, out_ref = refs
    for at, (rank, panel) in enumerate(plan.tri):
        local, owner = divmod(rank, plan.group_count)
        part = slice(local * plan.nb, (local + 1) * plan.nb)
        out_ref[at] = plan.chosen(owner, [source[panel, :, part] for source in sources])


def second_kernel(plan, tri_ref, tri_other, factor_ref, factor_other, out_ref):
    for side, (tri, factor) in enumerate(((tri_ref, factor_ref), (tri_other, factor_other))):
        out_ref[side, : len(plan.tri)] = tri[...]
        for panel in range(plan.early, plan.panels):
            for block in range(plan.wide):
                at = (plan.sure + block) * plan.nb
                to = len(plan.tri) + (panel - plan.early) * plan.wide + block
                out_ref[side, to] = factor[panel, :, at : at + plan.nb]


def below(plan, panel, block, mats, start):
    at = start + panel * plan.wide + block
    return mats[0][at], mats[1][at]


def prep_kernel(plan, *refs):
    pieces, right_ref = refs[: plan.chips + 1], refs[plan.chips + 1]
    received = refs[plan.chips + 2 : -5]
    high_ref, low_ref, x_ref, total_ref, whole_ref = refs[-5:]
    assemble(pieces, high_ref, low_ref, whole_ref, plan.chips)
    answer = dot3(
        (high_ref[0], low_ref[0]), split(plan.panel_rows(0, right_ref, received)), PLAIN
    )
    x_ref[...] = answer
    solved = split(answer)
    for block in range(plan.wide):
        rows = slice(block * plan.nb, (block + 1) * plan.nb)
        total = right_ref[plan.sure * plan.nb + block * plan.nb : plan.sure * plan.nb + (block + 1) * plan.nb]
        total_ref[rows] = total - dot3(below(plan, 0, block, (high_ref, low_ref), plan.panels), solved, ROWS)


def final_kernel(plan, *refs):
    pieces = refs[: plan.chips + 1]
    first_high, first_low, x_first, total_ref, right_ref = refs[plan.chips + 1 : plan.chips + 6]
    received = refs[plan.chips + 6 : -5]
    out_ref, x_ref, high_ref, low_ref, whole_ref = refs[-5:]
    panels, nb, wide = plan.panels, plan.nb, plan.wide
    assemble(pieces, high_ref, low_ref, whole_ref, plan.chips)
    x_ref[0] = x_first[...]
    solved = [split(x_first[...])]
    for panel in range(1, panels):
        current = plan.panel_rows(panel, right_ref, received)
        for before in range(panel):
            tri = plan.tri.index((panel, before))
            current = current - dot3((high_ref[tri], low_ref[tri]), solved[before], ROWS)
        answer = dot3((first_high[panel], first_low[panel]), split(current), PLAIN)
        x_ref[panel] = answer
        solved.append(split(answer))
    for block in range(wide):
        total = total_ref[block * nb : (block + 1) * nb]
        for panel in range(1, panels):
            if panel < plan.early:
                mat = below(plan, panel, block, (first_high, first_low), panels)
            else:
                mat = below(plan, panel - plan.early, block, (high_ref, low_ref), len(plan.tri))
            total = total - dot3(mat, solved[panel], ROWS)
        out_ref[(plan.sure + block) * nb : (plan.sure + block + 1) * nb] = total
    for local in range(plan.held):
        rank = local * plan.group_count + lax.axis_index("row")

        @pl.when(rank < panels)
        def _(rank=rank, local=local):
            out_ref[local * nb : (local + 1) * nb] = x_ref[rank]


def per_device(right_side, factor_panels, inverses):
    group_count = lax.axis_size("row")
    chips = lax.axis_size("col") // 2
    panels, depth, rows = factor_panels.shape
    nb = inverses.shape[2]
    columns = right_side.shape[1]
    plan = Plan(group_count, chips, panels, nb, rows)
    swap = [(i, i ^ 1) for i in range(2 * chips)]
    shifts = [
        [((g + shift) % group_count, g) for g in range(group_count)] for shift in range(1, group_count)
    ]
    f32, bf16 = jnp.float32, jnp.bfloat16
    shape = jax.ShapeDtypeStruct
    bound = functools.partial

    inverses_other = lax.ppermute(inverses, "col", swap)
    factor_other = lax.ppermute(factor_panels, "col", swap)
    own = factor_panels[: plan.deep, :, : plan.held * nb]
    tri = [own] + [lax.ppermute(own, "row", pairs) for pairs in shifts]
    above = right_side[: plan.held * nb]
    received = [lax.ppermute(above, "row", pairs) for pairs in shifts]

    first = kernel_call(
        bound(first_kernel, plan),
        shape((2, plan.first, depth, nb), f32),
        [],
        (inverses, inverses_other, factor_panels, factor_other),
    )
    half = kernel_call(bound(tri_kernel, plan), shape((len(plan.tri), depth, nb), f32), [], tri)
    half_other = lax.ppermute(half, "col", swap)
    second = kernel_call(
        bound(second_kernel, plan),
        shape((2, plan.second, depth, nb), f32),
        [],
        (half, half_other, factor_panels, factor_other),
    )
    first_pieces = ring(first, chips)
    second_pieces = ring(second, chips)

    high, low, x_first, total = kernel_call(
        bound(prep_kernel, plan),
        [
            shape((plan.first, nb, nb), bf16),
            shape((plan.first, nb, nb), bf16),
            shape((nb, columns), f32),
            shape((plan.wide * nb, columns), f32),
        ],
        split_scratch(plan.first, nb, depth)[2:],
        (*first_pieces, right_side, *received),
        flops=6 * 3 * nb * nb * columns,
    )
    return kernel_call(
        bound(final_kernel, plan),
        shape(right_side.shape, f32),
        [pltpu.VMEM((panels, nb, columns), f32)] + split_scratch(plan.second, nb, depth),
        (*second_pieces, high, low, x_first, total, right_side, *received),
        flops=6 * 15 * nb * nb * columns,
    )


def solution(mesh):
    in_specs = (P("row", "col"), P(None, "col", "row"), P(None, "col", None))
    out_specs = P("row", "col")

    return jax.shard_map(per_device, mesh=mesh, in_specs=in_specs, out_specs=out_specs, check_vma=False)
```

time: 49.5 us -> 49.3 us (level)
  waiting for transfers between devices: 15 us -> 19.9 us
  starting transfers between devices: 26.3 us -> 22.3 us
  other arithmetic: 0.97 us -> 0 us
    ppermute x1, waiting for transfers between devices: 1.45 us -> 4.8 us  [per_device(): received = [lax.ppermute(above, 'row', pairs) for pairs in shifts]]
    ppermute x12 -> x8, starting transfers between devices: 19 us -> 16.8 us  [ring(): moving = lax.ppermute(moving if step < steps else moving[0], 'col', nearest)]
    unnamed x4 -> x8, local copies, waits for them, and re-layouts: 0.01 us -> 1.8 us
    ppermute x3, starting transfers between devices: 2.8 us -> 1.71 us  [the longest x1 1.58 us: per_device(): tri = [own] + [lax.ppermute(own, 'row', pairs) for pairs in shifts]]
    another operation x2 -> x0, local copies, waits for them, and re-layouts: 0.92 us -> none  [per_device(): jnp.stack([factor_panels[:, :, sure:], factor_other[:, :, sure:]])]
    select_n x2 -> x0, other arithmetic: 0.91 us -> none  [per_device(): value = jnp.where((me + shift) % group_count == owner, tri[shift], value)]
    slice x4 -> x2, local copies, waits for them, and re-layouts: 0.94 us -> 0.04 us  [the longest x1 0.03 us: per_device(): above = right_side[:plan.held * nb]]
    ppermute x12 -> x8, waiting for transfers between devices: 0.03 us -> 0.88 us  [ring(): pieces += [moving, lax.ppermute(moving, 'col', swap)]]
  transfers between devices with their start and end apart: 29 -> 21, of which waited for: 9 -> 10; matrix products, arithmetic and copies ran while one was open for 6% -> 0% of each run, Pallas kernels for 5% -> 2%
where the time goes in v2:
time: 49.3 us; the launch traced here: 49.2 us
  starting transfers between devices  22.3 us (45%)
  waiting for transfers between devices  19.9 us (40%)
  Pallas kernels  5.02 us (10%)
  local copies, waits for them, and re-layouts  1.86 us (4%)
    ppermute x8, starting transfers between devices, ring(): moving = lax.ppermute(moving if step < steps else moving[0], 'col', nearest)  16.8 us
    ppermute x8, waiting for transfers between devices, ring(): moving = lax.ppermute(moving if step < steps else moving[0], 'col', nearest)  11.5 us
    pallas_call x5, Pallas kernels, kernel_call(): pl.pallas_call(body, out_shape=out_shapes, in_specs=[vmem] * len(operands...  5.02 us
    ppermute x1, waiting for transfers between devices, per_device(): received = [lax.ppermute(above, 'row', pairs) for pairs in shifts]  4.8 us
    unnamed x8, local copies, waits for them, and re-layouts  1.8 us
    ppermute x8, starting transfers between devices, ring(): pieces += [moving, lax.ppermute(moving, 'col', swap)]  1.74 us
    ppermute x1, starting transfers between devices, per_device(): received = [lax.ppermute(above, 'row', pairs) for pairs in shifts]  1.58 us
    ppermute x1, starting transfers between devices, per_device(): tri = [own] + [lax.ppermute(own, 'row', pairs) for pairs in shifts]  1.58 us
  transfers between devices with their start and end apart: 21, of which 10 were waited for; matrix products, arithmetic and copies ran while one was open for 0% of the time, Pallas kernels for 2%

profile of v2, /device:TPU:0, one launch (start us, length us, event | category | flops | bytes accessed | tf_op | source)
XLA Modules:
  0.0 49.2 jit_solution(10528321369870075473)
XLA Ops:
  0.6 1.4 %collective-permute-done.11.inv_other = f32[4,16,256]{2,1,0:T(8,128)S(1)} collective-permute-done((f32[4,16,256]{2,1,0:T(8,128)}, f32[4,16,256]{2,1,0:T(8,128)S(1)}, u32[]{:S(2)}, u32[]{:S(2)}) %collective-permute-start.11) | collective-permute-done | bytes 65568 | tf_op jit(solution)/shard_map/ppermute | solution.py:244
  2.0 0.9 %copy-done.1 = f32[4,16,1024]{2,1,0:T(8,128)S(1)} copy-done((f32[4,16,1024]{2,1,0:T(8,128)S(1)}, f32[4,16,1024]{2,1,0:T(8,128)}, u32[]{:S(2)}) %copy-start.1) | copy-done | bytes 262168
  2.9 0.8 %copy-done.3 = f32[4,16,256]{2,1,0:T(8,128)S(1)} copy-done((f32[4,16,256]{2,1,0:T(8,128)S(1)}, f32[4,16,256]{2,1,0:T(8,128)}, u32[]{:S(2)}) %copy-start.3) | copy-done | bytes 65560
  3.8 3.0 %collective-permute-start.12 = (f32[2,10,16,256]{3,2,1,0:T(8,128)S(1)}, f32[2,10,16,256]{3,2,1,0:T(8,128)S(1)}, u32[]{:S(2)}, u32[]{:S(2)}) collective-permute-start(f32[2,10,16,256]{3,2,1,0:T(8,128)S(1)} %shard_map.39.refs_0_), channel_id=1, source_target_pairs={{0,4},{1,3},{4,8},{5,1},{8,12},{9,5},{12,14},{13,9},{14,10},{15,13... | collective-permute-start | bytes 983048 | tf_op jit(solution)/shard_map/ppermute | solution.py:63
  6.8 1.6 %collective-permute-start = (f32[3,16,512]{2,1,0:T(8,128)S(1)}, f32[3,16,512]{2,1,0:T(8,128)S(1)}, u32[]{:S(2)}, u32[]{:S(2)}) collective-permute-start(f32[3,16,512]{2,1,0:T(8,128)S(1)} %slice.12.refs_0_), channel_id=1, source_target_pairs={{16,0},{0,16},{17,1},{1,17},{18,2},{2,18},{19,3},{3,19},{20,4},{4,... | collective-permute-start | bytes 294920 | tf_op jit(solution)/shard_map/ppermute | solution.py:247
  8.4 3.4 %collective-permute-done.12.refs_1_ = f32[2,10,16,256]{3,2,1,0:T(8,128)S(1)} collective-permute-done((f32[2,10,16,256]{3,2,1,0:T(8,128)S(1)}, f32[2,10,16,256]{3,2,1,0:T(8,128)S(1)}, u32[]{:S(2)}, u32[]{:S(2)}) %collective-permute-start.12) | collective-permute-done | bytes 327712 | tf_op jit(solution)/shard_map/ppermute | solution.py:63
  11.7 2.1 %collective-permute-start.14 = (f32[2,10,16,256]{3,2,1,0:T(8,128)S(1)}, f32[2,10,16,256]{3,2,1,0:T(8,128)S(1)}, u32[]{:S(2)}, u32[]{:S(2)}) collective-permute-start(f32[2,10,16,256]{3,2,1,0:T(8,128)S(1)} %collective-permute-done.12.refs_1_), channel_id=1, source_target_pairs={{0,4},{1,3},{4,8},{5,1},{8,12},{9,5},{12,14},{13,9},{14,10},{15,13... | collective-permute-start | bytes 983048 | tf_op jit(solution)/shard_map/ppermute | solution.py:63
  14.0 1.3 %collective-permute-done.1.tri_other = f32[6,16,256]{2,1,0:T(8,128)S(1)} collective-permute-done((f32[6,16,256]{2,1,0:T(8,128)S(1)}, f32[6,16,256]{2,1,0:T(8,128)S(1)}, u32[]{:S(2)}, u32[]{:S(2)}) %collective-permute-start.1) | collective-permute-done | bytes 98336 | tf_op jit(solution)/shard_map/ppermute | solution.py:258
  15.3 1.6 %collective-permute-start.3 = (f32[2,8,16,256]{3,2,1,0:T(8,128)S(1)}, f32[2,8,16,256]{3,2,1,0:T(8,128)S(1)}, u32[]{:S(2)}, u32[]{:S(2)}) collective-permute-start(f32[2,8,16,256]{3,2,1,0:T(8,128)S(1)} %shard_map.38.refs_0_), channel_id=1, source_target_pairs={{0,4},{1,3},{4,8},{5,1},{8,12},{9,5},{12,14},{13,9},{14,10},{15,13... | collective-permute-start | bytes 786440 | tf_op jit(solution)/shard_map/ppermute | solution.py:63
  16.9 1.9 %collective-permute-done.14.refs_3_ = f32[2,10,16,256]{3,2,1,0:T(8,128)S(1)} collective-permute-done((f32[2,10,16,256]{3,2,1,0:T(8,128)S(1)}, f32[2,10,16,256]{3,2,1,0:T(8,128)S(1)}, u32[]{:S(2)}, u32[]{:S(2)}) %collective-permute-start.14) | collective-permute-done | bytes 327712 | tf_op jit(solution)/shard_map/ppermute | solution.py:63
  18.8 2.1 %collective-permute-start.16 = (f32[2,10,16,256]{3,2,1,0:T(8,128)S(1)}, f32[2,10,16,256]{3,2,1,0:T(8,128)S(1)}, u32[]{:S(2)}, u32[]{:S(2)}) collective-permute-start(f32[2,10,16,256]{3,2,1,0:T(8,128)S(1)} %collective-permute-done.14.refs_3_), channel_id=1, source_target_pairs={{0,4},{1,3},{4,8},{5,1},{8,12},{9,5},{12,14},{13,9},{14,10},{15,13... | collective-permute-start | bytes 983048 | tf_op jit(solution)/shard_map/ppermute | solution.py:63
  20.9 0.8 %collective-permute-done.3.refs_1_ = f32[2,8,16,256]{3,2,1,0:T(8,128)S(1)} collective-permute-done((f32[2,8,16,256]{3,2,1,0:T(8,128)S(1)}, f32[2,8,16,256]{3,2,1,0:T(8,128)S(1)}, u32[]{:S(2)}, u32[]{:S(2)}) %collective-permute-start.3) | collective-permute-done | bytes 262176 | tf_op jit(solution)/shard_map/ppermute | solution.py:63
  21.7 2.0 %collective-permute-start.5 = (f32[2,8,16,256]{3,2,1,0:T(8,128)S(1)}, f32[2,8,16,256]{3,2,1,0:T(8,128)S(1)}, u32[]{:S(2)}, u32[]{:S(2)}) collective-permute-start(f32[2,8,16,256]{3,2,1,0:T(8,128)S(1)} %collective-permute-done.3.refs_1_), channel_id=1, source_target_pairs={{0,4},{1,3},{4,8},{5,1},{8,12},{9,5},{12,14},{13,9},{14,10},{15,13... | collective-permute-start | bytes 786440 | tf_op jit(solution)/shard_map/ppermute | solution.py:63
  23.7 5.0 %collective-permute-done.5.refs_3_ = f32[2,8,16,256]{3,2,1,0:T(8,128)S(1)} collective-permute-done((f32[2,8,16,256]{3,2,1,0:T(8,128)S(1)}, f32[2,8,16,256]{3,2,1,0:T(8,128)S(1)}, u32[]{:S(2)}, u32[]{:S(2)}) %collective-permute-start.5) | collective-permute-done | bytes 262176 | tf_op jit(solution)/shard_map/ppermute | solution.py:63
  28.7 2.1 %collective-permute-start.7 = (f32[2,8,16,256]{3,2,1,0:T(8,128)S(1)}, f32[2,8,16,256]{3,2,1,0:T(8,128)S(1)}, u32[]{:S(2)}, u32[]{:S(2)}) collective-permute-start(f32[2,8,16,256]{3,2,1,0:T(8,128)S(1)} %collective-permute-done.5.refs_3_), channel_id=1, source_target_pairs={{0,4},{1,3},{4,8},{5,1},{8,12},{9,5},{12,14},{13,9},{14,10},{15,13... | collective-permute-start | bytes 786440 | tf_op jit(solution)/shard_map/ppermute | solution.py:63
  30.8 1.6 %collective-permute-start.20 = (f32[512,256]{1,0:T(8,128)S(1)}, f32[512,256]{1,0:T(8,128)S(1)}, u32[]{:S(2)}, u32[]{:S(2)}) collective-permute-start(f32[512,256]{1,0:T(8,128)S(1)} %slice.15), channel_id=1, source_target_pairs={{16,0},{0,16},{17,1},{1,17},{18,2},{2,18},{19,3},{3,19},{20,4},{4,... | collective-permute-start | bytes 1572872 | tf_op jit(solution)/shard_map/ppermute | solution.py:249
  32.4 0.5 %collective-permute-start.15 = (f32[2,10,16,256]{3,2,1,0:T(8,128)S(1)}, f32[2,10,16,256]{3,2,1,0:T(8,128)S(1)}, u32[]{:S(2)}, u32[]{:S(2)}) collective-permute-start(f32[2,10,16,256]{3,2,1,0:T(8,128)S(1)} %collective-permute-done.14.refs_3_), channel_id=1, source_target_pairs={{0,1},{1,0},{2,3},{3,2},{4,5},{5,4},{6,7},{7,6},{8,9},{9,8},{10,11... | collective-permute-start | bytes 983048 | tf_op jit(solution)/shard_map/ppermute | solution.py:64
  33.0 1.6 %collective-permute-start.18 = (f32[10,16,256]{2,1,0:T(8,128)S(1)}, f32[10,16,256]{2,1,0:T(8,128)S(1)}, u32[]{:S(2)}, u32[]{:S(2)}) collective-permute-start(f32[10,16,256]{2,1,0:T(8,128)S(1)} %slice_bitcast_fusion), channel_id=1, source_target_pairs={{0,4},{1,3},{4,8},{5,1},{8,12},{9,5},{12,14},{13,9},{14,10},{15,13... | collective-permute-start | bytes 491528 | tf_op jit(solution)/shard_map/ppermute | solution.py:63
  35.1 2.2 %collective-permute-start.9 = (f32[8,16,256]{2,1,0:T(8,128)S(1)}, f32[8,16,256]{2,1,0:T(8,128)S(1)}, u32[]{:S(2)}, u32[]{:S(2)}) collective-permute-start(f32[8,16,256]{2,1,0:T(8,128)S(1)} %slice_bitcast_fusion.1), channel_id=1, source_target_pairs={{0,4},{1,3},{4,8},{5,1},{8,12},{9,5},{12,14},{13,9},{14,10},{15,13... | collective-permute-start | bytes 393224 | tf_op jit(solution)/shard_map/ppermute | solution.py:63
  37.2 4.8 %collective-permute-done.20.refs_10_.refs_14_ = f32[512,256]{1,0:T(8,128)S(1)} collective-permute-done((f32[512,256]{1,0:T(8,128)S(1)}, f32[512,256]{1,0:T(8,128)S(1)}, u32[]{:S(2)}, u32[]{:S(2)}) %collective-permute-start.20) | collective-permute-done | bytes 524320 | tf_op jit(solution)/shard_map/ppermute | solution.py:249
  42.1 0.5 %collective-permute-start.19 = (f32[10,16,256]{2,1,0:T(8,128)S(1)}, f32[10,16,256]{2,1,0:T(8,128)S(1)}, u32[]{:S(2)}, u32[]{:S(2)}) collective-permute-start(f32[10,16,256]{2,1,0:T(8,128)S(1)} %collective-permute-done.18.refs_7_), channel_id=1, source_target_pairs={{0,1},{1,0},{2,3},{3,2},{4,5},{5,4},{6,7},{7,6},{8,9},{9,8},{10,11... | collective-permute-start | bytes 491528 | tf_op jit(solution)/shard_map/ppermute | solution.py:64
  43.2 0.8 %collective-permute-done.19.refs_8_ = f32[10,16,256]{2,1,0:T(8,128)S(1)} collective-permute-done((f32[10,16,256]{2,1,0:T(8,128)S(1)}, f32[10,16,256]{2,1,0:T(8,128)S(1)}, u32[]{:S(2)}, u32[]{:S(2)}) %collective-permute-start.19) | collective-permute-done | bytes 163872 | tf_op jit(solution)/shard_map/ppermute | solution.py:64
  44.1 1.1 %shard_map.40 = (bf16[10,256,256]{2,1,0:T(8,128)(2,1)S(1)}, bf16[10,256,256]{2,1,0:T(8,128)(2,1)S(1)}, f32[256,256]{1,0:T(8,128)S(1)}, f32[512,256]{1,0:T(8,128)S(1)}) custom-call(f32[2,10,16,256]{3,2,1,0:T(8,128)S(1)} %shard_map.39.refs_0_, f32[2,10,16,256]{3,2,1,0:T(8,128)S(1)} %collective-permute-done.12.refs_1_, ...), custom_call_target="tpu_custom_call" | custom-call | flops 301989888 | bytes 4194304 | tf_op jit(solution)/shard_map/pallas_call | solution.py:41
  45.3 3.9 %shard_map.41 = f32[1024,256]{1,0:T(8,128)} custom-call(f32[2,8,16,256]{3,2,1,0:T(8,128)S(1)} %shard_map.38.refs_0_, f32[2,8,16,256]{3,2,1,0:T(8,128)S(1)} %collective-permute-done.3.refs_1_, f32[2,8,16,256]{3,2,1,0:T(8,128)S(1)} %collective-permute-done.4.refs_2_, f32[2,8,16,256]{3,2,1,0:T(8,128)S(1)} %collective-permute-done.5.refs_3_, ...), custom_call_target="tpu_custom_call" | custom-call | flops 1509949440 | bytes 4194304 | tf_op jit(solution)/shard_map/pallas_call | solution.py:41
  (35 shorter events, 2.1 us)
Async XLA Ops:
  0.0 30.8 %copy-start = (f32[1024,256]{1,0:T(8,128)S(1)}, f32[1024,256]{1,0:T(8,128)}, u32[]{:S(2)}) copy-start(f32[1024,256]{1,0:T(8,128)} %refs_13_.1) | copy-start | bytes 3145732
  0.0 2.0 %collective-permute-start.2 = (f32[4,16,1024]{2,1,0:T(8,128)}, f32[4,16,1024]{2,1,0:T(8,128)S(1)}, u32[]{:S(2)}, u32[]{:S(2)}) collective-permute-start(f32[4,16,1024]{2,1,0:T(8,128)} %factor_ref.3), channel_id=1, source_target_pairs={{0,1},{1,0},{2,3},{3,2},{4,5},{5,4},{6,7},{7,6},{8,9},{9,8},{10,11... | collective-permute-start | bytes 786440 | tf_op jit(solution)/shard_map/ppermute | solution.py:245
  0.5 1.5 %collective-permute-start.11 = (f32[4,16,256]{2,1,0:T(8,128)}, f32[4,16,256]{2,1,0:T(8,128)S(1)}, u32[]{:S(2)}, u32[]{:S(2)}) collective-permute-start(f32[4,16,256]{2,1,0:T(8,128)} %inv_ref.1), channel_id=1, source_target_pairs={{0,1},{1,0},{2,3},{3,2},{4,5},{5,4},{6,7},{7,6},{8,9},{9,8},{10,11... | collective-permute-start | bytes 196616 | tf_op jit(solution)/shard_map/ppermute | solution.py:244
  2.0 1.0 %copy-start.1 = (f32[4,16,1024]{2,1,0:T(8,128)S(1)}, f32[4,16,1024]{2,1,0:T(8,128)}, u32[]{:S(2)}) copy-start(f32[4,16,1024]{2,1,0:T(8,128)} %factor_ref.3) | copy-start | bytes 786436
  3.8 11.5 %copy-start.2 = (f32[4,16,1024]{2,1,0:T(8,128)S(1)}, f32[4,16,1024]{2,1,0:T(8,128)}, u32[]{:S(2)}) copy-start(f32[4,16,1024]{2,1,0:T(8,128)} %factor_ref.3) | copy-start | bytes 786436
  3.8 8.0 %collective-permute-start.12 = (f32[2,10,16,256]{3,2,1,0:T(8,128)S(1)}, f32[2,10,16,256]{3,2,1,0:T(8,128)S(1)}, u32[]{:S(2)}, u32[]{:S(2)}) collective-permute-start(f32[2,10,16,256]{3,2,1,0:T(8,128)S(1)} %shard_map.39.refs_0_), channel_id=1, source_target_pairs={{0,4},{1,3},{4,8},{5,1},{8,12},{9,5},{12,14},{13,9},{14,10},{15,13... | collective-permute-start | bytes 983048 | tf_op jit(solution)/shard_map/ppermute | solution.py:63
  6.8 7.1 %collective-permute-start = (f32[3,16,512]{2,1,0:T(8,128)S(1)}, f32[3,16,512]{2,1,0:T(8,128)S(1)}, u32[]{:S(2)}, u32[]{:S(2)}) collective-permute-start(f32[3,16,512]{2,1,0:T(8,128)S(1)} %slice.12.refs_0_), channel_id=1, source_target_pairs={{16,0},{0,16},{17,1},{1,17},{18,2},{2,18},{19,3},{3,19},{20,4},{4,... | collective-permute-start | bytes 294920 | tf_op jit(solution)/shard_map/ppermute | solution.py:247
  11.7 7.1 %collective-permute-start.14 = (f32[2,10,16,256]{3,2,1,0:T(8,128)S(1)}, f32[2,10,16,256]{3,2,1,0:T(8,128)S(1)}, u32[]{:S(2)}, u32[]{:S(2)}) collective-permute-start(f32[2,10,16,256]{3,2,1,0:T(8,128)S(1)} %collective-permute-done.12.refs_1_), channel_id=1, source_target_pairs={{0,4},{1,3},{4,8},{5,1},{8,12},{9,5},{12,14},{13,9},{14,10},{15,13... | collective-permute-start | bytes 983048 | tf_op jit(solution)/shard_map/ppermute | solution.py:63
  13.9 1.4 %collective-permute-start.1 = (f32[6,16,256]{2,1,0:T(8,128)S(1)}, f32[6,16,256]{2,1,0:T(8,128)S(1)}, u32[]{:S(2)}, u32[]{:S(2)}) collective-permute-start(f32[6,16,256]{2,1,0:T(8,128)S(1)} %shard_map.37.tri_ref), channel_id=1, source_target_pairs={{0,1},{1,0},{2,3},{3,2},{4,5},{5,4},{6,7},{7,6},{8,9},{9,8},{10,11... | collective-permute-start | bytes 294920 | tf_op jit(solution)/shard_map/ppermute | solution.py:258
  15.3 6.4 %collective-permute-start.3 = (f32[2,8,16,256]{3,2,1,0:T(8,128)S(1)}, f32[2,8,16,256]{3,2,1,0:T(8,128)S(1)}, u32[]{:S(2)}, u32[]{:S(2)}) collective-permute-start(f32[2,8,16,256]{3,2,1,0:T(8,128)S(1)} %shard_map.38.refs_0_), channel_id=1, source_target_pairs={{0,4},{1,3},{4,8},{5,1},{8,12},{9,5},{12,14},{13,9},{14,10},{15,13... | collective-permute-start | bytes 786440 | tf_op jit(solution)/shard_map/ppermute | solution.py:63
  18.8 14.1 %collective-permute-start.16 = (f32[2,10,16,256]{3,2,1,0:T(8,128)S(1)}, f32[2,10,16,256]{3,2,1,0:T(8,128)S(1)}, u32[]{:S(2)}, u32[]{:S(2)}) collective-permute-start(f32[2,10,16,256]{3,2,1,0:T(8,128)S(1)} %collective-permute-done.14.refs_3_), channel_id=1, source_target_pairs={{0,4},{1,3},{4,8},{5,1},{8,12},{9,5},{12,14},{13,9},{14,10},{15,13... | collective-permute-start | bytes 983048 | tf_op jit(solution)/shard_map/ppermute | solution.py:63
  21.7 7.0 %collective-permute-start.5 = (f32[2,8,16,256]{3,2,1,0:T(8,128)S(1)}, f32[2,8,16,256]{3,2,1,0:T(8,128)S(1)}, u32[]{:S(2)}, u32[]{:S(2)}) collective-permute-start(f32[2,8,16,256]{3,2,1,0:T(8,128)S(1)} %collective-permute-done.3.refs_1_), channel_id=1, source_target_pairs={{0,4},{1,3},{4,8},{5,1},{8,12},{9,5},{12,14},{13,9},{14,10},{15,13... | collective-permute-start | bytes 786440 | tf_op jit(solution)/shard_map/ppermute | solution.py:63
  28.7 6.4 %collective-permute-start.7 = (f32[2,8,16,256]{3,2,1,0:T(8,128)S(1)}, f32[2,8,16,256]{3,2,1,0:T(8,128)S(1)}, u32[]{:S(2)}, u32[]{:S(2)}) collective-permute-start(f32[2,8,16,256]{3,2,1,0:T(8,128)S(1)} %collective-permute-done.5.refs_3_), channel_id=1, source_target_pairs={{0,4},{1,3},{4,8},{5,1},{8,12},{9,5},{12,14},{13,9},{14,10},{15,13... | collective-permute-start | bytes 786440 | tf_op jit(solution)/shard_map/ppermute | solution.py:63
  30.8 11.2 %collective-permute-start.20 = (f32[512,256]{1,0:T(8,128)S(1)}, f32[512,256]{1,0:T(8,128)S(1)}, u32[]{:S(2)}, u32[]{:S(2)}) collective-permute-start(f32[512,256]{1,0:T(8,128)S(1)} %slice.15), channel_id=1, source_target_pairs={{16,0},{0,16},{17,1},{1,17},{18,2},{2,18},{19,3},{3,19},{20,4},{4,... | collective-permute-start | bytes 1572872 | tf_op jit(solution)/shard_map/ppermute | solution.py:249
  32.4 10.1 %collective-permute-start.13 = (f32[2,10,16,256]{3,2,1,0:T(8,128)S(1)}, f32[2,10,16,256]{3,2,1,0:T(8,128)S(1)}, u32[]{:S(2)}, u32[]{:S(2)}) collective-permute-start(f32[2,10,16,256]{3,2,1,0:T(8,128)S(1)} %collective-permute-done.12.refs_1_), channel_id=1, source_target_pairs={{0,1},{1,0},{2,3},{3,2},{4,5},{5,4},{6,7},{7,6},{8,9},{9,8},{10,11... | collective-permute-start | bytes 983048 | tf_op jit(solution)/shard_map/ppermute | solution.py:64
  32.4 10.6 %collective-permute-start.15 = (f32[2,10,16,256]{3,2,1,0:T(8,128)S(1)}, f32[2,10,16,256]{3,2,1,0:T(8,128)S(1)}, u32[]{:S(2)}, u32[]{:S(2)}) collective-permute-start(f32[2,10,16,256]{3,2,1,0:T(8,128)S(1)} %collective-permute-done.14.refs_3_), channel_id=1, source_target_pairs={{0,1},{1,0},{2,3},{3,2},{4,5},{5,4},{6,7},{7,6},{8,9},{9,8},{10,11... | collective-permute-start | bytes 983048 | tf_op jit(solution)/shard_map/ppermute | solution.py:64
  33.0 9.1 %collective-permute-start.18 = (f32[10,16,256]{2,1,0:T(8,128)S(1)}, f32[10,16,256]{2,1,0:T(8,128)S(1)}, u32[]{:S(2)}, u32[]{:S(2)}) collective-permute-start(f32[10,16,256]{2,1,0:T(8,128)S(1)} %slice_bitcast_fusion), channel_id=1, source_target_pairs={{0,4},{1,3},{4,8},{5,1},{8,12},{9,5},{12,14},{13,9},{14,10},{15,13... | collective-permute-start | bytes 491528 | tf_op jit(solution)/shard_map/ppermute | solution.py:63
  35.1 7.6 %collective-permute-start.9 = (f32[8,16,256]{2,1,0:T(8,128)S(1)}, f32[8,16,256]{2,1,0:T(8,128)S(1)}, u32[]{:S(2)}, u32[]{:S(2)}) collective-permute-start(f32[8,16,256]{2,1,0:T(8,128)S(1)} %slice_bitcast_fusion.1), channel_id=1, source_target_pairs={{0,4},{1,3},{4,8},{5,1},{8,12},{9,5},{12,14},{13,9},{14,10},{15,13... | collective-permute-start | bytes 393224 | tf_op jit(solution)/shard_map/ppermute | solution.py:63
  42.0 2.0 %collective-permute-start.17 = (f32[2,10,16,256]{3,2,1,0:T(8,128)S(1)}, f32[2,10,16,256]{3,2,1,0:T(8,128)S(1)}, u32[]{:S(2)}, u32[]{:S(2)}) collective-permute-start(f32[2,10,16,256]{3,2,1,0:T(8,128)S(1)} %collective-permute-done.16.refs_5_), channel_id=1, source_target_pairs={{0,1},{1,0},{2,3},{3,2},{4,5},{5,4},{6,7},{7,6},{8,9},{9,8},{10,11... | collective-permute-start | bytes 983048 | tf_op jit(solution)/shard_map/ppermute | solution.py:64
  42.1 1.9 %collective-permute-start.19 = (f32[10,16,256]{2,1,0:T(8,128)S(1)}, f32[10,16,256]{2,1,0:T(8,128)S(1)}, u32[]{:S(2)}, u32[]{:S(2)}) collective-permute-start(f32[10,16,256]{2,1,0:T(8,128)S(1)} %collective-permute-done.18.refs_7_), channel_id=1, source_target_pairs={{0,1},{1,0},{2,3},{3,2},{4,5},{5,4},{6,7},{7,6},{8,9},{9,8},{10,11... | collective-permute-start | bytes 491528 | tf_op jit(solution)/shard_map/ppermute | solution.py:64
  42.6 2.6 %collective-permute-start.4 = (f32[2,8,16,256]{3,2,1,0:T(8,128)S(1)}, f32[2,8,16,256]{3,2,1,0:T(8,128)S(1)}, u32[]{:S(2)}, u32[]{:S(2)}) collective-permute-start(f32[2,8,16,256]{3,2,1,0:T(8,128)S(1)} %collective-permute-done.3.refs_1_), channel_id=1, source_target_pairs={{0,1},{1,0},{2,3},{3,2},{4,5},{5,4},{6,7},{7,6},{8,9},{9,8},{10,11... | collective-permute-start | bytes 786440 | tf_op jit(solution)/shard_map/ppermute | solution.py:64
  42.6 2.5 %collective-permute-start.6 = (f32[2,8,16,256]{3,2,1,0:T(8,128)S(1)}, f32[2,8,16,256]{3,2,1,0:T(8,128)S(1)}, u32[]{:S(2)}, u32[]{:S(2)}) collective-permute-start(f32[2,8,16,256]{3,2,1,0:T(8,128)S(1)} %collective-permute-done.5.refs_3_), channel_id=1, source_target_pairs={{0,1},{1,0},{2,3},{3,2},{4,5},{5,4},{6,7},{7,6},{8,9},{9,8},{10,11... | collective-permute-start | bytes 786440 | tf_op jit(solution)/shard_map/ppermute | solution.py:64
  43.1 2.2 %collective-permute-start.8 = (f32[2,8,16,256]{3,2,1,0:T(8,128)S(1)}, f32[2,8,16,256]{3,2,1,0:T(8,128)S(1)}, u32[]{:S(2)}, u32[]{:S(2)}) collective-permute-start(f32[2,8,16,256]{3,2,1,0:T(8,128)S(1)} %collective-permute-done.7.refs_5_), channel_id=1, source_target_pairs={{0,1},{1,0},{2,3},{3,2},{4,5},{5,4},{6,7},{7,6},{8,9},{9,8},{10,11... | collective-permute-start | bytes 786440 | tf_op jit(solution)/shard_map/ppermute | solution.py:64
  43.9 1.3 %collective-permute-start.10 = (f32[8,16,256]{2,1,0:T(8,128)S(1)}, f32[8,16,256]{2,1,0:T(8,128)S(1)}, u32[]{:S(2)}, u32[]{:S(2)}) collective-permute-start(f32[8,16,256]{2,1,0:T(8,128)S(1)} %collective-permute-done.9.refs_7_), channel_id=1, source_target_pairs={{0,1},{1,0},{2,3},{3,2},{4,5},{5,4},{6,7},{7,6},{8,9},{9,8},{10,11... | collective-permute-start | bytes 393224 | tf_op jit(solution)/shard_map/ppermute | solution.py:64
  (1 other events, 0.8 us)

commit v3 on v2

v3 whole, which is shorter than its diff:
```python
import functools

import jax
import jax.numpy as jnp
from jax import lax
from jax.experimental import pallas as pl
from jax.experimental.pallas import tpu as pltpu
from jax.sharding import PartitionSpec as P

CHUNKS = 2
ROWS = ((0,), (0,))
PLAIN = ((1,), (0,))


def ring_place(chip, chips):
    return jnp.where(chip % 2 == 0, chip // 2, chips - 1 - chip // 2)


def ring_chip(place, chips):
    up = 2 * place
    down = 2 * (chips - 1 - place) + 1
    if isinstance(place, int):
        return up if place < chips // 2 else down
    return jnp.where(place < chips // 2, up, down)


def split(value):
    high = value.astype(jnp.bfloat16)
    low = (value - high.astype(jnp.float32)).astype(jnp.bfloat16)
    return high, low


def dot3(left, right, dims):
    mult = functools.partial(
        lax.dot_general, dimension_numbers=(dims, ((), ())), preferred_element_type=jnp.float32
    )
    return mult(left[0], right[0]) + (mult(left[0], right[1]) + mult(left[1], right[0]))


def kernel_call(body, out_shapes, scratch, operands, flops=0, in_hbm=0, out_hbm=0, aliases={}):
    vmem, hbm = pl.BlockSpec(memory_space=pltpu.VMEM), pl.BlockSpec(memory_space=pltpu.HBM)
    return pl.pallas_call(
        body,
        out_shape=out_shapes,
        in_specs=[hbm] * in_hbm + [vmem] * (len(operands) - in_hbm),
        out_specs=jax.tree.map(lambda _: vmem, out_shapes)
        if not out_hbm
        else [hbm] * out_hbm + [vmem] * (len(out_shapes) - out_hbm),
        input_output_aliases=aliases,
        scratch_shapes=scratch,
        cost_estimate=pl.CostEstimate(flops=flops, bytes_accessed=4 << 20, transcendentals=0),
        compiler_params=pltpu.CompilerParams(vmem_limit_bytes=20 << 20),
    )(*operands)


def ring(first, chips):
    steps = chips // 2
    nearest = []
    for place in range(chips):
        here = ring_chip(place, chips)
        nearest.append((2 * here, 2 * ring_chip((place + 1) % chips, chips)))
        nearest.append((2 * here + 1, 2 * ring_chip((place - 1) % chips, chips) + 1))
    swap = [(i, i ^ 1) for i in range(2 * chips)]
    moving = first
    pieces = [first]
    for step in range(1, steps + 1):
        moving = lax.ppermute(moving if step < steps else moving[0], "col", nearest)
        pieces += [moving, lax.ppermute(moving, "col", swap)]
    return pieces


def streams(chips):
    core = lax.axis_index("col") % 2
    here = ring_place(lax.axis_index("col") // 2, chips)
    found = [(lax.axis_index("col") // 2, core)]
    for step in range(1, chips // 2 + 1):
        turn = step * (1 - 2 * core)
        found.append((ring_chip((here - turn + chips) % chips, chips), core))
        found.append((ring_chip((here + turn + chips) % chips, chips), 1 - core))
    return found


def assemble(piece_refs, high_ref, low_ref, whole_ref, chips, chosen=slice(None)):
    depth = piece_refs[0].shape[-2]

    def put(row, value):
        rows = pl.ds(pl.multiple_of(row, value.shape[1]), value.shape[1])
        if depth % 16 == 0:
            high_ref[:, rows, :], low_ref[:, rows, :] = split(value)
        else:
            whole_ref[:, rows, :] = value

    table = list(enumerate(streams(chips)))[chosen]
    for ref, (at, (chip, core)) in zip(piece_refs, table):
        if depth % 16 == 0:
            if at < chips - 1:
                for half in range(2):
                    put((2 * chip + half) * depth, ref[jnp.where(core == 0, half, 1 - half)])
            else:
                put((2 * chip + core) * depth, ref[...])
            continue
        if at == chips:
            continue
        pair = [ref[0], ref[1]] if at < chips - 1 else [ref[...], piece_refs[-1][...]]
        low, high = jnp.where(core == 0, pair[0], pair[1]), jnp.where(core == 0, pair[1], pair[0])
        put(2 * chip * depth, jnp.concatenate([low, high], axis=1))
    if depth % 16 != 0:
        high_ref[...], low_ref[...] = split(whole_ref[...])


def whole_scratch(count, nb, depth):
    return pltpu.VMEM((count, nb, nb) if depth % 16 != 0 else (1, 8, nb), jnp.float32)


class Plan:
    def __init__(self, group_count, chips, panels, nb, rows):
        self.group_count, self.chips, self.panels, self.nb = group_count, chips, panels, nb
        self.held = -(-panels // group_count)
        self.sure = panels // group_count
        self.wide = rows // nb - self.sure
        self.tri = [(rank, panel) for rank in range(1, panels) for panel in range(rank)]
        self.deep = max(
            min(rank, panels - 1) for rank in range((self.held - 1) * group_count, self.held * group_count)
        )
        low = [(panel, block) for panel in range(panels) for block in range(self.wide)]
        total = panels + len(self.tri) + len(low)
        inv = [("inv", panel) for panel in range(panels)]
        tri = [("tri", at) for at in range(len(self.tri))]
        low = [("low", *pair) for pair in low]
        last = max(total // CHUNKS, len(tri))
        rest = inv + low[: total - panels - last]
        size = -(-len(rest) // (CHUNKS - 1))
        self.chunks = [rest[at : at + size] for at in range(0, len(rest), size)]
        self.chunks.append(tri + low[total - panels - last :])
        self.where = {b: (c, at) for c, chunk in enumerate(self.chunks) for at, b in enumerate(chunk)}

    def mat(self, mats, *block):
        chunk, at = self.where[block]
        high, low = mats[chunk]
        return high[at], low[at]

    def chosen(self, owner, sources):
        me = lax.axis_index("row")
        value = sources[0]
        for shift in range(1, self.group_count):
            value = jnp.where((me + shift) % self.group_count == owner, sources[shift], value)
        return value

    def panel_rows(self, rank, right_ref, received):
        local, owner = divmod(rank, self.group_count)
        rows = slice(local * self.nb, (local + 1) * self.nb)
        return self.chosen(owner, [right_ref[rows]] + [r[rows] for r in received])


def load_kernel(factor_hbm, inv_hbm, factor_ref, inv_ref, own_ref, sems):
    deep, _, part = own_ref.shape
    copies = [
        pltpu.make_async_copy(factor_hbm.at[:deep, :, :part], own_ref, sems.at[0]),
        pltpu.make_async_copy(factor_hbm, factor_ref, sems.at[1]),
        pltpu.make_async_copy(inv_hbm, inv_ref, sems.at[2]),
    ]
    for copy in copies:
        copy.start()
    for copy in copies:
        copy.wait()


def pack_kernel(plan, chunk, *refs):
    out_ref = refs[-1]
    for side in range(2):
        head, factor = refs[2 * side : 2 * side + 2]
        for to, (kind, *which) in enumerate(plan.chunks[chunk]):
            if kind == "low":
                panel, block = which
                at = (plan.sure + block) * plan.nb
                out_ref[side, to] = factor[panel, :, at : at + plan.nb]
            else:
                out_ref[side, to] = head[which[0]]


def tri_kernel(plan, *refs):
    *sources, out_ref = refs
    for at, (rank, panel) in enumerate(plan.tri):
        local, owner = divmod(rank, plan.group_count)
        part = slice(local * plan.nb, (local + 1) * plan.nb)
        out_ref[at] = plan.chosen(owner, [source[panel, :, part] for source in sources])


def prep_kernel(plan, *refs):
    count, early = plan.chips + 1, len(plan.chunks) - 1
    pieces = [refs[c * count : (c + 1) * count] for c in range(early)]
    right_ref = refs[early * count]
    outs = refs[-3 * early - 2 :]
    received = refs[early * count + 1 : -3 * early - 2]
    mats = [outs[2 * c : 2 * c + 2] for c in range(early)]
    x_ref, total_ref = outs[2 * early : 2 * early + 2]
    for c in range(early):
        assemble(pieces[c], *mats[c], outs[2 * early + 2 + c], plan.chips)
    nb = plan.nb
    answer = dot3(plan.mat(mats, "inv", 0), split(plan.panel_rows(0, right_ref, received)), PLAIN)
    x_ref[...] = answer
    solved = split(answer)
    for block in range(plan.wide):
        at = (plan.sure + block) * nb
        total = right_ref[at : at + nb] - dot3(plan.mat(mats, "low", 0, block), solved, ROWS)
        total_ref[block * nb : (block + 1) * nb] = total


def place_kernel(plan, *refs):
    high_ref, low_ref, whole_ref = refs[-3:]
    assemble(refs[:-3], high_ref, low_ref, whole_ref, plan.chips, slice(0, plan.chips - 1))


def final_kernel(plan, late, *refs):
    early = len(plan.chunks) - 1
    pieces, at = refs[:late], late
    mats = [refs[at + 2 * c : at + 2 * c + 2] for c in range(early)]
    at += 2 * early
    x_first, total_ref, right_ref = refs[at + 2 : at + 5]
    received = refs[at + 5 : -7]
    out_hbm, high_ref, low_ref, x_ref, low_rows, whole_ref, sems = refs[-7:]
    panels, nb, wide = plan.panels, plan.nb, plan.wide
    me = lax.axis_index("row")
    fresh = slice(plan.chips - 1, None) if late == 2 else slice(None)
    assemble(pieces, high_ref, low_ref, whole_ref, plan.chips, fresh)
    mats.append((high_ref, low_ref))

    def copy_out(rank, local):
        rows = pl.ds(local * nb, nb)
        return pltpu.make_async_copy(x_ref.at[rank], out_hbm.at[rows], sems.at[local])

    x_ref[0] = x_first[...]
    solved = [split(x_first[...])]
    currents = [plan.panel_rows(panel, right_ref, received) for panel in range(panels)]
    totals = [total_ref[block * nb : (block + 1) * nb] for block in range(wide)]
    for panel in range(1, panels):
        for after in range(panel, panels):
            mat = plan.mat(mats, "tri", plan.tri.index((after, panel - 1)))
            currents[after] = currents[after] - dot3(mat, solved[panel - 1], ROWS)
        answer = dot3(plan.mat(mats, "inv", panel), split(currents[panel]), PLAIN)
        x_ref[panel] = answer
        if panel > 1:
            for block in range(wide):
                mat = plan.mat(mats, "low", panel - 1, block)
                totals[block] = totals[block] - dot3(mat, solved[panel - 1], ROWS)
        solved.append(split(answer))
    for local in range(plan.held):
        rank = local * plan.group_count + me

        @pl.when(rank < panels)
        def _(rank=rank, local=local):
            copy_out(rank, local).start()

    outs = []
    for block in range(wide):
        mat = plan.mat(mats, "low", panels - 1, block)
        low_rows[block] = totals[block] - dot3(mat, solved[panels - 1], ROWS)
        local = plan.sure + block
        out = pltpu.make_async_copy(
            low_rows.at[block], out_hbm.at[pl.ds(local * nb, nb)], sems.at[local]
        )
        if local < plan.held:
            below = local * plan.group_count + me >= panels
            pl.when(below)(out.start)
            pl.when(below)(out.wait)
        else:
            out.start()
            outs.append(out)
    for local in range(plan.held):
        rank = local * plan.group_count + me

        @pl.when(rank < panels)
        def _(rank=rank, local=local):
            copy_out(rank, local).wait()

    for out in outs:
        out.wait()


def per_device(right_side, factor_panels, inverses):
    group_count = lax.axis_size("row")
    chips = lax.axis_size("col") // 2
    panels, depth, rows = factor_panels.shape
    nb = inverses.shape[2]
    columns = right_side.shape[1]
    plan = Plan(group_count, chips, panels, nb, rows)
    swap = [(i, i ^ 1) for i in range(2 * chips)]
    shifts = [
        [((g + shift) % group_count, g) for g in range(group_count)] for shift in range(1, group_count)
    ]
    f32, bf16 = jnp.float32, jnp.bfloat16
    shape = jax.ShapeDtypeStruct
    bound = functools.partial

    factor, inv, own = kernel_call(
        load_kernel,
        [
            shape(factor_panels.shape, f32),
            shape(inverses.shape, f32),
            shape((plan.deep, depth, plan.held * nb), f32),
        ],
        [pltpu.SemaphoreType.DMA((3,))],
        (factor_panels, inverses),
        in_hbm=2,
    )
    inv_other = lax.ppermute(inv, "col", swap)
    factor_other = lax.ppermute(factor, "col", swap)
    tri = [own] + [lax.ppermute(own, "row", pairs) for pairs in shifts]
    above = right_side[: plan.held * nb]
    received = [lax.ppermute(above, "row", pairs) for pairs in shifts]
    half = kernel_call(bound(tri_kernel, plan), shape((len(plan.tri), depth, nb), f32), [], tri)
    half_other = lax.ppermute(half, "col", swap)

    pieces = []
    last = len(plan.chunks) - 1
    for chunk in range(last + 1):
        heads = (half, half_other) if chunk == last else (inv, inv_other)
        packed = kernel_call(
            bound(pack_kernel, plan, chunk),
            shape((2, len(plan.chunks[chunk]), depth, nb), f32),
            [],
            (heads[0], factor, heads[1], factor_other),
        )
        pieces.append(ring(packed, chips))

    split_shapes = [[shape((len(chunk), nb, nb), bf16)] * 2 for chunk in plan.chunks]
    *mats, x_first, total = kernel_call(
        bound(prep_kernel, plan),
        [s for pair in split_shapes[:-1] for s in pair]
        + [shape((nb, columns), f32), shape((plan.wide * nb, columns), f32)],
        [whole_scratch(len(chunk), nb, depth) for chunk in plan.chunks[:-1]],
        (*(piece for chunk in pieces[:-1] for piece in chunk), right_side, *received),
        flops=6 * 3 * nb * nb * columns,
    )
    whole = whole_scratch(len(plan.chunks[-1]), nb, depth)
    aligned = depth % 16 == 0
    if aligned:
        placed = kernel_call(
            bound(place_kernel, plan), split_shapes[-1], [whole], pieces[-1][: chips - 1]
        )
        late = pieces[-1][chips - 1 :]
    else:
        placed = [jnp.zeros(s.shape, s.dtype) for s in split_shapes[-1]]
        late = pieces[-1]
    at = len(late) + len(mats)
    out, _, _ = kernel_call(
        bound(final_kernel, plan, len(late)),
        [shape(right_side.shape, f32), *split_shapes[-1]],
        [
            pltpu.VMEM((panels, nb, columns), f32),
            pltpu.VMEM((plan.wide, nb, columns), f32),
            whole,
            pltpu.SemaphoreType.DMA((rows // nb,)),
        ],
        (*late, *mats, *placed, x_first, total, right_side, *received),
        flops=6 * 15 * nb * nb * columns,
        out_hbm=1,
        aliases={at: 1, at + 1: 2},
    )
    return out


def solution(mesh):
    in_specs = (P("row", "col"), P(None, "col", "row"), P(None, "col", None))
    out_specs = P("row", "col")

    return jax.shard_map(per_device, mesh=mesh, in_specs=in_specs, out_specs=out_specs, check_vma=False)
```

time: 49.3 us -> 51.7 us (1.049)
  waiting for transfers between devices: 19.9 us -> 25.3 us
  starting transfers between devices: 22.3 us -> 19.4 us
    ppermute x8, starting transfers between devices: 16.8 us -> 13.4 us  [ring(): moving = lax.ppermute(moving if step < steps else moving[0], 'col', nearest)]
    ppermute x1, waiting for transfers between devices: 0.01 us -> 3.1 us  [per_device(): tri = [own] + [lax.ppermute(own, 'row', pairs) for pairs in shifts]]
    ppermute x1, waiting for transfers between devices: 4.8 us -> 7.02 us  [per_device(): received = [lax.ppermute(above, 'row', pairs) for pairs in shifts]]
    ppermute x8, waiting for transfers between devices: 11.5 us -> 12.1 us  [ring(): moving = lax.ppermute(moving if step < steps else moving[0], 'col', nearest)]
    ppermute x8, starting transfers between devices: 1.74 us -> 2.26 us  [ring(): pieces += [moving, lax.ppermute(moving, 'col', swap)]]
    pallas_call x5 -> x7, Pallas kernels: 5.02 us -> 4.88 us  [kernel_call(): pl.pallas_call(body, out_shape=out_shapes, in_specs=[hbm] * in_hbm + [vme...]
    unnamed x8 -> x6, local copies, waits for them, and re-layouts: 1.8 us -> 1.79 us
  transfers between devices with their start and end apart: 21 -> 21, of which waited for: 10 -> 10; matrix products, arithmetic and copies ran while one was open for 0% -> 0% of each run, Pallas kernels for 2% -> 3%
where the time goes in v3:
time: 51.7 us; the launch traced here: 51.6 us
  waiting for transfers between devices  25.3 us (49%)
  starting transfers between devices  19.4 us (38%)
  Pallas kernels  4.88 us (9%)
  local copies, waits for them, and re-layouts  1.85 us (4%)
    ppermute x8, starting transfers between devices, ring(): moving = lax.ppermute(moving if step < steps else moving[0], 'col', nearest)  13.4 us
    ppermute x8, waiting for transfers between devices, ring(): moving = lax.ppermute(moving if step < steps else moving[0], 'col', nearest)  12.1 us
    ppermute x1, waiting for transfers between devices, per_device(): received = [lax.ppermute(above, 'row', pairs) for pairs in shifts]  7.02 us
    pallas_call x7, Pallas kernels, kernel_call(): pl.pallas_call(body, out_shape=out_shapes, in_specs=[hbm] * in_hbm + [vme...  4.88 us
    ppermute x1, waiting for transfers between devices, per_device(): tri = [own] + [lax.ppermute(own, 'row', pairs) for pairs in shifts]  3.1 us
    ppermute x8, starting transfers between devices, ring(): pieces += [moving, lax.ppermute(moving, 'col', swap)]  2.26 us
    unnamed x6, local copies, waits for them, and re-layouts  1.79 us
    ppermute x1, starting transfers between devices, per_device(): received = [lax.ppermute(above, 'row', pairs) for pairs in shifts]  1.58 us
  transfers between devices with their start and end apart: 21, of which 10 were waited for; matrix products, arithmetic and copies ran while one was open for 0% of the time, Pallas kernels for 3%

profile of v3, /device:TPU:0, one launch (start us, length us, event | category | flops | bytes accessed | tf_op | source)
XLA Modules:
  0.0 51.6 jit_solution(13511973094095263644)
XLA Ops:
  0.0 0.9 %copy-done.1 = f32[4,16,1024]{2,1,0:T(8,128)S(1)} copy-done((f32[4,16,1024]{2,1,0:T(8,128)S(1)}, f32[4,16,1024]{2,1,0:T(8,128)}, u32[]{:S(2)}) %copy-start.1) | copy-done | bytes 262168
  1.0 0.8 %copy-done.2 = f32[4,16,256]{2,1,0:T(8,128)S(1)} copy-done((f32[4,16,256]{2,1,0:T(8,128)S(1)}, f32[4,16,256]{2,1,0:T(8,128)}, u32[]{:S(2)}) %copy-start.2) | copy-done | bytes 65560
  2.6 1.2 %collective-permute-done.8.refs_2_ = f32[4,16,256]{2,1,0:T(8,128)S(1)} collective-permute-done((f32[4,16,256]{2,1,0:T(8,128)S(1)}, f32[4,16,256]{2,1,0:T(8,128)S(1)}, u32[]{:S(2)}, u32[]{:S(2)}) %collective-permute-start.8) | collective-permute-done | bytes 65568 | tf_op jit(solution)/shard_map/ppermute | solution.py:306
  3.8 3.0 %collective-permute-start.9 = (f32[2,9,16,256]{3,2,1,0:T(8,128)S(1)}, f32[2,9,16,256]{3,2,1,0:T(8,128)S(1)}, u32[]{:S(2)}, u32[]{:S(2)}) collective-permute-start(f32[2,9,16,256]{3,2,1,0:T(8,128)S(1)} %shard_map.40.refs_0_), channel_id=1, source_target_pairs={{0,4},{1,3},{4,8},{5,1},{8,12},{9,5},{12,14},{13,9},{14,10},{15,13... | collective-permute-start | bytes 884744 | tf_op jit(solution)/shard_map/ppermute | solution.py:67
  6.8 1.5 %collective-permute-start = (f32[3,16,512]{2,1,0:T(8,128)S(1)}, f32[3,16,512]{2,1,0:T(8,128)S(1)}, u32[]{:S(2)}, u32[]{:S(2)}) collective-permute-start(f32[3,16,512]{2,1,0:T(8,128)S(1)} %get-tuple-element.15.refs_0_), channel_id=1, source_target_pairs={{16,0},{0,16},{17,1},{1,17},{18,2},{2,18},{19,3},{3,19},{20,4},{4,... | collective-permute-start | bytes 294920 | tf_op jit(solution)/shard_map/ppermute | solution.py:308
  8.3 3.1 %collective-permute-done.refs_1_ = f32[3,16,512]{2,1,0:T(8,128)S(1)} collective-permute-done((f32[3,16,512]{2,1,0:T(8,128)S(1)}, f32[3,16,512]{2,1,0:T(8,128)S(1)}, u32[]{:S(2)}, u32[]{:S(2)}) %collective-permute-start) | collective-permute-done | bytes 98336 | tf_op jit(solution)/shard_map/ppermute | solution.py:308
  11.5 1.3 %collective-permute-done.1.refs_2_ = f32[6,16,256]{2,1,0:T(8,128)S(1)} collective-permute-done((f32[6,16,256]{2,1,0:T(8,128)S(1)}, f32[6,16,256]{2,1,0:T(8,128)S(1)}, u32[]{:S(2)}, u32[]{:S(2)}) %collective-permute-start.1) | collective-permute-done | bytes 98336 | tf_op jit(solution)/shard_map/ppermute | solution.py:312
  12.8 1.6 %collective-permute-start.3 = (f32[2,9,16,256]{3,2,1,0:T(8,128)S(1)}, f32[2,9,16,256]{3,2,1,0:T(8,128)S(1)}, u32[]{:S(2)}, u32[]{:S(2)}) collective-permute-start(f32[2,9,16,256]{3,2,1,0:T(8,128)S(1)} %shard_map.39.refs_0_), channel_id=1, source_target_pairs={{0,4},{1,3},{4,8},{5,1},{8,12},{9,5},{12,14},{13,9},{14,10},{15,13... | collective-permute-start | bytes 884744 | tf_op jit(solution)/shard_map/ppermute | solution.py:67
  14.5 1.6 %collective-permute-start.11 = (f32[2,9,16,256]{3,2,1,0:T(8,128)S(1)}, f32[2,9,16,256]{3,2,1,0:T(8,128)S(1)}, u32[]{:S(2)}, u32[]{:S(2)}) collective-permute-start(f32[2,9,16,256]{3,2,1,0:T(8,128)S(1)} %collective-permute-done.9.refs_1_), channel_id=1, source_target_pairs={{0,4},{1,3},{4,8},{5,1},{8,12},{9,5},{12,14},{13,9},{14,10},{15,13... | collective-permute-start | bytes 884744 | tf_op jit(solution)/shard_map/ppermute | solution.py:67
  16.0 3.6 %collective-permute-done.3.refs_1_ = f32[2,9,16,256]{3,2,1,0:T(8,128)S(1)} collective-permute-done((f32[2,9,16,256]{3,2,1,0:T(8,128)S(1)}, f32[2,9,16,256]{3,2,1,0:T(8,128)S(1)}, u32[]{:S(2)}, u32[]{:S(2)}) %collective-permute-start.3) | collective-permute-done | bytes 294944 | tf_op jit(solution)/shard_map/ppermute | solution.py:67
  19.6 1.6 %collective-permute-start.4 = (f32[2,9,16,256]{3,2,1,0:T(8,128)S(1)}, f32[2,9,16,256]{3,2,1,0:T(8,128)S(1)}, u32[]{:S(2)}, u32[]{:S(2)}) collective-permute-start(f32[2,9,16,256]{3,2,1,0:T(8,128)S(1)} %collective-permute-done.3.refs_1_), channel_id=1, source_target_pairs={{0,4},{1,3},{4,8},{5,1},{8,12},{9,5},{12,14},{13,9},{14,10},{15,13... | collective-permute-start | bytes 884744 | tf_op jit(solution)/shard_map/ppermute | solution.py:67
  21.2 1.6 %collective-permute-done.11.refs_3_ = f32[2,9,16,256]{3,2,1,0:T(8,128)S(1)} collective-permute-done((f32[2,9,16,256]{3,2,1,0:T(8,128)S(1)}, f32[2,9,16,256]{3,2,1,0:T(8,128)S(1)}, u32[]{:S(2)}, u32[]{:S(2)}) %collective-permute-start.11) | collective-permute-done | bytes 294944 | tf_op jit(solution)/shard_map/ppermute | solution.py:67
  22.8 1.6 %collective-permute-start.13 = (f32[2,9,16,256]{3,2,1,0:T(8,128)S(1)}, f32[2,9,16,256]{3,2,1,0:T(8,128)S(1)}, u32[]{:S(2)}, u32[]{:S(2)}) collective-permute-start(f32[2,9,16,256]{3,2,1,0:T(8,128)S(1)} %collective-permute-done.11.refs_3_), channel_id=1, source_target_pairs={{0,4},{1,3},{4,8},{5,1},{8,12},{9,5},{12,14},{13,9},{14,10},{15,13... | collective-permute-start | bytes 884744 | tf_op jit(solution)/shard_map/ppermute | solution.py:67
  24.3 2.0 %collective-permute-done.4.refs_3_ = f32[2,9,16,256]{3,2,1,0:T(8,128)S(1)} collective-permute-done((f32[2,9,16,256]{3,2,1,0:T(8,128)S(1)}, f32[2,9,16,256]{3,2,1,0:T(8,128)S(1)}, u32[]{:S(2)}, u32[]{:S(2)}) %collective-permute-start.4) | collective-permute-done | bytes 294944 | tf_op jit(solution)/shard_map/ppermute | solution.py:67
  26.3 1.6 %collective-permute-start.5 = (f32[2,9,16,256]{3,2,1,0:T(8,128)S(1)}, f32[2,9,16,256]{3,2,1,0:T(8,128)S(1)}, u32[]{:S(2)}, u32[]{:S(2)}) collective-permute-start(f32[2,9,16,256]{3,2,1,0:T(8,128)S(1)} %collective-permute-done.4.refs_3_), channel_id=1, source_target_pairs={{0,4},{1,3},{4,8},{5,1},{8,12},{9,5},{12,14},{13,9},{14,10},{15,13... | collective-permute-start | bytes 884744 | tf_op jit(solution)/shard_map/ppermute | solution.py:67
  27.9 1.6 %collective-permute-start.17 = (f32[512,256]{1,0:T(8,128)S(1)}, f32[512,256]{1,0:T(8,128)S(1)}, u32[]{:S(2)}, u32[]{:S(2)}) collective-permute-start(f32[512,256]{1,0:T(8,128)S(1)} %slice.11), channel_id=1, source_target_pairs={{16,0},{0,16},{17,1},{1,17},{18,2},{2,18},{19,3},{3,19},{20,4},{4,... | collective-permute-start | bytes 1572872 | tf_op jit(solution)/shard_map/ppermute | solution.py:310
  30.1 1.6 %collective-permute-start.15 = (f32[9,16,256]{2,1,0:T(8,128)S(1)}, f32[9,16,256]{2,1,0:T(8,128)S(1)}, u32[]{:S(2)}, u32[]{:S(2)}) collective-permute-start(f32[9,16,256]{2,1,0:T(8,128)S(1)} %slice_bitcast_fusion), channel_id=1, source_target_pairs={{0,4},{1,3},{4,8},{5,1},{8,12},{9,5},{12,14},{13,9},{14,10},{15,13... | collective-permute-start | bytes 442376 | tf_op jit(solution)/shard_map/ppermute | solution.py:67
  31.7 1.4 %collective-permute-done.5.refs_5_ = f32[2,9,16,256]{3,2,1,0:T(8,128)S(1)} collective-permute-done((f32[2,9,16,256]{3,2,1,0:T(8,128)S(1)}, f32[2,9,16,256]{3,2,1,0:T(8,128)S(1)}, u32[]{:S(2)}, u32[]{:S(2)}) %collective-permute-start.5) | collective-permute-done | bytes 294944 | tf_op jit(solution)/shard_map/ppermute | solution.py:67
  33.1 7.0 %collective-permute-done.17.refs_10_.refs_9_ = f32[512,256]{1,0:T(8,128)S(1)} collective-permute-done((f32[512,256]{1,0:T(8,128)S(1)}, f32[512,256]{1,0:T(8,128)S(1)}, u32[]{:S(2)}, u32[]{:S(2)}) %collective-permute-start.17) | collective-permute-done | bytes 524320 | tf_op jit(solution)/shard_map/ppermute | solution.py:310
  40.6 0.8 %collective-permute-start.6 = (f32[9,16,256]{2,1,0:T(8,128)S(1)}, f32[9,16,256]{2,1,0:T(8,128)S(1)}, u32[]{:S(2)}, u32[]{:S(2)}) collective-permute-start(f32[9,16,256]{2,1,0:T(8,128)S(1)} %slice_bitcast_fusion.1), channel_id=1, source_target_pairs={{0,4},{1,3},{4,8},{5,1},{8,12},{9,5},{12,14},{13,9},{14,10},{15,13... | collective-permute-start | bytes 442376 | tf_op jit(solution)/shard_map/ppermute | solution.py:67
  41.4 0.7 %collective-permute-start.14 = (f32[2,9,16,256]{3,2,1,0:T(8,128)S(1)}, f32[2,9,16,256]{3,2,1,0:T(8,128)S(1)}, u32[]{:S(2)}, u32[]{:S(2)}) collective-permute-start(f32[2,9,16,256]{3,2,1,0:T(8,128)S(1)} %collective-permute-done.13.refs_5_), channel_id=1, source_target_pairs={{0,1},{1,0},{2,3},{3,2},{4,5},{5,4},{6,7},{7,6},{8,9},{9,8},{10,11... | collective-permute-start | bytes 884744 | tf_op jit(solution)/shard_map/ppermute | solution.py:68
  42.1 3.6 %collective-permute-done.6.refs_0_ = f32[9,16,256]{2,1,0:T(8,128)S(1)} collective-permute-done((f32[9,16,256]{2,1,0:T(8,128)S(1)}, f32[9,16,256]{2,1,0:T(8,128)S(1)}, u32[]{:S(2)}, u32[]{:S(2)}) %collective-permute-start.6) | collective-permute-done | bytes 147488 | tf_op jit(solution)/shard_map/ppermute | solution.py:67
  47.1 1.0 %shard_map.41 = (bf16[9,256,256]{2,1,0:T(8,128)(2,1)S(1)}, bf16[9,256,256]{2,1,0:T(8,128)(2,1)S(1)}, f32[256,256]{1,0:T(8,128)S(1)}, f32[512,256]{1,0:T(8,128)S(1)}) custom-call(f32[2,9,16,256]{3,2,1,0:T(8,128)S(1)} %shard_map.40.refs_0_, f32[2,9,16,256]{3,2,1,0:T(8,128)S(1)} %collective-permute-done.9.refs_1_, ...), custom_call_target="tpu_custom_call" | custom-call | flops 301989888 | bytes 4194304 | tf_op jit(solution)/shard_map/pallas_call | solution.py:42
  48.2 3.4 %shard_map.43 = (f32[1024,256]{1,0:T(8,128)}, bf16[9,256,256]{2,1,0:T(8,128)(2,1)S(1)}, bf16[9,256,256]{2,1,0:T(8,128)(2,1)S(1)}) custom-call(f32[9,16,256]{2,1,0:T(8,128)S(1)} %collective-permute-done.6.refs_0_, f32[9,16,256]{2,1,0:T(8,128)S(1)} %collective-permute-done.7.refs_1_, ...), custom_call_target="tpu_custom_call", output_to_operand_aliasing={{1}: (4, {}), {2}: (5, {})} | custom-call | flops 1509949440 | bytes 4194304 | tf_op jit(solution)/shard_map/pallas_call | solution.py:42
  (34 shorter events, 3.4 us)
Async XLA Ops:
  0.0 0.9 %copy-start.1 = (f32[4,16,1024]{2,1,0:T(8,128)S(1)}, f32[4,16,1024]{2,1,0:T(8,128)}, u32[]{:S(2)}) copy-start(f32[4,16,1024]{2,1,0:T(8,128)} %factor_hbm.1) | copy-start | bytes 786436
  1.0 0.8 %copy-start.2 = (f32[4,16,256]{2,1,0:T(8,128)S(1)}, f32[4,16,256]{2,1,0:T(8,128)}, u32[]{:S(2)}) copy-start(f32[4,16,256]{2,1,0:T(8,128)} %inv_hbm.1) | copy-start | bytes 196612
  1.9 26.0 %copy-start = (f32[1024,256]{1,0:T(8,128)S(1)}, f32[1024,256]{1,0:T(8,128)}, u32[]{:S(2)}) copy-start(f32[1024,256]{1,0:T(8,128)} %refs_8_.1) | copy-start | bytes 3145732
  2.0 1.8 %collective-permute-start.2 = (f32[4,16,1024]{2,1,0:T(8,128)S(1)}, f32[4,16,1024]{2,1,0:T(8,128)S(1)}, u32[]{:S(2)}, u32[]{:S(2)}) collective-permute-start(f32[4,16,1024]{2,1,0:T(8,128)S(1)} %get-tuple-element.16.refs_1_), channel_id=1, source_target_pairs={{0,1},{1,0},{2,3},{3,2},{4,5},{5,4},{6,7},{7,6},{8,9},{9,8},{10,11... | collective-permute-start | bytes 786440 | tf_op jit(solution)/shard_map/ppermute | solution.py:307
  2.5 1.3 %collective-permute-start.8 = (f32[4,16,256]{2,1,0:T(8,128)S(1)}, f32[4,16,256]{2,1,0:T(8,128)S(1)}, u32[]{:S(2)}, u32[]{:S(2)}) collective-permute-start(f32[4,16,256]{2,1,0:T(8,128)S(1)} %get-tuple-element.17.refs_0_), channel_id=1, source_target_pairs={{0,1},{1,0},{2,3},{3,2},{4,5},{5,4},{6,7},{7,6},{8,9},{9,8},{10,11... | collective-permute-start | bytes 196616 | tf_op jit(solution)/shard_map/ppermute | solution.py:306
  3.8 10.7 %collective-permute-start.9 = (f32[2,9,16,256]{3,2,1,0:T(8,128)S(1)}, f32[2,9,16,256]{3,2,1,0:T(8,128)S(1)}, u32[]{:S(2)}, u32[]{:S(2)}) collective-permute-start(f32[2,9,16,256]{3,2,1,0:T(8,128)S(1)} %shard_map.40.refs_0_), channel_id=1, source_target_pairs={{0,4},{1,3},{4,8},{5,1},{8,12},{9,5},{12,14},{13,9},{14,10},{15,13... | collective-permute-start | bytes 884744 | tf_op jit(solution)/shard_map/ppermute | solution.py:67
  6.8 4.6 %collective-permute-start = (f32[3,16,512]{2,1,0:T(8,128)S(1)}, f32[3,16,512]{2,1,0:T(8,128)S(1)}, u32[]{:S(2)}, u32[]{:S(2)}) collective-permute-start(f32[3,16,512]{2,1,0:T(8,128)S(1)} %get-tuple-element.15.refs_0_), channel_id=1, source_target_pairs={{16,0},{0,16},{17,1},{1,17},{18,2},{2,18},{19,3},{3,19},{20,4},{4,... | collective-permute-start | bytes 294920 | tf_op jit(solution)/shard_map/ppermute | solution.py:308
  11.4 1.4 %collective-permute-start.1 = (f32[6,16,256]{2,1,0:T(8,128)S(1)}, f32[6,16,256]{2,1,0:T(8,128)S(1)}, u32[]{:S(2)}, u32[]{:S(2)}) collective-permute-start(f32[6,16,256]{2,1,0:T(8,128)S(1)} %shard_map.38.refs_0_), channel_id=1, source_target_pairs={{0,1},{1,0},{2,3},{3,2},{4,5},{5,4},{6,7},{7,6},{8,9},{9,8},{10,11... | collective-permute-start | bytes 294920 | tf_op jit(solution)/shard_map/ppermute | solution.py:312
  12.8 6.8 %collective-permute-start.3 = (f32[2,9,16,256]{3,2,1,0:T(8,128)S(1)}, f32[2,9,16,256]{3,2,1,0:T(8,128)S(1)}, u32[]{:S(2)}, u32[]{:S(2)}) collective-permute-start(f32[2,9,16,256]{3,2,1,0:T(8,128)S(1)} %shard_map.39.refs_0_), channel_id=1, source_target_pairs={{0,4},{1,3},{4,8},{5,1},{8,12},{9,5},{12,14},{13,9},{14,10},{15,13... | collective-permute-start | bytes 884744 | tf_op jit(solution)/shard_map/ppermute | solution.py:67
  14.5 8.3 %collective-permute-start.11 = (f32[2,9,16,256]{3,2,1,0:T(8,128)S(1)}, f32[2,9,16,256]{3,2,1,0:T(8,128)S(1)}, u32[]{:S(2)}, u32[]{:S(2)}) collective-permute-start(f32[2,9,16,256]{3,2,1,0:T(8,128)S(1)} %collective-permute-done.9.refs_1_), channel_id=1, source_target_pairs={{0,4},{1,3},{4,8},{5,1},{8,12},{9,5},{12,14},{13,9},{14,10},{15,13... | collective-permute-start | bytes 884744 | tf_op jit(solution)/shard_map/ppermute | solution.py:67
  19.6 6.7 %collective-permute-start.4 = (f32[2,9,16,256]{3,2,1,0:T(8,128)S(1)}, f32[2,9,16,256]{3,2,1,0:T(8,128)S(1)}, u32[]{:S(2)}, u32[]{:S(2)}) collective-permute-start(f32[2,9,16,256]{3,2,1,0:T(8,128)S(1)} %collective-permute-done.3.refs_1_), channel_id=1, source_target_pairs={{0,4},{1,3},{4,8},{5,1},{8,12},{9,5},{12,14},{13,9},{14,10},{15,13... | collective-permute-start | bytes 884744 | tf_op jit(solution)/shard_map/ppermute | solution.py:67
  22.8 7.3 %collective-permute-start.13 = (f32[2,9,16,256]{3,2,1,0:T(8,128)S(1)}, f32[2,9,16,256]{3,2,1,0:T(8,128)S(1)}, u32[]{:S(2)}, u32[]{:S(2)}) collective-permute-start(f32[2,9,16,256]{3,2,1,0:T(8,128)S(1)} %collective-permute-done.11.refs_3_), channel_id=1, source_target_pairs={{0,4},{1,3},{4,8},{5,1},{8,12},{9,5},{12,14},{13,9},{14,10},{15,13... | collective-permute-start | bytes 884744 | tf_op jit(solution)/shard_map/ppermute | solution.py:67
  26.3 6.7 %collective-permute-start.5 = (f32[2,9,16,256]{3,2,1,0:T(8,128)S(1)}, f32[2,9,16,256]{3,2,1,0:T(8,128)S(1)}, u32[]{:S(2)}, u32[]{:S(2)}) collective-permute-start(f32[2,9,16,256]{3,2,1,0:T(8,128)S(1)} %collective-permute-done.4.refs_3_), channel_id=1, source_target_pairs={{0,4},{1,3},{4,8},{5,1},{8,12},{9,5},{12,14},{13,9},{14,10},{15,13... | collective-permute-start | bytes 884744 | tf_op jit(solution)/shard_map/ppermute | solution.py:67
  27.9 12.1 %collective-permute-start.17 = (f32[512,256]{1,0:T(8,128)S(1)}, f32[512,256]{1,0:T(8,128)S(1)}, u32[]{:S(2)}, u32[]{:S(2)}) collective-permute-start(f32[512,256]{1,0:T(8,128)S(1)} %slice.11), channel_id=1, source_target_pairs={{16,0},{0,16},{17,1},{1,17},{18,2},{2,18},{19,3},{3,19},{20,4},{4,... | collective-permute-start | bytes 1572872 | tf_op jit(solution)/shard_map/ppermute | solution.py:310
  29.5 10.6 %collective-permute-start.18 = (f32[2,9,16,256]{3,2,1,0:T(8,128)S(1)}, f32[2,9,16,256]{3,2,1,0:T(8,128)S(1)}, u32[]{:S(2)}, u32[]{:S(2)}) collective-permute-start(f32[2,9,16,256]{3,2,1,0:T(8,128)S(1)} %collective-permute-done.3.refs_1_), channel_id=1, source_target_pairs={{0,1},{1,0},{2,3},{3,2},{4,5},{5,4},{6,7},{7,6},{8,9},{9,8},{10,11... | collective-permute-start | bytes 884744 | tf_op jit(solution)/shard_map/ppermute | solution.py:68
  29.5 11.1 %collective-permute-start.19 = (f32[2,9,16,256]{3,2,1,0:T(8,128)S(1)}, f32[2,9,16,256]{3,2,1,0:T(8,128)S(1)}, u32[]{:S(2)}, u32[]{:S(2)}) collective-permute-start(f32[2,9,16,256]{3,2,1,0:T(8,128)S(1)} %collective-permute-done.4.refs_3_), channel_id=1, source_target_pairs={{0,1},{1,0},{2,3},{3,2},{4,5},{5,4},{6,7},{7,6},{8,9},{9,8},{10,11... | collective-permute-start | bytes 884744 | tf_op jit(solution)/shard_map/ppermute | solution.py:68
  30.1 11.4 %collective-permute-start.15 = (f32[9,16,256]{2,1,0:T(8,128)S(1)}, f32[9,16,256]{2,1,0:T(8,128)S(1)}, u32[]{:S(2)}, u32[]{:S(2)}) collective-permute-start(f32[9,16,256]{2,1,0:T(8,128)S(1)} %slice_bitcast_fusion), channel_id=1, source_target_pairs={{0,4},{1,3},{4,8},{5,1},{8,12},{9,5},{12,14},{13,9},{14,10},{15,13... | collective-permute-start | bytes 442376 | tf_op jit(solution)/shard_map/ppermute | solution.py:67
  33.0 12.7 %collective-permute-start.20 = (f32[2,9,16,256]{3,2,1,0:T(8,128)S(1)}, f32[2,9,16,256]{3,2,1,0:T(8,128)S(1)}, u32[]{:S(2)}, u32[]{:S(2)}) collective-permute-start(f32[2,9,16,256]{3,2,1,0:T(8,128)S(1)} %collective-permute-done.5.refs_5_), channel_id=1, source_target_pairs={{0,1},{1,0},{2,3},{3,2},{4,5},{5,4},{6,7},{7,6},{8,9},{9,8},{10,11... | collective-permute-start | bytes 884744 | tf_op jit(solution)/shard_map/ppermute | solution.py:68
  40.1 6.4 %collective-permute-start.10 = (f32[2,9,16,256]{3,2,1,0:T(8,128)S(1)}, f32[2,9,16,256]{3,2,1,0:T(8,128)S(1)}, u32[]{:S(2)}, u32[]{:S(2)}) collective-permute-start(f32[2,9,16,256]{3,2,1,0:T(8,128)S(1)} %collective-permute-done.9.refs_1_), channel_id=1, source_target_pairs={{0,1},{1,0},{2,3},{3,2},{4,5},{5,4},{6,7},{7,6},{8,9},{9,8},{10,11... | collective-permute-start | bytes 884744 | tf_op jit(solution)/shard_map/ppermute | solution.py:68
  40.1 6.4 %collective-permute-start.12 = (f32[2,9,16,256]{3,2,1,0:T(8,128)S(1)}, f32[2,9,16,256]{3,2,1,0:T(8,128)S(1)}, u32[]{:S(2)}, u32[]{:S(2)}) collective-permute-start(f32[2,9,16,256]{3,2,1,0:T(8,128)S(1)} %collective-permute-done.11.refs_3_), channel_id=1, source_target_pairs={{0,1},{1,0},{2,3},{3,2},{4,5},{5,4},{6,7},{7,6},{8,9},{9,8},{10,11... | collective-permute-start | bytes 884744 | tf_op jit(solution)/shard_map/ppermute | solution.py:68
  40.6 5.1 %collective-permute-start.6 = (f32[9,16,256]{2,1,0:T(8,128)S(1)}, f32[9,16,256]{2,1,0:T(8,128)S(1)}, u32[]{:S(2)}, u32[]{:S(2)}) collective-permute-start(f32[9,16,256]{2,1,0:T(8,128)S(1)} %slice_bitcast_fusion.1), channel_id=1, source_target_pairs={{0,4},{1,3},{4,8},{5,1},{8,12},{9,5},{12,14},{13,9},{14,10},{15,13... | collective-permute-start | bytes 442376 | tf_op jit(solution)/shard_map/ppermute | solution.py:67
  41.4 5.7 %collective-permute-start.14 = (f32[2,9,16,256]{3,2,1,0:T(8,128)S(1)}, f32[2,9,16,256]{3,2,1,0:T(8,128)S(1)}, u32[]{:S(2)}, u32[]{:S(2)}) collective-permute-start(f32[2,9,16,256]{3,2,1,0:T(8,128)S(1)} %collective-permute-done.13.refs_5_), channel_id=1, source_target_pairs={{0,1},{1,0},{2,3},{3,2},{4,5},{5,4},{6,7},{7,6},{8,9},{9,8},{10,11... | collective-permute-start | bytes 884744 | tf_op jit(solution)/shard_map/ppermute | solution.py:68
  45.7 1.4 %collective-permute-start.16 = (f32[9,16,256]{2,1,0:T(8,128)S(1)}, f32[9,16,256]{2,1,0:T(8,128)S(1)}, u32[]{:S(2)}, u32[]{:S(2)}) collective-permute-start(f32[9,16,256]{2,1,0:T(8,128)S(1)} %collective-permute-done.15.refs_7_), channel_id=1, source_target_pairs={{0,1},{1,0},{2,3},{3,2},{4,5},{5,4},{6,7},{7,6},{8,9},{9,8},{10,11... | collective-permute-start | bytes 442376 | tf_op jit(solution)/shard_map/ppermute | solution.py:68
  45.7 2.4 %collective-permute-start.7 = (f32[9,16,256]{2,1,0:T(8,128)S(1)}, f32[9,16,256]{2,1,0:T(8,128)S(1)}, u32[]{:S(2)}, u32[]{:S(2)}) collective-permute-start(f32[9,16,256]{2,1,0:T(8,128)S(1)} %collective-permute-done.6.refs_0_), channel_id=1, source_target_pairs={{0,1},{1,0},{2,3},{3,2},{4,5},{5,4},{6,7},{7,6},{8,9},{9,8},{10,11... | collective-permute-start | bytes 442376 | tf_op jit(solution)/shard_map/ppermute | solution.py:68

commit v4 on v3

--- a/solution.py
+++ b/solution.py
@@ -7,7 +7,6 @@
 from jax.experimental.pallas import tpu as pltpu
 from jax.sharding import PartitionSpec as P
 
-CHUNKS = 2
 ROWS = ((0,), (0,))
 PLAIN = ((1,), (0,))
 
@@ -38,14 +37,14 @@
 
 
 def kernel_call(body, out_shapes, scratch, operands, flops=0, in_hbm=0, out_hbm=0, aliases={}):
-    vmem, hbm = pl.BlockSpec(memory_space=pltpu.VMEM), pl.BlockSpec(memory_space=pltpu.HBM)
+    near, hbm = pl.BlockSpec(memory_space=pltpu.VMEM), pl.BlockSpec(memory_space=pltpu.HBM)
     return pl.pallas_call(
         body,
         out_shape=out_shapes,
-        in_specs=[hbm] * in_hbm + [vmem] * (len(operands) - in_hbm),
-        out_specs=jax.tree.map(lambda _: vmem, out_shapes)
+        in_specs=[hbm] * in_hbm + [near] * (len(operands) - in_hbm),
+        out_specs=jax.tree.map(lambda _: near, out_shapes)
         if not out_hbm
-        else [hbm] * out_hbm + [vmem] * (len(out_shapes) - out_hbm),
+        else [hbm] * out_hbm + [near] * (len(out_shapes) - out_hbm),
         input_output_aliases=aliases,
         scratch_shapes=scratch,
         cost_estimate=pl.CostEstimate(flops=flops, bytes_accessed=4 << 20, transcendentals=0),
@@ -122,16 +121,12 @@
         self.deep = max(
             min(rank, panels - 1) for rank in range((self.held - 1) * group_count, self.held * group_count)
         )
-        low = [(panel, block) for panel in range(panels) for block in range(self.wide)]
-        total = panels + len(self.tri) + len(low)
-        inv = [("inv", panel) for panel in range(panels)]
-        tri = [("tri", at) for at in range(len(self.tri))]
-        low = [("low", *pair) for pair in low]
-        last = max(total // CHUNKS, len(tri))
-        rest = inv + low[: total - panels - last]
-        size = -(-len(rest) // (CHUNKS - 1))
-        self.chunks = [rest[at : at + size] for at in range(0, len(rest), size)]
-        self.chunks.append(tri + low[total - panels - last :])
+        low = [("low", panel, block) for panel in range(panels) for block in range(self.wide)]
+        self.chunks = [
+            [("inv", panel) for panel in range(panels)] + low[: self.wide],
+            low[self.wide :],
+            [("tri", at) for at in range(len(self.tri))],
+        ]
         self.where = {b: (c, at) for c, chunk in enumerate(self.chunks) for at, b in enumerate(chunk)}
 
     def mat(self, mats, *block):
@@ -187,16 +182,11 @@
 
 
 def prep_kernel(plan, *refs):
-    count, early = plan.chips + 1, len(plan.chunks) - 1
-    pieces = [refs[c * count : (c + 1) * count] for c in range(early)]
-    right_ref = refs[early * count]
-    outs = refs[-3 * early - 2 :]
-    received = refs[early * count + 1 : -3 * early - 2]
-    mats = [outs[2 * c : 2 * c + 2] for c in range(early)]
-    x_ref, total_ref = outs[2 * early : 2 * early + 2]
-    for c in range(early):
-        assemble(pieces[c], *mats[c], outs[2 * early + 2 + c], plan.chips)
-    nb = plan.nb
+    pieces, right_ref = refs[: plan.chips + 1], refs[plan.chips + 1]
+    received = refs[plan.chips + 2 : -5]
+    high_ref, low_ref, x_ref, total_ref, whole_ref = refs[-5:]
+    assemble(pieces, high_ref, low_ref, whole_ref, plan.chips)
+    mats, nb = [(high_ref, low_ref)], plan.nb
     answer = dot3(plan.mat(mats, "inv", 0), split(plan.panel_rows(0, right_ref, received)), PLAIN)
     x_ref[...] = answer
     solved = split(answer)
@@ -211,68 +201,72 @@
     assemble(refs[:-3], high_ref, low_ref, whole_ref, plan.chips, slice(0, plan.chips - 1))
 
 
+def late_pieces(plan, late):
+    return slice(plan.chips - 1, None) if late == 2 else slice(None)
+
+
+def solve_kernel(plan, late, *refs):
+    pieces = refs[:late]
+    inv_high, inv_low, x_first, right_ref = refs[late + 2 : late + 6]
+    received = refs[late + 6 : -6]
+    x_ref, x_high, x_low, high_ref, low_ref, whole_ref = refs[-6:]
+    assemble(pieces, high_ref, low_ref, whole_ref, plan.chips, late_pieces(plan, late))
+    mats = [(inv_high, inv_low), None, (high_ref, low_ref)]
+    panels = plan.panels
+    currents = [plan.panel_rows(panel, right_ref, received) for panel in range(panels)]
+    answer = x_first[...]
+    for panel in range(panels):
+        if panel > 0:
+            answer = dot3(plan.mat(mats, "inv", panel), split(currents[panel]), PLAIN)
+        x_ref[panel] = answer
+        solved = split(answer)
+        x_high[panel], x_low[panel] = solved
+        for after in range(panel + 1, panels):
+            mat = plan.mat(mats, "tri", plan.tri.index((after, panel)))
+            currents[after] = currents[after] - dot3(mat, solved, ROWS)
+
+
 def final_kernel(plan, late, *refs):
-    early = len(plan.chunks) - 1
-    pieces, at = refs[:late], late
-    mats = [refs[at + 2 * c : at + 2 * c + 2] for c in range(early)]
-    at += 2 * early
-    x_first, total_ref, right_ref = refs[at + 2 : at + 5]
-    received = refs[at + 5 : -7]
-    out_hbm, high_ref, low_ref, x_ref, low_rows, whole_ref, sems = refs[-7:]
-    panels, nb, wide = plan.panels, plan.nb, plan.wide
+    pieces = refs[:late]
+    x_ref, x_high, x_low, total_ref = refs[late + 2 : late + 6]
+    out_hbm, high_ref, low_ref, low_rows, whole_ref, sems = refs[-6:]
+    panels, nb = plan.panels, plan.nb
     me = lax.axis_index("row")
-    fresh = slice(plan.chips - 1, None) if late == 2 else slice(None)
-    assemble(pieces, high_ref, low_ref, whole_ref, plan.chips, fresh)
-    mats.append((high_ref, low_ref))
-
-    def copy_out(rank, local):
+
+    def panel_out(rank, local):
         rows = pl.ds(local * nb, nb)
         return pltpu.make_async_copy(x_ref.at[rank], out_hbm.at[rows], sems.at[local])
 
-    x_ref[0] = x_first[...]
-    solved = [split(x_first[...])]
-    currents = [plan.panel_rows(panel, right_ref, received) for panel in range(panels)]
-    totals = [total_ref[block * nb : (block + 1) * nb] for block in range(wide)]
-    for panel in range(1, panels):
-        for after in range(panel, panels):
-            mat = plan.mat(mats, "tri", plan.tri.index((after, panel - 1)))
-            currents[after] = currents[after] - dot3(mat, solved[panel - 1], ROWS)
-        answer = dot3(plan.mat(mats, "inv", panel), split(currents[panel]), PLAIN)
-        x_ref[panel] = answer
-        if panel > 1:
-            for block in range(wide):
-                mat = plan.mat(mats, "low", panel - 1, block)
-                totals[block] = totals[block] - dot3(mat, solved[panel - 1], ROWS)
-        solved.append(split(answer))
-    for local in range(plan.held):
-        rank = local * plan.group_count + me
-
-        @pl.when(rank < panels)
-        def _(rank=rank, local=local):
-            copy_out(rank, local).start()
-
+    def for_panels(act):
+        for local in range(plan.held):
+            rank = local * plan.group_count + me
+
+            @pl.when(rank < panels)
+            def _(rank=rank, local=local):
+                act(panel_out(rank, local))
+
+    for_panels(lambda copy: copy.start())
+    assemble(pieces, high_ref, low_ref, whole_ref, plan.chips, late_pieces(plan, late))
+    mats = [None, (high_ref, low_ref)]
     outs = []
-    for block in range(wide):
-        mat = plan.mat(mats, "low", panels - 1, block)
-        low_rows[block] = totals[block] - dot3(mat, solved[panels - 1], ROWS)
+    for block in range(plan.wide):
+        total = total_ref[block * nb : (block + 1) * nb]
+        for panel in range(1, panels):
+            mat = plan.mat(mats, "low", panel, block)
+            total = total - dot3(mat, (x_high[panel], x_low[panel]), ROWS)
+        low_rows[block] = total
         local = plan.sure + block
         out = pltpu.make_async_copy(
             low_rows.at[block], out_hbm.at[pl.ds(local * nb, nb)], sems.at[local]
         )
         if local < plan.held:
-            below = local * plan.group_count + me >= panels
-            pl.when(below)(out.start)
-            pl.when(below)(out.wait)
+            mine = local * plan.group_count + me >= panels
+            pl.when(mine)(out.start)
+            pl.when(mine)(out.wait)
         else:
             out.start()
             outs.append(out)
-    for local in range(plan.held):
-        rank = local * plan.group_count + me
-
-        @pl.when(rank < panels)
-        def _(rank=rank, local=local):
-            copy_out(rank, local).wait()
-
+    for_panels(lambda copy: copy.wait())
     for out in outs:
         out.wait()
 
@@ -300,7 +294,7 @@
             shape((plan.deep, depth, plan.held * nb), f32),
         ],
         [pltpu.SemaphoreType.DMA((3,))],
-        (factor_panels, inverses),
+        [pltpu.with_memory_space_constraint(a, pltpu.HBM) for a in (factor_panels, inverses)],
         in_hbm=2,
     )
     inv_other = lax.ppermute(inv, "col", swap)
@@ -312,50 +306,57 @@
     half_other = lax.ppermute(half, "col", swap)
 
     pieces = []
-    last = len(plan.chunks) - 1
-    for chunk in range(last + 1):
-        heads = (half, half_other) if chunk == last else (inv, inv_other)
+    for chunk, blocks in enumerate(plan.chunks):
+        heads = (half, half_other) if chunk == len(plan.chunks) - 1 else (inv, inv_other)
         packed = kernel_call(
             bound(pack_kernel, plan, chunk),
-            shape((2, len(plan.chunks[chunk]), depth, nb), f32),
+            shape((2, len(blocks), depth, nb), f32),
             [],
             (heads[0], factor, heads[1], factor_other),
         )
         pieces.append(ring(packed, chips))
 
-    split_shapes = [[shape((len(chunk), nb, nb), bf16)] * 2 for chunk in plan.chunks]
-    *mats, x_first, total = kernel_call(
+    pairs = [[shape((len(blocks), nb, nb), bf16)] * 2 for blocks in plan.chunks]
+    wholes = [whole_scratch(len(blocks), nb, depth) for blocks in plan.chunks]
+
+    def place(chunk):
+        if depth % 16 != 0:
+            return [jnp.zeros(s.shape, s.dtype) for s in pairs[chunk]], pieces[chunk]
+        done = kernel_call(
+            bound(place_kernel, plan), pairs[chunk], [wholes[chunk]], pieces[chunk][: chips - 1]
+        )
+        return done, pieces[chunk][chips - 1 :]
+
+    inv_high, inv_low, x_first, total = kernel_call(
         bound(prep_kernel, plan),
-        [s for pair in split_shapes[:-1] for s in pair]
-        + [shape((nb, columns), f32), shape((plan.wide * nb, columns), f32)],
-        [whole_scratch(len(chunk), nb, depth) for chunk in plan.chunks[:-1]],
-        (*(piece for chunk in pieces[:-1] for piece in chunk), right_side, *received),
+        [*pairs[0], shape((nb, columns), f32), shape((plan.wide * nb, columns), f32)],
+        [wholes[0]],
+        (*pieces[0], right_side, *received),
         flops=6 * 3 * nb * nb * columns,
     )
-    whole = whole_scratch(len(plan.chunks[-1]), nb, depth)
-    aligned = depth % 16 == 0
-    if aligned:
-        placed = kernel_call(
-            bound(place_kernel, plan), split_shapes[-1], [whole], pieces[-1][: chips - 1]
-        )
-        late = pieces[-1][chips - 1 :]
-    else:
-        placed = [jnp.zeros(s.shape, s.dtype) for s in split_shapes[-1]]
-        late = pieces[-1]
-    at = len(late) + len(mats)
+    placed, late = place(2)
+    answers = [shape((panels, nb, columns), t) for t in (f32, bf16, bf16)]
+    x, x_high, x_low, _, _ = kernel_call(
+        bound(solve_kernel, plan, len(late)),
+        [*answers, *pairs[2]],
+        [wholes[2]],
+        (*late, *placed, inv_high, inv_low, x_first, right_side, *received),
+        flops=6 * 9 * nb * nb * columns,
+        aliases={len(late): 3, len(late) + 1: 4},
+    )
+    placed, late = place(1)
     out, _, _ = kernel_call(
         bound(final_kernel, plan, len(late)),
-        [shape(right_side.shape, f32), *split_shapes[-1]],
+        [shape(right_side.shape, f32), *pairs[1]],
         [
-            pltpu.VMEM((panels, nb, columns), f32),
             pltpu.VMEM((plan.wide, nb, columns), f32),
-            whole,
+            wholes[1],
             pltpu.SemaphoreType.DMA((rows // nb,)),
         ],
-        (*late, *mats, *placed, x_first, total, right_side, *received),
-        flops=6 * 15 * nb * nb * columns,
+        (*late, *placed, x, x_high, x_low, total),
+        flops=6 * 6 * nb * nb * columns,
         out_hbm=1,
-        aliases={at: 1, at + 1: 2},
+        aliases={len(late): 1, len(late) + 1: 2},
     )
     return out
 

time: 51.7 us -> 45.6 us (0.88)
  waiting for transfers between devices: 25.3 us -> 13.1 us
  starting transfers between devices: 19.4 us -> 25.8 us
  local copies, waits for them, and re-layouts: 1.85 us -> 0.06 us
  Pallas kernels: 4.88 us -> 6.32 us
    ppermute x1, waiting for transfers between devices: 7.02 us -> 0.28 us  [per_device(): received = [lax.ppermute(above, 'row', pairs) for pairs in shifts]]
    ppermute x8 -> x12, starting transfers between devices: 13.4 us -> 18.9 us  [ring(): moving = lax.ppermute(moving if step < steps else moving[0], 'col', nearest)]
    ppermute x8 -> x12, waiting for transfers between devices: 12.1 us -> 10.1 us  [ring(): moving = lax.ppermute(moving if step < steps else moving[0], 'col', nearest)]
    unnamed x6 -> x2, local copies, waits for them, and re-layouts: 1.79 us -> 0.01 us
    ppermute x1, waiting for transfers between devices: 3.1 us -> 1.38 us  [per_device(): tri = [own] + [lax.ppermute(own, 'row', pairs) for pairs in shifts]]
    pallas_call x7 -> x10, Pallas kernels: 4.88 us -> 6.32 us  [kernel_call(): pl.pallas_call(body, out_shape=out_shapes, in_specs=[hbm] * in_hbm + [nea...]
    ppermute x1, starting transfers between devices: 1.52 us -> 2.93 us  [per_device(): tri = [own] + [lax.ppermute(own, 'row', pairs) for pairs in shifts]]
    ppermute x1, waiting for transfers between devices: 1.18 us -> 0.01 us  [per_device(): inv_other = lax.ppermute(inv, 'col', swap)]
  transfers between devices with their start and end apart: 21 -> 29, of which waited for: 10 -> 12; matrix products, arithmetic and copies ran while one was open for 0% -> 0% of each run, Pallas kernels for 3% -> 8%
where the time goes in v4:
time: 45.6 us; the launch traced here: 45.4 us
  starting transfers between devices  25.8 us (57%)
  waiting for transfers between devices  13.1 us (29%)
  Pallas kernels  6.32 us (14%)
    ppermute x12, starting transfers between devices, ring(): moving = lax.ppermute(moving if step < steps else moving[0], 'col', nearest)  18.9 us
    ppermute x12, waiting for transfers between devices, ring(): moving = lax.ppermute(moving if step < steps else moving[0], 'col', nearest)  10.1 us
    pallas_call x10, Pallas kernels, kernel_call(): pl.pallas_call(body, out_shape=out_shapes, in_specs=[hbm] * in_hbm + [nea...  6.32 us
    ppermute x1, starting transfers between devices, per_device(): tri = [own] + [lax.ppermute(own, 'row', pairs) for pairs in shifts]  2.93 us
    ppermute x12, starting transfers between devices, ring(): pieces += [moving, lax.ppermute(moving, 'col', swap)]  1.61 us
    ppermute x1, starting transfers between devices, per_device(): received = [lax.ppermute(above, 'row', pairs) for pairs in shifts]  1.58 us
    ppermute x1, waiting for transfers between devices, per_device(): tri = [own] + [lax.ppermute(own, 'row', pairs) for pairs in shifts]  1.38 us
    ppermute x1, waiting for transfers between devices, per_device(): half_other = lax.ppermute(half, 'col', swap)  1.29 us
  transfers between devices with their start and end apart: 29, of which 12 were waited for; matrix products, arithmetic and copies ran while one was open for 0% of the time, Pallas kernels for 8%

profile of v4, /device:TPU:0, one launch (start us, length us, event | category | flops | bytes accessed | tf_op | source)
XLA Modules:
  0.0 45.4 jit_solution(15365018005879183342)
XLA Ops:
  0.0 1.1 %shard_map.37 = (f32[4,16,1024]{2,1,0:T(8,128)S(1)}, f32[4,16,256]{2,1,0:T(8,128)S(1)}, f32[3,16,512]{2,1,0:T(8,128)S(1)}) custom-call(f32[4,16,1024]{2,1,0:T(8,128)} %factor_hbm.1, f32[4,16,256]{2,1,0:T(8,128)} %inv_hbm.1), custom_call_target="tpu_custom_call" | custom-call | bytes 4194304 | tf_op jit(solution)/shard_map/pallas_call | solution.py:41
  1.7 2.9 %collective-permute-start.10 = (f32[3,16,512]{2,1,0:T(8,128)S(1)}, f32[3,16,512]{2,1,0:T(8,128)S(1)}, u32[]{:S(2)}, u32[]{:S(2)}) collective-permute-start(f32[3,16,512]{2,1,0:T(8,128)S(1)} %get-tuple-element.24.refs_0_), channel_id=1, source_target_pairs={{16,0},{0,16},{17,1},{1,17},{18,2},{2,18},{19,3},{3,19},{20,4},{4,... | collective-permute-start | bytes 294920 | tf_op jit(solution)/shard_map/ppermute | solution.py:302
  4.7 1.6 %collective-permute-start.20 = (f32[2,6,16,256]{3,2,1,0:T(8,128)S(1)}, f32[2,6,16,256]{3,2,1,0:T(8,128)S(1)}, u32[]{:S(2)}, u32[]{:S(2)}) collective-permute-start(f32[2,6,16,256]{3,2,1,0:T(8,128)S(1)} %shard_map.43.refs_0_), channel_id=1, source_target_pairs={{0,4},{1,3},{4,8},{5,1},{8,12},{9,5},{12,14},{13,9},{14,10},{15,13... | collective-permute-start | bytes 589832 | tf_op jit(solution)/shard_map/ppermute | solution.py:66
  6.3 1.4 %collective-permute-done.10.refs_1_ = f32[3,16,512]{2,1,0:T(8,128)S(1)} collective-permute-done((f32[3,16,512]{2,1,0:T(8,128)S(1)}, f32[3,16,512]{2,1,0:T(8,128)S(1)}, u32[]{:S(2)}, u32[]{:S(2)}) %collective-permute-start.10) | collective-permute-done | bytes 98336 | tf_op jit(solution)/shard_map/ppermute | solution.py:302
  7.8 1.3 %collective-permute-done.11.refs_2_ = f32[6,16,256]{2,1,0:T(8,128)S(1)} collective-permute-done((f32[6,16,256]{2,1,0:T(8,128)S(1)}, f32[6,16,256]{2,1,0:T(8,128)S(1)}, u32[]{:S(2)}, u32[]{:S(2)}) %collective-permute-start.11) | collective-permute-done | bytes 98336 | tf_op jit(solution)/shard_map/ppermute | solution.py:306
  9.1 1.9 %collective-permute-start.12 = (f32[2,6,16,256]{3,2,1,0:T(8,128)S(1)}, f32[2,6,16,256]{3,2,1,0:T(8,128)S(1)}, u32[]{:S(2)}, u32[]{:S(2)}) collective-permute-start(f32[2,6,16,256]{3,2,1,0:T(8,128)S(1)} %shard_map.41.refs_0_), channel_id=1, source_target_pairs={{0,4},{1,3},{4,8},{5,1},{8,12},{9,5},{12,14},{13,9},{14,10},{15,13... | collective-permute-start | bytes 589832 | tf_op jit(solution)/shard_map/ppermute | solution.py:66
  11.0 1.6 %collective-permute-start.22 = (f32[2,6,16,256]{3,2,1,0:T(8,128)S(1)}, f32[2,6,16,256]{3,2,1,0:T(8,128)S(1)}, u32[]{:S(2)}, u32[]{:S(2)}) collective-permute-start(f32[2,6,16,256]{3,2,1,0:T(8,128)S(1)} %collective-permute-done.20.refs_1_), channel_id=1, source_target_pairs={{0,4},{1,3},{4,8},{5,1},{8,12},{9,5},{12,14},{13,9},{14,10},{15,13... | collective-permute-start | bytes 589832 | tf_op jit(solution)/shard_map/ppermute | solution.py:66
  12.6 1.6 %collective-permute-start.28 = (f32[512,256]{1,0:T(8,128)S(1)}, f32[512,256]{1,0:T(8,128)S(1)}, u32[]{:S(2)}, u32[]{:S(2)}) collective-permute-start(f32[512,256]{1,0:T(8,128)S(1)} %slice.15), channel_id=1, source_target_pairs={{16,0},{0,16},{17,1},{1,17},{18,2},{2,18},{19,3},{3,19},{20,4},{4,... | collective-permute-start | bytes 1572872 | tf_op jit(solution)/shard_map/ppermute | solution.py:304
  14.2 1.6 %collective-permute-start.2 = (f32[2,6,16,256]{3,2,1,0:T(8,128)S(1)}, f32[2,6,16,256]{3,2,1,0:T(8,128)S(1)}, u32[]{:S(2)}, u32[]{:S(2)}) collective-permute-start(f32[2,6,16,256]{3,2,1,0:T(8,128)S(1)} %shard_map.38.refs_0_), channel_id=1, source_target_pairs={{0,4},{1,3},{4,8},{5,1},{8,12},{9,5},{12,14},{13,9},{14,10},{15,13... | collective-permute-start | bytes 589832 | tf_op jit(solution)/shard_map/ppermute | solution.py:66
  15.8 1.5 %collective-permute-start.13 = (f32[2,6,16,256]{3,2,1,0:T(8,128)S(1)}, f32[2,6,16,256]{3,2,1,0:T(8,128)S(1)}, u32[]{:S(2)}, u32[]{:S(2)}) collective-permute-start(f32[2,6,16,256]{3,2,1,0:T(8,128)S(1)} %collective-permute-done.12.refs_1_), channel_id=1, source_target_pairs={{0,4},{1,3},{4,8},{5,1},{8,12},{9,5},{12,14},{13,9},{14,10},{15,13... | collective-permute-start | bytes 589832 | tf_op jit(solution)/shard_map/ppermute | solution.py:66
  17.3 1.4 %collective-permute-start.24 = (f32[2,6,16,256]{3,2,1,0:T(8,128)S(1)}, f32[2,6,16,256]{3,2,1,0:T(8,128)S(1)}, u32[]{:S(2)}, u32[]{:S(2)}) collective-permute-start(f32[2,6,16,256]{3,2,1,0:T(8,128)S(1)} %collective-permute-done.22.refs_3_), channel_id=1, source_target_pairs={{0,4},{1,3},{4,8},{5,1},{8,12},{9,5},{12,14},{13,9},{14,10},{15,13... | collective-permute-start | bytes 589832 | tf_op jit(solution)/shard_map/ppermute | solution.py:66
  18.7 1.2 %collective-permute-done.2.refs_1_ = f32[2,6,16,256]{3,2,1,0:T(8,128)S(1)} collective-permute-done((f32[2,6,16,256]{3,2,1,0:T(8,128)S(1)}, f32[2,6,16,256]{3,2,1,0:T(8,128)S(1)}, u32[]{:S(2)}, u32[]{:S(2)}) %collective-permute-start.2) | collective-permute-done | bytes 196640 | tf_op jit(solution)/shard_map/ppermute | solution.py:66
  19.9 2.1 %collective-permute-done.13.refs_3_ = f32[2,6,16,256]{3,2,1,0:T(8,128)S(1)} collective-permute-done((f32[2,6,16,256]{3,2,1,0:T(8,128)S(1)}, f32[2,6,16,256]{3,2,1,0:T(8,128)S(1)}, u32[]{:S(2)}, u32[]{:S(2)}) %collective-permute-start.13) | collective-permute-done | bytes 196640 | tf_op jit(solution)/shard_map/ppermute | solution.py:66
  22.0 1.6 %collective-permute-start.3 = (f32[2,6,16,256]{3,2,1,0:T(8,128)S(1)}, f32[2,6,16,256]{3,2,1,0:T(8,128)S(1)}, u32[]{:S(2)}, u32[]{:S(2)}) collective-permute-start(f32[2,6,16,256]{3,2,1,0:T(8,128)S(1)} %collective-permute-done.2.refs_1_), channel_id=1, source_target_pairs={{0,4},{1,3},{4,8},{5,1},{8,12},{9,5},{12,14},{13,9},{14,10},{15,13... | collective-permute-start | bytes 589832 | tf_op jit(solution)/shard_map/ppermute | solution.py:66
  24.1 1.6 %collective-permute-start.14 = (f32[2,6,16,256]{3,2,1,0:T(8,128)S(1)}, f32[2,6,16,256]{3,2,1,0:T(8,128)S(1)}, u32[]{:S(2)}, u32[]{:S(2)}) collective-permute-start(f32[2,6,16,256]{3,2,1,0:T(8,128)S(1)} %collective-permute-done.13.refs_3_), channel_id=1, source_target_pairs={{0,4},{1,3},{4,8},{5,1},{8,12},{9,5},{12,14},{13,9},{14,10},{15,13... | collective-permute-start | bytes 589832 | tf_op jit(solution)/shard_map/ppermute | solution.py:66
  26.5 1.2 %collective-permute-done.3.refs_3_ = f32[2,6,16,256]{3,2,1,0:T(8,128)S(1)} collective-permute-done((f32[2,6,16,256]{3,2,1,0:T(8,128)S(1)}, f32[2,6,16,256]{3,2,1,0:T(8,128)S(1)}, u32[]{:S(2)}, u32[]{:S(2)}) %collective-permute-start.3) | collective-permute-done | bytes 196640 | tf_op jit(solution)/shard_map/ppermute | solution.py:66
  27.7 1.6 %collective-permute-start.4 = (f32[2,6,16,256]{3,2,1,0:T(8,128)S(1)}, f32[2,6,16,256]{3,2,1,0:T(8,128)S(1)}, u32[]{:S(2)}, u32[]{:S(2)}) collective-permute-start(f32[2,6,16,256]{3,2,1,0:T(8,128)S(1)} %collective-permute-done.3.refs_3_), channel_id=1, source_target_pairs={{0,4},{1,3},{4,8},{5,1},{8,12},{9,5},{12,14},{13,9},{14,10},{15,13... | collective-permute-start | bytes 589832 | tf_op jit(solution)/shard_map/ppermute | solution.py:66
  29.8 1.6 %collective-permute-start.26 = (f32[6,16,256]{2,1,0:T(8,128)S(1)}, f32[6,16,256]{2,1,0:T(8,128)S(1)}, u32[]{:S(2)}, u32[]{:S(2)}) collective-permute-start(f32[6,16,256]{2,1,0:T(8,128)S(1)} %slice_bitcast_fusion), channel_id=1, source_target_pairs={{0,4},{1,3},{4,8},{5,1},{8,12},{9,5},{12,14},{13,9},{14,10},{15,13... | collective-permute-start | bytes 294920 | tf_op jit(solution)/shard_map/ppermute | solution.py:66
  31.5 1.5 %collective-permute-start.15 = (f32[6,16,256]{2,1,0:T(8,128)S(1)}, f32[6,16,256]{2,1,0:T(8,128)S(1)}, u32[]{:S(2)}, u32[]{:S(2)}) collective-permute-start(f32[6,16,256]{2,1,0:T(8,128)S(1)} %slice_bitcast_fusion.1), channel_id=1, source_target_pairs={{0,4},{1,3},{4,8},{5,1},{8,12},{9,5},{12,14},{13,9},{14,10},{15,13... | collective-permute-start | bytes 294920 | tf_op jit(solution)/shard_map/ppermute | solution.py:66
  34.4 1.7 %collective-permute-done.15.refs_0_ = f32[6,16,256]{2,1,0:T(8,128)S(1)} collective-permute-done((f32[6,16,256]{2,1,0:T(8,128)S(1)}, f32[6,16,256]{2,1,0:T(8,128)S(1)}, u32[]{:S(2)}, u32[]{:S(2)}) %collective-permute-start.15) | collective-permute-done | bytes 98336 | tf_op jit(solution)/shard_map/ppermute | solution.py:66
  36.1 1.5 %collective-permute-start.5 = (f32[6,16,256]{2,1,0:T(8,128)S(1)}, f32[6,16,256]{2,1,0:T(8,128)S(1)}, u32[]{:S(2)}, u32[]{:S(2)}) collective-permute-start(f32[6,16,256]{2,1,0:T(8,128)S(1)} %slice_bitcast_fusion.2), channel_id=1, source_target_pairs={{0,4},{1,3},{4,8},{5,1},{8,12},{9,5},{12,14},{13,9},{14,10},{15,13... | collective-permute-start | bytes 294920 | tf_op jit(solution)/shard_map/ppermute | solution.py:66
  38.7 2.0 %collective-permute-done.5.refs_0_ = f32[6,16,256]{2,1,0:T(8,128)S(1)} collective-permute-done((f32[6,16,256]{2,1,0:T(8,128)S(1)}, f32[6,16,256]{2,1,0:T(8,128)S(1)}, u32[]{:S(2)}, u32[]{:S(2)}) %collective-permute-start.5) | collective-permute-done | bytes 98336 | tf_op jit(solution)/shard_map/ppermute | solution.py:66
  41.7 2.1 %shard_map.45 = (f32[4,256,256]{2,1,0:T(8,128)S(1)}, bf16[4,256,256]{2,1,0:T(8,128)(2,1)S(1)}, bf16[4,256,256]{2,1,0:T(8,128)(2,1)S(1)}, bf16[6,256,256]{2,1,0:T(8,128)(2,1)S(1)}, bf16[6,256,256]{2,1,0:T(8,128)(2,1)S(1)}) custom-call(f32[6,16,256]{2,1,0:T(8,128)S(1)} %collective-permute-done.15.refs_0_, ...), custom_call_target="tpu_custom_call", output_to_operand_aliasing={{3}: (2, {}), {4}: (3, {})} | custom-call | flops 905969664 | bytes 4194304 | tf_op jit(solution)/shard_map/pallas_call | solution.py:41
  43.8 1.6 %shard_map.46 = (f32[1024,256]{1,0:T(8,128)}, bf16[6,256,256]{2,1,0:T(8,128)(2,1)S(1)}, bf16[6,256,256]{2,1,0:T(8,128)(2,1)S(1)}) custom-call(f32[6,16,256]{2,1,0:T(8,128)S(1)} %collective-permute-done.5.refs_0_, f32[6,16,256]{2,1,0:T(8,128)S(1)} %collective-permute-done.6.refs_1_, ...), custom_call_target="tpu_custom_call", output_to_operand_aliasing={{1}: (2, {}), {2}: (3, {})} | custom-call | flops 603979776 | bytes 4194304 | tf_op jit(solution)/shard_map/pallas_call | solution.py:41
  (50 shorter events, 6.2 us)
Async XLA Ops:
  1.1 3.6 %collective-permute-start.1 = (f32[4,16,1024]{2,1,0:T(8,128)S(1)}, f32[4,16,1024]{2,1,0:T(8,128)S(1)}, u32[]{:S(2)}, u32[]{:S(2)}) collective-permute-start(f32[4,16,1024]{2,1,0:T(8,128)S(1)} %get-tuple-element.21.refs_1_), channel_id=1, source_target_pairs={{0,1},{1,0},{2,3},{3,2},{4,5},{5,4},{6,7},{7,6},{8,9},{9,8},{10,11... | collective-permute-start | bytes 786440 | tf_op jit(solution)/shard_map/ppermute | solution.py:301
  1.7 6.0 %collective-permute-start.10 = (f32[3,16,512]{2,1,0:T(8,128)S(1)}, f32[3,16,512]{2,1,0:T(8,128)S(1)}, u32[]{:S(2)}, u32[]{:S(2)}) collective-permute-start(f32[3,16,512]{2,1,0:T(8,128)S(1)} %get-tuple-element.24.refs_0_), channel_id=1, source_target_pairs={{16,0},{0,16},{17,1},{1,17},{18,2},{2,18},{19,3},{3,19},{20,4},{4,... | collective-permute-start | bytes 294920 | tf_op jit(solution)/shard_map/ppermute | solution.py:302
  4.7 6.3 %collective-permute-start.20 = (f32[2,6,16,256]{3,2,1,0:T(8,128)S(1)}, f32[2,6,16,256]{3,2,1,0:T(8,128)S(1)}, u32[]{:S(2)}, u32[]{:S(2)}) collective-permute-start(f32[2,6,16,256]{3,2,1,0:T(8,128)S(1)} %shard_map.43.refs_0_), channel_id=1, source_target_pairs={{0,4},{1,3},{4,8},{5,1},{8,12},{9,5},{12,14},{13,9},{14,10},{15,13... | collective-permute-start | bytes 589832 | tf_op jit(solution)/shard_map/ppermute | solution.py:66
  9.1 6.7 %collective-permute-start.12 = (f32[2,6,16,256]{3,2,1,0:T(8,128)S(1)}, f32[2,6,16,256]{3,2,1,0:T(8,128)S(1)}, u32[]{:S(2)}, u32[]{:S(2)}) collective-permute-start(f32[2,6,16,256]{3,2,1,0:T(8,128)S(1)} %shard_map.41.refs_0_), channel_id=1, source_target_pairs={{0,4},{1,3},{4,8},{5,1},{8,12},{9,5},{12,14},{13,9},{14,10},{15,13... | collective-permute-start | bytes 589832 | tf_op jit(solution)/shard_map/ppermute | solution.py:66
  11.0 6.3 %collective-permute-start.22 = (f32[2,6,16,256]{3,2,1,0:T(8,128)S(1)}, f32[2,6,16,256]{3,2,1,0:T(8,128)S(1)}, u32[]{:S(2)}, u32[]{:S(2)}) collective-permute-start(f32[2,6,16,256]{3,2,1,0:T(8,128)S(1)} %collective-permute-done.20.refs_1_), channel_id=1, source_target_pairs={{0,4},{1,3},{4,8},{5,1},{8,12},{9,5},{12,14},{13,9},{14,10},{15,13... | collective-permute-start | bytes 589832 | tf_op jit(solution)/shard_map/ppermute | solution.py:66
  12.6 13.4 %collective-permute-start.28 = (f32[512,256]{1,0:T(8,128)S(1)}, f32[512,256]{1,0:T(8,128)S(1)}, u32[]{:S(2)}, u32[]{:S(2)}) collective-permute-start(f32[512,256]{1,0:T(8,128)S(1)} %slice.15), channel_id=1, source_target_pairs={{16,0},{0,16},{17,1},{1,17},{18,2},{2,18},{19,3},{3,19},{20,4},{4,... | collective-permute-start | bytes 1572872 | tf_op jit(solution)/shard_map/ppermute | solution.py:304
  14.2 5.7 %collective-permute-start.2 = (f32[2,6,16,256]{3,2,1,0:T(8,128)S(1)}, f32[2,6,16,256]{3,2,1,0:T(8,128)S(1)}, u32[]{:S(2)}, u32[]{:S(2)}) collective-permute-start(f32[2,6,16,256]{3,2,1,0:T(8,128)S(1)} %shard_map.38.refs_0_), channel_id=1, source_target_pairs={{0,4},{1,3},{4,8},{5,1},{8,12},{9,5},{12,14},{13,9},{14,10},{15,13... | collective-permute-start | bytes 589832 | tf_op jit(solution)/shard_map/ppermute | solution.py:66
  15.8 6.2 %collective-permute-start.13 = (f32[2,6,16,256]{3,2,1,0:T(8,128)S(1)}, f32[2,6,16,256]{3,2,1,0:T(8,128)S(1)}, u32[]{:S(2)}, u32[]{:S(2)}) collective-permute-start(f32[2,6,16,256]{3,2,1,0:T(8,128)S(1)} %collective-permute-done.12.refs_1_), channel_id=1, source_target_pairs={{0,4},{1,3},{4,8},{5,1},{8,12},{9,5},{12,14},{13,9},{14,10},{15,13... | collective-permute-start | bytes 589832 | tf_op jit(solution)/shard_map/ppermute | solution.py:66
  17.3 6.8 %collective-permute-start.24 = (f32[2,6,16,256]{3,2,1,0:T(8,128)S(1)}, f32[2,6,16,256]{3,2,1,0:T(8,128)S(1)}, u32[]{:S(2)}, u32[]{:S(2)}) collective-permute-start(f32[2,6,16,256]{3,2,1,0:T(8,128)S(1)} %collective-permute-done.22.refs_3_), channel_id=1, source_target_pairs={{0,4},{1,3},{4,8},{5,1},{8,12},{9,5},{12,14},{13,9},{14,10},{15,13... | collective-permute-start | bytes 589832 | tf_op jit(solution)/shard_map/ppermute | solution.py:66
  18.7 7.3 %collective-permute-start.21 = (f32[2,6,16,256]{3,2,1,0:T(8,128)S(1)}, f32[2,6,16,256]{3,2,1,0:T(8,128)S(1)}, u32[]{:S(2)}, u32[]{:S(2)}) collective-permute-start(f32[2,6,16,256]{3,2,1,0:T(8,128)S(1)} %collective-permute-done.20.refs_1_), channel_id=1, source_target_pairs={{0,1},{1,0},{2,3},{3,2},{4,5},{5,4},{6,7},{7,6},{8,9},{9,8},{10,11... | collective-permute-start | bytes 589832 | tf_op jit(solution)/shard_map/ppermute | solution.py:67
  19.9 9.4 %collective-permute-start.17 = (f32[2,6,16,256]{3,2,1,0:T(8,128)S(1)}, f32[2,6,16,256]{3,2,1,0:T(8,128)S(1)}, u32[]{:S(2)}, u32[]{:S(2)}) collective-permute-start(f32[2,6,16,256]{3,2,1,0:T(8,128)S(1)} %collective-permute-done.12.refs_1_), channel_id=1, source_target_pairs={{0,1},{1,0},{2,3},{3,2},{4,5},{5,4},{6,7},{7,6},{8,9},{9,8},{10,11... | collective-permute-start | bytes 589832 | tf_op jit(solution)/shard_map/ppermute | solution.py:67
  22.0 5.7 %collective-permute-start.3 = (f32[2,6,16,256]{3,2,1,0:T(8,128)S(1)}, f32[2,6,16,256]{3,2,1,0:T(8,128)S(1)}, u32[]{:S(2)}, u32[]{:S(2)}) collective-permute-start(f32[2,6,16,256]{3,2,1,0:T(8,128)S(1)} %collective-permute-done.2.refs_1_), channel_id=1, source_target_pairs={{0,4},{1,3},{4,8},{5,1},{8,12},{9,5},{12,14},{13,9},{14,10},{15,13... | collective-permute-start | bytes 589832 | tf_op jit(solution)/shard_map/ppermute | solution.py:66
  24.1 5.7 %collective-permute-start.14 = (f32[2,6,16,256]{3,2,1,0:T(8,128)S(1)}, f32[2,6,16,256]{3,2,1,0:T(8,128)S(1)}, u32[]{:S(2)}, u32[]{:S(2)}) collective-permute-start(f32[2,6,16,256]{3,2,1,0:T(8,128)S(1)} %collective-permute-done.13.refs_3_), channel_id=1, source_target_pairs={{0,4},{1,3},{4,8},{5,1},{8,12},{9,5},{12,14},{13,9},{14,10},{15,13... | collective-permute-start | bytes 589832 | tf_op jit(solution)/shard_map/ppermute | solution.py:66
  26.0 5.4 %collective-permute-start.7 = (f32[2,6,16,256]{3,2,1,0:T(8,128)S(1)}, f32[2,6,16,256]{3,2,1,0:T(8,128)S(1)}, u32[]{:S(2)}, u32[]{:S(2)}) collective-permute-start(f32[2,6,16,256]{3,2,1,0:T(8,128)S(1)} %collective-permute-done.2.refs_1_), channel_id=1, source_target_pairs={{0,1},{1,0},{2,3},{3,2},{4,5},{5,4},{6,7},{7,6},{8,9},{9,8},{10,11... | collective-permute-start | bytes 589832 | tf_op jit(solution)/shard_map/ppermute | solution.py:67
  26.0 5.5 %collective-permute-start.18 = (f32[2,6,16,256]{3,2,1,0:T(8,128)S(1)}, f32[2,6,16,256]{3,2,1,0:T(8,128)S(1)}, u32[]{:S(2)}, u32[]{:S(2)}) collective-permute-start(f32[2,6,16,256]{3,2,1,0:T(8,128)S(1)} %collective-permute-done.13.refs_3_), channel_id=1, source_target_pairs={{0,1},{1,0},{2,3},{3,2},{4,5},{5,4},{6,7},{7,6},{8,9},{9,8},{10,11... | collective-permute-start | bytes 589832 | tf_op jit(solution)/shard_map/ppermute | solution.py:67
  27.7 5.7 %collective-permute-start.4 = (f32[2,6,16,256]{3,2,1,0:T(8,128)S(1)}, f32[2,6,16,256]{3,2,1,0:T(8,128)S(1)}, u32[]{:S(2)}, u32[]{:S(2)}) collective-permute-start(f32[2,6,16,256]{3,2,1,0:T(8,128)S(1)} %collective-permute-done.3.refs_3_), channel_id=1, source_target_pairs={{0,4},{1,3},{4,8},{5,1},{8,12},{9,5},{12,14},{13,9},{14,10},{15,13... | collective-permute-start | bytes 589832 | tf_op jit(solution)/shard_map/ppermute | solution.py:66
  29.3 4.1 %collective-permute-start.8 = (f32[2,6,16,256]{3,2,1,0:T(8,128)S(1)}, f32[2,6,16,256]{3,2,1,0:T(8,128)S(1)}, u32[]{:S(2)}, u32[]{:S(2)}) collective-permute-start(f32[2,6,16,256]{3,2,1,0:T(8,128)S(1)} %collective-permute-done.3.refs_3_), channel_id=1, source_target_pairs={{0,1},{1,0},{2,3},{3,2},{4,5},{5,4},{6,7},{7,6},{8,9},{9,8},{10,11... | collective-permute-start | bytes 589832 | tf_op jit(solution)/shard_map/ppermute | solution.py:67
  29.8 4.6 %collective-permute-start.26 = (f32[6,16,256]{2,1,0:T(8,128)S(1)}, f32[6,16,256]{2,1,0:T(8,128)S(1)}, u32[]{:S(2)}, u32[]{:S(2)}) collective-permute-start(f32[6,16,256]{2,1,0:T(8,128)S(1)} %slice_bitcast_fusion), channel_id=1, source_target_pairs={{0,4},{1,3},{4,8},{5,1},{8,12},{9,5},{12,14},{13,9},{14,10},{15,13... | collective-permute-start | bytes 294920 | tf_op jit(solution)/shard_map/ppermute | solution.py:66
  31.4 9.4 %collective-permute-start.23 = (f32[2,6,16,256]{3,2,1,0:T(8,128)S(1)}, f32[2,6,16,256]{3,2,1,0:T(8,128)S(1)}, u32[]{:S(2)}, u32[]{:S(2)}) collective-permute-start(f32[2,6,16,256]{3,2,1,0:T(8,128)S(1)} %collective-permute-done.22.refs_3_), channel_id=1, source_target_pairs={{0,1},{1,0},{2,3},{3,2},{4,5},{5,4},{6,7},{7,6},{8,9},{9,8},{10,11... | collective-permute-start | bytes 589832 | tf_op jit(solution)/shard_map/ppermute | solution.py:67
  31.5 4.7 %collective-permute-start.15 = (f32[6,16,256]{2,1,0:T(8,128)S(1)}, f32[6,16,256]{2,1,0:T(8,128)S(1)}, u32[]{:S(2)}, u32[]{:S(2)}) collective-permute-start(f32[6,16,256]{2,1,0:T(8,128)S(1)} %slice_bitcast_fusion.1), channel_id=1, source_target_pairs={{0,4},{1,3},{4,8},{5,1},{8,12},{9,5},{12,14},{13,9},{14,10},{15,13... | collective-permute-start | bytes 294920 | tf_op jit(solution)/shard_map/ppermute | solution.py:66
  33.3 7.4 %collective-permute-start.25 = (f32[2,6,16,256]{3,2,1,0:T(8,128)S(1)}, f32[2,6,16,256]{3,2,1,0:T(8,128)S(1)}, u32[]{:S(2)}, u32[]{:S(2)}) collective-permute-start(f32[2,6,16,256]{3,2,1,0:T(8,128)S(1)} %collective-permute-done.24.refs_5_), channel_id=1, source_target_pairs={{0,1},{1,0},{2,3},{3,2},{4,5},{5,4},{6,7},{7,6},{8,9},{9,8},{10,11... | collective-permute-start | bytes 589832 | tf_op jit(solution)/shard_map/ppermute | solution.py:67
  33.4 4.3 %collective-permute-start.19 = (f32[2,6,16,256]{3,2,1,0:T(8,128)S(1)}, f32[2,6,16,256]{3,2,1,0:T(8,128)S(1)}, u32[]{:S(2)}, u32[]{:S(2)}) collective-permute-start(f32[2,6,16,256]{3,2,1,0:T(8,128)S(1)} %collective-permute-done.14.refs_5_), channel_id=1, source_target_pairs={{0,1},{1,0},{2,3},{3,2},{4,5},{5,4},{6,7},{7,6},{8,9},{9,8},{10,11... | collective-permute-start | bytes 589832 | tf_op jit(solution)/shard_map/ppermute | solution.py:67
  36.1 4.6 %collective-permute-start.5 = (f32[6,16,256]{2,1,0:T(8,128)S(1)}, f32[6,16,256]{2,1,0:T(8,128)S(1)}, u32[]{:S(2)}, u32[]{:S(2)}) collective-permute-start(f32[6,16,256]{2,1,0:T(8,128)S(1)} %slice_bitcast_fusion.2), channel_id=1, source_target_pairs={{0,4},{1,3},{4,8},{5,1},{8,12},{9,5},{12,14},{13,9},{14,10},{15,13... | collective-permute-start | bytes 294920 | tf_op jit(solution)/shard_map/ppermute | solution.py:66
  37.6 4.0 %collective-permute-start.16 = (f32[6,16,256]{2,1,0:T(8,128)S(1)}, f32[6,16,256]{2,1,0:T(8,128)S(1)}, u32[]{:S(2)}, u32[]{:S(2)}) collective-permute-start(f32[6,16,256]{2,1,0:T(8,128)S(1)} %collective-permute-done.15.refs_0_), channel_id=1, source_target_pairs={{0,1},{1,0},{2,3},{3,2},{4,5},{5,4},{6,7},{7,6},{8,9},{9,8},{10,11... | collective-permute-start | bytes 294920 | tf_op jit(solution)/shard_map/ppermute | solution.py:67
  (6 other events, 25.2 us)

commit v5 on v4

--- a/solution.py
+++ b/solution.py
@@ -198,77 +198,71 @@
 
 def place_kernel(plan, *refs):
     high_ref, low_ref, whole_ref = refs[-3:]
-    assemble(refs[:-3], high_ref, low_ref, whole_ref, plan.chips, slice(0, plan.chips - 1))
+    assemble(refs[:-3], high_ref, low_ref, whole_ref, plan.chips, slice(0, len(refs) - 3))
 
 
 def late_pieces(plan, late):
     return slice(plan.chips - 1, None) if late == 2 else slice(None)
 
 
-def solve_kernel(plan, late, *refs):
-    pieces = refs[:late]
-    inv_high, inv_low, x_first, right_ref = refs[late + 2 : late + 6]
-    received = refs[late + 6 : -6]
-    x_ref, x_high, x_low, high_ref, low_ref, whole_ref = refs[-6:]
+def final_kernel(plan, late, *refs):
+    pieces, at = refs[:late], late + 2
+    mats = [refs[at : at + 2], refs[at + 2 : at + 4]]
+    x_first, total_ref, right_ref = refs[at + 4 : at + 7]
+    received = refs[at + 7 : -7]
+    out_hbm, high_ref, low_ref, x_ref, low_rows, whole_ref, sems = refs[-7:]
+    panels, nb = plan.panels, plan.nb
+    me = lax.axis_index("row")
     assemble(pieces, high_ref, low_ref, whole_ref, plan.chips, late_pieces(plan, late))
-    mats = [(inv_high, inv_low), None, (high_ref, low_ref)]
-    panels = plan.panels
+    mats.append((high_ref, low_ref))
     currents = [plan.panel_rows(panel, right_ref, received) for panel in range(panels)]
+    totals = [total_ref[block * nb : (block + 1) * nb] for block in range(plan.wide)]
+
+    def panel_out(local):
+        rank = local * plan.group_count + me
+        rows = pl.ds(local * nb, nb)
+        return pltpu.make_async_copy(x_ref.at[rank], out_hbm.at[rows], sems.at[local])
+
+    def rows_out(block):
+        local = plan.sure + block
+        rows = pl.ds(local * nb, nb)
+        return pltpu.make_async_copy(low_rows.at[block], out_hbm.at[rows], sems.at[local])
+
+    def each_out(act):
+        for local in range(plan.sure):
+            act(panel_out(local))
+        for local in range(plan.sure, plan.held):
+            pl.when(local * plan.group_count + me < panels)(functools.partial(act, panel_out(local)))
+
     answer = x_first[...]
     for panel in range(panels):
         if panel > 0:
             answer = dot3(plan.mat(mats, "inv", panel), split(currents[panel]), PLAIN)
         x_ref[panel] = answer
         solved = split(answer)
-        x_high[panel], x_low[panel] = solved
         for after in range(panel + 1, panels):
             mat = plan.mat(mats, "tri", plan.tri.index((after, panel)))
             currents[after] = currents[after] - dot3(mat, solved, ROWS)
-
-
-def final_kernel(plan, late, *refs):
-    pieces = refs[:late]
-    x_ref, x_high, x_low, total_ref = refs[late + 2 : late + 6]
-    out_hbm, high_ref, low_ref, low_rows, whole_ref, sems = refs[-6:]
-    panels, nb = plan.panels, plan.nb
-    me = lax.axis_index("row")
-
-    def panel_out(rank, local):
-        rows = pl.ds(local * nb, nb)
-        return pltpu.make_async_copy(x_ref.at[rank], out_hbm.at[rows], sems.at[local])
-
-    def for_panels(act):
-        for local in range(plan.held):
-            rank = local * plan.group_count + me
-
-            @pl.when(rank < panels)
-            def _(rank=rank, local=local):
-                act(panel_out(rank, local))
-
-    for_panels(lambda copy: copy.start())
-    assemble(pieces, high_ref, low_ref, whole_ref, plan.chips, late_pieces(plan, late))
-    mats = [None, (high_ref, low_ref)]
-    outs = []
+        if panel == panels - 1:
+            each_out(lambda copy: copy.start())
+        for block in range(plan.wide):
+            if panel > 0:
+                mat = plan.mat(mats, "low", panel, block)
+                totals[block] = totals[block] - dot3(mat, solved, ROWS)
+            if panel == panels - 1:
+                low_rows[block] = totals[block]
+                if plan.sure + block >= plan.held:
+                    rows_out(block).start()
+
+    each_out(lambda copy: copy.wait())
     for block in range(plan.wide):
-        total = total_ref[block * nb : (block + 1) * nb]
-        for panel in range(1, panels):
-            mat = plan.mat(mats, "low", panel, block)
-            total = total - dot3(mat, (x_high[panel], x_low[panel]), ROWS)
-        low_rows[block] = total
         local = plan.sure + block
-        out = pltpu.make_async_copy(
-            low_rows.at[block], out_hbm.at[pl.ds(local * nb, nb)], sems.at[local]
-        )
         if local < plan.held:
             mine = local * plan.group_count + me >= panels
-            pl.when(mine)(out.start)
-            pl.when(mine)(out.wait)
+            pl.when(mine)(rows_out(block).start)
+            pl.when(mine)(rows_out(block).wait)
         else:
-            out.start()
-            outs.append(out)
-    for_panels(lambda copy: copy.wait())
-    for out in outs:
-        out.wait()
+            rows_out(block).wait()
 
 
 def per_device(right_side, factor_panels, inverses):
@@ -319,13 +313,10 @@
     pairs = [[shape((len(blocks), nb, nb), bf16)] * 2 for blocks in plan.chunks]
     wholes = [whole_scratch(len(blocks), nb, depth) for blocks in plan.chunks]
 
-    def place(chunk):
-        if depth % 16 != 0:
-            return [jnp.zeros(s.shape, s.dtype) for s in pairs[chunk]], pieces[chunk]
-        done = kernel_call(
-            bound(place_kernel, plan), pairs[chunk], [wholes[chunk]], pieces[chunk][: chips - 1]
+    def place(chunk, count):
+        return kernel_call(
+            bound(place_kernel, plan), pairs[chunk], [wholes[chunk]], pieces[chunk][:count]
         )
-        return done, pieces[chunk][chips - 1 :]
 
     inv_high, inv_low, x_first, total = kernel_call(
         bound(prep_kernel, plan),
@@ -334,27 +325,22 @@
         (*pieces[0], right_side, *received),
         flops=6 * 3 * nb * nb * columns,
     )
-    placed, late = place(2)
-    answers = [shape((panels, nb, columns), t) for t in (f32, bf16, bf16)]
-    x, x_high, x_low, _, _ = kernel_call(
-        bound(solve_kernel, plan, len(late)),
-        [*answers, *pairs[2]],
-        [wholes[2]],
-        (*late, *placed, inv_high, inv_low, x_first, right_side, *received),
-        flops=6 * 9 * nb * nb * columns,
-        aliases={len(late): 3, len(late) + 1: 4},
-    )
-    placed, late = place(1)
+    below = place(1, chips + 1)
+    if depth % 16 == 0:
+        placed, late = place(2, chips - 1), pieces[2][chips - 1 :]
+    else:
+        placed, late = [jnp.zeros(s.shape, s.dtype) for s in pairs[2]], pieces[2]
     out, _, _ = kernel_call(
         bound(final_kernel, plan, len(late)),
-        [shape(right_side.shape, f32), *pairs[1]],
+        [shape(right_side.shape, f32), *pairs[2]],
         [
+            pltpu.VMEM((panels, nb, columns), f32),
             pltpu.VMEM((plan.wide, nb, columns), f32),
-            wholes[1],
+            wholes[2],
             pltpu.SemaphoreType.DMA((rows // nb,)),
         ],
-        (*late, *placed, x, x_high, x_low, total),
-        flops=6 * 6 * nb * nb * columns,
+        (*late, *placed, inv_high, inv_low, *below, x_first, total, right_side, *received),
+        flops=6 * 15 * nb * nb * columns,
         out_hbm=1,
         aliases={len(late): 1, len(late) + 1: 2},
     )

time: 45.6 us -> 49 us (1.075)
  waiting for transfers between devices: 13.1 us -> 16.1 us
  starting transfers between devices: 25.8 us -> 26.6 us
    ppermute x12, waiting for transfers between devices: 10.1 us -> 12.6 us  [ring(): moving = lax.ppermute(moving if step < steps else moving[0], 'col', nearest)]
    ppermute x12, starting transfers between devices: 18.9 us -> 20.8 us  [ring(): moving = lax.ppermute(moving if step < steps else moving[0], 'col', nearest)]
    ppermute x1, starting transfers between devices: 2.93 us -> 1.52 us  [per_device(): tri = [own] + [lax.ppermute(own, 'row', pairs) for pairs in shifts]]
    ppermute x1, waiting for transfers between devices: 1.38 us -> 0.01 us  [per_device(): tri = [own] + [lax.ppermute(own, 'row', pairs) for pairs in shifts]]
    ppermute x1, waiting for transfers between devices: 0.01 us -> 1.18 us  [per_device(): inv_other = lax.ppermute(inv, 'col', swap)]
    ppermute x12, waiting for transfers between devices: 0.03 us -> 1.02 us  [ring(): pieces += [moving, lax.ppermute(moving, 'col', swap)]]
    pallas_call x10 -> x9, Pallas kernels: 6.32 us -> 5.99 us  [kernel_call(): pl.pallas_call(body, out_shape=out_shapes, in_specs=[hbm] * in_hbm + [nea...]
  transfers between devices with their start and end apart: 29 -> 29, of which waited for: 12 -> 11; matrix products, arithmetic and copies ran while one was open for 0% -> 0% of each run, Pallas kernels for 8% -> 3%
where the time goes in v5:
time: 49 us; the launch traced here: 48.9 us
  starting transfers between devices  26.6 us (54%)
  waiting for transfers between devices  16.1 us (33%)
  Pallas kernels  5.99 us (12%)
    ppermute x12, starting transfers between devices, ring(): moving = lax.ppermute(moving if step < steps else moving[0], 'col', nearest)  20.8 us
    ppermute x12, waiting for transfers between devices, ring(): moving = lax.ppermute(moving if step < steps else moving[0], 'col', nearest)  12.6 us
    pallas_call x9, Pallas kernels, kernel_call(): pl.pallas_call(body, out_shape=out_shapes, in_specs=[hbm] * in_hbm + [nea...  5.99 us
    ppermute x12, starting transfers between devices, ring(): pieces += [moving, lax.ppermute(moving, 'col', swap)]  1.91 us
    ppermute x1, starting transfers between devices, per_device(): received = [lax.ppermute(above, 'row', pairs) for pairs in shifts]  1.58 us
    ppermute x1, starting transfers between devices, per_device(): tri = [own] + [lax.ppermute(own, 'row', pairs) for pairs in shifts]  1.52 us
    ppermute x1, waiting for transfers between devices, per_device(): half_other = lax.ppermute(half, 'col', swap)  1.29 us
    ppermute x1, waiting for transfers between devices, per_device(): inv_other = lax.ppermute(inv, 'col', swap)  1.18 us
  transfers between devices with their start and end apart: 29, of which 11 were waited for; matrix products, arithmetic and copies ran while one was open for 0% of the time, Pallas kernels for 3%

profile of v5, /device:TPU:0, one launch (start us, length us, event | category | flops | bytes accessed | tf_op | source)
XLA Modules:
  0.0 48.9 jit_solution(6764878103264959572)
XLA Ops:
  0.0 1.1 %shard_map.37 = (f32[4,16,1024]{2,1,0:T(8,128)S(1)}, f32[4,16,256]{2,1,0:T(8,128)S(1)}, f32[3,16,512]{2,1,0:T(8,128)S(1)}) custom-call(f32[4,16,1024]{2,1,0:T(8,128)} %factor_hbm.1, f32[4,16,256]{2,1,0:T(8,128)} %inv_hbm.1), custom_call_target="tpu_custom_call" | custom-call | bytes 4194304 | tf_op jit(solution)/shard_map/pallas_call | solution.py:41
  1.7 1.2 %collective-permute-done.11.refs_2_ = f32[4,16,256]{2,1,0:T(8,128)S(1)} collective-permute-done((f32[4,16,256]{2,1,0:T(8,128)S(1)}, f32[4,16,256]{2,1,0:T(8,128)S(1)}, u32[]{:S(2)}, u32[]{:S(2)}) %collective-permute-start.11) | collective-permute-done | bytes 65568 | tf_op jit(solution)/shard_map/ppermute | solution.py:294
  2.9 3.0 %collective-permute-start.12 = (f32[2,6,16,256]{3,2,1,0:T(8,128)S(1)}, f32[2,6,16,256]{3,2,1,0:T(8,128)S(1)}, u32[]{:S(2)}, u32[]{:S(2)}) collective-permute-start(f32[2,6,16,256]{3,2,1,0:T(8,128)S(1)} %shard_map.41.refs_0_), channel_id=1, source_target_pairs={{0,4},{1,3},{4,8},{5,1},{8,12},{9,5},{12,14},{13,9},{14,10},{15,13... | collective-permute-start | bytes 589832 | tf_op jit(solution)/shard_map/ppermute | solution.py:66
  5.9 1.5 %collective-permute-start = (f32[3,16,512]{2,1,0:T(8,128)S(1)}, f32[3,16,512]{2,1,0:T(8,128)S(1)}, u32[]{:S(2)}, u32[]{:S(2)}) collective-permute-start(f32[3,16,512]{2,1,0:T(8,128)S(1)} %get-tuple-element.17.refs_0_), channel_id=1, source_target_pairs={{16,0},{0,16},{17,1},{1,17},{18,2},{2,18},{19,3},{3,19},{20,4},{4,... | collective-permute-start | bytes 294920 | tf_op jit(solution)/shard_map/ppermute | solution.py:296
  7.4 1.6 %collective-permute-start.21 = (f32[2,6,16,256]{3,2,1,0:T(8,128)S(1)}, f32[2,6,16,256]{3,2,1,0:T(8,128)S(1)}, u32[]{:S(2)}, u32[]{:S(2)}) collective-permute-start(f32[2,6,16,256]{3,2,1,0:T(8,128)S(1)} %shard_map.43.refs_0_), channel_id=1, source_target_pairs={{0,4},{1,3},{4,8},{5,1},{8,12},{9,5},{12,14},{13,9},{14,10},{15,13... | collective-permute-start | bytes 589832 | tf_op jit(solution)/shard_map/ppermute | solution.py:66
  9.5 2.1 %collective-permute-start.14 = (f32[2,6,16,256]{3,2,1,0:T(8,128)S(1)}, f32[2,6,16,256]{3,2,1,0:T(8,128)S(1)}, u32[]{:S(2)}, u32[]{:S(2)}) collective-permute-start(f32[2,6,16,256]{3,2,1,0:T(8,128)S(1)} %collective-permute-done.12.refs_1_), channel_id=1, source_target_pairs={{0,4},{1,3},{4,8},{5,1},{8,12},{9,5},{12,14},{13,9},{14,10},{15,13... | collective-permute-start | bytes 589832 | tf_op jit(solution)/shard_map/ppermute | solution.py:66
  11.7 1.3 %collective-permute-done.1.refs_2_ = f32[6,16,256]{2,1,0:T(8,128)S(1)} collective-permute-done((f32[6,16,256]{2,1,0:T(8,128)S(1)}, f32[6,16,256]{2,1,0:T(8,128)S(1)}, u32[]{:S(2)}, u32[]{:S(2)}) %collective-permute-start.1) | collective-permute-done | bytes 98336 | tf_op jit(solution)/shard_map/ppermute | solution.py:300
  13.0 1.6 %collective-permute-start.3 = (f32[2,6,16,256]{3,2,1,0:T(8,128)S(1)}, f32[2,6,16,256]{3,2,1,0:T(8,128)S(1)}, u32[]{:S(2)}, u32[]{:S(2)}) collective-permute-start(f32[2,6,16,256]{3,2,1,0:T(8,128)S(1)} %shard_map.39.refs_0_), channel_id=1, source_target_pairs={{0,4},{1,3},{4,8},{5,1},{8,12},{9,5},{12,14},{13,9},{14,10},{15,13... | collective-permute-start | bytes 589832 | tf_op jit(solution)/shard_map/ppermute | solution.py:66
  14.6 1.6 %collective-permute-start.23 = (f32[2,6,16,256]{3,2,1,0:T(8,128)S(1)}, f32[2,6,16,256]{3,2,1,0:T(8,128)S(1)}, u32[]{:S(2)}, u32[]{:S(2)}) collective-permute-start(f32[2,6,16,256]{3,2,1,0:T(8,128)S(1)} %collective-permute-done.21.refs_1_), channel_id=1, source_target_pairs={{0,4},{1,3},{4,8},{5,1},{8,12},{9,5},{12,14},{13,9},{14,10},{15,13... | collective-permute-start | bytes 589832 | tf_op jit(solution)/shard_map/ppermute | solution.py:66
  16.2 1.5 %collective-permute-start.16 = (f32[2,6,16,256]{3,2,1,0:T(8,128)S(1)}, f32[2,6,16,256]{3,2,1,0:T(8,128)S(1)}, u32[]{:S(2)}, u32[]{:S(2)}) collective-permute-start(f32[2,6,16,256]{3,2,1,0:T(8,128)S(1)} %collective-permute-done.14.refs_3_), channel_id=1, source_target_pairs={{0,4},{1,3},{4,8},{5,1},{8,12},{9,5},{12,14},{13,9},{14,10},{15,13... | collective-permute-start | bytes 589832 | tf_op jit(solution)/shard_map/ppermute | solution.py:66
  17.7 1.6 %collective-permute-start.20 = (f32[512,256]{1,0:T(8,128)S(1)}, f32[512,256]{1,0:T(8,128)S(1)}, u32[]{:S(2)}, u32[]{:S(2)}) collective-permute-start(f32[512,256]{1,0:T(8,128)S(1)} %slice.14), channel_id=1, source_target_pairs={{16,0},{0,16},{17,1},{1,17},{18,2},{2,18},{19,3},{3,19},{20,4},{4,... | collective-permute-start | bytes 1572872 | tf_op jit(solution)/shard_map/ppermute | solution.py:298
  20.8 1.6 %collective-permute-start.4 = (f32[2,6,16,256]{3,2,1,0:T(8,128)S(1)}, f32[2,6,16,256]{3,2,1,0:T(8,128)S(1)}, u32[]{:S(2)}, u32[]{:S(2)}) collective-permute-start(f32[2,6,16,256]{3,2,1,0:T(8,128)S(1)} %collective-permute-done.3.refs_1_), channel_id=1, source_target_pairs={{0,4},{1,3},{4,8},{5,1},{8,12},{9,5},{12,14},{13,9},{14,10},{15,13... | collective-permute-start | bytes 589832 | tf_op jit(solution)/shard_map/ppermute | solution.py:66
  22.9 1.6 %collective-permute-start.25 = (f32[2,6,16,256]{3,2,1,0:T(8,128)S(1)}, f32[2,6,16,256]{3,2,1,0:T(8,128)S(1)}, u32[]{:S(2)}, u32[]{:S(2)}) collective-permute-start(f32[2,6,16,256]{3,2,1,0:T(8,128)S(1)} %collective-permute-done.23.refs_3_), channel_id=1, source_target_pairs={{0,4},{1,3},{4,8},{5,1},{8,12},{9,5},{12,14},{13,9},{14,10},{15,13... | collective-permute-start | bytes 589832 | tf_op jit(solution)/shard_map/ppermute | solution.py:66
  24.5 2.0 %collective-permute-done.4.refs_3_ = f32[2,6,16,256]{3,2,1,0:T(8,128)S(1)} collective-permute-done((f32[2,6,16,256]{3,2,1,0:T(8,128)S(1)}, f32[2,6,16,256]{3,2,1,0:T(8,128)S(1)}, u32[]{:S(2)}, u32[]{:S(2)}) %collective-permute-start.4) | collective-permute-done | bytes 196640 | tf_op jit(solution)/shard_map/ppermute | solution.py:66
  26.5 2.1 %collective-permute-done.25.refs_5_ = f32[2,6,16,256]{3,2,1,0:T(8,128)S(1)} collective-permute-done((f32[2,6,16,256]{3,2,1,0:T(8,128)S(1)}, f32[2,6,16,256]{3,2,1,0:T(8,128)S(1)}, u32[]{:S(2)}, u32[]{:S(2)}) %collective-permute-start.25) | collective-permute-done | bytes 196640 | tf_op jit(solution)/shard_map/ppermute | solution.py:66
  28.6 1.6 %collective-permute-start.5 = (f32[2,6,16,256]{3,2,1,0:T(8,128)S(1)}, f32[2,6,16,256]{3,2,1,0:T(8,128)S(1)}, u32[]{:S(2)}, u32[]{:S(2)}) collective-permute-start(f32[2,6,16,256]{3,2,1,0:T(8,128)S(1)} %collective-permute-done.4.refs_3_), channel_id=1, source_target_pairs={{0,4},{1,3},{4,8},{5,1},{8,12},{9,5},{12,14},{13,9},{14,10},{15,13... | collective-permute-start | bytes 589832 | tf_op jit(solution)/shard_map/ppermute | solution.py:66
  30.3 4.0 %collective-permute-done.5.refs_5_ = f32[2,6,16,256]{3,2,1,0:T(8,128)S(1)} collective-permute-done((f32[2,6,16,256]{3,2,1,0:T(8,128)S(1)}, f32[2,6,16,256]{3,2,1,0:T(8,128)S(1)}, u32[]{:S(2)}, u32[]{:S(2)}) %collective-permute-start.5) | collective-permute-done | bytes 196640 | tf_op jit(solution)/shard_map/ppermute | solution.py:66
  34.3 1.6 %collective-permute-start.18 = (f32[6,16,256]{2,1,0:T(8,128)S(1)}, f32[6,16,256]{2,1,0:T(8,128)S(1)}, u32[]{:S(2)}, u32[]{:S(2)}) collective-permute-start(f32[6,16,256]{2,1,0:T(8,128)S(1)} %slice_bitcast_fusion.1), channel_id=1, source_target_pairs={{0,4},{1,3},{4,8},{5,1},{8,12},{9,5},{12,14},{13,9},{14,10},{15,13... | collective-permute-start | bytes 294920 | tf_op jit(solution)/shard_map/ppermute | solution.py:66
  35.9 1.6 %collective-permute-start.27 = (f32[6,16,256]{2,1,0:T(8,128)S(1)}, f32[6,16,256]{2,1,0:T(8,128)S(1)}, u32[]{:S(2)}, u32[]{:S(2)}) collective-permute-start(f32[6,16,256]{2,1,0:T(8,128)S(1)} %slice_bitcast_fusion), channel_id=1, source_target_pairs={{0,4},{1,3},{4,8},{5,1},{8,12},{9,5},{12,14},{13,9},{14,10},{15,13... | collective-permute-start | bytes 294920 | tf_op jit(solution)/shard_map/ppermute | solution.py:66
  37.5 1.5 %collective-permute-start.6 = (f32[6,16,256]{2,1,0:T(8,128)S(1)}, f32[6,16,256]{2,1,0:T(8,128)S(1)}, u32[]{:S(2)}, u32[]{:S(2)}) collective-permute-start(f32[6,16,256]{2,1,0:T(8,128)S(1)} %slice_bitcast_fusion.2), channel_id=1, source_target_pairs={{0,4},{1,3},{4,8},{5,1},{8,12},{9,5},{12,14},{13,9},{14,10},{15,13... | collective-permute-start | bytes 294920 | tf_op jit(solution)/shard_map/ppermute | solution.py:66
  39.5 1.0 %collective-permute-done.27.refs_7_ = f32[6,16,256]{2,1,0:T(8,128)S(1)} collective-permute-done((f32[6,16,256]{2,1,0:T(8,128)S(1)}, f32[6,16,256]{2,1,0:T(8,128)S(1)}, u32[]{:S(2)}, u32[]{:S(2)}) %collective-permute-start.27) | collective-permute-done | bytes 98336 | tf_op jit(solution)/shard_map/ppermute | solution.py:66
  40.5 1.6 %collective-permute-done.6.refs_0_ = f32[6,16,256]{2,1,0:T(8,128)S(1)} collective-permute-done((f32[6,16,256]{2,1,0:T(8,128)S(1)}, f32[6,16,256]{2,1,0:T(8,128)S(1)}, u32[]{:S(2)}, u32[]{:S(2)}) %collective-permute-start.6) | collective-permute-done | bytes 98336 | tf_op jit(solution)/shard_map/ppermute | solution.py:66
  42.7 1.0 %collective-permute-done.28.refs_8_ = f32[6,16,256]{2,1,0:T(8,128)S(1)} collective-permute-done((f32[6,16,256]{2,1,0:T(8,128)S(1)}, f32[6,16,256]{2,1,0:T(8,128)S(1)}, u32[]{:S(2)}, u32[]{:S(2)}) %collective-permute-start.28) | collective-permute-done | bytes 98336 | tf_op jit(solution)/shard_map/ppermute | solution.py:67
  45.5 3.4 %shard_map.45 = (f32[1024,256]{1,0:T(8,128)}, bf16[6,256,256]{2,1,0:T(8,128)(2,1)S(1)}, bf16[6,256,256]{2,1,0:T(8,128)(2,1)S(1)}) custom-call(f32[6,16,256]{2,1,0:T(8,128)S(1)} %collective-permute-done.6.refs_0_, f32[6,16,256]{2,1,0:T(8,128)S(1)} %collective-permute-done.7.refs_1_, ...), custom_call_target="tpu_custom_call", output_to_operand_aliasing={{1}: (2, {}), {2}: (3, {})} | custom-call | flops 1509949440 | bytes 4194304 | tf_op jit(solution)/shard_map/pallas_call | solution.py:41
  (49 shorter events, 6.2 us)
Async XLA Ops:
  2.9 6.5 %collective-permute-start.12 = (f32[2,6,16,256]{3,2,1,0:T(8,128)S(1)}, f32[2,6,16,256]{3,2,1,0:T(8,128)S(1)}, u32[]{:S(2)}, u32[]{:S(2)}) collective-permute-start(f32[2,6,16,256]{3,2,1,0:T(8,128)S(1)} %shard_map.41.refs_0_), channel_id=1, source_target_pairs={{0,4},{1,3},{4,8},{5,1},{8,12},{9,5},{12,14},{13,9},{14,10},{15,13... | collective-permute-start | bytes 589832 | tf_op jit(solution)/shard_map/ppermute | solution.py:66
  5.9 5.7 %collective-permute-start = (f32[3,16,512]{2,1,0:T(8,128)S(1)}, f32[3,16,512]{2,1,0:T(8,128)S(1)}, u32[]{:S(2)}, u32[]{:S(2)}) collective-permute-start(f32[3,16,512]{2,1,0:T(8,128)S(1)} %get-tuple-element.17.refs_0_), channel_id=1, source_target_pairs={{16,0},{0,16},{17,1},{1,17},{18,2},{2,18},{19,3},{3,19},{20,4},{4,... | collective-permute-start | bytes 294920 | tf_op jit(solution)/shard_map/ppermute | solution.py:296
  7.4 7.2 %collective-permute-start.21 = (f32[2,6,16,256]{3,2,1,0:T(8,128)S(1)}, f32[2,6,16,256]{3,2,1,0:T(8,128)S(1)}, u32[]{:S(2)}, u32[]{:S(2)}) collective-permute-start(f32[2,6,16,256]{3,2,1,0:T(8,128)S(1)} %shard_map.43.refs_0_), channel_id=1, source_target_pairs={{0,4},{1,3},{4,8},{5,1},{8,12},{9,5},{12,14},{13,9},{14,10},{15,13... | collective-permute-start | bytes 589832 | tf_op jit(solution)/shard_map/ppermute | solution.py:66
  9.5 6.7 %collective-permute-start.14 = (f32[2,6,16,256]{3,2,1,0:T(8,128)S(1)}, f32[2,6,16,256]{3,2,1,0:T(8,128)S(1)}, u32[]{:S(2)}, u32[]{:S(2)}) collective-permute-start(f32[2,6,16,256]{3,2,1,0:T(8,128)S(1)} %collective-permute-done.12.refs_1_), channel_id=1, source_target_pairs={{0,4},{1,3},{4,8},{5,1},{8,12},{9,5},{12,14},{13,9},{14,10},{15,13... | collective-permute-start | bytes 589832 | tf_op jit(solution)/shard_map/ppermute | solution.py:66
  13.0 6.3 %collective-permute-start.3 = (f32[2,6,16,256]{3,2,1,0:T(8,128)S(1)}, f32[2,6,16,256]{3,2,1,0:T(8,128)S(1)}, u32[]{:S(2)}, u32[]{:S(2)}) collective-permute-start(f32[2,6,16,256]{3,2,1,0:T(8,128)S(1)} %shard_map.39.refs_0_), channel_id=1, source_target_pairs={{0,4},{1,3},{4,8},{5,1},{8,12},{9,5},{12,14},{13,9},{14,10},{15,13... | collective-permute-start | bytes 589832 | tf_op jit(solution)/shard_map/ppermute | solution.py:66
  14.6 6.2 %collective-permute-start.23 = (f32[2,6,16,256]{3,2,1,0:T(8,128)S(1)}, f32[2,6,16,256]{3,2,1,0:T(8,128)S(1)}, u32[]{:S(2)}, u32[]{:S(2)}) collective-permute-start(f32[2,6,16,256]{3,2,1,0:T(8,128)S(1)} %collective-permute-done.21.refs_1_), channel_id=1, source_target_pairs={{0,4},{1,3},{4,8},{5,1},{8,12},{9,5},{12,14},{13,9},{14,10},{15,13... | collective-permute-start | bytes 589832 | tf_op jit(solution)/shard_map/ppermute | solution.py:66
  16.2 6.7 %collective-permute-start.16 = (f32[2,6,16,256]{3,2,1,0:T(8,128)S(1)}, f32[2,6,16,256]{3,2,1,0:T(8,128)S(1)}, u32[]{:S(2)}, u32[]{:S(2)}) collective-permute-start(f32[2,6,16,256]{3,2,1,0:T(8,128)S(1)} %collective-permute-done.14.refs_3_), channel_id=1, source_target_pairs={{0,4},{1,3},{4,8},{5,1},{8,12},{9,5},{12,14},{13,9},{14,10},{15,13... | collective-permute-start | bytes 589832 | tf_op jit(solution)/shard_map/ppermute | solution.py:66
  17.7 12.4 %collective-permute-start.20 = (f32[512,256]{1,0:T(8,128)S(1)}, f32[512,256]{1,0:T(8,128)S(1)}, u32[]{:S(2)}, u32[]{:S(2)}) collective-permute-start(f32[512,256]{1,0:T(8,128)S(1)} %slice.14), channel_id=1, source_target_pairs={{16,0},{0,16},{17,1},{1,17},{18,2},{2,18},{19,3},{3,19},{20,4},{4,... | collective-permute-start | bytes 1572872 | tf_op jit(solution)/shard_map/ppermute | solution.py:298
  19.3 15.0 %collective-permute-start.22 = (f32[2,6,16,256]{3,2,1,0:T(8,128)S(1)}, f32[2,6,16,256]{3,2,1,0:T(8,128)S(1)}, u32[]{:S(2)}, u32[]{:S(2)}) collective-permute-start(f32[2,6,16,256]{3,2,1,0:T(8,128)S(1)} %collective-permute-done.21.refs_1_), channel_id=1, source_target_pairs={{0,1},{1,0},{2,3},{3,2},{4,5},{5,4},{6,7},{7,6},{8,9},{9,8},{10,11... | collective-permute-start | bytes 589832 | tf_op jit(solution)/shard_map/ppermute | solution.py:67
  19.3 16.6 %collective-permute-start.8 = (f32[2,6,16,256]{3,2,1,0:T(8,128)S(1)}, f32[2,6,16,256]{3,2,1,0:T(8,128)S(1)}, u32[]{:S(2)}, u32[]{:S(2)}) collective-permute-start(f32[2,6,16,256]{3,2,1,0:T(8,128)S(1)} %collective-permute-done.3.refs_1_), channel_id=1, source_target_pairs={{0,1},{1,0},{2,3},{3,2},{4,5},{5,4},{6,7},{7,6},{8,9},{9,8},{10,11... | collective-permute-start | bytes 589832 | tf_op jit(solution)/shard_map/ppermute | solution.py:67
  20.8 5.7 %collective-permute-start.4 = (f32[2,6,16,256]{3,2,1,0:T(8,128)S(1)}, f32[2,6,16,256]{3,2,1,0:T(8,128)S(1)}, u32[]{:S(2)}, u32[]{:S(2)}) collective-permute-start(f32[2,6,16,256]{3,2,1,0:T(8,128)S(1)} %collective-permute-done.3.refs_1_), channel_id=1, source_target_pairs={{0,4},{1,3},{4,8},{5,1},{8,12},{9,5},{12,14},{13,9},{14,10},{15,13... | collective-permute-start | bytes 589832 | tf_op jit(solution)/shard_map/ppermute | solution.py:66
  22.9 5.7 %collective-permute-start.25 = (f32[2,6,16,256]{3,2,1,0:T(8,128)S(1)}, f32[2,6,16,256]{3,2,1,0:T(8,128)S(1)}, u32[]{:S(2)}, u32[]{:S(2)}) collective-permute-start(f32[2,6,16,256]{3,2,1,0:T(8,128)S(1)} %collective-permute-done.23.refs_3_), channel_id=1, source_target_pairs={{0,4},{1,3},{4,8},{5,1},{8,12},{9,5},{12,14},{13,9},{14,10},{15,13... | collective-permute-start | bytes 589832 | tf_op jit(solution)/shard_map/ppermute | solution.py:66
  26.5 11.0 %collective-permute-start.24 = (f32[2,6,16,256]{3,2,1,0:T(8,128)S(1)}, f32[2,6,16,256]{3,2,1,0:T(8,128)S(1)}, u32[]{:S(2)}, u32[]{:S(2)}) collective-permute-start(f32[2,6,16,256]{3,2,1,0:T(8,128)S(1)} %collective-permute-done.23.refs_3_), channel_id=1, source_target_pairs={{0,1},{1,0},{2,3},{3,2},{4,5},{5,4},{6,7},{7,6},{8,9},{9,8},{10,11... | collective-permute-start | bytes 589832 | tf_op jit(solution)/shard_map/ppermute | solution.py:67
  28.6 5.7 %collective-permute-start.5 = (f32[2,6,16,256]{3,2,1,0:T(8,128)S(1)}, f32[2,6,16,256]{3,2,1,0:T(8,128)S(1)}, u32[]{:S(2)}, u32[]{:S(2)}) collective-permute-start(f32[2,6,16,256]{3,2,1,0:T(8,128)S(1)} %collective-permute-done.4.refs_3_), channel_id=1, source_target_pairs={{0,4},{1,3},{4,8},{5,1},{8,12},{9,5},{12,14},{13,9},{14,10},{15,13... | collective-permute-start | bytes 589832 | tf_op jit(solution)/shard_map/ppermute | solution.py:66
  30.2 8.8 %collective-permute-start.9 = (f32[2,6,16,256]{3,2,1,0:T(8,128)S(1)}, f32[2,6,16,256]{3,2,1,0:T(8,128)S(1)}, u32[]{:S(2)}, u32[]{:S(2)}) collective-permute-start(f32[2,6,16,256]{3,2,1,0:T(8,128)S(1)} %collective-permute-done.4.refs_3_), channel_id=1, source_target_pairs={{0,1},{1,0},{2,3},{3,2},{4,5},{5,4},{6,7},{7,6},{8,9},{9,8},{10,11... | collective-permute-start | bytes 589832 | tf_op jit(solution)/shard_map/ppermute | solution.py:67
  34.3 7.9 %collective-permute-start.26 = (f32[2,6,16,256]{3,2,1,0:T(8,128)S(1)}, f32[2,6,16,256]{3,2,1,0:T(8,128)S(1)}, u32[]{:S(2)}, u32[]{:S(2)}) collective-permute-start(f32[2,6,16,256]{3,2,1,0:T(8,128)S(1)} %collective-permute-done.25.refs_5_), channel_id=1, source_target_pairs={{0,1},{1,0},{2,3},{3,2},{4,5},{5,4},{6,7},{7,6},{8,9},{9,8},{10,11... | collective-permute-start | bytes 589832 | tf_op jit(solution)/shard_map/ppermute | solution.py:67
  34.3 4.7 %collective-permute-start.18 = (f32[6,16,256]{2,1,0:T(8,128)S(1)}, f32[6,16,256]{2,1,0:T(8,128)S(1)}, u32[]{:S(2)}, u32[]{:S(2)}) collective-permute-start(f32[6,16,256]{2,1,0:T(8,128)S(1)} %slice_bitcast_fusion.1), channel_id=1, source_target_pairs={{0,4},{1,3},{4,8},{5,1},{8,12},{9,5},{12,14},{13,9},{14,10},{15,13... | collective-permute-start | bytes 294920 | tf_op jit(solution)/shard_map/ppermute | solution.py:66
  35.9 4.6 %collective-permute-start.27 = (f32[6,16,256]{2,1,0:T(8,128)S(1)}, f32[6,16,256]{2,1,0:T(8,128)S(1)}, u32[]{:S(2)}, u32[]{:S(2)}) collective-permute-start(f32[6,16,256]{2,1,0:T(8,128)S(1)} %slice_bitcast_fusion), channel_id=1, source_target_pairs={{0,4},{1,3},{4,8},{5,1},{8,12},{9,5},{12,14},{13,9},{14,10},{15,13... | collective-permute-start | bytes 294920 | tf_op jit(solution)/shard_map/ppermute | solution.py:66
  37.5 4.6 %collective-permute-start.6 = (f32[6,16,256]{2,1,0:T(8,128)S(1)}, f32[6,16,256]{2,1,0:T(8,128)S(1)}, u32[]{:S(2)}, u32[]{:S(2)}) collective-permute-start(f32[6,16,256]{2,1,0:T(8,128)S(1)} %slice_bitcast_fusion.2), channel_id=1, source_target_pairs={{0,4},{1,3},{4,8},{5,1},{8,12},{9,5},{12,14},{13,9},{14,10},{15,13... | collective-permute-start | bytes 294920 | tf_op jit(solution)/shard_map/ppermute | solution.py:66
  39.0 3.6 %collective-permute-start.10 = (f32[2,6,16,256]{3,2,1,0:T(8,128)S(1)}, f32[2,6,16,256]{3,2,1,0:T(8,128)S(1)}, u32[]{:S(2)}, u32[]{:S(2)}) collective-permute-start(f32[2,6,16,256]{3,2,1,0:T(8,128)S(1)} %collective-permute-done.5.refs_5_), channel_id=1, source_target_pairs={{0,1},{1,0},{2,3},{3,2},{4,5},{5,4},{6,7},{7,6},{8,9},{9,8},{10,11... | collective-permute-start | bytes 589832 | tf_op jit(solution)/shard_map/ppermute | solution.py:67
  39.0 5.5 %collective-permute-start.13 = (f32[2,6,16,256]{3,2,1,0:T(8,128)S(1)}, f32[2,6,16,256]{3,2,1,0:T(8,128)S(1)}, u32[]{:S(2)}, u32[]{:S(2)}) collective-permute-start(f32[2,6,16,256]{3,2,1,0:T(8,128)S(1)} %collective-permute-done.12.refs_1_), channel_id=1, source_target_pairs={{0,1},{1,0},{2,3},{3,2},{4,5},{5,4},{6,7},{7,6},{8,9},{9,8},{10,11... | collective-permute-start | bytes 589832 | tf_op jit(solution)/shard_map/ppermute | solution.py:67
  40.5 4.0 %collective-permute-start.15 = (f32[2,6,16,256]{3,2,1,0:T(8,128)S(1)}, f32[2,6,16,256]{3,2,1,0:T(8,128)S(1)}, u32[]{:S(2)}, u32[]{:S(2)}) collective-permute-start(f32[2,6,16,256]{3,2,1,0:T(8,128)S(1)} %collective-permute-done.14.refs_3_), channel_id=1, source_target_pairs={{0,1},{1,0},{2,3},{3,2},{4,5},{5,4},{6,7},{7,6},{8,9},{9,8},{10,11... | collective-permute-start | bytes 589832 | tf_op jit(solution)/shard_map/ppermute | solution.py:67
  42.1 2.4 %collective-permute-start.17 = (f32[2,6,16,256]{3,2,1,0:T(8,128)S(1)}, f32[2,6,16,256]{3,2,1,0:T(8,128)S(1)}, u32[]{:S(2)}, u32[]{:S(2)}) collective-permute-start(f32[2,6,16,256]{3,2,1,0:T(8,128)S(1)} %collective-permute-done.16.refs_5_), channel_id=1, source_target_pairs={{0,1},{1,0},{2,3},{3,2},{4,5},{5,4},{6,7},{7,6},{8,9},{9,8},{10,11... | collective-permute-start | bytes 589832 | tf_op jit(solution)/shard_map/ppermute | solution.py:67
  42.6 1.9 %collective-permute-start.19 = (f32[6,16,256]{2,1,0:T(8,128)S(1)}, f32[6,16,256]{2,1,0:T(8,128)S(1)}, u32[]{:S(2)}, u32[]{:S(2)}) collective-permute-start(f32[6,16,256]{2,1,0:T(8,128)S(1)} %collective-permute-done.18.refs_7_), channel_id=1, source_target_pairs={{0,1},{1,0},{2,3},{3,2},{4,5},{5,4},{6,7},{7,6},{8,9},{9,8},{10,11... | collective-permute-start | bytes 294920 | tf_op jit(solution)/shard_map/ppermute | solution.py:67
  (6 other events, 22.6 us)

commit v6 on v5

--- a/solution.py
+++ b/solution.py
@@ -9,6 +9,7 @@
 
 ROWS = ((0,), (0,))
 PLAIN = ((1,), (0,))
+ABOVE = ((1,), (1,))
 
 
 def ring_place(chip, chips):
@@ -63,8 +64,10 @@
     moving = first
     pieces = [first]
     for step in range(1, steps + 1):
-        moving = lax.ppermute(moving if step < steps else moving[0], "col", nearest)
-        pieces += [moving, lax.ppermute(moving, "col", swap)]
+        moving = lax.ppermute(moving, "col", nearest)
+        pieces.append(moving)
+        if step < steps:
+            pieces.append(lax.ppermute(moving, "col", swap))
     return pieces
 
 
@@ -75,7 +78,8 @@
     for step in range(1, chips // 2 + 1):
         turn = step * (1 - 2 * core)
         found.append((ring_chip((here - turn + chips) % chips, chips), core))
-        found.append((ring_chip((here + turn + chips) % chips, chips), 1 - core))
+        if step < chips // 2:
+            found.append((ring_chip((here + turn + chips) % chips, chips), 1 - core))
     return found
 
 
@@ -89,20 +93,14 @@
         else:
             whole_ref[:, rows, :] = value
 
-    table = list(enumerate(streams(chips)))[chosen]
-    for ref, (at, (chip, core)) in zip(piece_refs, table):
+    for ref, (chip, core) in zip(piece_refs, streams(chips)[chosen]):
         if depth % 16 == 0:
-            if at < chips - 1:
-                for half in range(2):
-                    put((2 * chip + half) * depth, ref[jnp.where(core == 0, half, 1 - half)])
-            else:
-                put((2 * chip + core) * depth, ref[...])
-            continue
-        if at == chips:
-            continue
-        pair = [ref[0], ref[1]] if at < chips - 1 else [ref[...], piece_refs[-1][...]]
-        low, high = jnp.where(core == 0, pair[0], pair[1]), jnp.where(core == 0, pair[1], pair[0])
-        put(2 * chip * depth, jnp.concatenate([low, high], axis=1))
+            for half in range(2):
+                put((2 * chip + half) * depth, ref[jnp.where(core == 0, half, 1 - half)])
+        else:
+            low = jnp.where(core == 0, ref[0], ref[1])
+            high = jnp.where(core == 0, ref[1], ref[0])
+            put(2 * chip * depth, jnp.concatenate([low, high], axis=1))
     if depth % 16 != 0:
         high_ref[...], low_ref[...] = split(whole_ref[...])
 
@@ -182,13 +180,15 @@
 
 
 def prep_kernel(plan, *refs):
-    pieces, right_ref = refs[: plan.chips + 1], refs[plan.chips + 1]
-    received = refs[plan.chips + 2 : -5]
-    high_ref, low_ref, x_ref, total_ref, whole_ref = refs[-5:]
+    pieces, right_ref = refs[: plan.chips], refs[plan.chips]
+    received = refs[plan.chips + 1 : -6]
+    high_ref, low_ref, x_ref, wait_ref, total_ref, whole_ref = refs[-6:]
     assemble(pieces, high_ref, low_ref, whole_ref, plan.chips)
     mats, nb = [(high_ref, low_ref)], plan.nb
     answer = dot3(plan.mat(mats, "inv", 0), split(plan.panel_rows(0, right_ref, received)), PLAIN)
     x_ref[...] = answer
+    for panel in range(1, plan.panels):
+        wait_ref[panel - 1] = plan.panel_rows(panel, right_ref, received)
     solved = split(answer)
     for block in range(plan.wide):
         at = (plan.sure + block) * nb
@@ -202,20 +202,18 @@
 
 
 def late_pieces(plan, late):
-    return slice(plan.chips - 1, None) if late == 2 else slice(None)
+    return slice(plan.chips - 1, None) if late == 1 else slice(None)
 
 
 def final_kernel(plan, late, *refs):
     pieces, at = refs[:late], late + 2
     mats = [refs[at : at + 2], refs[at + 2 : at + 4]]
-    x_first, total_ref, right_ref = refs[at + 4 : at + 7]
-    received = refs[at + 7 : -7]
+    x_first, wait_ref, total_ref = refs[at + 4 : at + 7]
     out_hbm, high_ref, low_ref, x_ref, low_rows, whole_ref, sems = refs[-7:]
     panels, nb = plan.panels, plan.nb
     me = lax.axis_index("row")
     assemble(pieces, high_ref, low_ref, whole_ref, plan.chips, late_pieces(plan, late))
     mats.append((high_ref, low_ref))
-    currents = [plan.panel_rows(panel, right_ref, received) for panel in range(panels)]
     totals = [total_ref[block * nb : (block + 1) * nb] for block in range(plan.wide)]
 
     def panel_out(local):
@@ -228,23 +226,37 @@
         rows = pl.ds(local * nb, nb)
         return pltpu.make_async_copy(low_rows.at[block], out_hbm.at[rows], sems.at[local])
 
-    def each_out(act):
-        for local in range(plan.sure):
-            act(panel_out(local))
-        for local in range(plan.sure, plan.held):
-            pl.when(local * plan.group_count + me < panels)(functools.partial(act, panel_out(local)))
+    def each_out(act, locals_=range(plan.held)):
+        for local in locals_:
+            if local < plan.sure:
+                act(panel_out(local))
+            else:
+                pl.when(local * plan.group_count + me < panels)(functools.partial(act, panel_out(local)))
+
+    def tri(rank, panel):
+        return plan.mat(mats, "tri", plan.tri.index((rank, panel)))
+
+    def inverse(panel):
+        return plan.mat(mats, "inv", panel)
 
     answer = x_first[...]
+    rests = [None] + [wait_ref[panel - 1] for panel in range(1, panels)]
+    steps = [None] * 2 + [split(dot3(inverse(p), tri(p, p - 1), ABOVE)) for p in range(2, panels)]
     for panel in range(panels):
-        if panel > 0:
-            answer = dot3(plan.mat(mats, "inv", panel), split(currents[panel]), PLAIN)
+        if panel == 1:
+            rest = split(rests[1] - dot3(tri(1, 0), solved, ROWS))
+            answer = dot3(inverse(1), rest, PLAIN)
+        elif panel > 1:
+            answer = dot3(inverse(panel), split(rests[panel]), PLAIN) - dot3(steps[panel], solved, PLAIN)
         x_ref[panel] = answer
         solved = split(answer)
-        for after in range(panel + 1, panels):
-            mat = plan.mat(mats, "tri", plan.tri.index((after, panel)))
-            currents[after] = currents[after] - dot3(mat, solved, ROWS)
+        for after in range(panel + 2, panels):
+            rests[after] = rests[after] - dot3(tri(after, panel), solved, ROWS)
+        done = (panel + 1) // plan.group_count
+        if (panel + 1) % plan.group_count == 0 and done <= plan.sure:
+            each_out(lambda copy: copy.start(), [done - 1])
         if panel == panels - 1:
-            each_out(lambda copy: copy.start())
+            each_out(lambda copy: copy.start(), range(plan.sure, plan.held))
         for block in range(plan.wide):
             if panel > 0:
                 mat = plan.mat(mats, "low", panel, block)
@@ -318,14 +330,19 @@
             bound(place_kernel, plan), pairs[chunk], [wholes[chunk]], pieces[chunk][:count]
         )
 
-    inv_high, inv_low, x_first, total = kernel_call(
+    inv_high, inv_low, x_first, waiting, total = kernel_call(
         bound(prep_kernel, plan),
-        [*pairs[0], shape((nb, columns), f32), shape((plan.wide * nb, columns), f32)],
+        [
+            *pairs[0],
+            shape((nb, columns), f32),
+            shape((panels - 1, nb, columns), f32),
+            shape((plan.wide * nb, columns), f32),
+        ],
         [wholes[0]],
         (*pieces[0], right_side, *received),
         flops=6 * 3 * nb * nb * columns,
     )
-    below = place(1, chips + 1)
+    below = place(1, chips)
     if depth % 16 == 0:
         placed, late = place(2, chips - 1), pieces[2][chips - 1 :]
     else:
@@ -339,7 +356,7 @@
             wholes[2],
             pltpu.SemaphoreType.DMA((rows // nb,)),
         ],
-        (*late, *placed, inv_high, inv_low, *below, x_first, total, right_side, *received),
+        (*late, *placed, inv_high, inv_low, *below, x_first, waiting, total),
         flops=6 * 15 * nb * nb * columns,
         out_hbm=1,
         aliases={len(late): 1, len(late) + 1: 2},

time: 49 us -> 45.3 us (0.924)
  waiting for transfers between devices: 16.1 us -> 11.6 us
  local copies, waits for them, and re-layouts: 0.06 us -> 1.08 us
  starting transfers between devices: 26.6 us -> 26.1 us
    ppermute x24 -> x21, waiting for transfers between devices: 13.6 us -> 8.47 us  [the longest x12 8.45 us: ring(): moving = lax.ppermute(moving, 'col', nearest)]
    ppermute x1, waiting for transfers between devices: 0.01 us -> 2.23 us  [per_device(): tri = [own] + [lax.ppermute(own, 'row', pairs) for pairs in shifts]]
    ppermute x1, starting transfers between devices: 1.58 us -> 0.08 us  [per_device(): received = [lax.ppermute(above, 'row', pairs) for pairs in shifts]]
    ppermute x1, waiting for transfers between devices: 1.29 us -> 0.01 us  [per_device(): half_other = lax.ppermute(half, 'col', swap)]
    ppermute x1, starting transfers between devices: 1.52 us -> 2.58 us  [per_device(): tri = [own] + [lax.ppermute(own, 'row', pairs) for pairs in shifts]]
    slice x1, local copies, waits for them, and re-layouts: 0.03 us -> 1.08 us  [per_device(): above = right_side[:plan.held * nb]]
    ppermute x24 -> x21, starting transfers between devices: 22.8 us -> 22.3 us  [the longest x12 20.7 us: ring(): moving = lax.ppermute(moving, 'col', nearest)]
  transfers between devices with their start and end apart: 29 -> 26, of which waited for: 11 -> 12; matrix products, arithmetic and copies ran while one was open for 0% -> 2% of each run, Pallas kernels for 3% -> 4%
where the time goes in v6:
time: 45.3 us; the launch traced here: 45.1 us
  starting transfers between devices  26.1 us (58%)
  waiting for transfers between devices  11.6 us (26%)
  Pallas kernels  6.21 us (14%)
  local copies, waits for them, and re-layouts  1.08 us (2%)
    ppermute x12, starting transfers between devices, ring(): moving = lax.ppermute(moving, 'col', nearest)  20.7 us
    ppermute x12, waiting for transfers between devices, ring(): moving = lax.ppermute(moving, 'col', nearest)  8.45 us
    pallas_call x9, Pallas kernels, kernel_call(): pl.pallas_call(body, out_shape=out_shapes, in_specs=[hbm] * in_hbm + [nea...  6.21 us
    ppermute x1, starting transfers between devices, per_device(): tri = [own] + [lax.ppermute(own, 'row', pairs) for pairs in shifts]  2.58 us
    ppermute x1, waiting for transfers between devices, per_device(): tri = [own] + [lax.ppermute(own, 'row', pairs) for pairs in shifts]  2.23 us
    ppermute x9, starting transfers between devices, ring(): pieces.append(lax.ppermute(moving, 'col', swap))  1.6 us
    slice x1, local copies, waits for them, and re-layouts, per_device(): above = right_side[:plan.held * nb]  1.08 us
  transfers between devices with their start and end apart: 26, of which 12 were waited for; matrix products, arithmetic and copies ran while one was open for 2% of the time, Pallas kernels for 4%

profile of v6, /device:TPU:0, one launch (start us, length us, event | category | flops | bytes accessed | tf_op | source)
XLA Modules:
  0.0 45.1 jit_solution(17508078573690608761)
XLA Ops:
  0.0 1.1 %shard_map.37 = (f32[4,16,1024]{2,1,0:T(8,128)S(1)}, f32[4,16,256]{2,1,0:T(8,128)S(1)}, f32[3,16,512]{2,1,0:T(8,128)S(1)}) custom-call(f32[4,16,1024]{2,1,0:T(8,128)} %factor_hbm.1, f32[4,16,256]{2,1,0:T(8,128)} %inv_hbm.1), custom_call_target="tpu_custom_call" | custom-call | bytes 4194304 | tf_op jit(solution)/shard_map/pallas_call | solution.py:42
  1.6 2.6 %collective-permute-start = (f32[3,16,512]{2,1,0:T(8,128)S(1)}, f32[3,16,512]{2,1,0:T(8,128)S(1)}, u32[]{:S(2)}, u32[]{:S(2)}) collective-permute-start(f32[3,16,512]{2,1,0:T(8,128)S(1)} %get-tuple-element.18.refs_0_), channel_id=1, source_target_pairs={{16,0},{0,16},{17,1},{1,17},{18,2},{2,18},{19,3},{3,19},{20,4},{4,... | collective-permute-start | bytes 294920 | tf_op jit(solution)/shard_map/ppermute | solution.py:308
  4.2 1.1 %slice.3 = f32[512,256]{1,0:T(8,128)S(1)} slice(f32[1024,256]{1,0:T(8,128)} %refs_8_.1), slice={[0:512], [0:256]} | slice | bytes 1048576 | tf_op jit(solution)/shard_map/slice | solution.py:309
  5.4 2.2 %collective-permute-done.refs_1_ = f32[3,16,512]{2,1,0:T(8,128)S(1)} collective-permute-done((f32[3,16,512]{2,1,0:T(8,128)S(1)}, f32[3,16,512]{2,1,0:T(8,128)S(1)}, u32[]{:S(2)}, u32[]{:S(2)}) %collective-permute-start) | collective-permute-done | bytes 98336 | tf_op jit(solution)/shard_map/ppermute | solution.py:308
  8.2 0.9 %collective-permute-done.10.refs_2_ = f32[4,16,256]{2,1,0:T(8,128)S(1)} collective-permute-done((f32[4,16,256]{2,1,0:T(8,128)S(1)}, f32[4,16,256]{2,1,0:T(8,128)S(1)}, u32[]{:S(2)}, u32[]{:S(2)}) %collective-permute-start.10) | collective-permute-done | bytes 65568 | tf_op jit(solution)/shard_map/ppermute | solution.py:306
  9.1 1.9 %collective-permute-start.19 = (f32[2,6,16,256]{3,2,1,0:T(8,128)S(1)}, f32[2,6,16,256]{3,2,1,0:T(8,128)S(1)}, u32[]{:S(2)}, u32[]{:S(2)}) collective-permute-start(f32[2,6,16,256]{3,2,1,0:T(8,128)S(1)} %shard_map.43.refs_0_), channel_id=1, source_target_pairs={{0,4},{1,3},{4,8},{5,1},{8,12},{9,5},{12,14},{13,9},{14,10},{15,13... | collective-permute-start | bytes 589832 | tf_op jit(solution)/shard_map/ppermute | solution.py:67
  11.0 1.6 %collective-permute-start.11 = (f32[2,6,16,256]{3,2,1,0:T(8,128)S(1)}, f32[2,6,16,256]{3,2,1,0:T(8,128)S(1)}, u32[]{:S(2)}, u32[]{:S(2)}) collective-permute-start(f32[2,6,16,256]{3,2,1,0:T(8,128)S(1)} %shard_map.41.refs_0_), channel_id=1, source_target_pairs={{0,4},{1,3},{4,8},{5,1},{8,12},{9,5},{12,14},{13,9},{14,10},{15,13... | collective-permute-start | bytes 589832 | tf_op jit(solution)/shard_map/ppermute | solution.py:67
  12.6 1.6 %collective-permute-start.3 = (f32[2,6,16,256]{3,2,1,0:T(8,128)S(1)}, f32[2,6,16,256]{3,2,1,0:T(8,128)S(1)}, u32[]{:S(2)}, u32[]{:S(2)}) collective-permute-start(f32[2,6,16,256]{3,2,1,0:T(8,128)S(1)} %shard_map.39.refs_0_), channel_id=1, source_target_pairs={{0,4},{1,3},{4,8},{5,1},{8,12},{9,5},{12,14},{13,9},{14,10},{15,13... | collective-permute-start | bytes 589832 | tf_op jit(solution)/shard_map/ppermute | solution.py:67
  14.3 0.6 %collective-permute-done.19.refs_1_ = f32[2,6,16,256]{3,2,1,0:T(8,128)S(1)} collective-permute-done((f32[2,6,16,256]{3,2,1,0:T(8,128)S(1)}, f32[2,6,16,256]{3,2,1,0:T(8,128)S(1)}, u32[]{:S(2)}, u32[]{:S(2)}) %collective-permute-start.19) | collective-permute-done | bytes 196640 | tf_op jit(solution)/shard_map/ppermute | solution.py:67
  14.8 1.8 %collective-permute-start.21 = (f32[2,6,16,256]{3,2,1,0:T(8,128)S(1)}, f32[2,6,16,256]{3,2,1,0:T(8,128)S(1)}, u32[]{:S(2)}, u32[]{:S(2)}) collective-permute-start(f32[2,6,16,256]{3,2,1,0:T(8,128)S(1)} %collective-permute-done.19.refs_1_), channel_id=1, source_target_pairs={{0,4},{1,3},{4,8},{5,1},{8,12},{9,5},{12,14},{13,9},{14,10},{15,13... | collective-permute-start | bytes 589832 | tf_op jit(solution)/shard_map/ppermute | solution.py:67
  17.0 1.8 %collective-permute-start.13 = (f32[2,6,16,256]{3,2,1,0:T(8,128)S(1)}, f32[2,6,16,256]{3,2,1,0:T(8,128)S(1)}, u32[]{:S(2)}, u32[]{:S(2)}) collective-permute-start(f32[2,6,16,256]{3,2,1,0:T(8,128)S(1)} %collective-permute-done.11.refs_1_), channel_id=1, source_target_pairs={{0,4},{1,3},{4,8},{5,1},{8,12},{9,5},{12,14},{13,9},{14,10},{15,13... | collective-permute-start | bytes 589832 | tf_op jit(solution)/shard_map/ppermute | solution.py:67
  19.1 1.8 %collective-permute-start.4 = (f32[2,6,16,256]{3,2,1,0:T(8,128)S(1)}, f32[2,6,16,256]{3,2,1,0:T(8,128)S(1)}, u32[]{:S(2)}, u32[]{:S(2)}) collective-permute-start(f32[2,6,16,256]{3,2,1,0:T(8,128)S(1)} %collective-permute-done.3.refs_1_), channel_id=1, source_target_pairs={{0,4},{1,3},{4,8},{5,1},{8,12},{9,5},{12,14},{13,9},{14,10},{15,13... | collective-permute-start | bytes 589832 | tf_op jit(solution)/shard_map/ppermute | solution.py:67
  21.4 1.6 %collective-permute-start.23 = (f32[2,6,16,256]{3,2,1,0:T(8,128)S(1)}, f32[2,6,16,256]{3,2,1,0:T(8,128)S(1)}, u32[]{:S(2)}, u32[]{:S(2)}) collective-permute-start(f32[2,6,16,256]{3,2,1,0:T(8,128)S(1)} %collective-permute-done.21.refs_3_), channel_id=1, source_target_pairs={{0,4},{1,3},{4,8},{5,1},{8,12},{9,5},{12,14},{13,9},{14,10},{15,13... | collective-permute-start | bytes 589832 | tf_op jit(solution)/shard_map/ppermute | solution.py:67
  23.3 1.8 %collective-permute-start.15 = (f32[2,6,16,256]{3,2,1,0:T(8,128)S(1)}, f32[2,6,16,256]{3,2,1,0:T(8,128)S(1)}, u32[]{:S(2)}, u32[]{:S(2)}) collective-permute-start(f32[2,6,16,256]{3,2,1,0:T(8,128)S(1)} %collective-permute-done.13.refs_3_), channel_id=1, source_target_pairs={{0,4},{1,3},{4,8},{5,1},{8,12},{9,5},{12,14},{13,9},{14,10},{15,13... | collective-permute-start | bytes 589832 | tf_op jit(solution)/shard_map/ppermute | solution.py:67
  25.4 1.8 %collective-permute-start.5 = (f32[2,6,16,256]{3,2,1,0:T(8,128)S(1)}, f32[2,6,16,256]{3,2,1,0:T(8,128)S(1)}, u32[]{:S(2)}, u32[]{:S(2)}) collective-permute-start(f32[2,6,16,256]{3,2,1,0:T(8,128)S(1)} %collective-permute-done.4.refs_3_), channel_id=1, source_target_pairs={{0,4},{1,3},{4,8},{5,1},{8,12},{9,5},{12,14},{13,9},{14,10},{15,13... | collective-permute-start | bytes 589832 | tf_op jit(solution)/shard_map/ppermute | solution.py:67
  27.7 1.6 %collective-permute-start.25 = (f32[2,6,16,256]{3,2,1,0:T(8,128)S(1)}, f32[2,6,16,256]{3,2,1,0:T(8,128)S(1)}, u32[]{:S(2)}, u32[]{:S(2)}) collective-permute-start(f32[2,6,16,256]{3,2,1,0:T(8,128)S(1)} %collective-permute-done.23.refs_5_), channel_id=1, source_target_pairs={{0,4},{1,3},{4,8},{5,1},{8,12},{9,5},{12,14},{13,9},{14,10},{15,13... | collective-permute-start | bytes 589832 | tf_op jit(solution)/shard_map/ppermute | solution.py:67
  29.6 2.1 %collective-permute-done.5.refs_5_ = f32[2,6,16,256]{3,2,1,0:T(8,128)S(1)} collective-permute-done((f32[2,6,16,256]{3,2,1,0:T(8,128)S(1)}, f32[2,6,16,256]{3,2,1,0:T(8,128)S(1)}, u32[]{:S(2)}, u32[]{:S(2)}) %collective-permute-start.5) | collective-permute-done | bytes 196640 | tf_op jit(solution)/shard_map/ppermute | solution.py:67
  32.3 1.5 %collective-permute-done.25.refs_7_ = f32[2,6,16,256]{3,2,1,0:T(8,128)S(1)} collective-permute-done((f32[2,6,16,256]{3,2,1,0:T(8,128)S(1)}, f32[2,6,16,256]{3,2,1,0:T(8,128)S(1)}, u32[]{:S(2)}, u32[]{:S(2)}) %collective-permute-start.25) | collective-permute-done | bytes 196640 | tf_op jit(solution)/shard_map/ppermute | solution.py:67
  33.8 1.8 %collective-permute-start.17 = (f32[2,6,16,256]{3,2,1,0:T(8,128)S(1)}, f32[2,6,16,256]{3,2,1,0:T(8,128)S(1)}, u32[]{:S(2)}, u32[]{:S(2)}) collective-permute-start(f32[2,6,16,256]{3,2,1,0:T(8,128)S(1)} %collective-permute-done.15.refs_5_), channel_id=1, source_target_pairs={{0,4},{1,3},{4,8},{5,1},{8,12},{9,5},{12,14},{13,9},{14,10},{15,13... | collective-permute-start | bytes 589832 | tf_op jit(solution)/shard_map/ppermute | solution.py:67
  35.6 1.6 %collective-permute-start.6 = (f32[2,6,16,256]{3,2,1,0:T(8,128)S(1)}, f32[2,6,16,256]{3,2,1,0:T(8,128)S(1)}, u32[]{:S(2)}, u32[]{:S(2)}) collective-permute-start(f32[2,6,16,256]{3,2,1,0:T(8,128)S(1)} %collective-permute-done.5.refs_5_), channel_id=1, source_target_pairs={{0,4},{1,3},{4,8},{5,1},{8,12},{9,5},{12,14},{13,9},{14,10},{15,13... | collective-permute-start | bytes 589832 | tf_op jit(solution)/shard_map/ppermute | solution.py:67
  37.9 1.6 %collective-permute-done.17.refs_7_ = f32[2,6,16,256]{3,2,1,0:T(8,128)S(1)} collective-permute-done((f32[2,6,16,256]{3,2,1,0:T(8,128)S(1)}, f32[2,6,16,256]{3,2,1,0:T(8,128)S(1)}, u32[]{:S(2)}, u32[]{:S(2)}) %collective-permute-start.17) | collective-permute-done | bytes 196640 | tf_op jit(solution)/shard_map/ppermute | solution.py:67
  39.5 0.9 %shard_map.42 = (bf16[6,256,256]{2,1,0:T(8,128)(2,1)S(1)}, bf16[6,256,256]{2,1,0:T(8,128)(2,1)S(1)}, f32[256,256]{1,0:T(8,128)S(1)}, f32[3,256,256]{2,1,0:T(8,128)S(1)}, f32[512,256]{1,0:T(8,128)S(1)}) custom-call(f32[2,6,16,256]{3,2,1,0:T(8,128)S(1)} %shard_map.41.refs_0_, f32[2,6,16,256]{3,2,1,0:T(8,128)S(1)} %collective-permute-done.11.refs_1_, ...), custom_call_target="tpu_custom_call" | custom-call | flops 301989888 | bytes 4194304 | tf_op jit(solution)/shard_map/pallas_call | solution.py:42
  40.4 1.2 %collective-permute-done.6.refs_0_ = f32[2,6,16,256]{3,2,1,0:T(8,128)S(1)} collective-permute-done((f32[2,6,16,256]{3,2,1,0:T(8,128)S(1)}, f32[2,6,16,256]{3,2,1,0:T(8,128)S(1)}, u32[]{:S(2)}, u32[]{:S(2)}) %collective-permute-start.6) | collective-permute-done | bytes 196640 | tf_op jit(solution)/shard_map/ppermute | solution.py:67
  41.6 3.5 %shard_map.45 = (f32[1024,256]{1,0:T(8,128)}, bf16[6,256,256]{2,1,0:T(8,128)(2,1)S(1)}, bf16[6,256,256]{2,1,0:T(8,128)(2,1)S(1)}) custom-call(f32[2,6,16,256]{3,2,1,0:T(8,128)S(1)} %collective-permute-done.6.refs_0_, bf16[6,256,256]{2,1,0:T(8,128)(2,1)S(1)} %get-tuple-element.20.refs_1_, ...), custom_call_target="tpu_custom_call", output_to_operand_aliasing={{1}: (1, {}), {2}: (2, {})} | custom-call | flops 1509949440 | bytes 4194304 | tf_op jit(solution)/shard_map/pallas_call | solution.py:42
  (40 shorter events, 5.1 us)
Async XLA Ops:
  1.1 8.0 %collective-permute-start.2 = (f32[4,16,1024]{2,1,0:T(8,128)S(1)}, f32[4,16,1024]{2,1,0:T(8,128)S(1)}, u32[]{:S(2)}, u32[]{:S(2)}) collective-permute-start(f32[4,16,1024]{2,1,0:T(8,128)S(1)} %get-tuple-element.19.refs_1_), channel_id=1, source_target_pairs={{0,1},{1,0},{2,3},{3,2},{4,5},{5,4},{6,7},{7,6},{8,9},{9,8},{10,11... | collective-permute-start | bytes 786440 | tf_op jit(solution)/shard_map/ppermute | solution.py:307
  1.6 6.0 %collective-permute-start = (f32[3,16,512]{2,1,0:T(8,128)S(1)}, f32[3,16,512]{2,1,0:T(8,128)S(1)}, u32[]{:S(2)}, u32[]{:S(2)}) collective-permute-start(f32[3,16,512]{2,1,0:T(8,128)S(1)} %get-tuple-element.18.refs_0_), channel_id=1, source_target_pairs={{16,0},{0,16},{17,1},{1,17},{18,2},{2,18},{19,3},{3,19},{20,4},{4,... | collective-permute-start | bytes 294920 | tf_op jit(solution)/shard_map/ppermute | solution.py:308
  5.3 15.6 %collective-permute-start.18 = (f32[512,256]{1,0:T(8,128)S(1)}, f32[512,256]{1,0:T(8,128)S(1)}, u32[]{:S(2)}, u32[]{:S(2)}) collective-permute-start(f32[512,256]{1,0:T(8,128)S(1)} %slice.3), channel_id=1, source_target_pairs={{16,0},{0,16},{17,1},{1,17},{18,2},{2,18},{19,3},{3,19},{20,4},{4,... | collective-permute-start | bytes 1572872 | tf_op jit(solution)/shard_map/ppermute | solution.py:310
  7.6 5.0 %collective-permute-start.1 = (f32[6,16,256]{2,1,0:T(8,128)S(1)}, f32[6,16,256]{2,1,0:T(8,128)S(1)}, u32[]{:S(2)}, u32[]{:S(2)}) collective-permute-start(f32[6,16,256]{2,1,0:T(8,128)S(1)} %shard_map.38.refs_0_), channel_id=1, source_target_pairs={{0,1},{1,0},{2,3},{3,2},{4,5},{5,4},{6,7},{7,6},{8,9},{9,8},{10,11... | collective-permute-start | bytes 294920 | tf_op jit(solution)/shard_map/ppermute | solution.py:312
  9.1 5.7 %collective-permute-start.19 = (f32[2,6,16,256]{3,2,1,0:T(8,128)S(1)}, f32[2,6,16,256]{3,2,1,0:T(8,128)S(1)}, u32[]{:S(2)}, u32[]{:S(2)}) collective-permute-start(f32[2,6,16,256]{3,2,1,0:T(8,128)S(1)} %shard_map.43.refs_0_), channel_id=1, source_target_pairs={{0,4},{1,3},{4,8},{5,1},{8,12},{9,5},{12,14},{13,9},{14,10},{15,13... | collective-permute-start | bytes 589832 | tf_op jit(solution)/shard_map/ppermute | solution.py:67
  11.0 6.0 %collective-permute-start.11 = (f32[2,6,16,256]{3,2,1,0:T(8,128)S(1)}, f32[2,6,16,256]{3,2,1,0:T(8,128)S(1)}, u32[]{:S(2)}, u32[]{:S(2)}) collective-permute-start(f32[2,6,16,256]{3,2,1,0:T(8,128)S(1)} %shard_map.41.refs_0_), channel_id=1, source_target_pairs={{0,4},{1,3},{4,8},{5,1},{8,12},{9,5},{12,14},{13,9},{14,10},{15,13... | collective-permute-start | bytes 589832 | tf_op jit(solution)/shard_map/ppermute | solution.py:67
  12.6 6.4 %collective-permute-start.3 = (f32[2,6,16,256]{3,2,1,0:T(8,128)S(1)}, f32[2,6,16,256]{3,2,1,0:T(8,128)S(1)}, u32[]{:S(2)}, u32[]{:S(2)}) collective-permute-start(f32[2,6,16,256]{3,2,1,0:T(8,128)S(1)} %shard_map.39.refs_0_), channel_id=1, source_target_pairs={{0,4},{1,3},{4,8},{5,1},{8,12},{9,5},{12,14},{13,9},{14,10},{15,13... | collective-permute-start | bytes 589832 | tf_op jit(solution)/shard_map/ppermute | solution.py:67
  14.8 6.5 %collective-permute-start.21 = (f32[2,6,16,256]{3,2,1,0:T(8,128)S(1)}, f32[2,6,16,256]{3,2,1,0:T(8,128)S(1)}, u32[]{:S(2)}, u32[]{:S(2)}) collective-permute-start(f32[2,6,16,256]{3,2,1,0:T(8,128)S(1)} %collective-permute-done.19.refs_1_), channel_id=1, source_target_pairs={{0,4},{1,3},{4,8},{5,1},{8,12},{9,5},{12,14},{13,9},{14,10},{15,13... | collective-permute-start | bytes 589832 | tf_op jit(solution)/shard_map/ppermute | solution.py:67
  17.0 6.3 %collective-permute-start.13 = (f32[2,6,16,256]{3,2,1,0:T(8,128)S(1)}, f32[2,6,16,256]{3,2,1,0:T(8,128)S(1)}, u32[]{:S(2)}, u32[]{:S(2)}) collective-permute-start(f32[2,6,16,256]{3,2,1,0:T(8,128)S(1)} %collective-permute-done.11.refs_1_), channel_id=1, source_target_pairs={{0,4},{1,3},{4,8},{5,1},{8,12},{9,5},{12,14},{13,9},{14,10},{15,13... | collective-permute-start | bytes 589832 | tf_op jit(solution)/shard_map/ppermute | solution.py:67
  19.1 6.3 %collective-permute-start.4 = (f32[2,6,16,256]{3,2,1,0:T(8,128)S(1)}, f32[2,6,16,256]{3,2,1,0:T(8,128)S(1)}, u32[]{:S(2)}, u32[]{:S(2)}) collective-permute-start(f32[2,6,16,256]{3,2,1,0:T(8,128)S(1)} %collective-permute-done.3.refs_1_), channel_id=1, source_target_pairs={{0,4},{1,3},{4,8},{5,1},{8,12},{9,5},{12,14},{13,9},{14,10},{15,13... | collective-permute-start | bytes 589832 | tf_op jit(solution)/shard_map/ppermute | solution.py:67
  20.9 6.3 %collective-permute-start.20 = (f32[2,6,16,256]{3,2,1,0:T(8,128)S(1)}, f32[2,6,16,256]{3,2,1,0:T(8,128)S(1)}, u32[]{:S(2)}, u32[]{:S(2)}) collective-permute-start(f32[2,6,16,256]{3,2,1,0:T(8,128)S(1)} %collective-permute-done.19.refs_1_), channel_id=1, source_target_pairs={{0,1},{1,0},{2,3},{3,2},{4,5},{5,4},{6,7},{7,6},{8,9},{9,8},{10,11... | collective-permute-start | bytes 589832 | tf_op jit(solution)/shard_map/ppermute | solution.py:70
  20.9 6.3 %collective-permute-start.7 = (f32[2,6,16,256]{3,2,1,0:T(8,128)S(1)}, f32[2,6,16,256]{3,2,1,0:T(8,128)S(1)}, u32[]{:S(2)}, u32[]{:S(2)}) collective-permute-start(f32[2,6,16,256]{3,2,1,0:T(8,128)S(1)} %collective-permute-done.3.refs_1_), channel_id=1, source_target_pairs={{0,1},{1,0},{2,3},{3,2},{4,5},{5,4},{6,7},{7,6},{8,9},{9,8},{10,11... | collective-permute-start | bytes 589832 | tf_op jit(solution)/shard_map/ppermute | solution.py:70
  21.4 6.3 %collective-permute-start.23 = (f32[2,6,16,256]{3,2,1,0:T(8,128)S(1)}, f32[2,6,16,256]{3,2,1,0:T(8,128)S(1)}, u32[]{:S(2)}, u32[]{:S(2)}) collective-permute-start(f32[2,6,16,256]{3,2,1,0:T(8,128)S(1)} %collective-permute-done.21.refs_3_), channel_id=1, source_target_pairs={{0,4},{1,3},{4,8},{5,1},{8,12},{9,5},{12,14},{13,9},{14,10},{15,13... | collective-permute-start | bytes 589832 | tf_op jit(solution)/shard_map/ppermute | solution.py:67
  23.3 6.3 %collective-permute-start.15 = (f32[2,6,16,256]{3,2,1,0:T(8,128)S(1)}, f32[2,6,16,256]{3,2,1,0:T(8,128)S(1)}, u32[]{:S(2)}, u32[]{:S(2)}) collective-permute-start(f32[2,6,16,256]{3,2,1,0:T(8,128)S(1)} %collective-permute-done.13.refs_3_), channel_id=1, source_target_pairs={{0,4},{1,3},{4,8},{5,1},{8,12},{9,5},{12,14},{13,9},{14,10},{15,13... | collective-permute-start | bytes 589832 | tf_op jit(solution)/shard_map/ppermute | solution.py:67
  25.4 6.3 %collective-permute-start.5 = (f32[2,6,16,256]{3,2,1,0:T(8,128)S(1)}, f32[2,6,16,256]{3,2,1,0:T(8,128)S(1)}, u32[]{:S(2)}, u32[]{:S(2)}) collective-permute-start(f32[2,6,16,256]{3,2,1,0:T(8,128)S(1)} %collective-permute-done.4.refs_3_), channel_id=1, source_target_pairs={{0,4},{1,3},{4,8},{5,1},{8,12},{9,5},{12,14},{13,9},{14,10},{15,13... | collective-permute-start | bytes 589832 | tf_op jit(solution)/shard_map/ppermute | solution.py:67
  27.2 4.5 %collective-permute-start.22 = (f32[2,6,16,256]{3,2,1,0:T(8,128)S(1)}, f32[2,6,16,256]{3,2,1,0:T(8,128)S(1)}, u32[]{:S(2)}, u32[]{:S(2)}) collective-permute-start(f32[2,6,16,256]{3,2,1,0:T(8,128)S(1)} %collective-permute-done.21.refs_3_), channel_id=1, source_target_pairs={{0,1},{1,0},{2,3},{3,2},{4,5},{5,4},{6,7},{7,6},{8,9},{9,8},{10,11... | collective-permute-start | bytes 589832 | tf_op jit(solution)/shard_map/ppermute | solution.py:70
  27.2 5.0 %collective-permute-start.8 = (f32[2,6,16,256]{3,2,1,0:T(8,128)S(1)}, f32[2,6,16,256]{3,2,1,0:T(8,128)S(1)}, u32[]{:S(2)}, u32[]{:S(2)}) collective-permute-start(f32[2,6,16,256]{3,2,1,0:T(8,128)S(1)} %collective-permute-done.4.refs_3_), channel_id=1, source_target_pairs={{0,1},{1,0},{2,3},{3,2},{4,5},{5,4},{6,7},{7,6},{8,9},{9,8},{10,11... | collective-permute-start | bytes 589832 | tf_op jit(solution)/shard_map/ppermute | solution.py:70
  27.7 6.1 %collective-permute-start.25 = (f32[2,6,16,256]{3,2,1,0:T(8,128)S(1)}, f32[2,6,16,256]{3,2,1,0:T(8,128)S(1)}, u32[]{:S(2)}, u32[]{:S(2)}) collective-permute-start(f32[2,6,16,256]{3,2,1,0:T(8,128)S(1)} %collective-permute-done.23.refs_5_), channel_id=1, source_target_pairs={{0,4},{1,3},{4,8},{5,1},{8,12},{9,5},{12,14},{13,9},{14,10},{15,13... | collective-permute-start | bytes 589832 | tf_op jit(solution)/shard_map/ppermute | solution.py:67
  29.6 6.0 %collective-permute-start.24 = (f32[2,6,16,256]{3,2,1,0:T(8,128)S(1)}, f32[2,6,16,256]{3,2,1,0:T(8,128)S(1)}, u32[]{:S(2)}, u32[]{:S(2)}) collective-permute-start(f32[2,6,16,256]{3,2,1,0:T(8,128)S(1)} %collective-permute-done.23.refs_5_), channel_id=1, source_target_pairs={{0,1},{1,0},{2,3},{3,2},{4,5},{5,4},{6,7},{7,6},{8,9},{9,8},{10,11... | collective-permute-start | bytes 589832 | tf_op jit(solution)/shard_map/ppermute | solution.py:70
  31.7 3.9 %collective-permute-start.9 = (f32[2,6,16,256]{3,2,1,0:T(8,128)S(1)}, f32[2,6,16,256]{3,2,1,0:T(8,128)S(1)}, u32[]{:S(2)}, u32[]{:S(2)}) collective-permute-start(f32[2,6,16,256]{3,2,1,0:T(8,128)S(1)} %collective-permute-done.5.refs_5_), channel_id=1, source_target_pairs={{0,1},{1,0},{2,3},{3,2},{4,5},{5,4},{6,7},{7,6},{8,9},{9,8},{10,11... | collective-permute-start | bytes 589832 | tf_op jit(solution)/shard_map/ppermute | solution.py:70
  31.7 6.2 %collective-permute-start.12 = (f32[2,6,16,256]{3,2,1,0:T(8,128)S(1)}, f32[2,6,16,256]{3,2,1,0:T(8,128)S(1)}, u32[]{:S(2)}, u32[]{:S(2)}) collective-permute-start(f32[2,6,16,256]{3,2,1,0:T(8,128)S(1)} %collective-permute-done.11.refs_1_), channel_id=1, source_target_pairs={{0,1},{1,0},{2,3},{3,2},{4,5},{5,4},{6,7},{7,6},{8,9},{9,8},{10,11... | collective-permute-start | bytes 589832 | tf_op jit(solution)/shard_map/ppermute | solution.py:70
  32.2 5.7 %collective-permute-start.14 = (f32[2,6,16,256]{3,2,1,0:T(8,128)S(1)}, f32[2,6,16,256]{3,2,1,0:T(8,128)S(1)}, u32[]{:S(2)}, u32[]{:S(2)}) collective-permute-start(f32[2,6,16,256]{3,2,1,0:T(8,128)S(1)} %collective-permute-done.13.refs_3_), channel_id=1, source_target_pairs={{0,1},{1,0},{2,3},{3,2},{4,5},{5,4},{6,7},{7,6},{8,9},{9,8},{10,11... | collective-permute-start | bytes 589832 | tf_op jit(solution)/shard_map/ppermute | solution.py:70
  33.8 5.7 %collective-permute-start.17 = (f32[2,6,16,256]{3,2,1,0:T(8,128)S(1)}, f32[2,6,16,256]{3,2,1,0:T(8,128)S(1)}, u32[]{:S(2)}, u32[]{:S(2)}) collective-permute-start(f32[2,6,16,256]{3,2,1,0:T(8,128)S(1)} %collective-permute-done.15.refs_5_), channel_id=1, source_target_pairs={{0,4},{1,3},{4,8},{5,1},{8,12},{9,5},{12,14},{13,9},{14,10},{15,13... | collective-permute-start | bytes 589832 | tf_op jit(solution)/shard_map/ppermute | solution.py:67
  35.6 6.0 %collective-permute-start.6 = (f32[2,6,16,256]{3,2,1,0:T(8,128)S(1)}, f32[2,6,16,256]{3,2,1,0:T(8,128)S(1)}, u32[]{:S(2)}, u32[]{:S(2)}) collective-permute-start(f32[2,6,16,256]{3,2,1,0:T(8,128)S(1)} %collective-permute-done.5.refs_5_), channel_id=1, source_target_pairs={{0,4},{1,3},{4,8},{5,1},{8,12},{9,5},{12,14},{13,9},{14,10},{15,13... | collective-permute-start | bytes 589832 | tf_op jit(solution)/shard_map/ppermute | solution.py:67
  (3 other events, 7.2 us)

commit v7 on v6

--- a/solution.py
+++ b/solution.py
@@ -127,6 +127,9 @@
         ]
         self.where = {b: (c, at) for c, chunk in enumerate(self.chunks) for at, b in enumerate(chunk)}
 
+    def tri_of(self, rank):
+        return slice(rank * (rank - 1) // 2, rank * (rank + 1) // 2)
+
     def mat(self, mats, *block):
         chunk, at = self.where[block]
         high, low = mats[chunk]
@@ -181,15 +184,16 @@
 
 def prep_kernel(plan, *refs):
     pieces, right_ref = refs[: plan.chips], refs[plan.chips]
-    received = refs[plan.chips + 1 : -6]
-    high_ref, low_ref, x_ref, wait_ref, total_ref, whole_ref = refs[-6:]
+    received = refs[plan.chips + 1 : -5]
+    high_ref, low_ref, start_ref, total_ref, whole_ref = refs[-5:]
     assemble(pieces, high_ref, low_ref, whole_ref, plan.chips)
     mats, nb = [(high_ref, low_ref)], plan.nb
-    answer = dot3(plan.mat(mats, "inv", 0), split(plan.panel_rows(0, right_ref, received)), PLAIN)
-    x_ref[...] = answer
-    for panel in range(1, plan.panels):
-        wait_ref[panel - 1] = plan.panel_rows(panel, right_ref, received)
-    solved = split(answer)
+    for panel in range(plan.panels):
+        rows = split(plan.panel_rows(panel, right_ref, received))
+        answer = dot3(plan.mat(mats, "inv", panel), rows, PLAIN)
+        start_ref[panel] = answer
+        if panel == 0:
+            solved = split(answer)
     for block in range(plan.wide):
         at = (plan.sure + block) * nb
         total = right_ref[at : at + nb] - dot3(plan.mat(mats, "low", 0, block), solved, ROWS)
@@ -201,19 +205,34 @@
     assemble(refs[:-3], high_ref, low_ref, whole_ref, plan.chips, slice(0, len(refs) - 3))
 
 
-def late_pieces(plan, late):
-    return slice(plan.chips - 1, None) if late == 1 else slice(None)
+def triangle_kernel(plan, count, *refs):
+    inv_high, inv_low, high_ref, low_ref, tri_high, tri_low, whole_ref = refs[count:]
+    assemble(refs[:count], tri_high, tri_low, whole_ref, plan.chips, slice(0, count))
+    for rank in range(1, plan.panels):
+        rows = plan.tri_of(rank)
+        flat = (rank * plan.nb, plan.nb)
+        tri = tri_high[rows].reshape(flat), tri_low[rows].reshape(flat)
+        step = dot3(tri, (inv_high[rank], inv_low[rank]), ABOVE).reshape(rank, plan.nb, plan.nb)
+        high_ref[rows], low_ref[rows] = split(step)
 
 
 def final_kernel(plan, late, *refs):
     pieces, at = refs[:late], late + 2
     mats = [refs[at : at + 2], refs[at + 2 : at + 4]]
-    x_first, wait_ref, total_ref = refs[at + 4 : at + 7]
-    out_hbm, high_ref, low_ref, x_ref, low_rows, whole_ref, sems = refs[-7:]
+    start_ref, total_ref = refs[at + 4 : at + 6]
+    out_hbm, high_ref, low_ref, x_ref, low_rows, sems = refs[-6:]
     panels, nb = plan.panels, plan.nb
     me = lax.axis_index("row")
-    assemble(pieces, high_ref, low_ref, whole_ref, plan.chips, late_pieces(plan, late))
-    mats.append((high_ref, low_ref))
+    for ref, (chip, core) in zip(pieces, streams(plan.chips)[plan.chips - late :]):
+        depth = ref.shape[2]
+        place = pl.ds(pl.multiple_of(2 * depth * chip, 2 * depth), 2 * depth)
+        sides = [ref[jnp.where(core == 0, half, 1 - half)] for half in range(2)]
+        both = jnp.concatenate(sides, axis=1)
+        for rank in range(1, panels):
+            rows = plan.tri_of(rank)
+            flat = split(both[rows].reshape(rank * 2 * depth, nb))
+            step = dot3(flat, plan.mat(mats, "inv", rank), ABOVE).reshape(rank, 2 * depth, nb)
+            high_ref[rows, place, :], low_ref[rows, place, :] = split(step)
     totals = [total_ref[block * nb : (block + 1) * nb] for block in range(plan.wide)]
 
     def panel_out(local):
@@ -233,38 +252,33 @@
             else:
                 pl.when(local * plan.group_count + me < panels)(functools.partial(act, panel_out(local)))
 
-    def tri(rank, panel):
-        return plan.mat(mats, "tri", plan.tri.index((rank, panel)))
-
-    def inverse(panel):
-        return plan.mat(mats, "inv", panel)
-
-    answer = x_first[...]
-    rests = [None] + [wait_ref[panel - 1] for panel in range(1, panels)]
-    steps = [None] * 2 + [split(dot3(inverse(p), tri(p, p - 1), ABOVE)) for p in range(2, panels)]
+    def step(rank, panel):
+        at = plan.tri.index((rank, panel))
+        return high_ref[at], low_ref[at]
+
+    def take(panel):
+        for block in range(plan.wide):
+            mat = plan.mat(mats, "low", panel, block)
+            totals[block] = totals[block] - dot3(mat, solved[panel], ROWS)
+
+    rests = [start_ref[panel] for panel in range(panels)]
+    solved = []
     for panel in range(panels):
-        if panel == 1:
-            rest = split(rests[1] - dot3(tri(1, 0), solved, ROWS))
-            answer = dot3(inverse(1), rest, PLAIN)
-        elif panel > 1:
-            answer = dot3(inverse(panel), split(rests[panel]), PLAIN) - dot3(steps[panel], solved, PLAIN)
-        x_ref[panel] = answer
-        solved = split(answer)
-        for after in range(panel + 2, panels):
-            rests[after] = rests[after] - dot3(tri(after, panel), solved, ROWS)
+        x_ref[panel] = rests[panel]
+        solved.append(split(rests[panel]))
+        for after in range(panel + 1, panels):
+            rests[after] = rests[after] - dot3(step(after, panel), solved[panel], ROWS)
         done = (panel + 1) // plan.group_count
         if (panel + 1) % plan.group_count == 0 and done <= plan.sure:
             each_out(lambda copy: copy.start(), [done - 1])
-        if panel == panels - 1:
-            each_out(lambda copy: copy.start(), range(plan.sure, plan.held))
-        for block in range(plan.wide):
-            if panel > 0:
-                mat = plan.mat(mats, "low", panel, block)
-                totals[block] = totals[block] - dot3(mat, solved, ROWS)
-            if panel == panels - 1:
-                low_rows[block] = totals[block]
-                if plan.sure + block >= plan.held:
-                    rows_out(block).start()
+    each_out(lambda copy: copy.start(), range(plan.sure, plan.held))
+    for panel in range(1, panels - 1):
+        take(panel)
+    for block in range(plan.wide):
+        mat = plan.mat(mats, "low", panels - 1, block)
+        low_rows[block] = totals[block] - dot3(mat, solved[panels - 1], ROWS)
+        if plan.sure + block >= plan.held:
+            rows_out(block).start()
 
     each_out(lambda copy: copy.wait())
     for block in range(plan.wide):
@@ -325,38 +339,36 @@
     pairs = [[shape((len(blocks), nb, nb), bf16)] * 2 for blocks in plan.chunks]
     wholes = [whole_scratch(len(blocks), nb, depth) for blocks in plan.chunks]
 
-    def place(chunk, count):
-        return kernel_call(
-            bound(place_kernel, plan), pairs[chunk], [wholes[chunk]], pieces[chunk][:count]
-        )
-
-    inv_high, inv_low, x_first, waiting, total = kernel_call(
+    inv_high, inv_low, start, total = kernel_call(
         bound(prep_kernel, plan),
         [
             *pairs[0],
-            shape((nb, columns), f32),
-            shape((panels - 1, nb, columns), f32),
+            shape((panels, nb, columns), f32),
             shape((plan.wide * nb, columns), f32),
         ],
         [wholes[0]],
         (*pieces[0], right_side, *received),
         flops=6 * 3 * nb * nb * columns,
     )
-    below = place(1, chips)
-    if depth % 16 == 0:
-        placed, late = place(2, chips - 1), pieces[2][chips - 1 :]
-    else:
-        placed, late = [jnp.zeros(s.shape, s.dtype) for s in pairs[2]], pieces[2]
+    count = chips - 1 if depth % 16 == 0 else chips
+    early, late = pieces[2][:count], pieces[2][count:]
+    steps = kernel_call(
+        bound(triangle_kernel, plan, count),
+        pairs[2],
+        [pltpu.VMEM(s.shape, s.dtype) for s in pairs[2]] + [wholes[2]],
+        (*early, inv_high, inv_low),
+        flops=6 * 6 * nb * nb * nb,
+    )
+    below = kernel_call(bound(place_kernel, plan), pairs[1], [wholes[1]], pieces[1])
     out, _, _ = kernel_call(
         bound(final_kernel, plan, len(late)),
         [shape(right_side.shape, f32), *pairs[2]],
         [
             pltpu.VMEM((panels, nb, columns), f32),
             pltpu.VMEM((plan.wide, nb, columns), f32),
-            wholes[2],
             pltpu.SemaphoreType.DMA((rows // nb,)),
         ],
-        (*late, *placed, inv_high, inv_low, *below, x_first, waiting, total),
+        (*late, *steps, inv_high, inv_low, *below, start, total),
         flops=6 * 15 * nb * nb * columns,
         out_hbm=1,
         aliases={len(late): 1, len(late) + 1: 2},

time: 45.3 us -> 52.7 us (1.16)
  waiting for transfers between devices: 11.6 us -> 19.4 us
  starting transfers between devices: 26.1 us -> 25.5 us
    ppermute x1, waiting for transfers between devices: 2.23 us -> 10.1 us  [per_device(): tri = [own] + [lax.ppermute(own, 'row', pairs) for pairs in shifts]]
    ppermute x1, starting transfers between devices: 0.08 us -> 2.58 us  [per_device(): received = [lax.ppermute(above, 'row', pairs) for pairs in shifts]]
    ppermute x1, starting transfers between devices: 2.58 us -> 0.36 us  [per_device(): tri = [own] + [lax.ppermute(own, 'row', pairs) for pairs in shifts]]
    ppermute x1, waiting for transfers between devices: 0.01 us -> 1.29 us  [per_device(): half_other = lax.ppermute(half, 'col', swap)]
    ppermute x12, waiting for transfers between devices: 8.45 us -> 7.27 us  [ring(): moving = lax.ppermute(moving, 'col', nearest)]
  transfers between devices with their start and end apart: 26 -> 26, of which waited for: 12 -> 11; matrix products, arithmetic and copies ran while one was open for 2% -> 2% of each run, Pallas kernels for 4% -> 5%
where the time goes in v7:
time: 52.7 us; the launch traced here: 52.5 us
  starting transfers between devices  25.5 us (48%)
  waiting for transfers between devices  19.4 us (37%)
  Pallas kernels  6.41 us (12%)
  local copies, waits for them, and re-layouts  1.08 us (2%)
    ppermute x12, starting transfers between devices, ring(): moving = lax.ppermute(moving, 'col', nearest)  20.6 us
    ppermute x1, waiting for transfers between devices, per_device(): tri = [own] + [lax.ppermute(own, 'row', pairs) for pairs in shifts]  10.1 us
    ppermute x12, waiting for transfers between devices, ring(): moving = lax.ppermute(moving, 'col', nearest)  7.27 us
    pallas_call x9, Pallas kernels, kernel_call(): pl.pallas_call(body, out_shape=out_shapes, in_specs=[hbm] * in_hbm + [nea...  6.41 us
    ppermute x1, starting transfers between devices, per_device(): received = [lax.ppermute(above, 'row', pairs) for pairs in shifts]  2.58 us
    ppermute x1, waiting for transfers between devices, per_device(): half_other = lax.ppermute(half, 'col', swap)  1.29 us
    ppermute x9, starting transfers between devices, ring(): pieces.append(lax.ppermute(moving, 'col', swap))  1.1 us
    slice x1, local copies, waits for them, and re-layouts, per_device(): above = right_side[:plan.held * nb]  1.08 us
  transfers between devices with their start and end apart: 26, of which 11 were waited for; matrix products, arithmetic and copies ran while one was open for 2% of the time, Pallas kernels for 5%

profile of v7, /device:TPU:0, one launch (start us, length us, event | category | flops | bytes accessed | tf_op | source)
XLA Modules:
  0.0 52.5 jit_solution(7350899857547078268)
XLA Ops:
  0.0 1.1 %shard_map.37 = (f32[4,16,1024]{2,1,0:T(8,128)S(1)}, f32[4,16,256]{2,1,0:T(8,128)S(1)}, f32[3,16,512]{2,1,0:T(8,128)S(1)}) custom-call(f32[4,16,1024]{2,1,0:T(8,128)} %factor_hbm.1, f32[4,16,256]{2,1,0:T(8,128)} %inv_hbm.1), custom_call_target="tpu_custom_call" | custom-call | bytes 4194304 | tf_op jit(solution)/shard_map/pallas_call | solution.py:42
  1.6 1.1 %slice.3 = f32[512,256]{1,0:T(8,128)S(1)} slice(f32[1024,256]{1,0:T(8,128)} %refs_8_.1), slice={[0:512], [0:256]} | slice | bytes 1048576 | tf_op jit(solution)/shard_map/slice | solution.py:323
  2.7 2.6 %collective-permute-start.18 = (f32[512,256]{1,0:T(8,128)S(1)}, f32[512,256]{1,0:T(8,128)S(1)}, u32[]{:S(2)}, u32[]{:S(2)}) collective-permute-start(f32[512,256]{1,0:T(8,128)S(1)} %slice.3), channel_id=1, source_target_pairs={{16,0},{0,16},{17,1},{1,17},{18,2},{2,18},{19,3},{3,19},{20,4},{4,... | collective-permute-start | bytes 1572872 | tf_op jit(solution)/shard_map/ppermute | solution.py:324
  6.6 1.6 %collective-permute-start.11 = (f32[2,6,16,256]{3,2,1,0:T(8,128)S(1)}, f32[2,6,16,256]{3,2,1,0:T(8,128)S(1)}, u32[]{:S(2)}, u32[]{:S(2)}) collective-permute-start(f32[2,6,16,256]{3,2,1,0:T(8,128)S(1)} %shard_map.40.refs_0_), channel_id=1, source_target_pairs={{0,4},{1,3},{4,8},{5,1},{8,12},{9,5},{12,14},{13,9},{14,10},{15,13... | collective-permute-start | bytes 589832 | tf_op jit(solution)/shard_map/ppermute | solution.py:67
  8.2 1.6 %collective-permute-start.19 = (f32[2,6,16,256]{3,2,1,0:T(8,128)S(1)}, f32[2,6,16,256]{3,2,1,0:T(8,128)S(1)}, u32[]{:S(2)}, u32[]{:S(2)}) collective-permute-start(f32[2,6,16,256]{3,2,1,0:T(8,128)S(1)} %shard_map.43.refs_0_), channel_id=1, source_target_pairs={{0,4},{1,3},{4,8},{5,1},{8,12},{9,5},{12,14},{13,9},{14,10},{15,13... | collective-permute-start | bytes 589832 | tf_op jit(solution)/shard_map/ppermute | solution.py:67
  9.8 10.1 %collective-permute-done.refs_1_ = f32[3,16,512]{2,1,0:T(8,128)S(1)} collective-permute-done((f32[3,16,512]{2,1,0:T(8,128)S(1)}, f32[3,16,512]{2,1,0:T(8,128)S(1)}, u32[]{:S(2)}, u32[]{:S(2)}) %collective-permute-start) | collective-permute-done | bytes 98336 | tf_op jit(solution)/shard_map/ppermute | solution.py:322
  20.1 1.3 %collective-permute-done.1.refs_2_ = f32[6,16,256]{2,1,0:T(8,128)S(1)} collective-permute-done((f32[6,16,256]{2,1,0:T(8,128)S(1)}, f32[6,16,256]{2,1,0:T(8,128)S(1)}, u32[]{:S(2)}, u32[]{:S(2)}) %collective-permute-start.1) | collective-permute-done | bytes 98336 | tf_op jit(solution)/shard_map/ppermute | solution.py:326
  21.4 1.8 %collective-permute-start.3 = (f32[2,6,16,256]{3,2,1,0:T(8,128)S(1)}, f32[2,6,16,256]{3,2,1,0:T(8,128)S(1)}, u32[]{:S(2)}, u32[]{:S(2)}) collective-permute-start(f32[2,6,16,256]{3,2,1,0:T(8,128)S(1)} %shard_map.39.refs_0_), channel_id=1, source_target_pairs={{0,4},{1,3},{4,8},{5,1},{8,12},{9,5},{12,14},{13,9},{14,10},{15,13... | collective-permute-start | bytes 589832 | tf_op jit(solution)/shard_map/ppermute | solution.py:67
  23.3 1.6 %collective-permute-start.13 = (f32[2,6,16,256]{3,2,1,0:T(8,128)S(1)}, f32[2,6,16,256]{3,2,1,0:T(8,128)S(1)}, u32[]{:S(2)}, u32[]{:S(2)}) collective-permute-start(f32[2,6,16,256]{3,2,1,0:T(8,128)S(1)} %collective-permute-done.11.refs_1_), channel_id=1, source_target_pairs={{0,4},{1,3},{4,8},{5,1},{8,12},{9,5},{12,14},{13,9},{14,10},{15,13... | collective-permute-start | bytes 589832 | tf_op jit(solution)/shard_map/ppermute | solution.py:67
  24.8 1.6 %collective-permute-start.21 = (f32[2,6,16,256]{3,2,1,0:T(8,128)S(1)}, f32[2,6,16,256]{3,2,1,0:T(8,128)S(1)}, u32[]{:S(2)}, u32[]{:S(2)}) collective-permute-start(f32[2,6,16,256]{3,2,1,0:T(8,128)S(1)} %collective-permute-done.19.refs_1_), channel_id=1, source_target_pairs={{0,4},{1,3},{4,8},{5,1},{8,12},{9,5},{12,14},{13,9},{14,10},{15,13... | collective-permute-start | bytes 589832 | tf_op jit(solution)/shard_map/ppermute | solution.py:67
  26.4 0.7 %collective-permute-done.3.refs_1_ = f32[2,6,16,256]{3,2,1,0:T(8,128)S(1)} collective-permute-done((f32[2,6,16,256]{3,2,1,0:T(8,128)S(1)}, f32[2,6,16,256]{3,2,1,0:T(8,128)S(1)}, u32[]{:S(2)}, u32[]{:S(2)}) %collective-permute-start.3) | collective-permute-done | bytes 196640 | tf_op jit(solution)/shard_map/ppermute | solution.py:67
  27.1 1.8 %collective-permute-start.4 = (f32[2,6,16,256]{3,2,1,0:T(8,128)S(1)}, f32[2,6,16,256]{3,2,1,0:T(8,128)S(1)}, u32[]{:S(2)}, u32[]{:S(2)}) collective-permute-start(f32[2,6,16,256]{3,2,1,0:T(8,128)S(1)} %collective-permute-done.3.refs_1_), channel_id=1, source_target_pairs={{0,4},{1,3},{4,8},{5,1},{8,12},{9,5},{12,14},{13,9},{14,10},{15,13... | collective-permute-start | bytes 589832 | tf_op jit(solution)/shard_map/ppermute | solution.py:67
  29.2 1.8 %collective-permute-start.15 = (f32[2,6,16,256]{3,2,1,0:T(8,128)S(1)}, f32[2,6,16,256]{3,2,1,0:T(8,128)S(1)}, u32[]{:S(2)}, u32[]{:S(2)}) collective-permute-start(f32[2,6,16,256]{3,2,1,0:T(8,128)S(1)} %collective-permute-done.13.refs_3_), channel_id=1, source_target_pairs={{0,4},{1,3},{4,8},{5,1},{8,12},{9,5},{12,14},{13,9},{14,10},{15,13... | collective-permute-start | bytes 589832 | tf_op jit(solution)/shard_map/ppermute | solution.py:67
  31.3 1.8 %collective-permute-start.23 = (f32[2,6,16,256]{3,2,1,0:T(8,128)S(1)}, f32[2,6,16,256]{3,2,1,0:T(8,128)S(1)}, u32[]{:S(2)}, u32[]{:S(2)}) collective-permute-start(f32[2,6,16,256]{3,2,1,0:T(8,128)S(1)} %collective-permute-done.21.refs_3_), channel_id=1, source_target_pairs={{0,4},{1,3},{4,8},{5,1},{8,12},{9,5},{12,14},{13,9},{14,10},{15,13... | collective-permute-start | bytes 589832 | tf_op jit(solution)/shard_map/ppermute | solution.py:67
  33.7 1.6 %collective-permute-start.5 = (f32[2,6,16,256]{3,2,1,0:T(8,128)S(1)}, f32[2,6,16,256]{3,2,1,0:T(8,128)S(1)}, u32[]{:S(2)}, u32[]{:S(2)}) collective-permute-start(f32[2,6,16,256]{3,2,1,0:T(8,128)S(1)} %collective-permute-done.4.refs_3_), channel_id=1, source_target_pairs={{0,4},{1,3},{4,8},{5,1},{8,12},{9,5},{12,14},{13,9},{14,10},{15,13... | collective-permute-start | bytes 589832 | tf_op jit(solution)/shard_map/ppermute | solution.py:67
  35.5 1.8 %collective-permute-start.17 = (f32[2,6,16,256]{3,2,1,0:T(8,128)S(1)}, f32[2,6,16,256]{3,2,1,0:T(8,128)S(1)}, u32[]{:S(2)}, u32[]{:S(2)}) collective-permute-start(f32[2,6,16,256]{3,2,1,0:T(8,128)S(1)} %collective-permute-done.15.refs_5_), channel_id=1, source_target_pairs={{0,4},{1,3},{4,8},{5,1},{8,12},{9,5},{12,14},{13,9},{14,10},{15,13... | collective-permute-start | bytes 589832 | tf_op jit(solution)/shard_map/ppermute | solution.py:67
  37.7 1.8 %collective-permute-start.25 = (f32[2,6,16,256]{3,2,1,0:T(8,128)S(1)}, f32[2,6,16,256]{3,2,1,0:T(8,128)S(1)}, u32[]{:S(2)}, u32[]{:S(2)}) collective-permute-start(f32[2,6,16,256]{3,2,1,0:T(8,128)S(1)} %collective-permute-done.23.refs_5_), channel_id=1, source_target_pairs={{0,4},{1,3},{4,8},{5,1},{8,12},{9,5},{12,14},{13,9},{14,10},{15,13... | collective-permute-start | bytes 589832 | tf_op jit(solution)/shard_map/ppermute | solution.py:67
  40.0 1.8 %collective-permute-done.17.refs_7_ = f32[2,6,16,256]{3,2,1,0:T(8,128)S(1)} collective-permute-done((f32[2,6,16,256]{3,2,1,0:T(8,128)S(1)}, f32[2,6,16,256]{3,2,1,0:T(8,128)S(1)}, u32[]{:S(2)}, u32[]{:S(2)}) %collective-permute-start.17) | collective-permute-done | bytes 196640 | tf_op jit(solution)/shard_map/ppermute | solution.py:67
  41.9 2.1 %collective-permute-done.25.refs_7_ = f32[2,6,16,256]{3,2,1,0:T(8,128)S(1)} collective-permute-done((f32[2,6,16,256]{3,2,1,0:T(8,128)S(1)}, f32[2,6,16,256]{3,2,1,0:T(8,128)S(1)}, u32[]{:S(2)}, u32[]{:S(2)}) %collective-permute-start.25) | collective-permute-done | bytes 196640 | tf_op jit(solution)/shard_map/ppermute | solution.py:67
  44.0 1.8 %collective-permute-start.6 = (f32[2,6,16,256]{3,2,1,0:T(8,128)S(1)}, f32[2,6,16,256]{3,2,1,0:T(8,128)S(1)}, u32[]{:S(2)}, u32[]{:S(2)}) collective-permute-start(f32[2,6,16,256]{3,2,1,0:T(8,128)S(1)} %collective-permute-done.5.refs_5_), channel_id=1, source_target_pairs={{0,4},{1,3},{4,8},{5,1},{8,12},{9,5},{12,14},{13,9},{14,10},{15,13... | collective-permute-start | bytes 589832 | tf_op jit(solution)/shard_map/ppermute | solution.py:67
  46.1 1.1 %shard_map.41 = (bf16[6,256,256]{2,1,0:T(8,128)(2,1)S(1)}, bf16[6,256,256]{2,1,0:T(8,128)(2,1)S(1)}, f32[4,256,256]{2,1,0:T(8,128)S(1)}, f32[512,256]{1,0:T(8,128)S(1)}) custom-call(f32[2,6,16,256]{3,2,1,0:T(8,128)S(1)} %shard_map.40.refs_0_, f32[2,6,16,256]{3,2,1,0:T(8,128)S(1)} %collective-permute-done.11.refs_1_, ...), custom_call_target="tpu_custom_call" | custom-call | flops 301989888 | bytes 4194304 | tf_op jit(solution)/shard_map/pallas_call | solution.py:42
  47.3 1.0 %shard_map.42 = (bf16[6,256,256]{2,1,0:T(8,128)(2,1)S(1)}, bf16[6,256,256]{2,1,0:T(8,128)(2,1)S(1)}) custom-call(f32[2,6,16,256]{3,2,1,0:T(8,128)S(1)} %shard_map.39.refs_0_, f32[2,6,16,256]{3,2,1,0:T(8,128)S(1)} %collective-permute-done.3.refs_1_, f32[2,6,16,256]{3,2,1,0:T(8,128)S(1)} %collective-permute-done.7.refs_2_, ...), custom_call_target="tpu_custom_call" | custom-call | flops 603979776 | bytes 4194304 | tf_op jit(solution)/shard_map/pallas_call | solution.py:42
  48.3 1.4 %collective-permute-done.6.refs_0_ = f32[2,6,16,256]{3,2,1,0:T(8,128)S(1)} collective-permute-done((f32[2,6,16,256]{3,2,1,0:T(8,128)S(1)}, f32[2,6,16,256]{3,2,1,0:T(8,128)S(1)}, u32[]{:S(2)}, u32[]{:S(2)}) %collective-permute-start.6) | collective-permute-done | bytes 196640 | tf_op jit(solution)/shard_map/ppermute | solution.py:67
  49.7 2.9 %shard_map.45 = (f32[1024,256]{1,0:T(8,128)}, bf16[6,256,256]{2,1,0:T(8,128)(2,1)S(1)}, bf16[6,256,256]{2,1,0:T(8,128)(2,1)S(1)}) custom-call(f32[2,6,16,256]{3,2,1,0:T(8,128)S(1)} %collective-permute-done.6.refs_0_, bf16[6,256,256]{2,1,0:T(8,128)(2,1)S(1)} %get-tuple-element.22.refs_1_, ...), custom_call_target="tpu_custom_call", output_to_operand_aliasing={{1}: (1, {}), {2}: (2, {})} | custom-call | flops 1509949440 | bytes 4194304 | tf_op jit(solution)/shard_map/pallas_call | solution.py:42
  (40 shorter events, 4.6 us)
Async XLA Ops:
  1.1 5.5 %collective-permute-start.2 = (f32[4,16,1024]{2,1,0:T(8,128)S(1)}, f32[4,16,1024]{2,1,0:T(8,128)S(1)}, u32[]{:S(2)}, u32[]{:S(2)}) collective-permute-start(f32[4,16,1024]{2,1,0:T(8,128)S(1)} %get-tuple-element.18.refs_1_), channel_id=1, source_target_pairs={{0,1},{1,0},{2,3},{3,2},{4,5},{5,4},{6,7},{7,6},{8,9},{9,8},{10,11... | collective-permute-start | bytes 786440 | tf_op jit(solution)/shard_map/ppermute | solution.py:321
  2.7 24.4 %collective-permute-start.18 = (f32[512,256]{1,0:T(8,128)S(1)}, f32[512,256]{1,0:T(8,128)S(1)}, u32[]{:S(2)}, u32[]{:S(2)}) collective-permute-start(f32[512,256]{1,0:T(8,128)S(1)} %slice.3), channel_id=1, source_target_pairs={{16,0},{0,16},{17,1},{1,17},{18,2},{2,18},{19,3},{3,19},{20,4},{4,... | collective-permute-start | bytes 1572872 | tf_op jit(solution)/shard_map/ppermute | solution.py:324
  5.5 14.5 %collective-permute-start = (f32[3,16,512]{2,1,0:T(8,128)S(1)}, f32[3,16,512]{2,1,0:T(8,128)S(1)}, u32[]{:S(2)}, u32[]{:S(2)}) collective-permute-start(f32[3,16,512]{2,1,0:T(8,128)S(1)} %get-tuple-element.17.refs_0_), channel_id=1, source_target_pairs={{16,0},{0,16},{17,1},{1,17},{18,2},{2,18},{19,3},{3,19},{20,4},{4,... | collective-permute-start | bytes 294920 | tf_op jit(solution)/shard_map/ppermute | solution.py:322
  6.6 16.7 %collective-permute-start.11 = (f32[2,6,16,256]{3,2,1,0:T(8,128)S(1)}, f32[2,6,16,256]{3,2,1,0:T(8,128)S(1)}, u32[]{:S(2)}, u32[]{:S(2)}) collective-permute-start(f32[2,6,16,256]{3,2,1,0:T(8,128)S(1)} %shard_map.40.refs_0_), channel_id=1, source_target_pairs={{0,4},{1,3},{4,8},{5,1},{8,12},{9,5},{12,14},{13,9},{14,10},{15,13... | collective-permute-start | bytes 589832 | tf_op jit(solution)/shard_map/ppermute | solution.py:67
  8.2 16.6 %collective-permute-start.19 = (f32[2,6,16,256]{3,2,1,0:T(8,128)S(1)}, f32[2,6,16,256]{3,2,1,0:T(8,128)S(1)}, u32[]{:S(2)}, u32[]{:S(2)}) collective-permute-start(f32[2,6,16,256]{3,2,1,0:T(8,128)S(1)} %shard_map.43.refs_0_), channel_id=1, source_target_pairs={{0,4},{1,3},{4,8},{5,1},{8,12},{9,5},{12,14},{13,9},{14,10},{15,13... | collective-permute-start | bytes 589832 | tf_op jit(solution)/shard_map/ppermute | solution.py:67
  21.4 5.7 %collective-permute-start.3 = (f32[2,6,16,256]{3,2,1,0:T(8,128)S(1)}, f32[2,6,16,256]{3,2,1,0:T(8,128)S(1)}, u32[]{:S(2)}, u32[]{:S(2)}) collective-permute-start(f32[2,6,16,256]{3,2,1,0:T(8,128)S(1)} %shard_map.39.refs_0_), channel_id=1, source_target_pairs={{0,4},{1,3},{4,8},{5,1},{8,12},{9,5},{12,14},{13,9},{14,10},{15,13... | collective-permute-start | bytes 589832 | tf_op jit(solution)/shard_map/ppermute | solution.py:67
  23.3 6.0 %collective-permute-start.13 = (f32[2,6,16,256]{3,2,1,0:T(8,128)S(1)}, f32[2,6,16,256]{3,2,1,0:T(8,128)S(1)}, u32[]{:S(2)}, u32[]{:S(2)}) collective-permute-start(f32[2,6,16,256]{3,2,1,0:T(8,128)S(1)} %collective-permute-done.11.refs_1_), channel_id=1, source_target_pairs={{0,4},{1,3},{4,8},{5,1},{8,12},{9,5},{12,14},{13,9},{14,10},{15,13... | collective-permute-start | bytes 589832 | tf_op jit(solution)/shard_map/ppermute | solution.py:67
  24.8 6.5 %collective-permute-start.21 = (f32[2,6,16,256]{3,2,1,0:T(8,128)S(1)}, f32[2,6,16,256]{3,2,1,0:T(8,128)S(1)}, u32[]{:S(2)}, u32[]{:S(2)}) collective-permute-start(f32[2,6,16,256]{3,2,1,0:T(8,128)S(1)} %collective-permute-done.19.refs_1_), channel_id=1, source_target_pairs={{0,4},{1,3},{4,8},{5,1},{8,12},{9,5},{12,14},{13,9},{14,10},{15,13... | collective-permute-start | bytes 589832 | tf_op jit(solution)/shard_map/ppermute | solution.py:67
  26.4 6.7 %collective-permute-start.12 = (f32[2,6,16,256]{3,2,1,0:T(8,128)S(1)}, f32[2,6,16,256]{3,2,1,0:T(8,128)S(1)}, u32[]{:S(2)}, u32[]{:S(2)}) collective-permute-start(f32[2,6,16,256]{3,2,1,0:T(8,128)S(1)} %collective-permute-done.11.refs_1_), channel_id=1, source_target_pairs={{0,1},{1,0},{2,3},{3,2},{4,5},{5,4},{6,7},{7,6},{8,9},{9,8},{10,11... | collective-permute-start | bytes 589832 | tf_op jit(solution)/shard_map/ppermute | solution.py:70
  27.1 6.0 %collective-permute-start.20 = (f32[2,6,16,256]{3,2,1,0:T(8,128)S(1)}, f32[2,6,16,256]{3,2,1,0:T(8,128)S(1)}, u32[]{:S(2)}, u32[]{:S(2)}) collective-permute-start(f32[2,6,16,256]{3,2,1,0:T(8,128)S(1)} %collective-permute-done.19.refs_1_), channel_id=1, source_target_pairs={{0,1},{1,0},{2,3},{3,2},{4,5},{5,4},{6,7},{7,6},{8,9},{9,8},{10,11... | collective-permute-start | bytes 589832 | tf_op jit(solution)/shard_map/ppermute | solution.py:70
  27.1 6.5 %collective-permute-start.4 = (f32[2,6,16,256]{3,2,1,0:T(8,128)S(1)}, f32[2,6,16,256]{3,2,1,0:T(8,128)S(1)}, u32[]{:S(2)}, u32[]{:S(2)}) collective-permute-start(f32[2,6,16,256]{3,2,1,0:T(8,128)S(1)} %collective-permute-done.3.refs_1_), channel_id=1, source_target_pairs={{0,4},{1,3},{4,8},{5,1},{8,12},{9,5},{12,14},{13,9},{14,10},{15,13... | collective-permute-start | bytes 589832 | tf_op jit(solution)/shard_map/ppermute | solution.py:67
  29.2 6.3 %collective-permute-start.15 = (f32[2,6,16,256]{3,2,1,0:T(8,128)S(1)}, f32[2,6,16,256]{3,2,1,0:T(8,128)S(1)}, u32[]{:S(2)}, u32[]{:S(2)}) collective-permute-start(f32[2,6,16,256]{3,2,1,0:T(8,128)S(1)} %collective-permute-done.13.refs_3_), channel_id=1, source_target_pairs={{0,4},{1,3},{4,8},{5,1},{8,12},{9,5},{12,14},{13,9},{14,10},{15,13... | collective-permute-start | bytes 589832 | tf_op jit(solution)/shard_map/ppermute | solution.py:67
  31.3 6.3 %collective-permute-start.23 = (f32[2,6,16,256]{3,2,1,0:T(8,128)S(1)}, f32[2,6,16,256]{3,2,1,0:T(8,128)S(1)}, u32[]{:S(2)}, u32[]{:S(2)}) collective-permute-start(f32[2,6,16,256]{3,2,1,0:T(8,128)S(1)} %collective-permute-done.21.refs_3_), channel_id=1, source_target_pairs={{0,4},{1,3},{4,8},{5,1},{8,12},{9,5},{12,14},{13,9},{14,10},{15,13... | collective-permute-start | bytes 589832 | tf_op jit(solution)/shard_map/ppermute | solution.py:67
  33.1 6.3 %collective-permute-start.14 = (f32[2,6,16,256]{3,2,1,0:T(8,128)S(1)}, f32[2,6,16,256]{3,2,1,0:T(8,128)S(1)}, u32[]{:S(2)}, u32[]{:S(2)}) collective-permute-start(f32[2,6,16,256]{3,2,1,0:T(8,128)S(1)} %collective-permute-done.13.refs_3_), channel_id=1, source_target_pairs={{0,1},{1,0},{2,3},{3,2},{4,5},{5,4},{6,7},{7,6},{8,9},{9,8},{10,11... | collective-permute-start | bytes 589832 | tf_op jit(solution)/shard_map/ppermute | solution.py:70
  33.1 6.3 %collective-permute-start.22 = (f32[2,6,16,256]{3,2,1,0:T(8,128)S(1)}, f32[2,6,16,256]{3,2,1,0:T(8,128)S(1)}, u32[]{:S(2)}, u32[]{:S(2)}) collective-permute-start(f32[2,6,16,256]{3,2,1,0:T(8,128)S(1)} %collective-permute-done.21.refs_3_), channel_id=1, source_target_pairs={{0,1},{1,0},{2,3},{3,2},{4,5},{5,4},{6,7},{7,6},{8,9},{9,8},{10,11... | collective-permute-start | bytes 589832 | tf_op jit(solution)/shard_map/ppermute | solution.py:70
  33.7 6.3 %collective-permute-start.5 = (f32[2,6,16,256]{3,2,1,0:T(8,128)S(1)}, f32[2,6,16,256]{3,2,1,0:T(8,128)S(1)}, u32[]{:S(2)}, u32[]{:S(2)}) collective-permute-start(f32[2,6,16,256]{3,2,1,0:T(8,128)S(1)} %collective-permute-done.4.refs_3_), channel_id=1, source_target_pairs={{0,4},{1,3},{4,8},{5,1},{8,12},{9,5},{12,14},{13,9},{14,10},{15,13... | collective-permute-start | bytes 589832 | tf_op jit(solution)/shard_map/ppermute | solution.py:67
  35.5 6.3 %collective-permute-start.17 = (f32[2,6,16,256]{3,2,1,0:T(8,128)S(1)}, f32[2,6,16,256]{3,2,1,0:T(8,128)S(1)}, u32[]{:S(2)}, u32[]{:S(2)}) collective-permute-start(f32[2,6,16,256]{3,2,1,0:T(8,128)S(1)} %collective-permute-done.15.refs_5_), channel_id=1, source_target_pairs={{0,4},{1,3},{4,8},{5,1},{8,12},{9,5},{12,14},{13,9},{14,10},{15,13... | collective-permute-start | bytes 589832 | tf_op jit(solution)/shard_map/ppermute | solution.py:67
  37.7 6.3 %collective-permute-start.25 = (f32[2,6,16,256]{3,2,1,0:T(8,128)S(1)}, f32[2,6,16,256]{3,2,1,0:T(8,128)S(1)}, u32[]{:S(2)}, u32[]{:S(2)}) collective-permute-start(f32[2,6,16,256]{3,2,1,0:T(8,128)S(1)} %collective-permute-done.23.refs_5_), channel_id=1, source_target_pairs={{0,4},{1,3},{4,8},{5,1},{8,12},{9,5},{12,14},{13,9},{14,10},{15,13... | collective-permute-start | bytes 589832 | tf_op jit(solution)/shard_map/ppermute | solution.py:67
  39.5 4.5 %collective-permute-start.24 = (f32[2,6,16,256]{3,2,1,0:T(8,128)S(1)}, f32[2,6,16,256]{3,2,1,0:T(8,128)S(1)}, u32[]{:S(2)}, u32[]{:S(2)}) collective-permute-start(f32[2,6,16,256]{3,2,1,0:T(8,128)S(1)} %collective-permute-done.23.refs_5_), channel_id=1, source_target_pairs={{0,1},{1,0},{2,3},{3,2},{4,5},{5,4},{6,7},{7,6},{8,9},{9,8},{10,11... | collective-permute-start | bytes 589832 | tf_op jit(solution)/shard_map/ppermute | solution.py:70
  39.5 6.6 %collective-permute-start.16 = (f32[2,6,16,256]{3,2,1,0:T(8,128)S(1)}, f32[2,6,16,256]{3,2,1,0:T(8,128)S(1)}, u32[]{:S(2)}, u32[]{:S(2)}) collective-permute-start(f32[2,6,16,256]{3,2,1,0:T(8,128)S(1)} %collective-permute-done.15.refs_5_), channel_id=1, source_target_pairs={{0,1},{1,0},{2,3},{3,2},{4,5},{5,4},{6,7},{7,6},{8,9},{9,8},{10,11... | collective-permute-start | bytes 589832 | tf_op jit(solution)/shard_map/ppermute | solution.py:70
  40.0 7.3 %collective-permute-start.7 = (f32[2,6,16,256]{3,2,1,0:T(8,128)S(1)}, f32[2,6,16,256]{3,2,1,0:T(8,128)S(1)}, u32[]{:S(2)}, u32[]{:S(2)}) collective-permute-start(f32[2,6,16,256]{3,2,1,0:T(8,128)S(1)} %collective-permute-done.3.refs_1_), channel_id=1, source_target_pairs={{0,1},{1,0},{2,3},{3,2},{4,5},{5,4},{6,7},{7,6},{8,9},{9,8},{10,11... | collective-permute-start | bytes 589832 | tf_op jit(solution)/shard_map/ppermute | solution.py:70
  41.9 5.4 %collective-permute-start.8 = (f32[2,6,16,256]{3,2,1,0:T(8,128)S(1)}, f32[2,6,16,256]{3,2,1,0:T(8,128)S(1)}, u32[]{:S(2)}, u32[]{:S(2)}) collective-permute-start(f32[2,6,16,256]{3,2,1,0:T(8,128)S(1)} %collective-permute-done.4.refs_3_), channel_id=1, source_target_pairs={{0,1},{1,0},{2,3},{3,2},{4,5},{5,4},{6,7},{7,6},{8,9},{9,8},{10,11... | collective-permute-start | bytes 589832 | tf_op jit(solution)/shard_map/ppermute | solution.py:70
  44.0 3.3 %collective-permute-start.9 = (f32[2,6,16,256]{3,2,1,0:T(8,128)S(1)}, f32[2,6,16,256]{3,2,1,0:T(8,128)S(1)}, u32[]{:S(2)}, u32[]{:S(2)}) collective-permute-start(f32[2,6,16,256]{3,2,1,0:T(8,128)S(1)} %collective-permute-done.5.refs_5_), channel_id=1, source_target_pairs={{0,1},{1,0},{2,3},{3,2},{4,5},{5,4},{6,7},{7,6},{8,9},{9,8},{10,11... | collective-permute-start | bytes 589832 | tf_op jit(solution)/shard_map/ppermute | solution.py:70
  44.0 5.7 %collective-permute-start.6 = (f32[2,6,16,256]{3,2,1,0:T(8,128)S(1)}, f32[2,6,16,256]{3,2,1,0:T(8,128)S(1)}, u32[]{:S(2)}, u32[]{:S(2)}) collective-permute-start(f32[2,6,16,256]{3,2,1,0:T(8,128)S(1)} %collective-permute-done.5.refs_5_), channel_id=1, source_target_pairs={{0,4},{1,3},{4,8},{5,1},{8,12},{9,5},{12,14},{13,9},{14,10},{15,13... | collective-permute-start | bytes 589832 | tf_op jit(solution)/shard_map/ppermute | solution.py:67
  (3 other events, 28.7 us)

commit v8 on v7

--- a/solution.py
+++ b/solution.py
@@ -53,7 +53,7 @@
     )(*operands)
 
 
-def ring(first, chips):
+def ring(first, chips, halves=False):
     steps = chips // 2
     nearest = []
     for place in range(chips):
@@ -64,9 +64,10 @@
     moving = first
     pieces = [first]
     for step in range(1, steps + 1):
-        moving = lax.ppermute(moving, "col", nearest)
+        last = step == steps
+        moving = lax.ppermute(moving[0] if last and halves else moving, "col", nearest)
         pieces.append(moving)
-        if step < steps:
+        if not last or halves:
             pieces.append(lax.ppermute(moving, "col", swap))
     return pieces
 
@@ -78,8 +79,7 @@
     for step in range(1, chips // 2 + 1):
         turn = step * (1 - 2 * core)
         found.append((ring_chip((here - turn + chips) % chips, chips), core))
-        if step < chips // 2:
-            found.append((ring_chip((here + turn + chips) % chips, chips), 1 - core))
+        found.append((ring_chip((here + turn + chips) % chips, chips), 1 - core))
     return found
 
 
@@ -94,7 +94,9 @@
             whole_ref[:, rows, :] = value
 
     for ref, (chip, core) in zip(piece_refs, streams(chips)[chosen]):
-        if depth % 16 == 0:
+        if len(ref.shape) == 3:
+            put((2 * chip + core) * depth, ref[...])
+        elif depth % 16 == 0:
             for half in range(2):
                 put((2 * chip + half) * depth, ref[jnp.where(core == 0, half, 1 - half)])
         else:
@@ -116,9 +118,10 @@
         self.sure = panels // group_count
         self.wide = rows // nb - self.sure
         self.tri = [(rank, panel) for rank in range(1, panels) for panel in range(rank)]
-        self.deep = max(
-            min(rank, panels - 1) for rank in range((self.held - 1) * group_count, self.held * group_count)
-        )
+        self.deep = [
+            min(local * group_count + group_count, panels) - 1 for local in range(self.held)
+        ]
+        self.sent = [(local, panel) for local in range(self.held) for panel in range(self.deep[local])]
         low = [("low", panel, block) for panel in range(panels) for block in range(self.wide)]
         self.chunks = [
             [("inv", panel) for panel in range(panels)] + low[: self.wide],
@@ -148,13 +151,15 @@
         return self.chosen(owner, [right_ref[rows]] + [r[rows] for r in received])
 
 
-def load_kernel(factor_hbm, inv_hbm, factor_ref, inv_ref, own_ref, sems):
-    deep, _, part = own_ref.shape
+def load_kernel(plan, factor_hbm, inv_hbm, factor_ref, inv_ref, own_ref, sems):
     copies = [
-        pltpu.make_async_copy(factor_hbm.at[:deep, :, :part], own_ref, sems.at[0]),
-        pltpu.make_async_copy(factor_hbm, factor_ref, sems.at[1]),
-        pltpu.make_async_copy(inv_hbm, inv_ref, sems.at[2]),
+        pltpu.make_async_copy(factor_hbm, factor_ref, sems.at[0]),
+        pltpu.make_async_copy(inv_hbm, inv_ref, sems.at[1]),
     ]
+    for local, deep in enumerate(plan.deep):
+        source = factor_hbm.at[:deep, :, local * plan.nb : (local + 1) * plan.nb]
+        target = own_ref.at[pl.ds(plan.sent.index((local, 0)), deep)]
+        copies.append(pltpu.make_async_copy(source, target, sems.at[2 + local]))
     for copy in copies:
         copy.start()
     for copy in copies:
@@ -178,8 +183,8 @@
     *sources, out_ref = refs
     for at, (rank, panel) in enumerate(plan.tri):
         local, owner = divmod(rank, plan.group_count)
-        part = slice(local * plan.nb, (local + 1) * plan.nb)
-        out_ref[at] = plan.chosen(owner, [source[panel, :, part] for source in sources])
+        block = plan.sent.index((local, panel))
+        out_ref[at] = plan.chosen(owner, [source[block] for source in sources])
 
 
 def prep_kernel(plan, *refs):
@@ -223,7 +228,7 @@
     out_hbm, high_ref, low_ref, x_ref, low_rows, sems = refs[-6:]
     panels, nb = plan.panels, plan.nb
     me = lax.axis_index("row")
-    for ref, (chip, core) in zip(pieces, streams(plan.chips)[plan.chips - late :]):
+    for ref, (chip, core) in zip(pieces, streams(plan.chips)[plan.chips - late : plan.chips]):
         depth = ref.shape[2]
         place = pl.ds(pl.multiple_of(2 * depth * chip, 2 * depth), 2 * depth)
         sides = [ref[jnp.where(core == 0, half, 1 - half)] for half in range(2)]
@@ -307,13 +312,13 @@
     bound = functools.partial
 
     factor, inv, own = kernel_call(
-        load_kernel,
+        bound(load_kernel, plan),
         [
             shape(factor_panels.shape, f32),
             shape(inverses.shape, f32),
-            shape((plan.deep, depth, plan.held * nb), f32),
+            shape((len(plan.sent), depth, nb), f32),
         ],
-        [pltpu.SemaphoreType.DMA((3,))],
+        [pltpu.SemaphoreType.DMA((2 + plan.held,))],
         [pltpu.with_memory_space_constraint(a, pltpu.HBM) for a in (factor_panels, inverses)],
         in_hbm=2,
     )
@@ -334,7 +339,7 @@
             [],
             (heads[0], factor, heads[1], factor_other),
         )
-        pieces.append(ring(packed, chips))
+        pieces.append(ring(packed, chips, halves=chunk == 1 and depth % 16 == 0))
 
     pairs = [[shape((len(blocks), nb, nb), bf16)] * 2 for blocks in plan.chunks]
     wholes = [whole_scratch(len(blocks), nb, depth) for blocks in plan.chunks]

time: 52.7 us -> 51.4 us (0.975)
  waiting for transfers between devices: 19.4 us -> 17.8 us
    ppermute x1, waiting for transfers between devices: 10.1 us -> 8.92 us  [per_device(): tri = [own] + [lax.ppermute(own, 'row', pairs) for pairs in shifts]]
    ppermute x12, waiting for transfers between devices: 7.27 us -> 6.51 us  [ring(): lax.ppermute(moving[0] if last and halves else moving, 'col', nearest)]
    ppermute x9 -> x10, starting transfers between devices: 1.1 us -> 1.24 us  [ring(): pieces.append(lax.ppermute(moving, 'col', swap))]
  transfers between devices with their start and end apart: 26 -> 27, of which waited for: 11 -> 12; matrix products, arithmetic and copies ran while one was open for 2% -> 2% of each run, Pallas kernels for 5% -> 5%
where the time goes in v8:
time: 51.4 us; the launch traced here: 51.2 us
  starting transfers between devices  25.9 us (50%)
  waiting for transfers between devices  17.8 us (35%)
  Pallas kernels  6.33 us (12%)
  local copies, waits for them, and re-layouts  1.09 us (2%)
    ppermute x12, starting transfers between devices, ring(): lax.ppermute(moving[0] if last and halves else moving, 'col', nearest)  20.7 us
    ppermute x1, waiting for transfers between devices, per_device(): tri = [own] + [lax.ppermute(own, 'row', pairs) for pairs in shifts]  8.92 us
    ppermute x12, waiting for transfers between devices, ring(): lax.ppermute(moving[0] if last and halves else moving, 'col', nearest)  6.51 us
    pallas_call x9, Pallas kernels, kernel_call(): pl.pallas_call(body, out_shape=out_shapes, in_specs=[hbm] * in_hbm + [nea...  6.33 us
    ppermute x1, starting transfers between devices, per_device(): received = [lax.ppermute(above, 'row', pairs) for pairs in shifts]  2.58 us
    ppermute x1, waiting for transfers between devices, per_device(): half_other = lax.ppermute(half, 'col', swap)  1.29 us
    ppermute x10, starting transfers between devices, ring(): pieces.append(lax.ppermute(moving, 'col', swap))  1.24 us
    slice x1, local copies, waits for them, and re-layouts, per_device(): above = right_side[:plan.held * nb]  1.08 us
  transfers between devices with their start and end apart: 27, of which 12 were waited for; matrix products, arithmetic and copies ran while one was open for 2% of the time, Pallas kernels for 5%

profile of v8, /device:TPU:0, one launch (start us, length us, event | category | flops | bytes accessed | tf_op | source)
XLA Modules:
  0.0 51.2 jit_solution(6920157277572368490)
XLA Ops:
  0.0 1.0 %shard_map.37 = (f32[4,16,1024]{2,1,0:T(8,128)S(1)}, f32[4,16,256]{2,1,0:T(8,128)S(1)}, f32[4,16,256]{2,1,0:T(8,128)S(1)}) custom-call(f32[4,16,1024]{2,1,0:T(8,128)} %factor_hbm.1, f32[4,16,256]{2,1,0:T(8,128)} %inv_hbm.1), custom_call_target="tpu_custom_call" | custom-call | bytes 4194304 | tf_op jit(solution)/shard_map/pallas_call | solution.py:42
  1.6 1.1 %slice.6 = f32[512,256]{1,0:T(8,128)S(1)} slice(f32[1024,256]{1,0:T(8,128)} %refs_8_.1), slice={[0:512], [0:256]} | slice | bytes 1048576 | tf_op jit(solution)/shard_map/slice | solution.py:328
  2.6 2.6 %collective-permute-start.18 = (f32[512,256]{1,0:T(8,128)S(1)}, f32[512,256]{1,0:T(8,128)S(1)}, u32[]{:S(2)}, u32[]{:S(2)}) collective-permute-start(f32[512,256]{1,0:T(8,128)S(1)} %slice.6), channel_id=1, source_target_pairs={{16,0},{0,16},{17,1},{1,17},{18,2},{2,18},{19,3},{3,19},{20,4},{4,... | collective-permute-start | bytes 1572872 | tf_op jit(solution)/shard_map/ppermute | solution.py:329
  5.4 1.0 %collective-permute-done.10.refs_2_ = f32[4,16,256]{2,1,0:T(8,128)S(1)} collective-permute-done((f32[4,16,256]{2,1,0:T(8,128)S(1)}, f32[4,16,256]{2,1,0:T(8,128)S(1)}, u32[]{:S(2)}, u32[]{:S(2)}) %collective-permute-start.10) | collective-permute-done | bytes 65568 | tf_op jit(solution)/shard_map/ppermute | solution.py:325
  6.5 1.6 %collective-permute-start.11 = (f32[2,6,16,256]{3,2,1,0:T(8,128)S(1)}, f32[2,6,16,256]{3,2,1,0:T(8,128)S(1)}, u32[]{:S(2)}, u32[]{:S(2)}) collective-permute-start(f32[2,6,16,256]{3,2,1,0:T(8,128)S(1)} %shard_map.40.refs_0_), channel_id=1, source_target_pairs={{0,4},{1,3},{4,8},{5,1},{8,12},{9,5},{12,14},{13,9},{14,10},{15,13... | collective-permute-start | bytes 589832 | tf_op jit(solution)/shard_map/ppermute | solution.py:68
  8.2 1.6 %collective-permute-start.19 = (f32[2,6,16,256]{3,2,1,0:T(8,128)S(1)}, f32[2,6,16,256]{3,2,1,0:T(8,128)S(1)}, u32[]{:S(2)}, u32[]{:S(2)}) collective-permute-start(f32[2,6,16,256]{3,2,1,0:T(8,128)S(1)} %shard_map.43.refs_0_), channel_id=1, source_target_pairs={{0,4},{1,3},{4,8},{5,1},{8,12},{9,5},{12,14},{13,9},{14,10},{15,13... | collective-permute-start | bytes 589832 | tf_op jit(solution)/shard_map/ppermute | solution.py:68
  10.3 8.9 %collective-permute-done.refs_1_ = f32[4,16,256]{2,1,0:T(8,128)S(1)} collective-permute-done((f32[4,16,256]{2,1,0:T(8,128)S(1)}, f32[4,16,256]{2,1,0:T(8,128)S(1)}, u32[]{:S(2)}, u32[]{:S(2)}) %collective-permute-start) | collective-permute-done | bytes 65568 | tf_op jit(solution)/shard_map/ppermute | solution.py:327
  19.3 1.3 %collective-permute-done.1.refs_2_ = f32[6,16,256]{2,1,0:T(8,128)S(1)} collective-permute-done((f32[6,16,256]{2,1,0:T(8,128)S(1)}, f32[6,16,256]{2,1,0:T(8,128)S(1)}, u32[]{:S(2)}, u32[]{:S(2)}) %collective-permute-start.1) | collective-permute-done | bytes 98336 | tf_op jit(solution)/shard_map/ppermute | solution.py:331
  20.6 1.8 %collective-permute-start.3 = (f32[2,6,16,256]{3,2,1,0:T(8,128)S(1)}, f32[2,6,16,256]{3,2,1,0:T(8,128)S(1)}, u32[]{:S(2)}, u32[]{:S(2)}) collective-permute-start(f32[2,6,16,256]{3,2,1,0:T(8,128)S(1)} %shard_map.39.refs_0_), channel_id=1, source_target_pairs={{0,4},{1,3},{4,8},{5,1},{8,12},{9,5},{12,14},{13,9},{14,10},{15,13... | collective-permute-start | bytes 589832 | tf_op jit(solution)/shard_map/ppermute | solution.py:68
  22.5 1.6 %collective-permute-start.13 = (f32[2,6,16,256]{3,2,1,0:T(8,128)S(1)}, f32[2,6,16,256]{3,2,1,0:T(8,128)S(1)}, u32[]{:S(2)}, u32[]{:S(2)}) collective-permute-start(f32[2,6,16,256]{3,2,1,0:T(8,128)S(1)} %collective-permute-done.11.refs_1_), channel_id=1, source_target_pairs={{0,4},{1,3},{4,8},{5,1},{8,12},{9,5},{12,14},{13,9},{14,10},{15,13... | collective-permute-start | bytes 589832 | tf_op jit(solution)/shard_map/ppermute | solution.py:68
  24.0 1.6 %collective-permute-start.21 = (f32[2,6,16,256]{3,2,1,0:T(8,128)S(1)}, f32[2,6,16,256]{3,2,1,0:T(8,128)S(1)}, u32[]{:S(2)}, u32[]{:S(2)}) collective-permute-start(f32[2,6,16,256]{3,2,1,0:T(8,128)S(1)} %collective-permute-done.19.refs_1_), channel_id=1, source_target_pairs={{0,4},{1,3},{4,8},{5,1},{8,12},{9,5},{12,14},{13,9},{14,10},{15,13... | collective-permute-start | bytes 589832 | tf_op jit(solution)/shard_map/ppermute | solution.py:68
  25.6 0.7 %collective-permute-done.3.refs_1_ = f32[2,6,16,256]{3,2,1,0:T(8,128)S(1)} collective-permute-done((f32[2,6,16,256]{3,2,1,0:T(8,128)S(1)}, f32[2,6,16,256]{3,2,1,0:T(8,128)S(1)}, u32[]{:S(2)}, u32[]{:S(2)}) %collective-permute-start.3) | collective-permute-done | bytes 196640 | tf_op jit(solution)/shard_map/ppermute | solution.py:68
  26.3 1.8 %collective-permute-start.4 = (f32[2,6,16,256]{3,2,1,0:T(8,128)S(1)}, f32[2,6,16,256]{3,2,1,0:T(8,128)S(1)}, u32[]{:S(2)}, u32[]{:S(2)}) collective-permute-start(f32[2,6,16,256]{3,2,1,0:T(8,128)S(1)} %collective-permute-done.3.refs_1_), channel_id=1, source_target_pairs={{0,4},{1,3},{4,8},{5,1},{8,12},{9,5},{12,14},{13,9},{14,10},{15,13... | collective-permute-start | bytes 589832 | tf_op jit(solution)/shard_map/ppermute | solution.py:68
  28.4 1.8 %collective-permute-start.15 = (f32[2,6,16,256]{3,2,1,0:T(8,128)S(1)}, f32[2,6,16,256]{3,2,1,0:T(8,128)S(1)}, u32[]{:S(2)}, u32[]{:S(2)}) collective-permute-start(f32[2,6,16,256]{3,2,1,0:T(8,128)S(1)} %collective-permute-done.13.refs_3_), channel_id=1, source_target_pairs={{0,4},{1,3},{4,8},{5,1},{8,12},{9,5},{12,14},{13,9},{14,10},{15,13... | collective-permute-start | bytes 589832 | tf_op jit(solution)/shard_map/ppermute | solution.py:68
  30.5 1.8 %collective-permute-start.23 = (f32[2,6,16,256]{3,2,1,0:T(8,128)S(1)}, f32[2,6,16,256]{3,2,1,0:T(8,128)S(1)}, u32[]{:S(2)}, u32[]{:S(2)}) collective-permute-start(f32[2,6,16,256]{3,2,1,0:T(8,128)S(1)} %collective-permute-done.21.refs_3_), channel_id=1, source_target_pairs={{0,4},{1,3},{4,8},{5,1},{8,12},{9,5},{12,14},{13,9},{14,10},{15,13... | collective-permute-start | bytes 589832 | tf_op jit(solution)/shard_map/ppermute | solution.py:68
  32.9 1.6 %collective-permute-start.5 = (f32[2,6,16,256]{3,2,1,0:T(8,128)S(1)}, f32[2,6,16,256]{3,2,1,0:T(8,128)S(1)}, u32[]{:S(2)}, u32[]{:S(2)}) collective-permute-start(f32[2,6,16,256]{3,2,1,0:T(8,128)S(1)} %collective-permute-done.4.refs_3_), channel_id=1, source_target_pairs={{0,4},{1,3},{4,8},{5,1},{8,12},{9,5},{12,14},{13,9},{14,10},{15,13... | collective-permute-start | bytes 589832 | tf_op jit(solution)/shard_map/ppermute | solution.py:68
  34.8 1.8 %collective-permute-start.17 = (f32[2,6,16,256]{3,2,1,0:T(8,128)S(1)}, f32[2,6,16,256]{3,2,1,0:T(8,128)S(1)}, u32[]{:S(2)}, u32[]{:S(2)}) collective-permute-start(f32[2,6,16,256]{3,2,1,0:T(8,128)S(1)} %collective-permute-done.15.refs_5_), channel_id=1, source_target_pairs={{0,4},{1,3},{4,8},{5,1},{8,12},{9,5},{12,14},{13,9},{14,10},{15,13... | collective-permute-start | bytes 589832 | tf_op jit(solution)/shard_map/ppermute | solution.py:68
  36.9 1.8 %collective-permute-start.25 = (f32[6,16,256]{2,1,0:T(8,128)S(1)}, f32[6,16,256]{2,1,0:T(8,128)S(1)}, u32[]{:S(2)}, u32[]{:S(2)}) collective-permute-start(f32[6,16,256]{2,1,0:T(8,128)S(1)} %slice_bitcast_fusion), channel_id=1, source_target_pairs={{0,4},{1,3},{4,8},{5,1},{8,12},{9,5},{12,14},{13,9},{14,10},{15,13... | collective-permute-start | bytes 294920 | tf_op jit(solution)/shard_map/ppermute | solution.py:68
  39.5 2.6 %collective-permute-done.25.refs_7_ = f32[6,16,256]{2,1,0:T(8,128)S(1)} collective-permute-done((f32[6,16,256]{2,1,0:T(8,128)S(1)}, f32[6,16,256]{2,1,0:T(8,128)S(1)}, u32[]{:S(2)}, u32[]{:S(2)}) %collective-permute-start.25) | collective-permute-done | bytes 98336 | tf_op jit(solution)/shard_map/ppermute | solution.py:68
  42.6 1.8 %collective-permute-start.6 = (f32[2,6,16,256]{3,2,1,0:T(8,128)S(1)}, f32[2,6,16,256]{3,2,1,0:T(8,128)S(1)}, u32[]{:S(2)}, u32[]{:S(2)}) collective-permute-start(f32[2,6,16,256]{3,2,1,0:T(8,128)S(1)} %collective-permute-done.5.refs_5_), channel_id=1, source_target_pairs={{0,4},{1,3},{4,8},{5,1},{8,12},{9,5},{12,14},{13,9},{14,10},{15,13... | collective-permute-start | bytes 589832 | tf_op jit(solution)/shard_map/ppermute | solution.py:68
  44.5 1.1 %shard_map.41 = (bf16[6,256,256]{2,1,0:T(8,128)(2,1)S(1)}, bf16[6,256,256]{2,1,0:T(8,128)(2,1)S(1)}, f32[4,256,256]{2,1,0:T(8,128)S(1)}, f32[512,256]{1,0:T(8,128)S(1)}) custom-call(f32[2,6,16,256]{3,2,1,0:T(8,128)S(1)} %shard_map.40.refs_0_, f32[2,6,16,256]{3,2,1,0:T(8,128)S(1)} %collective-permute-done.11.refs_1_, ...), custom_call_target="tpu_custom_call" | custom-call | flops 301989888 | bytes 4194304 | tf_op jit(solution)/shard_map/pallas_call | solution.py:42
  45.6 1.0 %shard_map.42 = (bf16[6,256,256]{2,1,0:T(8,128)(2,1)S(1)}, bf16[6,256,256]{2,1,0:T(8,128)(2,1)S(1)}) custom-call(f32[2,6,16,256]{3,2,1,0:T(8,128)S(1)} %shard_map.39.refs_0_, f32[2,6,16,256]{3,2,1,0:T(8,128)S(1)} %collective-permute-done.3.refs_1_, f32[2,6,16,256]{3,2,1,0:T(8,128)S(1)} %collective-permute-done.7.refs_2_, ...), custom_call_target="tpu_custom_call" | custom-call | flops 603979776 | bytes 4194304 | tf_op jit(solution)/shard_map/pallas_call | solution.py:42
  46.9 1.4 %collective-permute-done.6.refs_0_ = f32[2,6,16,256]{3,2,1,0:T(8,128)S(1)} collective-permute-done((f32[2,6,16,256]{3,2,1,0:T(8,128)S(1)}, f32[2,6,16,256]{3,2,1,0:T(8,128)S(1)}, u32[]{:S(2)}, u32[]{:S(2)}) %collective-permute-start.6) | collective-permute-done | bytes 196640 | tf_op jit(solution)/shard_map/ppermute | solution.py:68
  48.3 2.9 %shard_map.45 = (f32[1024,256]{1,0:T(8,128)}, bf16[6,256,256]{2,1,0:T(8,128)(2,1)S(1)}, bf16[6,256,256]{2,1,0:T(8,128)(2,1)S(1)}) custom-call(f32[2,6,16,256]{3,2,1,0:T(8,128)S(1)} %collective-permute-done.6.refs_0_, bf16[6,256,256]{2,1,0:T(8,128)(2,1)S(1)} %get-tuple-element.22.refs_1_, ...), custom_call_target="tpu_custom_call", output_to_operand_aliasing={{1}: (1, {}), {2}: (2, {})} | custom-call | flops 1509949440 | bytes 4194304 | tf_op jit(solution)/shard_map/pallas_call | solution.py:42
  (43 shorter events, 4.8 us)
Async XLA Ops:
  1.0 5.5 %collective-permute-start.2 = (f32[4,16,1024]{2,1,0:T(8,128)S(1)}, f32[4,16,1024]{2,1,0:T(8,128)S(1)}, u32[]{:S(2)}, u32[]{:S(2)}) collective-permute-start(f32[4,16,1024]{2,1,0:T(8,128)S(1)} %get-tuple-element.18.refs_1_), channel_id=1, source_target_pairs={{0,1},{1,0},{2,3},{3,2},{4,5},{5,4},{6,7},{7,6},{8,9},{9,8},{10,11... | collective-permute-start | bytes 786440 | tf_op jit(solution)/shard_map/ppermute | solution.py:326
  2.6 25.5 %collective-permute-start.18 = (f32[512,256]{1,0:T(8,128)S(1)}, f32[512,256]{1,0:T(8,128)S(1)}, u32[]{:S(2)}, u32[]{:S(2)}) collective-permute-start(f32[512,256]{1,0:T(8,128)S(1)} %slice.6), channel_id=1, source_target_pairs={{16,0},{0,16},{17,1},{1,17},{18,2},{2,18},{19,3},{3,19},{20,4},{4,... | collective-permute-start | bytes 1572872 | tf_op jit(solution)/shard_map/ppermute | solution.py:329
  6.5 16.0 %collective-permute-start.11 = (f32[2,6,16,256]{3,2,1,0:T(8,128)S(1)}, f32[2,6,16,256]{3,2,1,0:T(8,128)S(1)}, u32[]{:S(2)}, u32[]{:S(2)}) collective-permute-start(f32[2,6,16,256]{3,2,1,0:T(8,128)S(1)} %shard_map.40.refs_0_), channel_id=1, source_target_pairs={{0,4},{1,3},{4,8},{5,1},{8,12},{9,5},{12,14},{13,9},{14,10},{15,13... | collective-permute-start | bytes 589832 | tf_op jit(solution)/shard_map/ppermute | solution.py:68
  8.2 15.9 %collective-permute-start.19 = (f32[2,6,16,256]{3,2,1,0:T(8,128)S(1)}, f32[2,6,16,256]{3,2,1,0:T(8,128)S(1)}, u32[]{:S(2)}, u32[]{:S(2)}) collective-permute-start(f32[2,6,16,256]{3,2,1,0:T(8,128)S(1)} %shard_map.43.refs_0_), channel_id=1, source_target_pairs={{0,4},{1,3},{4,8},{5,1},{8,12},{9,5},{12,14},{13,9},{14,10},{15,13... | collective-permute-start | bytes 589832 | tf_op jit(solution)/shard_map/ppermute | solution.py:68
  9.8 9.4 %collective-permute-start = (f32[4,16,256]{2,1,0:T(8,128)S(1)}, f32[4,16,256]{2,1,0:T(8,128)S(1)}, u32[]{:S(2)}, u32[]{:S(2)}) collective-permute-start(f32[4,16,256]{2,1,0:T(8,128)S(1)} %get-tuple-element.17.refs_0_), channel_id=1, source_target_pairs={{16,0},{0,16},{17,1},{1,17},{18,2},{2,18},{19,3},{3,19},{20,4},{4,... | collective-permute-start | bytes 196616 | tf_op jit(solution)/shard_map/ppermute | solution.py:327
  20.6 5.7 %collective-permute-start.3 = (f32[2,6,16,256]{3,2,1,0:T(8,128)S(1)}, f32[2,6,16,256]{3,2,1,0:T(8,128)S(1)}, u32[]{:S(2)}, u32[]{:S(2)}) collective-permute-start(f32[2,6,16,256]{3,2,1,0:T(8,128)S(1)} %shard_map.39.refs_0_), channel_id=1, source_target_pairs={{0,4},{1,3},{4,8},{5,1},{8,12},{9,5},{12,14},{13,9},{14,10},{15,13... | collective-permute-start | bytes 589832 | tf_op jit(solution)/shard_map/ppermute | solution.py:68
  22.5 6.0 %collective-permute-start.13 = (f32[2,6,16,256]{3,2,1,0:T(8,128)S(1)}, f32[2,6,16,256]{3,2,1,0:T(8,128)S(1)}, u32[]{:S(2)}, u32[]{:S(2)}) collective-permute-start(f32[2,6,16,256]{3,2,1,0:T(8,128)S(1)} %collective-permute-done.11.refs_1_), channel_id=1, source_target_pairs={{0,4},{1,3},{4,8},{5,1},{8,12},{9,5},{12,14},{13,9},{14,10},{15,13... | collective-permute-start | bytes 589832 | tf_op jit(solution)/shard_map/ppermute | solution.py:68
  24.0 6.5 %collective-permute-start.21 = (f32[2,6,16,256]{3,2,1,0:T(8,128)S(1)}, f32[2,6,16,256]{3,2,1,0:T(8,128)S(1)}, u32[]{:S(2)}, u32[]{:S(2)}) collective-permute-start(f32[2,6,16,256]{3,2,1,0:T(8,128)S(1)} %collective-permute-done.19.refs_1_), channel_id=1, source_target_pairs={{0,4},{1,3},{4,8},{5,1},{8,12},{9,5},{12,14},{13,9},{14,10},{15,13... | collective-permute-start | bytes 589832 | tf_op jit(solution)/shard_map/ppermute | solution.py:68
  25.6 6.7 %collective-permute-start.12 = (f32[2,6,16,256]{3,2,1,0:T(8,128)S(1)}, f32[2,6,16,256]{3,2,1,0:T(8,128)S(1)}, u32[]{:S(2)}, u32[]{:S(2)}) collective-permute-start(f32[2,6,16,256]{3,2,1,0:T(8,128)S(1)} %collective-permute-done.11.refs_1_), channel_id=1, source_target_pairs={{0,1},{1,0},{2,3},{3,2},{4,5},{5,4},{6,7},{7,6},{8,9},{9,8},{10,11... | collective-permute-start | bytes 589832 | tf_op jit(solution)/shard_map/ppermute | solution.py:71
  26.3 6.3 %collective-permute-start.4 = (f32[2,6,16,256]{3,2,1,0:T(8,128)S(1)}, f32[2,6,16,256]{3,2,1,0:T(8,128)S(1)}, u32[]{:S(2)}, u32[]{:S(2)}) collective-permute-start(f32[2,6,16,256]{3,2,1,0:T(8,128)S(1)} %collective-permute-done.3.refs_1_), channel_id=1, source_target_pairs={{0,4},{1,3},{4,8},{5,1},{8,12},{9,5},{12,14},{13,9},{14,10},{15,13... | collective-permute-start | bytes 589832 | tf_op jit(solution)/shard_map/ppermute | solution.py:68
  28.1 4.7 %collective-permute-start.7 = (f32[2,6,16,256]{3,2,1,0:T(8,128)S(1)}, f32[2,6,16,256]{3,2,1,0:T(8,128)S(1)}, u32[]{:S(2)}, u32[]{:S(2)}) collective-permute-start(f32[2,6,16,256]{3,2,1,0:T(8,128)S(1)} %collective-permute-done.3.refs_1_), channel_id=1, source_target_pairs={{0,1},{1,0},{2,3},{3,2},{4,5},{5,4},{6,7},{7,6},{8,9},{9,8},{10,11... | collective-permute-start | bytes 589832 | tf_op jit(solution)/shard_map/ppermute | solution.py:71
  28.4 6.3 %collective-permute-start.15 = (f32[2,6,16,256]{3,2,1,0:T(8,128)S(1)}, f32[2,6,16,256]{3,2,1,0:T(8,128)S(1)}, u32[]{:S(2)}, u32[]{:S(2)}) collective-permute-start(f32[2,6,16,256]{3,2,1,0:T(8,128)S(1)} %collective-permute-done.13.refs_3_), channel_id=1, source_target_pairs={{0,4},{1,3},{4,8},{5,1},{8,12},{9,5},{12,14},{13,9},{14,10},{15,13... | collective-permute-start | bytes 589832 | tf_op jit(solution)/shard_map/ppermute | solution.py:68
  30.5 6.3 %collective-permute-start.23 = (f32[2,6,16,256]{3,2,1,0:T(8,128)S(1)}, f32[2,6,16,256]{3,2,1,0:T(8,128)S(1)}, u32[]{:S(2)}, u32[]{:S(2)}) collective-permute-start(f32[2,6,16,256]{3,2,1,0:T(8,128)S(1)} %collective-permute-done.21.refs_3_), channel_id=1, source_target_pairs={{0,4},{1,3},{4,8},{5,1},{8,12},{9,5},{12,14},{13,9},{14,10},{15,13... | collective-permute-start | bytes 589832 | tf_op jit(solution)/shard_map/ppermute | solution.py:68
  32.3 4.5 %collective-permute-start.14 = (f32[2,6,16,256]{3,2,1,0:T(8,128)S(1)}, f32[2,6,16,256]{3,2,1,0:T(8,128)S(1)}, u32[]{:S(2)}, u32[]{:S(2)}) collective-permute-start(f32[2,6,16,256]{3,2,1,0:T(8,128)S(1)} %collective-permute-done.13.refs_3_), channel_id=1, source_target_pairs={{0,1},{1,0},{2,3},{3,2},{4,5},{5,4},{6,7},{7,6},{8,9},{9,8},{10,11... | collective-permute-start | bytes 589832 | tf_op jit(solution)/shard_map/ppermute | solution.py:71
  32.7 6.3 %collective-permute-start.8 = (f32[2,6,16,256]{3,2,1,0:T(8,128)S(1)}, f32[2,6,16,256]{3,2,1,0:T(8,128)S(1)}, u32[]{:S(2)}, u32[]{:S(2)}) collective-permute-start(f32[2,6,16,256]{3,2,1,0:T(8,128)S(1)} %collective-permute-done.4.refs_3_), channel_id=1, source_target_pairs={{0,1},{1,0},{2,3},{3,2},{4,5},{5,4},{6,7},{7,6},{8,9},{9,8},{10,11... | collective-permute-start | bytes 589832 | tf_op jit(solution)/shard_map/ppermute | solution.py:71
  32.9 6.1 %collective-permute-start.5 = (f32[2,6,16,256]{3,2,1,0:T(8,128)S(1)}, f32[2,6,16,256]{3,2,1,0:T(8,128)S(1)}, u32[]{:S(2)}, u32[]{:S(2)}) collective-permute-start(f32[2,6,16,256]{3,2,1,0:T(8,128)S(1)} %collective-permute-done.4.refs_3_), channel_id=1, source_target_pairs={{0,4},{1,3},{4,8},{5,1},{8,12},{9,5},{12,14},{13,9},{14,10},{15,13... | collective-permute-start | bytes 589832 | tf_op jit(solution)/shard_map/ppermute | solution.py:68
  34.8 7.4 %collective-permute-start.17 = (f32[2,6,16,256]{3,2,1,0:T(8,128)S(1)}, f32[2,6,16,256]{3,2,1,0:T(8,128)S(1)}, u32[]{:S(2)}, u32[]{:S(2)}) collective-permute-start(f32[2,6,16,256]{3,2,1,0:T(8,128)S(1)} %collective-permute-done.15.refs_5_), channel_id=1, source_target_pairs={{0,4},{1,3},{4,8},{5,1},{8,12},{9,5},{12,14},{13,9},{14,10},{15,13... | collective-permute-start | bytes 589832 | tf_op jit(solution)/shard_map/ppermute | solution.py:68
  36.9 5.8 %collective-permute-start.16 = (f32[2,6,16,256]{3,2,1,0:T(8,128)S(1)}, f32[2,6,16,256]{3,2,1,0:T(8,128)S(1)}, u32[]{:S(2)}, u32[]{:S(2)}) collective-permute-start(f32[2,6,16,256]{3,2,1,0:T(8,128)S(1)} %collective-permute-done.15.refs_5_), channel_id=1, source_target_pairs={{0,1},{1,0},{2,3},{3,2},{4,5},{5,4},{6,7},{7,6},{8,9},{9,8},{10,11... | collective-permute-start | bytes 589832 | tf_op jit(solution)/shard_map/ppermute | solution.py:71
  36.9 5.2 %collective-permute-start.25 = (f32[6,16,256]{2,1,0:T(8,128)S(1)}, f32[6,16,256]{2,1,0:T(8,128)S(1)}, u32[]{:S(2)}, u32[]{:S(2)}) collective-permute-start(f32[6,16,256]{2,1,0:T(8,128)S(1)} %slice_bitcast_fusion), channel_id=1, source_target_pairs={{0,4},{1,3},{4,8},{5,1},{8,12},{9,5},{12,14},{13,9},{14,10},{15,13... | collective-permute-start | bytes 294920 | tf_op jit(solution)/shard_map/ppermute | solution.py:68
  39.0 5.5 %collective-permute-start.9 = (f32[2,6,16,256]{3,2,1,0:T(8,128)S(1)}, f32[2,6,16,256]{3,2,1,0:T(8,128)S(1)}, u32[]{:S(2)}, u32[]{:S(2)}) collective-permute-start(f32[2,6,16,256]{3,2,1,0:T(8,128)S(1)} %collective-permute-done.5.refs_5_), channel_id=1, source_target_pairs={{0,1},{1,0},{2,3},{3,2},{4,5},{5,4},{6,7},{7,6},{8,9},{9,8},{10,11... | collective-permute-start | bytes 589832 | tf_op jit(solution)/shard_map/ppermute | solution.py:71
  39.0 7.6 %collective-permute-start.20 = (f32[2,6,16,256]{3,2,1,0:T(8,128)S(1)}, f32[2,6,16,256]{3,2,1,0:T(8,128)S(1)}, u32[]{:S(2)}, u32[]{:S(2)}) collective-permute-start(f32[2,6,16,256]{3,2,1,0:T(8,128)S(1)} %collective-permute-done.19.refs_1_), channel_id=1, source_target_pairs={{0,1},{1,0},{2,3},{3,2},{4,5},{5,4},{6,7},{7,6},{8,9},{9,8},{10,11... | collective-permute-start | bytes 589832 | tf_op jit(solution)/shard_map/ppermute | solution.py:71
  42.1 4.4 %collective-permute-start.22 = (f32[2,6,16,256]{3,2,1,0:T(8,128)S(1)}, f32[2,6,16,256]{3,2,1,0:T(8,128)S(1)}, u32[]{:S(2)}, u32[]{:S(2)}) collective-permute-start(f32[2,6,16,256]{3,2,1,0:T(8,128)S(1)} %collective-permute-done.21.refs_3_), channel_id=1, source_target_pairs={{0,1},{1,0},{2,3},{3,2},{4,5},{5,4},{6,7},{7,6},{8,9},{9,8},{10,11... | collective-permute-start | bytes 589832 | tf_op jit(solution)/shard_map/ppermute | solution.py:71
  42.1 4.4 %collective-permute-start.24 = (f32[2,6,16,256]{3,2,1,0:T(8,128)S(1)}, f32[2,6,16,256]{3,2,1,0:T(8,128)S(1)}, u32[]{:S(2)}, u32[]{:S(2)}) collective-permute-start(f32[2,6,16,256]{3,2,1,0:T(8,128)S(1)} %collective-permute-done.23.refs_5_), channel_id=1, source_target_pairs={{0,1},{1,0},{2,3},{3,2},{4,5},{5,4},{6,7},{7,6},{8,9},{9,8},{10,11... | collective-permute-start | bytes 589832 | tf_op jit(solution)/shard_map/ppermute | solution.py:71
  42.6 5.7 %collective-permute-start.6 = (f32[2,6,16,256]{3,2,1,0:T(8,128)S(1)}, f32[2,6,16,256]{3,2,1,0:T(8,128)S(1)}, u32[]{:S(2)}, u32[]{:S(2)}) collective-permute-start(f32[2,6,16,256]{3,2,1,0:T(8,128)S(1)} %collective-permute-done.5.refs_5_), channel_id=1, source_target_pairs={{0,4},{1,3},{4,8},{5,1},{8,12},{9,5},{12,14},{13,9},{14,10},{15,13... | collective-permute-start | bytes 589832 | tf_op jit(solution)/shard_map/ppermute | solution.py:68
  (4 other events, 42.7 us)

commit v9 on v8

--- a/solution.py
+++ b/solution.py
@@ -128,6 +128,8 @@
             low[self.wide :],
             [("tri", at) for at in range(len(self.tri))],
         ]
+        self.mine = self.chunks[0][:panels]
+        self.mine += [("low", panel, block) for block in range(self.wide) for panel in range(panels)]
         self.where = {b: (c, at) for c, chunk in enumerate(self.chunks) for at, b in enumerate(chunk)}
 
     def tri_of(self, rank):
@@ -151,32 +153,27 @@
         return self.chosen(owner, [right_ref[rows]] + [r[rows] for r in received])
 
 
-def load_kernel(plan, factor_hbm, inv_hbm, factor_ref, inv_ref, own_ref, sems):
-    copies = [
-        pltpu.make_async_copy(factor_hbm, factor_ref, sems.at[0]),
-        pltpu.make_async_copy(inv_hbm, inv_ref, sems.at[1]),
-    ]
+def load_kernel(plan, factor_hbm, inv_hbm, mine_ref, own_ref, sems):
+    panels, nb = plan.panels, plan.nb
+    copies = [(inv_hbm, mine_ref.at[:panels])]
     for local, deep in enumerate(plan.deep):
-        source = factor_hbm.at[:deep, :, local * plan.nb : (local + 1) * plan.nb]
-        target = own_ref.at[pl.ds(plan.sent.index((local, 0)), deep)]
-        copies.append(pltpu.make_async_copy(source, target, sems.at[2 + local]))
+        source = factor_hbm.at[:deep, :, local * nb : (local + 1) * nb]
+        copies.append((source, own_ref.at[pl.ds(plan.sent.index((local, 0)), deep)]))
+    for block in range(plan.wide):
+        at = (plan.sure + block) * nb
+        to = plan.mine.index(("low", 0, block))
+        copies.append((factor_hbm.at[:, :, at : at + nb], mine_ref.at[to : to + panels]))
+    copies = [pltpu.make_async_copy(*pair, sems.at[n]) for n, pair in enumerate(copies)]
     for copy in copies:
         copy.start()
     for copy in copies:
         copy.wait()
 
 
-def pack_kernel(plan, chunk, *refs):
-    out_ref = refs[-1]
-    for side in range(2):
-        head, factor = refs[2 * side : 2 * side + 2]
-        for to, (kind, *which) in enumerate(plan.chunks[chunk]):
-            if kind == "low":
-                panel, block = which
-                at = (plan.sure + block) * plan.nb
-                out_ref[side, to] = factor[panel, :, at : at + plan.nb]
-            else:
-                out_ref[side, to] = head[which[0]]
+def pack_kernel(held, chosen, own_ref, other_ref, out_ref):
+    for to, block in enumerate(chosen):
+        out_ref[0, to] = own_ref[held.index(block)]
+        out_ref[1, to] = other_ref[held.index(block)]
 
 
 def tri_kernel(plan, *refs):
@@ -311,19 +308,14 @@
     shape = jax.ShapeDtypeStruct
     bound = functools.partial
 
-    factor, inv, own = kernel_call(
+    mine, own = kernel_call(
         bound(load_kernel, plan),
-        [
-            shape(factor_panels.shape, f32),
-            shape(inverses.shape, f32),
-            shape((len(plan.sent), depth, nb), f32),
-        ],
-        [pltpu.SemaphoreType.DMA((2 + plan.held,))],
+        [shape((len(plan.mine), depth, nb), f32), shape((len(plan.sent), depth, nb), f32)],
+        [pltpu.SemaphoreType.DMA((1 + plan.held + plan.wide,))],
         [pltpu.with_memory_space_constraint(a, pltpu.HBM) for a in (factor_panels, inverses)],
         in_hbm=2,
     )
-    inv_other = lax.ppermute(inv, "col", swap)
-    factor_other = lax.ppermute(factor, "col", swap)
+    other = lax.ppermute(mine, "col", swap)
     tri = [own] + [lax.ppermute(own, "row", pairs) for pairs in shifts]
     above = right_side[: plan.held * nb]
     received = [lax.ppermute(above, "row", pairs) for pairs in shifts]
@@ -332,12 +324,12 @@
 
     pieces = []
     for chunk, blocks in enumerate(plan.chunks):
-        heads = (half, half_other) if chunk == len(plan.chunks) - 1 else (inv, inv_other)
+        last = chunk == len(plan.chunks) - 1
         packed = kernel_call(
-            bound(pack_kernel, plan, chunk),
+            bound(pack_kernel, blocks if last else plan.mine, blocks),
             shape((2, len(blocks), depth, nb), f32),
             [],
-            (heads[0], factor, heads[1], factor_other),
+            (half, half_other) if last else (mine, other),
         )
         pieces.append(ring(packed, chips, halves=chunk == 1 and depth % 16 == 0))
 

time: 51.4 us -> 48.8 us (0.949)
  waiting for transfers between devices: 17.8 us -> 12.4 us
  starting transfers between devices: 25.9 us -> 28.7 us
    ppermute x1, waiting for transfers between devices: 8.92 us -> 1.1 us  [per_device(): tri = [own] + [lax.ppermute(own, 'row', pairs) for pairs in shifts]]
    ppermute x12, starting transfers between devices: 20.7 us -> 23.7 us  [ring(): lax.ppermute(moving[0] if last and halves else moving, 'col', nearest)]
    ppermute x12, waiting for transfers between devices: 6.51 us -> 8.68 us  [ring(): lax.ppermute(moving[0] if last and halves else moving, 'col', nearest)]
    ppermute x1, starting transfers between devices: 2.58 us -> 0.57 us  [per_device(): received = [lax.ppermute(above, 'row', pairs) for pairs in shifts]]
    ppermute x1, starting transfers between devices: 0.51 us -> 1.52 us  [per_device(): tri = [own] + [lax.ppermute(own, 'row', pairs) for pairs in shifts]]
    ppermute x10, starting transfers between devices: 1.24 us -> 2.26 us  [ring(): pieces.append(lax.ppermute(moving, 'col', swap))]
    ppermute x2 -> x1, waiting for transfers between devices: 1.04 us -> 1.07 us  [per_device(): other = lax.ppermute(mine, 'col', swap)]
  transfers between devices with their start and end apart: 27 -> 26, of which waited for: 12 -> 12; matrix products, arithmetic and copies ran while one was open for 2% -> 2% of each run, Pallas kernels for 5% -> 5%
where the time goes in v9:
time: 48.8 us; the launch traced here: 48.6 us
  starting transfers between devices  28.7 us (59%)
  waiting for transfers between devices  12.4 us (25%)
  Pallas kernels  6.3 us (13%)
  local copies, waits for them, and re-layouts  1.09 us (2%)
    ppermute x12, starting transfers between devices, ring(): lax.ppermute(moving[0] if last and halves else moving, 'col', nearest)  23.7 us
    ppermute x12, waiting for transfers between devices, ring(): lax.ppermute(moving[0] if last and halves else moving, 'col', nearest)  8.68 us
    pallas_call x9, Pallas kernels, kernel_call(): pl.pallas_call(body, out_shape=out_shapes, in_specs=[hbm] * in_hbm + [nea...  6.3 us
    ppermute x10, starting transfers between devices, ring(): pieces.append(lax.ppermute(moving, 'col', swap))  2.26 us
    ppermute x1, starting transfers between devices, per_device(): tri = [own] + [lax.ppermute(own, 'row', pairs) for pairs in shifts]  1.52 us
    ppermute x1, waiting for transfers between devices, per_device(): half_other = lax.ppermute(half, 'col', swap)  1.29 us
    ppermute x1, waiting for transfers between devices, per_device(): tri = [own] + [lax.ppermute(own, 'row', pairs) for pairs in shifts]  1.1 us
    slice x1, local copies, waits for them, and re-layouts, per_device(): above = right_side[:plan.held * nb]  1.08 us
  transfers between devices with their start and end apart: 26, of which 12 were waited for; matrix products, arithmetic and copies ran while one was open for 2% of the time, Pallas kernels for 5%

profile of v9, /device:TPU:0, one launch (start us, length us, event | category | flops | bytes accessed | tf_op | source)
XLA Modules:
  0.0 48.6 jit_solution(5613618575934892358)
XLA Ops:
  0.0 1.0 %shard_map.37 = (f32[12,16,256]{2,1,0:T(8,128)S(1)}, f32[4,16,256]{2,1,0:T(8,128)S(1)}) custom-call(f32[4,16,1024]{2,1,0:T(8,128)} %factor_hbm.1, f32[4,16,256]{2,1,0:T(8,128)} %inv_hbm.1), custom_call_target="tpu_custom_call" | custom-call | bytes 4194304 | tf_op jit(solution)/shard_map/pallas_call | solution.py:42
  1.6 1.1 %collective-permute-done.9.other_ref = f32[12,16,256]{2,1,0:T(8,128)S(1)} collective-permute-done((f32[12,16,256]{2,1,0:T(8,128)S(1)}, f32[12,16,256]{2,1,0:T(8,128)S(1)}, u32[]{:S(2)}, u32[]{:S(2)}) %collective-permute-start.9) | collective-permute-done | bytes 196640 | tf_op jit(solution)/shard_map/ppermute | solution.py:318
  2.6 3.0 %collective-permute-start.18 = (f32[2,6,16,256]{3,2,1,0:T(8,128)S(1)}, f32[2,6,16,256]{3,2,1,0:T(8,128)S(1)}, u32[]{:S(2)}, u32[]{:S(2)}) collective-permute-start(f32[2,6,16,256]{3,2,1,0:T(8,128)S(1)} %shard_map.43.refs_0_), channel_id=1, source_target_pairs={{0,4},{1,3},{4,8},{5,1},{8,12},{9,5},{12,14},{13,9},{14,10},{15,13... | collective-permute-start | bytes 589832 | tf_op jit(solution)/shard_map/ppermute | solution.py:68
  5.6 1.5 %collective-permute-start = (f32[4,16,256]{2,1,0:T(8,128)S(1)}, f32[4,16,256]{2,1,0:T(8,128)S(1)}, u32[]{:S(2)}, u32[]{:S(2)}) collective-permute-start(f32[4,16,256]{2,1,0:T(8,128)S(1)} %get-tuple-element.16.refs_0_), channel_id=1, source_target_pairs={{16,0},{0,16},{17,1},{1,17},{18,2},{2,18},{19,3},{3,19},{20,4},{4,... | collective-permute-start | bytes 196616 | tf_op jit(solution)/shard_map/ppermute | solution.py:319
  7.1 1.1 %slice.6 = f32[512,256]{1,0:T(8,128)S(1)} slice(f32[1024,256]{1,0:T(8,128)} %refs_8_.1), slice={[0:512], [0:256]} | slice | bytes 1048576 | tf_op jit(solution)/shard_map/slice | solution.py:320
  8.8 1.1 %collective-permute-done.refs_1_ = f32[4,16,256]{2,1,0:T(8,128)S(1)} collective-permute-done((f32[4,16,256]{2,1,0:T(8,128)S(1)}, f32[4,16,256]{2,1,0:T(8,128)S(1)}, u32[]{:S(2)}, u32[]{:S(2)}) %collective-permute-start) | collective-permute-done | bytes 65568 | tf_op jit(solution)/shard_map/ppermute | solution.py:319
  10.0 1.3 %collective-permute-done.1.other_ref = f32[6,16,256]{2,1,0:T(8,128)S(1)} collective-permute-done((f32[6,16,256]{2,1,0:T(8,128)S(1)}, f32[6,16,256]{2,1,0:T(8,128)S(1)}, u32[]{:S(2)}, u32[]{:S(2)}) %collective-permute-start.1) | collective-permute-done | bytes 98336 | tf_op jit(solution)/shard_map/ppermute | solution.py:323
  11.3 2.2 %collective-permute-start.2 = (f32[2,6,16,256]{3,2,1,0:T(8,128)S(1)}, f32[2,6,16,256]{3,2,1,0:T(8,128)S(1)}, u32[]{:S(2)}, u32[]{:S(2)}) collective-permute-start(f32[2,6,16,256]{3,2,1,0:T(8,128)S(1)} %shard_map.39.refs_0_), channel_id=1, source_target_pairs={{0,4},{1,3},{4,8},{5,1},{8,12},{9,5},{12,14},{13,9},{14,10},{15,13... | collective-permute-start | bytes 589832 | tf_op jit(solution)/shard_map/ppermute | solution.py:68
  13.5 1.6 %collective-permute-start.10 = (f32[2,6,16,256]{3,2,1,0:T(8,128)S(1)}, f32[2,6,16,256]{3,2,1,0:T(8,128)S(1)}, u32[]{:S(2)}, u32[]{:S(2)}) collective-permute-start(f32[2,6,16,256]{3,2,1,0:T(8,128)S(1)} %shard_map.40.refs_0_), channel_id=1, source_target_pairs={{0,4},{1,3},{4,8},{5,1},{8,12},{9,5},{12,14},{13,9},{14,10},{15,13... | collective-permute-start | bytes 589832 | tf_op jit(solution)/shard_map/ppermute | solution.py:68
  15.1 1.4 %collective-permute-start.20 = (f32[2,6,16,256]{3,2,1,0:T(8,128)S(1)}, f32[2,6,16,256]{3,2,1,0:T(8,128)S(1)}, u32[]{:S(2)}, u32[]{:S(2)}) collective-permute-start(f32[2,6,16,256]{3,2,1,0:T(8,128)S(1)} %collective-permute-done.18.refs_1_), channel_id=1, source_target_pairs={{0,4},{1,3},{4,8},{5,1},{8,12},{9,5},{12,14},{13,9},{14,10},{15,13... | collective-permute-start | bytes 589832 | tf_op jit(solution)/shard_map/ppermute | solution.py:68
  17.0 2.1 %collective-permute-start.3 = (f32[2,6,16,256]{3,2,1,0:T(8,128)S(1)}, f32[2,6,16,256]{3,2,1,0:T(8,128)S(1)}, u32[]{:S(2)}, u32[]{:S(2)}) collective-permute-start(f32[2,6,16,256]{3,2,1,0:T(8,128)S(1)} %collective-permute-done.2.refs_1_), channel_id=1, source_target_pairs={{0,4},{1,3},{4,8},{5,1},{8,12},{9,5},{12,14},{13,9},{14,10},{15,13... | collective-permute-start | bytes 589832 | tf_op jit(solution)/shard_map/ppermute | solution.py:68
  19.2 2.0 %collective-permute-start.12 = (f32[2,6,16,256]{3,2,1,0:T(8,128)S(1)}, f32[2,6,16,256]{3,2,1,0:T(8,128)S(1)}, u32[]{:S(2)}, u32[]{:S(2)}) collective-permute-start(f32[2,6,16,256]{3,2,1,0:T(8,128)S(1)} %collective-permute-done.10.refs_1_), channel_id=1, source_target_pairs={{0,4},{1,3},{4,8},{5,1},{8,12},{9,5},{12,14},{13,9},{14,10},{15,13... | collective-permute-start | bytes 589832 | tf_op jit(solution)/shard_map/ppermute | solution.py:68
  21.3 2.0 %collective-permute-start.22 = (f32[2,6,16,256]{3,2,1,0:T(8,128)S(1)}, f32[2,6,16,256]{3,2,1,0:T(8,128)S(1)}, u32[]{:S(2)}, u32[]{:S(2)}) collective-permute-start(f32[2,6,16,256]{3,2,1,0:T(8,128)S(1)} %collective-permute-done.20.refs_3_), channel_id=1, source_target_pairs={{0,4},{1,3},{4,8},{5,1},{8,12},{9,5},{12,14},{13,9},{14,10},{15,13... | collective-permute-start | bytes 589832 | tf_op jit(solution)/shard_map/ppermute | solution.py:68
  23.9 1.6 %collective-permute-start.4 = (f32[2,6,16,256]{3,2,1,0:T(8,128)S(1)}, f32[2,6,16,256]{3,2,1,0:T(8,128)S(1)}, u32[]{:S(2)}, u32[]{:S(2)}) collective-permute-start(f32[2,6,16,256]{3,2,1,0:T(8,128)S(1)} %collective-permute-done.3.refs_3_), channel_id=1, source_target_pairs={{0,4},{1,3},{4,8},{5,1},{8,12},{9,5},{12,14},{13,9},{14,10},{15,13... | collective-permute-start | bytes 589832 | tf_op jit(solution)/shard_map/ppermute | solution.py:68
  25.5 2.0 %collective-permute-start.14 = (f32[2,6,16,256]{3,2,1,0:T(8,128)S(1)}, f32[2,6,16,256]{3,2,1,0:T(8,128)S(1)}, u32[]{:S(2)}, u32[]{:S(2)}) collective-permute-start(f32[2,6,16,256]{3,2,1,0:T(8,128)S(1)} %collective-permute-done.12.refs_3_), channel_id=1, source_target_pairs={{0,4},{1,3},{4,8},{5,1},{8,12},{9,5},{12,14},{13,9},{14,10},{15,13... | collective-permute-start | bytes 589832 | tf_op jit(solution)/shard_map/ppermute | solution.py:68
  28.2 3.6 %collective-permute-done.14.refs_5_ = f32[2,6,16,256]{3,2,1,0:T(8,128)S(1)} collective-permute-done((f32[2,6,16,256]{3,2,1,0:T(8,128)S(1)}, f32[2,6,16,256]{3,2,1,0:T(8,128)S(1)}, u32[]{:S(2)}, u32[]{:S(2)}) %collective-permute-start.14) | collective-permute-done | bytes 196640 | tf_op jit(solution)/shard_map/ppermute | solution.py:68
  31.9 2.0 %collective-permute-start.16 = (f32[2,6,16,256]{3,2,1,0:T(8,128)S(1)}, f32[2,6,16,256]{3,2,1,0:T(8,128)S(1)}, u32[]{:S(2)}, u32[]{:S(2)}) collective-permute-start(f32[2,6,16,256]{3,2,1,0:T(8,128)S(1)} %collective-permute-done.14.refs_5_), channel_id=1, source_target_pairs={{0,4},{1,3},{4,8},{5,1},{8,12},{9,5},{12,14},{13,9},{14,10},{15,13... | collective-permute-start | bytes 589832 | tf_op jit(solution)/shard_map/ppermute | solution.py:68
  33.9 1.6 %collective-permute-start.24 = (f32[6,16,256]{2,1,0:T(8,128)S(1)}, f32[6,16,256]{2,1,0:T(8,128)S(1)}, u32[]{:S(2)}, u32[]{:S(2)}) collective-permute-start(f32[6,16,256]{2,1,0:T(8,128)S(1)} %slice_bitcast_fusion), channel_id=1, source_target_pairs={{0,4},{1,3},{4,8},{5,1},{8,12},{9,5},{12,14},{13,9},{14,10},{15,13... | collective-permute-start | bytes 294920 | tf_op jit(solution)/shard_map/ppermute | solution.py:68
  35.5 3.1 %collective-permute-done.24.refs_7_ = f32[6,16,256]{2,1,0:T(8,128)S(1)} collective-permute-done((f32[6,16,256]{2,1,0:T(8,128)S(1)}, f32[6,16,256]{2,1,0:T(8,128)S(1)}, u32[]{:S(2)}, u32[]{:S(2)}) %collective-permute-start.24) | collective-permute-done | bytes 98336 | tf_op jit(solution)/shard_map/ppermute | solution.py:68
  40.1 2.0 %collective-permute-start.5 = (f32[2,6,16,256]{3,2,1,0:T(8,128)S(1)}, f32[2,6,16,256]{3,2,1,0:T(8,128)S(1)}, u32[]{:S(2)}, u32[]{:S(2)}) collective-permute-start(f32[2,6,16,256]{3,2,1,0:T(8,128)S(1)} %collective-permute-done.4.refs_5_), channel_id=1, source_target_pairs={{0,4},{1,3},{4,8},{5,1},{8,12},{9,5},{12,14},{13,9},{14,10},{15,13... | collective-permute-start | bytes 589832 | tf_op jit(solution)/shard_map/ppermute | solution.py:68
  42.4 1.1 %shard_map.41 = (bf16[6,256,256]{2,1,0:T(8,128)(2,1)S(1)}, bf16[6,256,256]{2,1,0:T(8,128)(2,1)S(1)}, f32[4,256,256]{2,1,0:T(8,128)S(1)}, f32[512,256]{1,0:T(8,128)S(1)}) custom-call(f32[2,6,16,256]{3,2,1,0:T(8,128)S(1)} %shard_map.40.refs_0_, f32[2,6,16,256]{3,2,1,0:T(8,128)S(1)} %collective-permute-done.10.refs_1_, ...), custom_call_target="tpu_custom_call" | custom-call | flops 301989888 | bytes 4194304 | tf_op jit(solution)/shard_map/pallas_call | solution.py:42
  43.5 1.0 %shard_map.42 = (bf16[6,256,256]{2,1,0:T(8,128)(2,1)S(1)}, bf16[6,256,256]{2,1,0:T(8,128)(2,1)S(1)}) custom-call(f32[2,6,16,256]{3,2,1,0:T(8,128)S(1)} %shard_map.39.refs_0_, f32[2,6,16,256]{3,2,1,0:T(8,128)S(1)} %collective-permute-done.2.refs_1_, f32[2,6,16,256]{3,2,1,0:T(8,128)S(1)} %collective-permute-done.6.refs_2_, ...), custom_call_target="tpu_custom_call" | custom-call | flops 603979776 | bytes 4194304 | tf_op jit(solution)/shard_map/pallas_call | solution.py:42
  44.5 1.2 %collective-permute-done.5.refs_0_ = f32[2,6,16,256]{3,2,1,0:T(8,128)S(1)} collective-permute-done((f32[2,6,16,256]{3,2,1,0:T(8,128)S(1)}, f32[2,6,16,256]{3,2,1,0:T(8,128)S(1)}, u32[]{:S(2)}, u32[]{:S(2)}) %collective-permute-start.5) | collective-permute-done | bytes 196640 | tf_op jit(solution)/shard_map/ppermute | solution.py:68
  45.7 2.9 %shard_map.45 = (f32[1024,256]{1,0:T(8,128)}, bf16[6,256,256]{2,1,0:T(8,128)(2,1)S(1)}, bf16[6,256,256]{2,1,0:T(8,128)(2,1)S(1)}) custom-call(f32[2,6,16,256]{3,2,1,0:T(8,128)S(1)} %collective-permute-done.5.refs_0_, bf16[6,256,256]{2,1,0:T(8,128)(2,1)S(1)} %get-tuple-element.20.refs_1_, ...), custom_call_target="tpu_custom_call", output_to_operand_aliasing={{1}: (1, {}), {2}: (2, {})} | custom-call | flops 1509949440 | bytes 4194304 | tf_op jit(solution)/shard_map/pallas_call | solution.py:42
  (41 shorter events, 4.9 us)
Async XLA Ops:
  1.0 1.6 %collective-permute-start.9 = (f32[12,16,256]{2,1,0:T(8,128)S(1)}, f32[12,16,256]{2,1,0:T(8,128)S(1)}, u32[]{:S(2)}, u32[]{:S(2)}) collective-permute-start(f32[12,16,256]{2,1,0:T(8,128)S(1)} %get-tuple-element.17.own_ref), channel_id=1, source_target_pairs={{0,1},{1,0},{2,3},{3,2},{4,5},{5,4},{6,7},{7,6},{8,9},{9,8},{10,11... | collective-permute-start | bytes 589832 | tf_op jit(solution)/shard_map/ppermute | solution.py:318
  2.6 12.5 %collective-permute-start.18 = (f32[2,6,16,256]{3,2,1,0:T(8,128)S(1)}, f32[2,6,16,256]{3,2,1,0:T(8,128)S(1)}, u32[]{:S(2)}, u32[]{:S(2)}) collective-permute-start(f32[2,6,16,256]{3,2,1,0:T(8,128)S(1)} %shard_map.43.refs_0_), channel_id=1, source_target_pairs={{0,4},{1,3},{4,8},{5,1},{8,12},{9,5},{12,14},{13,9},{14,10},{15,13... | collective-permute-start | bytes 589832 | tf_op jit(solution)/shard_map/ppermute | solution.py:68
  5.6 4.3 %collective-permute-start = (f32[4,16,256]{2,1,0:T(8,128)S(1)}, f32[4,16,256]{2,1,0:T(8,128)S(1)}, u32[]{:S(2)}, u32[]{:S(2)}) collective-permute-start(f32[4,16,256]{2,1,0:T(8,128)S(1)} %get-tuple-element.16.refs_0_), channel_id=1, source_target_pairs={{16,0},{0,16},{17,1},{1,17},{18,2},{2,18},{19,3},{3,19},{20,4},{4,... | collective-permute-start | bytes 196616 | tf_op jit(solution)/shard_map/ppermute | solution.py:319
  8.2 15.2 %collective-permute-start.17 = (f32[512,256]{1,0:T(8,128)S(1)}, f32[512,256]{1,0:T(8,128)S(1)}, u32[]{:S(2)}, u32[]{:S(2)}) collective-permute-start(f32[512,256]{1,0:T(8,128)S(1)} %slice.6), channel_id=1, source_target_pairs={{16,0},{0,16},{17,1},{1,17},{18,2},{2,18},{19,3},{3,19},{20,4},{4,... | collective-permute-start | bytes 1572872 | tf_op jit(solution)/shard_map/ppermute | solution.py:321
  11.3 5.7 %collective-permute-start.2 = (f32[2,6,16,256]{3,2,1,0:T(8,128)S(1)}, f32[2,6,16,256]{3,2,1,0:T(8,128)S(1)}, u32[]{:S(2)}, u32[]{:S(2)}) collective-permute-start(f32[2,6,16,256]{3,2,1,0:T(8,128)S(1)} %shard_map.39.refs_0_), channel_id=1, source_target_pairs={{0,4},{1,3},{4,8},{5,1},{8,12},{9,5},{12,14},{13,9},{14,10},{15,13... | collective-permute-start | bytes 589832 | tf_op jit(solution)/shard_map/ppermute | solution.py:68
  13.5 5.7 %collective-permute-start.10 = (f32[2,6,16,256]{3,2,1,0:T(8,128)S(1)}, f32[2,6,16,256]{3,2,1,0:T(8,128)S(1)}, u32[]{:S(2)}, u32[]{:S(2)}) collective-permute-start(f32[2,6,16,256]{3,2,1,0:T(8,128)S(1)} %shard_map.40.refs_0_), channel_id=1, source_target_pairs={{0,4},{1,3},{4,8},{5,1},{8,12},{9,5},{12,14},{13,9},{14,10},{15,13... | collective-permute-start | bytes 589832 | tf_op jit(solution)/shard_map/ppermute | solution.py:68
  15.1 6.2 %collective-permute-start.20 = (f32[2,6,16,256]{3,2,1,0:T(8,128)S(1)}, f32[2,6,16,256]{3,2,1,0:T(8,128)S(1)}, u32[]{:S(2)}, u32[]{:S(2)}) collective-permute-start(f32[2,6,16,256]{3,2,1,0:T(8,128)S(1)} %collective-permute-done.18.refs_1_), channel_id=1, source_target_pairs={{0,4},{1,3},{4,8},{5,1},{8,12},{9,5},{12,14},{13,9},{14,10},{15,13... | collective-permute-start | bytes 589832 | tf_op jit(solution)/shard_map/ppermute | solution.py:68
  17.0 6.9 %collective-permute-start.3 = (f32[2,6,16,256]{3,2,1,0:T(8,128)S(1)}, f32[2,6,16,256]{3,2,1,0:T(8,128)S(1)}, u32[]{:S(2)}, u32[]{:S(2)}) collective-permute-start(f32[2,6,16,256]{3,2,1,0:T(8,128)S(1)} %collective-permute-done.2.refs_1_), channel_id=1, source_target_pairs={{0,4},{1,3},{4,8},{5,1},{8,12},{9,5},{12,14},{13,9},{14,10},{15,13... | collective-permute-start | bytes 589832 | tf_op jit(solution)/shard_map/ppermute | solution.py:68
  19.2 6.3 %collective-permute-start.12 = (f32[2,6,16,256]{3,2,1,0:T(8,128)S(1)}, f32[2,6,16,256]{3,2,1,0:T(8,128)S(1)}, u32[]{:S(2)}, u32[]{:S(2)}) collective-permute-start(f32[2,6,16,256]{3,2,1,0:T(8,128)S(1)} %collective-permute-done.10.refs_1_), channel_id=1, source_target_pairs={{0,4},{1,3},{4,8},{5,1},{8,12},{9,5},{12,14},{13,9},{14,10},{15,13... | collective-permute-start | bytes 589832 | tf_op jit(solution)/shard_map/ppermute | solution.py:68
  21.3 6.3 %collective-permute-start.22 = (f32[2,6,16,256]{3,2,1,0:T(8,128)S(1)}, f32[2,6,16,256]{3,2,1,0:T(8,128)S(1)}, u32[]{:S(2)}, u32[]{:S(2)}) collective-permute-start(f32[2,6,16,256]{3,2,1,0:T(8,128)S(1)} %collective-permute-done.20.refs_3_), channel_id=1, source_target_pairs={{0,4},{1,3},{4,8},{5,1},{8,12},{9,5},{12,14},{13,9},{14,10},{15,13... | collective-permute-start | bytes 589832 | tf_op jit(solution)/shard_map/ppermute | solution.py:68
  23.4 4.3 %collective-permute-start.11 = (f32[2,6,16,256]{3,2,1,0:T(8,128)S(1)}, f32[2,6,16,256]{3,2,1,0:T(8,128)S(1)}, u32[]{:S(2)}, u32[]{:S(2)}) collective-permute-start(f32[2,6,16,256]{3,2,1,0:T(8,128)S(1)} %collective-permute-done.10.refs_1_), channel_id=1, source_target_pairs={{0,1},{1,0},{2,3},{3,2},{4,5},{5,4},{6,7},{7,6},{8,9},{9,8},{10,11... | collective-permute-start | bytes 589832 | tf_op jit(solution)/shard_map/ppermute | solution.py:71
  23.4 10.5 %collective-permute-start.19 = (f32[2,6,16,256]{3,2,1,0:T(8,128)S(1)}, f32[2,6,16,256]{3,2,1,0:T(8,128)S(1)}, u32[]{:S(2)}, u32[]{:S(2)}) collective-permute-start(f32[2,6,16,256]{3,2,1,0:T(8,128)S(1)} %collective-permute-done.18.refs_1_), channel_id=1, source_target_pairs={{0,1},{1,0},{2,3},{3,2},{4,5},{5,4},{6,7},{7,6},{8,9},{9,8},{10,11... | collective-permute-start | bytes 589832 | tf_op jit(solution)/shard_map/ppermute | solution.py:71
  23.9 11.6 %collective-permute-start.4 = (f32[2,6,16,256]{3,2,1,0:T(8,128)S(1)}, f32[2,6,16,256]{3,2,1,0:T(8,128)S(1)}, u32[]{:S(2)}, u32[]{:S(2)}) collective-permute-start(f32[2,6,16,256]{3,2,1,0:T(8,128)S(1)} %collective-permute-done.3.refs_3_), channel_id=1, source_target_pairs={{0,4},{1,3},{4,8},{5,1},{8,12},{9,5},{12,14},{13,9},{14,10},{15,13... | collective-permute-start | bytes 589832 | tf_op jit(solution)/shard_map/ppermute | solution.py:68
  25.5 6.3 %collective-permute-start.14 = (f32[2,6,16,256]{3,2,1,0:T(8,128)S(1)}, f32[2,6,16,256]{3,2,1,0:T(8,128)S(1)}, u32[]{:S(2)}, u32[]{:S(2)}) collective-permute-start(f32[2,6,16,256]{3,2,1,0:T(8,128)S(1)} %collective-permute-done.12.refs_3_), channel_id=1, source_target_pairs={{0,4},{1,3},{4,8},{5,1},{8,12},{9,5},{12,14},{13,9},{14,10},{15,13... | collective-permute-start | bytes 589832 | tf_op jit(solution)/shard_map/ppermute | solution.py:68
  27.7 10.9 %collective-permute-start.13 = (f32[2,6,16,256]{3,2,1,0:T(8,128)S(1)}, f32[2,6,16,256]{3,2,1,0:T(8,128)S(1)}, u32[]{:S(2)}, u32[]{:S(2)}) collective-permute-start(f32[2,6,16,256]{3,2,1,0:T(8,128)S(1)} %collective-permute-done.12.refs_3_), channel_id=1, source_target_pairs={{0,1},{1,0},{2,3},{3,2},{4,5},{5,4},{6,7},{7,6},{8,9},{9,8},{10,11... | collective-permute-start | bytes 589832 | tf_op jit(solution)/shard_map/ppermute | solution.py:71
  27.7 11.4 %collective-permute-start.21 = (f32[2,6,16,256]{3,2,1,0:T(8,128)S(1)}, f32[2,6,16,256]{3,2,1,0:T(8,128)S(1)}, u32[]{:S(2)}, u32[]{:S(2)}) collective-permute-start(f32[2,6,16,256]{3,2,1,0:T(8,128)S(1)} %collective-permute-done.20.refs_3_), channel_id=1, source_target_pairs={{0,1},{1,0},{2,3},{3,2},{4,5},{5,4},{6,7},{7,6},{8,9},{9,8},{10,11... | collective-permute-start | bytes 589832 | tf_op jit(solution)/shard_map/ppermute | solution.py:71
  31.9 7.3 %collective-permute-start.16 = (f32[2,6,16,256]{3,2,1,0:T(8,128)S(1)}, f32[2,6,16,256]{3,2,1,0:T(8,128)S(1)}, u32[]{:S(2)}, u32[]{:S(2)}) collective-permute-start(f32[2,6,16,256]{3,2,1,0:T(8,128)S(1)} %collective-permute-done.14.refs_5_), channel_id=1, source_target_pairs={{0,4},{1,3},{4,8},{5,1},{8,12},{9,5},{12,14},{13,9},{14,10},{15,13... | collective-permute-start | bytes 589832 | tf_op jit(solution)/shard_map/ppermute | solution.py:68
  33.9 4.7 %collective-permute-start.24 = (f32[6,16,256]{2,1,0:T(8,128)S(1)}, f32[6,16,256]{2,1,0:T(8,128)S(1)}, u32[]{:S(2)}, u32[]{:S(2)}) collective-permute-start(f32[6,16,256]{2,1,0:T(8,128)S(1)} %slice_bitcast_fusion), channel_id=1, source_target_pairs={{0,4},{1,3},{4,8},{5,1},{8,12},{9,5},{12,14},{13,9},{14,10},{15,13... | collective-permute-start | bytes 294920 | tf_op jit(solution)/shard_map/ppermute | solution.py:68
  35.5 4.6 %collective-permute-start.23 = (f32[2,6,16,256]{3,2,1,0:T(8,128)S(1)}, f32[2,6,16,256]{3,2,1,0:T(8,128)S(1)}, u32[]{:S(2)}, u32[]{:S(2)}) collective-permute-start(f32[2,6,16,256]{3,2,1,0:T(8,128)S(1)} %collective-permute-done.22.refs_5_), channel_id=1, source_target_pairs={{0,1},{1,0},{2,3},{3,2},{4,5},{5,4},{6,7},{7,6},{8,9},{9,8},{10,11... | collective-permute-start | bytes 589832 | tf_op jit(solution)/shard_map/ppermute | solution.py:71
  38.6 3.8 %collective-permute-start.15 = (f32[2,6,16,256]{3,2,1,0:T(8,128)S(1)}, f32[2,6,16,256]{3,2,1,0:T(8,128)S(1)}, u32[]{:S(2)}, u32[]{:S(2)}) collective-permute-start(f32[2,6,16,256]{3,2,1,0:T(8,128)S(1)} %collective-permute-done.14.refs_5_), channel_id=1, source_target_pairs={{0,1},{1,0},{2,3},{3,2},{4,5},{5,4},{6,7},{7,6},{8,9},{9,8},{10,11... | collective-permute-start | bytes 589832 | tf_op jit(solution)/shard_map/ppermute | solution.py:71
  39.1 4.4 %collective-permute-start.6 = (f32[2,6,16,256]{3,2,1,0:T(8,128)S(1)}, f32[2,6,16,256]{3,2,1,0:T(8,128)S(1)}, u32[]{:S(2)}, u32[]{:S(2)}) collective-permute-start(f32[2,6,16,256]{3,2,1,0:T(8,128)S(1)} %collective-permute-done.2.refs_1_), channel_id=1, source_target_pairs={{0,1},{1,0},{2,3},{3,2},{4,5},{5,4},{6,7},{7,6},{8,9},{9,8},{10,11... | collective-permute-start | bytes 589832 | tf_op jit(solution)/shard_map/ppermute | solution.py:71
  39.2 4.3 %collective-permute-start.7 = (f32[2,6,16,256]{3,2,1,0:T(8,128)S(1)}, f32[2,6,16,256]{3,2,1,0:T(8,128)S(1)}, u32[]{:S(2)}, u32[]{:S(2)}) collective-permute-start(f32[2,6,16,256]{3,2,1,0:T(8,128)S(1)} %collective-permute-done.3.refs_3_), channel_id=1, source_target_pairs={{0,1},{1,0},{2,3},{3,2},{4,5},{5,4},{6,7},{7,6},{8,9},{9,8},{10,11... | collective-permute-start | bytes 589832 | tf_op jit(solution)/shard_map/ppermute | solution.py:71
  39.9 3.6 %collective-permute-start.8 = (f32[2,6,16,256]{3,2,1,0:T(8,128)S(1)}, f32[2,6,16,256]{3,2,1,0:T(8,128)S(1)}, u32[]{:S(2)}, u32[]{:S(2)}) collective-permute-start(f32[2,6,16,256]{3,2,1,0:T(8,128)S(1)} %collective-permute-done.4.refs_5_), channel_id=1, source_target_pairs={{0,1},{1,0},{2,3},{3,2},{4,5},{5,4},{6,7},{7,6},{8,9},{9,8},{10,11... | collective-permute-start | bytes 589832 | tf_op jit(solution)/shard_map/ppermute | solution.py:71
  40.1 5.7 %collective-permute-start.5 = (f32[2,6,16,256]{3,2,1,0:T(8,128)S(1)}, f32[2,6,16,256]{3,2,1,0:T(8,128)S(1)}, u32[]{:S(2)}, u32[]{:S(2)}) collective-permute-start(f32[2,6,16,256]{3,2,1,0:T(8,128)S(1)} %collective-permute-done.4.refs_5_), channel_id=1, source_target_pairs={{0,4},{1,3},{4,8},{5,1},{8,12},{9,5},{12,14},{13,9},{14,10},{15,13... | collective-permute-start | bytes 589832 | tf_op jit(solution)/shard_map/ppermute | solution.py:68
  (3 other events, 33.8 us)

commit v10 on v9

--- a/solution.py
+++ b/solution.py
@@ -128,8 +128,8 @@
             low[self.wide :],
             [("tri", at) for at in range(len(self.tri))],
         ]
-        self.mine = self.chunks[0][:panels]
-        self.mine += [("low", panel, block) for block in range(self.wide) for panel in range(panels)]
+        later = [("low", panel, block) for block in range(self.wide) for panel in range(1, panels)]
+        self.held_as = [self.chunks[0], later, self.chunks[2]]
         self.where = {b: (c, at) for c, chunk in enumerate(self.chunks) for at, b in enumerate(chunk)}
 
     def tri_of(self, rank):
@@ -153,16 +153,17 @@
         return self.chosen(owner, [right_ref[rows]] + [r[rows] for r in received])
 
 
-def load_kernel(plan, factor_hbm, inv_hbm, mine_ref, own_ref, sems):
+def load_kernel(plan, factor_hbm, inv_hbm, inv_ref, low_ref, own_ref, sems):
     panels, nb = plan.panels, plan.nb
-    copies = [(inv_hbm, mine_ref.at[:panels])]
+    copies = [(inv_hbm, inv_ref.at[:panels])]
     for local, deep in enumerate(plan.deep):
         source = factor_hbm.at[:deep, :, local * nb : (local + 1) * nb]
         copies.append((source, own_ref.at[pl.ds(plan.sent.index((local, 0)), deep)]))
     for block in range(plan.wide):
         at = (plan.sure + block) * nb
-        to = plan.mine.index(("low", 0, block))
-        copies.append((factor_hbm.at[:, :, at : at + nb], mine_ref.at[to : to + panels]))
+        copies.append((factor_hbm.at[:1, :, at : at + nb], inv_ref.at[panels + block : panels + block + 1]))
+        to = pl.ds(block * (panels - 1), panels - 1)
+        copies.append((factor_hbm.at[1:, :, at : at + nb], low_ref.at[to]))
     copies = [pltpu.make_async_copy(*pair, sems.at[n]) for n, pair in enumerate(copies)]
     for copy in copies:
         copy.start()
@@ -308,14 +309,15 @@
     shape = jax.ShapeDtypeStruct
     bound = functools.partial
 
-    mine, own = kernel_call(
+    mine, later, own = kernel_call(
         bound(load_kernel, plan),
-        [shape((len(plan.mine), depth, nb), f32), shape((len(plan.sent), depth, nb), f32)],
-        [pltpu.SemaphoreType.DMA((1 + plan.held + plan.wide,))],
+        [shape((len(b), depth, nb), f32) for b in (plan.chunks[0], plan.chunks[1], plan.sent)],
+        [pltpu.SemaphoreType.DMA((1 + plan.held + 2 * plan.wide,))],
         [pltpu.with_memory_space_constraint(a, pltpu.HBM) for a in (factor_panels, inverses)],
         in_hbm=2,
     )
-    other = lax.ppermute(mine, "col", swap)
+    mine_other = lax.ppermute(mine, "col", swap)
+    later_other = lax.ppermute(later, "col", swap)
     tri = [own] + [lax.ppermute(own, "row", pairs) for pairs in shifts]
     above = right_side[: plan.held * nb]
     received = [lax.ppermute(above, "row", pairs) for pairs in shifts]
@@ -324,12 +326,11 @@
 
     pieces = []
     for chunk, blocks in enumerate(plan.chunks):
-        last = chunk == len(plan.chunks) - 1
         packed = kernel_call(
-            bound(pack_kernel, blocks if last else plan.mine, blocks),
+            bound(pack_kernel, plan.held_as[chunk], blocks),
             shape((2, len(blocks), depth, nb), f32),
             [],
-            (half, half_other) if last else (mine, other),
+            ((mine, mine_other), (later, later_other), (half, half_other))[chunk],
         )
         pieces.append(ring(packed, chips, halves=chunk == 1 and depth % 16 == 0))
 

time: 48.8 us -> 45.3 us (0.928)
  starting transfers between devices: 28.7 us -> 24.7 us
  waiting for transfers between devices: 12.4 us -> 13.9 us
  local copies, waits for them, and re-layouts: 1.09 us -> 0.05 us
    ppermute x12, starting transfers between devices: 23.7 us -> 19.8 us  [ring(): lax.ppermute(moving[0] if last and halves else moving, 'col', nearest)]
    ppermute x1, waiting for transfers between devices: 1.1 us -> 2.74 us  [per_device(): tri = [own] + [lax.ppermute(own, 'row', pairs) for pairs in shifts]]
    ppermute x1, waiting for transfers between devices: 1.29 us -> 0.01 us  [per_device(): half_other = lax.ppermute(half, 'col', swap)]
    ppermute x10, starting transfers between devices: 2.26 us -> 1.1 us  [ring(): pieces.append(lax.ppermute(moving, 'col', swap))]
    slice x1, local copies, waits for them, and re-layouts: 1.08 us -> 0.03 us  [per_device(): above = right_side[:plan.held * nb]]
    ppermute x1, starting transfers between devices: 0.57 us -> 1.58 us  [per_device(): received = [lax.ppermute(above, 'row', pairs) for pairs in shifts]]
    ppermute x12, waiting for transfers between devices: 8.68 us -> 9.47 us  [ring(): lax.ppermute(moving[0] if last and halves else moving, 'col', nearest)]
    ppermute x1 -> x2, waiting for transfers between devices: 1.07 us -> 0.95 us  [the longest x1 0.94 us: per_device(): later_other = lax.ppermute(later, 'col', swap)]
  transfers between devices with their start and end apart: 26 -> 27, of which waited for: 12 -> 10; matrix products, arithmetic and copies ran while one was open for 2% -> 0% of each run, Pallas kernels for 5% -> 5%
where the time goes in v10:
time: 45.3 us; the launch traced here: 45.1 us
  starting transfers between devices  24.7 us (55%)
  waiting for transfers between devices  13.9 us (31%)
  Pallas kernels  6.39 us (14%)
    ppermute x12, starting transfers between devices, ring(): lax.ppermute(moving[0] if last and halves else moving, 'col', nearest)  19.8 us
    ppermute x12, waiting for transfers between devices, ring(): lax.ppermute(moving[0] if last and halves else moving, 'col', nearest)  9.47 us
    pallas_call x9, Pallas kernels, kernel_call(): pl.pallas_call(body, out_shape=out_shapes, in_specs=[hbm] * in_hbm + [nea...  6.39 us
    ppermute x1, waiting for transfers between devices, per_device(): tri = [own] + [lax.ppermute(own, 'row', pairs) for pairs in shifts]  2.74 us
    ppermute x1, starting transfers between devices, per_device(): received = [lax.ppermute(above, 'row', pairs) for pairs in shifts]  1.58 us
    ppermute x1, starting transfers between devices, per_device(): tri = [own] + [lax.ppermute(own, 'row', pairs) for pairs in shifts]  1.52 us
    ppermute x10, starting transfers between devices, ring(): pieces.append(lax.ppermute(moving, 'col', swap))  1.1 us
    ppermute x1, waiting for transfers between devices, per_device(): later_other = lax.ppermute(later, 'col', swap)  0.94 us
  transfers between devices with their start and end apart: 27, of which 10 were waited for; matrix products, arithmetic and copies ran while one was open for 0% of the time, Pallas kernels for 5%

profile of v10, /device:TPU:0, one launch (start us, length us, event | category | flops | bytes accessed | tf_op | source)
XLA Modules:
  0.0 45.1 jit_solution(13847479572564511124)
XLA Ops:
  0.0 1.1 %shard_map.37 = (f32[6,16,256]{2,1,0:T(8,128)S(1)}, f32[6,16,256]{2,1,0:T(8,128)S(1)}, f32[4,16,256]{2,1,0:T(8,128)S(1)}) custom-call(f32[4,16,1024]{2,1,0:T(8,128)} %factor_hbm.1, f32[4,16,256]{2,1,0:T(8,128)} %inv_hbm.1), custom_call_target="tpu_custom_call" | custom-call | bytes 4194304 | tf_op jit(solution)/shard_map/pallas_call | solution.py:42
  2.6 3.0 %collective-permute-start.19 = (f32[2,6,16,256]{3,2,1,0:T(8,128)S(1)}, f32[2,6,16,256]{3,2,1,0:T(8,128)S(1)}, u32[]{:S(2)}, u32[]{:S(2)}) collective-permute-start(f32[2,6,16,256]{3,2,1,0:T(8,128)S(1)} %shard_map.43.refs_0_), channel_id=1, source_target_pairs={{0,4},{1,3},{4,8},{5,1},{8,12},{9,5},{12,14},{13,9},{14,10},{15,13... | collective-permute-start | bytes 589832 | tf_op jit(solution)/shard_map/ppermute | solution.py:68
  5.6 1.5 %collective-permute-start = (f32[4,16,256]{2,1,0:T(8,128)S(1)}, f32[4,16,256]{2,1,0:T(8,128)S(1)}, u32[]{:S(2)}, u32[]{:S(2)}) collective-permute-start(f32[4,16,256]{2,1,0:T(8,128)S(1)} %get-tuple-element.17.refs_0_), channel_id=1, source_target_pairs={{16,0},{0,16},{17,1},{1,17},{18,2},{2,18},{19,3},{3,19},{20,4},{4,... | collective-permute-start | bytes 196616 | tf_op jit(solution)/shard_map/ppermute | solution.py:321
  7.1 2.7 %collective-permute-done.refs_1_ = f32[4,16,256]{2,1,0:T(8,128)S(1)} collective-permute-done((f32[4,16,256]{2,1,0:T(8,128)S(1)}, f32[4,16,256]{2,1,0:T(8,128)S(1)}, u32[]{:S(2)}, u32[]{:S(2)}) %collective-permute-start) | collective-permute-done | bytes 65568 | tf_op jit(solution)/shard_map/ppermute | solution.py:321
  10.0 1.6 %collective-permute-start.10 = (f32[2,6,16,256]{3,2,1,0:T(8,128)S(1)}, f32[2,6,16,256]{3,2,1,0:T(8,128)S(1)}, u32[]{:S(2)}, u32[]{:S(2)}) collective-permute-start(f32[2,6,16,256]{3,2,1,0:T(8,128)S(1)} %shard_map.40.refs_0_), channel_id=1, source_target_pairs={{0,4},{1,3},{4,8},{5,1},{8,12},{9,5},{12,14},{13,9},{14,10},{15,13... | collective-permute-start | bytes 589832 | tf_op jit(solution)/shard_map/ppermute | solution.py:68
  11.6 1.6 %collective-permute-start.2 = (f32[2,6,16,256]{3,2,1,0:T(8,128)S(1)}, f32[2,6,16,256]{3,2,1,0:T(8,128)S(1)}, u32[]{:S(2)}, u32[]{:S(2)}) collective-permute-start(f32[2,6,16,256]{3,2,1,0:T(8,128)S(1)} %shard_map.39.refs_0_), channel_id=1, source_target_pairs={{0,4},{1,3},{4,8},{5,1},{8,12},{9,5},{12,14},{13,9},{14,10},{15,13... | collective-permute-start | bytes 589832 | tf_op jit(solution)/shard_map/ppermute | solution.py:68
  13.3 1.5 %collective-permute-start.21 = (f32[2,6,16,256]{3,2,1,0:T(8,128)S(1)}, f32[2,6,16,256]{3,2,1,0:T(8,128)S(1)}, u32[]{:S(2)}, u32[]{:S(2)}) collective-permute-start(f32[2,6,16,256]{3,2,1,0:T(8,128)S(1)} %collective-permute-done.19.refs_1_), channel_id=1, source_target_pairs={{0,4},{1,3},{4,8},{5,1},{8,12},{9,5},{12,14},{13,9},{14,10},{15,13... | collective-permute-start | bytes 589832 | tf_op jit(solution)/shard_map/ppermute | solution.py:68
  14.8 1.6 %collective-permute-start.17 = (f32[512,256]{1,0:T(8,128)S(1)}, f32[512,256]{1,0:T(8,128)S(1)}, u32[]{:S(2)}, u32[]{:S(2)}) collective-permute-start(f32[512,256]{1,0:T(8,128)S(1)} %slice.6), channel_id=1, source_target_pairs={{16,0},{0,16},{17,1},{1,17},{18,2},{2,18},{19,3},{3,19},{20,4},{4,... | collective-permute-start | bytes 1572872 | tf_op jit(solution)/shard_map/ppermute | solution.py:323
  16.4 1.2 %collective-permute-start.12 = (f32[2,6,16,256]{3,2,1,0:T(8,128)S(1)}, f32[2,6,16,256]{3,2,1,0:T(8,128)S(1)}, u32[]{:S(2)}, u32[]{:S(2)}) collective-permute-start(f32[2,6,16,256]{3,2,1,0:T(8,128)S(1)} %collective-permute-done.10.refs_1_), channel_id=1, source_target_pairs={{0,4},{1,3},{4,8},{5,1},{8,12},{9,5},{12,14},{13,9},{14,10},{15,13... | collective-permute-start | bytes 589832 | tf_op jit(solution)/shard_map/ppermute | solution.py:68
  17.8 2.1 %collective-permute-done.21.refs_3_ = f32[2,6,16,256]{3,2,1,0:T(8,128)S(1)} collective-permute-done((f32[2,6,16,256]{3,2,1,0:T(8,128)S(1)}, f32[2,6,16,256]{3,2,1,0:T(8,128)S(1)}, u32[]{:S(2)}, u32[]{:S(2)}) %collective-permute-start.21) | collective-permute-done | bytes 196640 | tf_op jit(solution)/shard_map/ppermute | solution.py:68
  19.9 1.6 %collective-permute-start.23 = (f32[2,6,16,256]{3,2,1,0:T(8,128)S(1)}, f32[2,6,16,256]{3,2,1,0:T(8,128)S(1)}, u32[]{:S(2)}, u32[]{:S(2)}) collective-permute-start(f32[2,6,16,256]{3,2,1,0:T(8,128)S(1)} %collective-permute-done.21.refs_3_), channel_id=1, source_target_pairs={{0,4},{1,3},{4,8},{5,1},{8,12},{9,5},{12,14},{13,9},{14,10},{15,13... | collective-permute-start | bytes 589832 | tf_op jit(solution)/shard_map/ppermute | solution.py:68
  21.5 1.6 %collective-permute-start.3 = (f32[2,6,16,256]{3,2,1,0:T(8,128)S(1)}, f32[2,6,16,256]{3,2,1,0:T(8,128)S(1)}, u32[]{:S(2)}, u32[]{:S(2)}) collective-permute-start(f32[2,6,16,256]{3,2,1,0:T(8,128)S(1)} %collective-permute-done.2.refs_1_), channel_id=1, source_target_pairs={{0,4},{1,3},{4,8},{5,1},{8,12},{9,5},{12,14},{13,9},{14,10},{15,13... | collective-permute-start | bytes 589832 | tf_op jit(solution)/shard_map/ppermute | solution.py:68
  23.1 1.5 %collective-permute-start.14 = (f32[2,6,16,256]{3,2,1,0:T(8,128)S(1)}, f32[2,6,16,256]{3,2,1,0:T(8,128)S(1)}, u32[]{:S(2)}, u32[]{:S(2)}) collective-permute-start(f32[2,6,16,256]{3,2,1,0:T(8,128)S(1)} %collective-permute-done.12.refs_3_), channel_id=1, source_target_pairs={{0,4},{1,3},{4,8},{5,1},{8,12},{9,5},{12,14},{13,9},{14,10},{15,13... | collective-permute-start | bytes 589832 | tf_op jit(solution)/shard_map/ppermute | solution.py:68
  24.6 1.0 %collective-permute-done.23.refs_5_ = f32[2,6,16,256]{3,2,1,0:T(8,128)S(1)} collective-permute-done((f32[2,6,16,256]{3,2,1,0:T(8,128)S(1)}, f32[2,6,16,256]{3,2,1,0:T(8,128)S(1)}, u32[]{:S(2)}, u32[]{:S(2)}) %collective-permute-start.23) | collective-permute-done | bytes 196640 | tf_op jit(solution)/shard_map/ppermute | solution.py:68
  25.6 2.1 %collective-permute-done.3.refs_3_ = f32[2,6,16,256]{3,2,1,0:T(8,128)S(1)} collective-permute-done((f32[2,6,16,256]{3,2,1,0:T(8,128)S(1)}, f32[2,6,16,256]{3,2,1,0:T(8,128)S(1)}, u32[]{:S(2)}, u32[]{:S(2)}) %collective-permute-start.3) | collective-permute-done | bytes 196640 | tf_op jit(solution)/shard_map/ppermute | solution.py:68
  27.7 1.6 %collective-permute-start.4 = (f32[2,6,16,256]{3,2,1,0:T(8,128)S(1)}, f32[2,6,16,256]{3,2,1,0:T(8,128)S(1)}, u32[]{:S(2)}, u32[]{:S(2)}) collective-permute-start(f32[2,6,16,256]{3,2,1,0:T(8,128)S(1)} %collective-permute-done.3.refs_3_), channel_id=1, source_target_pairs={{0,4},{1,3},{4,8},{5,1},{8,12},{9,5},{12,14},{13,9},{14,10},{15,13... | collective-permute-start | bytes 589832 | tf_op jit(solution)/shard_map/ppermute | solution.py:68
  29.3 1.6 %collective-permute-start.25 = (f32[6,16,256]{2,1,0:T(8,128)S(1)}, f32[6,16,256]{2,1,0:T(8,128)S(1)}, u32[]{:S(2)}, u32[]{:S(2)}) collective-permute-start(f32[6,16,256]{2,1,0:T(8,128)S(1)} %slice_bitcast_fusion), channel_id=1, source_target_pairs={{0,4},{1,3},{4,8},{5,1},{8,12},{9,5},{12,14},{13,9},{14,10},{15,13... | collective-permute-start | bytes 294920 | tf_op jit(solution)/shard_map/ppermute | solution.py:68
  30.9 1.5 %collective-permute-start.16 = (f32[2,6,16,256]{3,2,1,0:T(8,128)S(1)}, f32[2,6,16,256]{3,2,1,0:T(8,128)S(1)}, u32[]{:S(2)}, u32[]{:S(2)}) collective-permute-start(f32[2,6,16,256]{3,2,1,0:T(8,128)S(1)} %collective-permute-done.14.refs_5_), channel_id=1, source_target_pairs={{0,4},{1,3},{4,8},{5,1},{8,12},{9,5},{12,14},{13,9},{14,10},{15,13... | collective-permute-start | bytes 589832 | tf_op jit(solution)/shard_map/ppermute | solution.py:68
  32.4 2.0 %collective-permute-done.25.refs_7_ = f32[6,16,256]{2,1,0:T(8,128)S(1)} collective-permute-done((f32[6,16,256]{2,1,0:T(8,128)S(1)}, f32[6,16,256]{2,1,0:T(8,128)S(1)}, u32[]{:S(2)}, u32[]{:S(2)}) %collective-permute-start.25) | collective-permute-done | bytes 98336 | tf_op jit(solution)/shard_map/ppermute | solution.py:68
  36.6 1.5 %collective-permute-start.5 = (f32[2,6,16,256]{3,2,1,0:T(8,128)S(1)}, f32[2,6,16,256]{3,2,1,0:T(8,128)S(1)}, u32[]{:S(2)}, u32[]{:S(2)}) collective-permute-start(f32[2,6,16,256]{3,2,1,0:T(8,128)S(1)} %collective-permute-done.4.refs_5_), channel_id=1, source_target_pairs={{0,4},{1,3},{4,8},{5,1},{8,12},{9,5},{12,14},{13,9},{14,10},{15,13... | collective-permute-start | bytes 589832 | tf_op jit(solution)/shard_map/ppermute | solution.py:68
  38.4 1.1 %shard_map.41 = (bf16[6,256,256]{2,1,0:T(8,128)(2,1)S(1)}, bf16[6,256,256]{2,1,0:T(8,128)(2,1)S(1)}, f32[4,256,256]{2,1,0:T(8,128)S(1)}, f32[512,256]{1,0:T(8,128)S(1)}) custom-call(f32[2,6,16,256]{3,2,1,0:T(8,128)S(1)} %shard_map.40.refs_0_, f32[2,6,16,256]{3,2,1,0:T(8,128)S(1)} %collective-permute-done.10.refs_1_, ...), custom_call_target="tpu_custom_call" | custom-call | flops 301989888 | bytes 4194304 | tf_op jit(solution)/shard_map/pallas_call | solution.py:42
  39.5 1.0 %shard_map.42 = (bf16[6,256,256]{2,1,0:T(8,128)(2,1)S(1)}, bf16[6,256,256]{2,1,0:T(8,128)(2,1)S(1)}) custom-call(f32[2,6,16,256]{3,2,1,0:T(8,128)S(1)} %shard_map.39.refs_0_, f32[2,6,16,256]{3,2,1,0:T(8,128)S(1)} %collective-permute-done.2.refs_1_, f32[2,6,16,256]{3,2,1,0:T(8,128)S(1)} %collective-permute-done.6.refs_2_, ...), custom_call_target="tpu_custom_call" | custom-call | flops 603979776 | bytes 4194304 | tf_op jit(solution)/shard_map/pallas_call | solution.py:42
  40.5 1.7 %collective-permute-done.5.refs_0_ = f32[2,6,16,256]{3,2,1,0:T(8,128)S(1)} collective-permute-done((f32[2,6,16,256]{3,2,1,0:T(8,128)S(1)}, f32[2,6,16,256]{3,2,1,0:T(8,128)S(1)}, u32[]{:S(2)}, u32[]{:S(2)}) %collective-permute-start.5) | collective-permute-done | bytes 196640 | tf_op jit(solution)/shard_map/ppermute | solution.py:68
  42.2 2.9 %shard_map.45 = (f32[1024,256]{1,0:T(8,128)}, bf16[6,256,256]{2,1,0:T(8,128)(2,1)S(1)}, bf16[6,256,256]{2,1,0:T(8,128)(2,1)S(1)}) custom-call(f32[2,6,16,256]{3,2,1,0:T(8,128)S(1)} %collective-permute-done.5.refs_0_, bf16[6,256,256]{2,1,0:T(8,128)(2,1)S(1)} %get-tuple-element.21.refs_1_, ...), custom_call_target="tpu_custom_call", output_to_operand_aliasing={{1}: (1, {}), {2}: (2, {})} | custom-call | flops 1509949440 | bytes 4194304 | tf_op jit(solution)/shard_map/pallas_call | solution.py:42
  (43 shorter events, 4.4 us)
Async XLA Ops:
  2.6 10.6 %collective-permute-start.19 = (f32[2,6,16,256]{3,2,1,0:T(8,128)S(1)}, f32[2,6,16,256]{3,2,1,0:T(8,128)S(1)}, u32[]{:S(2)}, u32[]{:S(2)}) collective-permute-start(f32[2,6,16,256]{3,2,1,0:T(8,128)S(1)} %shard_map.43.refs_0_), channel_id=1, source_target_pairs={{0,4},{1,3},{4,8},{5,1},{8,12},{9,5},{12,14},{13,9},{14,10},{15,13... | collective-permute-start | bytes 589832 | tf_op jit(solution)/shard_map/ppermute | solution.py:68
  5.6 4.3 %collective-permute-start = (f32[4,16,256]{2,1,0:T(8,128)S(1)}, f32[4,16,256]{2,1,0:T(8,128)S(1)}, u32[]{:S(2)}, u32[]{:S(2)}) collective-permute-start(f32[4,16,256]{2,1,0:T(8,128)S(1)} %get-tuple-element.17.refs_0_), channel_id=1, source_target_pairs={{16,0},{0,16},{17,1},{1,17},{18,2},{2,18},{19,3},{3,19},{20,4},{4,... | collective-permute-start | bytes 196616 | tf_op jit(solution)/shard_map/ppermute | solution.py:321
  7.1 2.8 %collective-permute-start.9 = (f32[6,16,256]{2,1,0:T(8,128)S(1)}, f32[6,16,256]{2,1,0:T(8,128)S(1)}, u32[]{:S(2)}, u32[]{:S(2)}) collective-permute-start(f32[6,16,256]{2,1,0:T(8,128)S(1)} %get-tuple-element.18.own_ref), channel_id=1, source_target_pairs={{0,1},{1,0},{2,3},{3,2},{4,5},{5,4},{6,7},{7,6},{8,9},{9,8},{10,11... | collective-permute-start | bytes 294920 | tf_op jit(solution)/shard_map/ppermute | solution.py:319
  10.0 6.4 %collective-permute-start.10 = (f32[2,6,16,256]{3,2,1,0:T(8,128)S(1)}, f32[2,6,16,256]{3,2,1,0:T(8,128)S(1)}, u32[]{:S(2)}, u32[]{:S(2)}) collective-permute-start(f32[2,6,16,256]{3,2,1,0:T(8,128)S(1)} %shard_map.40.refs_0_), channel_id=1, source_target_pairs={{0,4},{1,3},{4,8},{5,1},{8,12},{9,5},{12,14},{13,9},{14,10},{15,13... | collective-permute-start | bytes 589832 | tf_op jit(solution)/shard_map/ppermute | solution.py:68
  11.6 6.2 %collective-permute-start.2 = (f32[2,6,16,256]{3,2,1,0:T(8,128)S(1)}, f32[2,6,16,256]{3,2,1,0:T(8,128)S(1)}, u32[]{:S(2)}, u32[]{:S(2)}) collective-permute-start(f32[2,6,16,256]{3,2,1,0:T(8,128)S(1)} %shard_map.39.refs_0_), channel_id=1, source_target_pairs={{0,4},{1,3},{4,8},{5,1},{8,12},{9,5},{12,14},{13,9},{14,10},{15,13... | collective-permute-start | bytes 589832 | tf_op jit(solution)/shard_map/ppermute | solution.py:68
  13.3 6.7 %collective-permute-start.21 = (f32[2,6,16,256]{3,2,1,0:T(8,128)S(1)}, f32[2,6,16,256]{3,2,1,0:T(8,128)S(1)}, u32[]{:S(2)}, u32[]{:S(2)}) collective-permute-start(f32[2,6,16,256]{3,2,1,0:T(8,128)S(1)} %collective-permute-done.19.refs_1_), channel_id=1, source_target_pairs={{0,4},{1,3},{4,8},{5,1},{8,12},{9,5},{12,14},{13,9},{14,10},{15,13... | collective-permute-start | bytes 589832 | tf_op jit(solution)/shard_map/ppermute | solution.py:68
  14.8 14.5 %collective-permute-start.17 = (f32[512,256]{1,0:T(8,128)S(1)}, f32[512,256]{1,0:T(8,128)S(1)}, u32[]{:S(2)}, u32[]{:S(2)}) collective-permute-start(f32[512,256]{1,0:T(8,128)S(1)} %slice.6), channel_id=1, source_target_pairs={{16,0},{0,16},{17,1},{1,17},{18,2},{2,18},{19,3},{3,19},{20,4},{4,... | collective-permute-start | bytes 1572872 | tf_op jit(solution)/shard_map/ppermute | solution.py:323
  16.4 5.1 %collective-permute-start.20 = (f32[2,6,16,256]{3,2,1,0:T(8,128)S(1)}, f32[2,6,16,256]{3,2,1,0:T(8,128)S(1)}, u32[]{:S(2)}, u32[]{:S(2)}) collective-permute-start(f32[2,6,16,256]{3,2,1,0:T(8,128)S(1)} %collective-permute-done.19.refs_1_), channel_id=1, source_target_pairs={{0,1},{1,0},{2,3},{3,2},{4,5},{5,4},{6,7},{7,6},{8,9},{9,8},{10,11... | collective-permute-start | bytes 589832 | tf_op jit(solution)/shard_map/ppermute | solution.py:71
  16.4 6.7 %collective-permute-start.12 = (f32[2,6,16,256]{3,2,1,0:T(8,128)S(1)}, f32[2,6,16,256]{3,2,1,0:T(8,128)S(1)}, u32[]{:S(2)}, u32[]{:S(2)}) collective-permute-start(f32[2,6,16,256]{3,2,1,0:T(8,128)S(1)} %collective-permute-done.10.refs_1_), channel_id=1, source_target_pairs={{0,4},{1,3},{4,8},{5,1},{8,12},{9,5},{12,14},{13,9},{14,10},{15,13... | collective-permute-start | bytes 589832 | tf_op jit(solution)/shard_map/ppermute | solution.py:68
  17.8 5.3 %collective-permute-start.11 = (f32[2,6,16,256]{3,2,1,0:T(8,128)S(1)}, f32[2,6,16,256]{3,2,1,0:T(8,128)S(1)}, u32[]{:S(2)}, u32[]{:S(2)}) collective-permute-start(f32[2,6,16,256]{3,2,1,0:T(8,128)S(1)} %collective-permute-done.10.refs_1_), channel_id=1, source_target_pairs={{0,1},{1,0},{2,3},{3,2},{4,5},{5,4},{6,7},{7,6},{8,9},{9,8},{10,11... | collective-permute-start | bytes 589832 | tf_op jit(solution)/shard_map/ppermute | solution.py:71
  19.9 5.7 %collective-permute-start.23 = (f32[2,6,16,256]{3,2,1,0:T(8,128)S(1)}, f32[2,6,16,256]{3,2,1,0:T(8,128)S(1)}, u32[]{:S(2)}, u32[]{:S(2)}) collective-permute-start(f32[2,6,16,256]{3,2,1,0:T(8,128)S(1)} %collective-permute-done.21.refs_3_), channel_id=1, source_target_pairs={{0,4},{1,3},{4,8},{5,1},{8,12},{9,5},{12,14},{13,9},{14,10},{15,13... | collective-permute-start | bytes 589832 | tf_op jit(solution)/shard_map/ppermute | solution.py:68
  21.5 6.2 %collective-permute-start.3 = (f32[2,6,16,256]{3,2,1,0:T(8,128)S(1)}, f32[2,6,16,256]{3,2,1,0:T(8,128)S(1)}, u32[]{:S(2)}, u32[]{:S(2)}) collective-permute-start(f32[2,6,16,256]{3,2,1,0:T(8,128)S(1)} %collective-permute-done.2.refs_1_), channel_id=1, source_target_pairs={{0,4},{1,3},{4,8},{5,1},{8,12},{9,5},{12,14},{13,9},{14,10},{15,13... | collective-permute-start | bytes 589832 | tf_op jit(solution)/shard_map/ppermute | solution.py:68
  23.1 7.8 %collective-permute-start.22 = (f32[2,6,16,256]{3,2,1,0:T(8,128)S(1)}, f32[2,6,16,256]{3,2,1,0:T(8,128)S(1)}, u32[]{:S(2)}, u32[]{:S(2)}) collective-permute-start(f32[2,6,16,256]{3,2,1,0:T(8,128)S(1)} %collective-permute-done.21.refs_3_), channel_id=1, source_target_pairs={{0,1},{1,0},{2,3},{3,2},{4,5},{5,4},{6,7},{7,6},{8,9},{9,8},{10,11... | collective-permute-start | bytes 589832 | tf_op jit(solution)/shard_map/ppermute | solution.py:71
  23.1 7.8 %collective-permute-start.14 = (f32[2,6,16,256]{3,2,1,0:T(8,128)S(1)}, f32[2,6,16,256]{3,2,1,0:T(8,128)S(1)}, u32[]{:S(2)}, u32[]{:S(2)}) collective-permute-start(f32[2,6,16,256]{3,2,1,0:T(8,128)S(1)} %collective-permute-done.12.refs_3_), channel_id=1, source_target_pairs={{0,4},{1,3},{4,8},{5,1},{8,12},{9,5},{12,14},{13,9},{14,10},{15,13... | collective-permute-start | bytes 589832 | tf_op jit(solution)/shard_map/ppermute | solution.py:68
  25.6 8.8 %collective-permute-start.13 = (f32[2,6,16,256]{3,2,1,0:T(8,128)S(1)}, f32[2,6,16,256]{3,2,1,0:T(8,128)S(1)}, u32[]{:S(2)}, u32[]{:S(2)}) collective-permute-start(f32[2,6,16,256]{3,2,1,0:T(8,128)S(1)} %collective-permute-done.12.refs_3_), channel_id=1, source_target_pairs={{0,1},{1,0},{2,3},{3,2},{4,5},{5,4},{6,7},{7,6},{8,9},{9,8},{10,11... | collective-permute-start | bytes 589832 | tf_op jit(solution)/shard_map/ppermute | solution.py:71
  27.7 7.2 %collective-permute-start.4 = (f32[2,6,16,256]{3,2,1,0:T(8,128)S(1)}, f32[2,6,16,256]{3,2,1,0:T(8,128)S(1)}, u32[]{:S(2)}, u32[]{:S(2)}) collective-permute-start(f32[2,6,16,256]{3,2,1,0:T(8,128)S(1)} %collective-permute-done.3.refs_3_), channel_id=1, source_target_pairs={{0,4},{1,3},{4,8},{5,1},{8,12},{9,5},{12,14},{13,9},{14,10},{15,13... | collective-permute-start | bytes 589832 | tf_op jit(solution)/shard_map/ppermute | solution.py:68
  29.3 5.1 %collective-permute-start.25 = (f32[6,16,256]{2,1,0:T(8,128)S(1)}, f32[6,16,256]{2,1,0:T(8,128)S(1)}, u32[]{:S(2)}, u32[]{:S(2)}) collective-permute-start(f32[6,16,256]{2,1,0:T(8,128)S(1)} %slice_bitcast_fusion), channel_id=1, source_target_pairs={{0,4},{1,3},{4,8},{5,1},{8,12},{9,5},{12,14},{13,9},{14,10},{15,13... | collective-permute-start | bytes 294920 | tf_op jit(solution)/shard_map/ppermute | solution.py:68
  30.8 5.0 %collective-permute-start.24 = (f32[2,6,16,256]{3,2,1,0:T(8,128)S(1)}, f32[2,6,16,256]{3,2,1,0:T(8,128)S(1)}, u32[]{:S(2)}, u32[]{:S(2)}) collective-permute-start(f32[2,6,16,256]{3,2,1,0:T(8,128)S(1)} %collective-permute-done.23.refs_5_), channel_id=1, source_target_pairs={{0,1},{1,0},{2,3},{3,2},{4,5},{5,4},{6,7},{7,6},{8,9},{9,8},{10,11... | collective-permute-start | bytes 589832 | tf_op jit(solution)/shard_map/ppermute | solution.py:71
  30.9 5.7 %collective-permute-start.16 = (f32[2,6,16,256]{3,2,1,0:T(8,128)S(1)}, f32[2,6,16,256]{3,2,1,0:T(8,128)S(1)}, u32[]{:S(2)}, u32[]{:S(2)}) collective-permute-start(f32[2,6,16,256]{3,2,1,0:T(8,128)S(1)} %collective-permute-done.14.refs_5_), channel_id=1, source_target_pairs={{0,4},{1,3},{4,8},{5,1},{8,12},{9,5},{12,14},{13,9},{14,10},{15,13... | collective-permute-start | bytes 589832 | tf_op jit(solution)/shard_map/ppermute | solution.py:68
  34.4 4.0 %collective-permute-start.15 = (f32[2,6,16,256]{3,2,1,0:T(8,128)S(1)}, f32[2,6,16,256]{3,2,1,0:T(8,128)S(1)}, u32[]{:S(2)}, u32[]{:S(2)}) collective-permute-start(f32[2,6,16,256]{3,2,1,0:T(8,128)S(1)} %collective-permute-done.14.refs_5_), channel_id=1, source_target_pairs={{0,1},{1,0},{2,3},{3,2},{4,5},{5,4},{6,7},{7,6},{8,9},{9,8},{10,11... | collective-permute-start | bytes 589832 | tf_op jit(solution)/shard_map/ppermute | solution.py:71
  34.9 4.6 %collective-permute-start.6 = (f32[2,6,16,256]{3,2,1,0:T(8,128)S(1)}, f32[2,6,16,256]{3,2,1,0:T(8,128)S(1)}, u32[]{:S(2)}, u32[]{:S(2)}) collective-permute-start(f32[2,6,16,256]{3,2,1,0:T(8,128)S(1)} %collective-permute-done.2.refs_1_), channel_id=1, source_target_pairs={{0,1},{1,0},{2,3},{3,2},{4,5},{5,4},{6,7},{7,6},{8,9},{9,8},{10,11... | collective-permute-start | bytes 589832 | tf_op jit(solution)/shard_map/ppermute | solution.py:71
  35.7 3.8 %collective-permute-start.7 = (f32[2,6,16,256]{3,2,1,0:T(8,128)S(1)}, f32[2,6,16,256]{3,2,1,0:T(8,128)S(1)}, u32[]{:S(2)}, u32[]{:S(2)}) collective-permute-start(f32[2,6,16,256]{3,2,1,0:T(8,128)S(1)} %collective-permute-done.3.refs_3_), channel_id=1, source_target_pairs={{0,1},{1,0},{2,3},{3,2},{4,5},{5,4},{6,7},{7,6},{8,9},{9,8},{10,11... | collective-permute-start | bytes 589832 | tf_op jit(solution)/shard_map/ppermute | solution.py:71
  35.9 3.6 %collective-permute-start.8 = (f32[2,6,16,256]{3,2,1,0:T(8,128)S(1)}, f32[2,6,16,256]{3,2,1,0:T(8,128)S(1)}, u32[]{:S(2)}, u32[]{:S(2)}) collective-permute-start(f32[2,6,16,256]{3,2,1,0:T(8,128)S(1)} %collective-permute-done.4.refs_5_), channel_id=1, source_target_pairs={{0,1},{1,0},{2,3},{3,2},{4,5},{5,4},{6,7},{7,6},{8,9},{9,8},{10,11... | collective-permute-start | bytes 589832 | tf_op jit(solution)/shard_map/ppermute | solution.py:71
  36.6 5.7 %collective-permute-start.5 = (f32[2,6,16,256]{3,2,1,0:T(8,128)S(1)}, f32[2,6,16,256]{3,2,1,0:T(8,128)S(1)}, u32[]{:S(2)}, u32[]{:S(2)}) collective-permute-start(f32[2,6,16,256]{3,2,1,0:T(8,128)S(1)} %collective-permute-done.4.refs_5_), channel_id=1, source_target_pairs={{0,4},{1,3},{4,8},{5,1},{8,12},{9,5},{12,14},{13,9},{14,10},{15,13... | collective-permute-start | bytes 589832 | tf_op jit(solution)/shard_map/ppermute | solution.py:68
  (4 other events, 19.3 us)

commit v11 on v10

--- a/solution.py
+++ b/solution.py
@@ -9,7 +9,6 @@
 
 ROWS = ((0,), (0,))
 PLAIN = ((1,), (0,))
-ABOVE = ((1,), (1,))
 
 
 def ring_place(chip, chips):
@@ -197,6 +196,9 @@
         start_ref[panel] = answer
         if panel == 0:
             solved = split(answer)
+        else:
+            at = plan.where[("inv", panel)][1]
+            high_ref[at], low_ref[at] = high_ref[at].T, low_ref[at].T
     for block in range(plan.wide):
         at = (plan.sure + block) * nb
         total = right_ref[at : at + nb] - dot3(plan.mat(mats, "low", 0, block), solved, ROWS)
@@ -215,7 +217,7 @@
         rows = plan.tri_of(rank)
         flat = (rank * plan.nb, plan.nb)
         tri = tri_high[rows].reshape(flat), tri_low[rows].reshape(flat)
-        step = dot3(tri, (inv_high[rank], inv_low[rank]), ABOVE).reshape(rank, plan.nb, plan.nb)
+        step = dot3(tri, (inv_high[rank], inv_low[rank]), PLAIN).reshape(rank, plan.nb, plan.nb)
         high_ref[rows], low_ref[rows] = split(step)
 
 
@@ -234,7 +236,7 @@
         for rank in range(1, panels):
             rows = plan.tri_of(rank)
             flat = split(both[rows].reshape(rank * 2 * depth, nb))
-            step = dot3(flat, plan.mat(mats, "inv", rank), ABOVE).reshape(rank, 2 * depth, nb)
+            step = dot3(flat, plan.mat(mats, "inv", rank), PLAIN).reshape(rank, 2 * depth, nb)
             high_ref[rows, place, :], low_ref[rows, place, :] = split(step)
     totals = [total_ref[block * nb : (block + 1) * nb] for block in range(plan.wide)]
 

time: 45.3 us -> 45.1 us (level)
  no operation moved by 1% of the time
where the time goes in v11:
time: 45.1 us; the launch traced here: 44.9 us
  starting transfers between devices  24.7 us (55%)
  waiting for transfers between devices  13.9 us (31%)
  Pallas kernels  6.15 us (14%)
    ppermute x12, starting transfers between devices, ring(): lax.ppermute(moving[0] if last and halves else moving, 'col', nearest)  19.8 us
    ppermute x12, waiting for transfers between devices, ring(): lax.ppermute(moving[0] if last and halves else moving, 'col', nearest)  9.49 us
    pallas_call x9, Pallas kernels, kernel_call(): pl.pallas_call(body, out_shape=out_shapes, in_specs=[hbm] * in_hbm + [nea...  6.15 us
    ppermute x1, waiting for transfers between devices, per_device(): tri = [own] + [lax.ppermute(own, 'row', pairs) for pairs in shifts]  2.74 us
    ppermute x1, starting transfers between devices, per_device(): received = [lax.ppermute(above, 'row', pairs) for pairs in shifts]  1.58 us
    ppermute x1, starting transfers between devices, per_device(): tri = [own] + [lax.ppermute(own, 'row', pairs) for pairs in shifts]  1.52 us
    ppermute x10, starting transfers between devices, ring(): pieces.append(lax.ppermute(moving, 'col', swap))  1.1 us
    ppermute x1, waiting for transfers between devices, per_device(): later_other = lax.ppermute(later, 'col', swap)  0.94 us
  transfers between devices with their start and end apart: 27, of which 10 were waited for; matrix products, arithmetic and copies ran while one was open for 0% of the time, Pallas kernels for 5%

profile of v11, /device:TPU:0, one launch (start us, length us, event | category | flops | bytes accessed | tf_op | source)
XLA Modules:
  0.0 44.9 jit_solution(5772624529791435601)
XLA Ops:
  0.0 1.1 %shard_map.37 = (f32[6,16,256]{2,1,0:T(8,128)S(1)}, f32[6,16,256]{2,1,0:T(8,128)S(1)}, f32[4,16,256]{2,1,0:T(8,128)S(1)}) custom-call(f32[4,16,1024]{2,1,0:T(8,128)} %factor_hbm.1, f32[4,16,256]{2,1,0:T(8,128)} %inv_hbm.1), custom_call_target="tpu_custom_call" | custom-call | bytes 4194304 | tf_op jit(solution)/shard_map/pallas_call | solution.py:41
  2.6 3.0 %collective-permute-start.19 = (f32[2,6,16,256]{3,2,1,0:T(8,128)S(1)}, f32[2,6,16,256]{3,2,1,0:T(8,128)S(1)}, u32[]{:S(2)}, u32[]{:S(2)}) collective-permute-start(f32[2,6,16,256]{3,2,1,0:T(8,128)S(1)} %shard_map.43.refs_0_), channel_id=1, source_target_pairs={{0,4},{1,3},{4,8},{5,1},{8,12},{9,5},{12,14},{13,9},{14,10},{15,13... | collective-permute-start | bytes 589832 | tf_op jit(solution)/shard_map/ppermute | solution.py:67
  5.6 1.5 %collective-permute-start = (f32[4,16,256]{2,1,0:T(8,128)S(1)}, f32[4,16,256]{2,1,0:T(8,128)S(1)}, u32[]{:S(2)}, u32[]{:S(2)}) collective-permute-start(f32[4,16,256]{2,1,0:T(8,128)S(1)} %get-tuple-element.17.refs_0_), channel_id=1, source_target_pairs={{16,0},{0,16},{17,1},{1,17},{18,2},{2,18},{19,3},{3,19},{20,4},{4,... | collective-permute-start | bytes 196616 | tf_op jit(solution)/shard_map/ppermute | solution.py:323
  7.1 2.7 %collective-permute-done.refs_1_ = f32[4,16,256]{2,1,0:T(8,128)S(1)} collective-permute-done((f32[4,16,256]{2,1,0:T(8,128)S(1)}, f32[4,16,256]{2,1,0:T(8,128)S(1)}, u32[]{:S(2)}, u32[]{:S(2)}) %collective-permute-start) | collective-permute-done | bytes 65568 | tf_op jit(solution)/shard_map/ppermute | solution.py:323
  10.0 1.6 %collective-permute-start.10 = (f32[2,6,16,256]{3,2,1,0:T(8,128)S(1)}, f32[2,6,16,256]{3,2,1,0:T(8,128)S(1)}, u32[]{:S(2)}, u32[]{:S(2)}) collective-permute-start(f32[2,6,16,256]{3,2,1,0:T(8,128)S(1)} %shard_map.40.refs_0_), channel_id=1, source_target_pairs={{0,4},{1,3},{4,8},{5,1},{8,12},{9,5},{12,14},{13,9},{14,10},{15,13... | collective-permute-start | bytes 589832 | tf_op jit(solution)/shard_map/ppermute | solution.py:67
  11.6 1.6 %collective-permute-start.2 = (f32[2,6,16,256]{3,2,1,0:T(8,128)S(1)}, f32[2,6,16,256]{3,2,1,0:T(8,128)S(1)}, u32[]{:S(2)}, u32[]{:S(2)}) collective-permute-start(f32[2,6,16,256]{3,2,1,0:T(8,128)S(1)} %shard_map.39.refs_0_), channel_id=1, source_target_pairs={{0,4},{1,3},{4,8},{5,1},{8,12},{9,5},{12,14},{13,9},{14,10},{15,13... | collective-permute-start | bytes 589832 | tf_op jit(solution)/shard_map/ppermute | solution.py:67
  13.3 1.5 %collective-permute-start.21 = (f32[2,6,16,256]{3,2,1,0:T(8,128)S(1)}, f32[2,6,16,256]{3,2,1,0:T(8,128)S(1)}, u32[]{:S(2)}, u32[]{:S(2)}) collective-permute-start(f32[2,6,16,256]{3,2,1,0:T(8,128)S(1)} %collective-permute-done.19.refs_1_), channel_id=1, source_target_pairs={{0,4},{1,3},{4,8},{5,1},{8,12},{9,5},{12,14},{13,9},{14,10},{15,13... | collective-permute-start | bytes 589832 | tf_op jit(solution)/shard_map/ppermute | solution.py:67
  14.8 1.6 %collective-permute-start.17 = (f32[512,256]{1,0:T(8,128)S(1)}, f32[512,256]{1,0:T(8,128)S(1)}, u32[]{:S(2)}, u32[]{:S(2)}) collective-permute-start(f32[512,256]{1,0:T(8,128)S(1)} %slice.6), channel_id=1, source_target_pairs={{16,0},{0,16},{17,1},{1,17},{18,2},{2,18},{19,3},{3,19},{20,4},{4,... | collective-permute-start | bytes 1572872 | tf_op jit(solution)/shard_map/ppermute | solution.py:325
  16.4 1.2 %collective-permute-start.12 = (f32[2,6,16,256]{3,2,1,0:T(8,128)S(1)}, f32[2,6,16,256]{3,2,1,0:T(8,128)S(1)}, u32[]{:S(2)}, u32[]{:S(2)}) collective-permute-start(f32[2,6,16,256]{3,2,1,0:T(8,128)S(1)} %collective-permute-done.10.refs_1_), channel_id=1, source_target_pairs={{0,4},{1,3},{4,8},{5,1},{8,12},{9,5},{12,14},{13,9},{14,10},{15,13... | collective-permute-start | bytes 589832 | tf_op jit(solution)/shard_map/ppermute | solution.py:67
  17.8 2.1 %collective-permute-done.21.refs_3_ = f32[2,6,16,256]{3,2,1,0:T(8,128)S(1)} collective-permute-done((f32[2,6,16,256]{3,2,1,0:T(8,128)S(1)}, f32[2,6,16,256]{3,2,1,0:T(8,128)S(1)}, u32[]{:S(2)}, u32[]{:S(2)}) %collective-permute-start.21) | collective-permute-done | bytes 196640 | tf_op jit(solution)/shard_map/ppermute | solution.py:67
  19.9 1.6 %collective-permute-start.23 = (f32[2,6,16,256]{3,2,1,0:T(8,128)S(1)}, f32[2,6,16,256]{3,2,1,0:T(8,128)S(1)}, u32[]{:S(2)}, u32[]{:S(2)}) collective-permute-start(f32[2,6,16,256]{3,2,1,0:T(8,128)S(1)} %collective-permute-done.21.refs_3_), channel_id=1, source_target_pairs={{0,4},{1,3},{4,8},{5,1},{8,12},{9,5},{12,14},{13,9},{14,10},{15,13... | collective-permute-start | bytes 589832 | tf_op jit(solution)/shard_map/ppermute | solution.py:67
  21.5 1.6 %collective-permute-start.3 = (f32[2,6,16,256]{3,2,1,0:T(8,128)S(1)}, f32[2,6,16,256]{3,2,1,0:T(8,128)S(1)}, u32[]{:S(2)}, u32[]{:S(2)}) collective-permute-start(f32[2,6,16,256]{3,2,1,0:T(8,128)S(1)} %collective-permute-done.2.refs_1_), channel_id=1, source_target_pairs={{0,4},{1,3},{4,8},{5,1},{8,12},{9,5},{12,14},{13,9},{14,10},{15,13... | collective-permute-start | bytes 589832 | tf_op jit(solution)/shard_map/ppermute | solution.py:67
  23.1 1.5 %collective-permute-start.14 = (f32[2,6,16,256]{3,2,1,0:T(8,128)S(1)}, f32[2,6,16,256]{3,2,1,0:T(8,128)S(1)}, u32[]{:S(2)}, u32[]{:S(2)}) collective-permute-start(f32[2,6,16,256]{3,2,1,0:T(8,128)S(1)} %collective-permute-done.12.refs_3_), channel_id=1, source_target_pairs={{0,4},{1,3},{4,8},{5,1},{8,12},{9,5},{12,14},{13,9},{14,10},{15,13... | collective-permute-start | bytes 589832 | tf_op jit(solution)/shard_map/ppermute | solution.py:67
  24.6 1.0 %collective-permute-done.23.refs_5_ = f32[2,6,16,256]{3,2,1,0:T(8,128)S(1)} collective-permute-done((f32[2,6,16,256]{3,2,1,0:T(8,128)S(1)}, f32[2,6,16,256]{3,2,1,0:T(8,128)S(1)}, u32[]{:S(2)}, u32[]{:S(2)}) %collective-permute-start.23) | collective-permute-done | bytes 196640 | tf_op jit(solution)/shard_map/ppermute | solution.py:67
  25.6 2.1 %collective-permute-done.3.refs_3_ = f32[2,6,16,256]{3,2,1,0:T(8,128)S(1)} collective-permute-done((f32[2,6,16,256]{3,2,1,0:T(8,128)S(1)}, f32[2,6,16,256]{3,2,1,0:T(8,128)S(1)}, u32[]{:S(2)}, u32[]{:S(2)}) %collective-permute-start.3) | collective-permute-done | bytes 196640 | tf_op jit(solution)/shard_map/ppermute | solution.py:67
  27.7 1.6 %collective-permute-start.4 = (f32[2,6,16,256]{3,2,1,0:T(8,128)S(1)}, f32[2,6,16,256]{3,2,1,0:T(8,128)S(1)}, u32[]{:S(2)}, u32[]{:S(2)}) collective-permute-start(f32[2,6,16,256]{3,2,1,0:T(8,128)S(1)} %collective-permute-done.3.refs_3_), channel_id=1, source_target_pairs={{0,4},{1,3},{4,8},{5,1},{8,12},{9,5},{12,14},{13,9},{14,10},{15,13... | collective-permute-start | bytes 589832 | tf_op jit(solution)/shard_map/ppermute | solution.py:67
  29.3 1.6 %collective-permute-start.25 = (f32[6,16,256]{2,1,0:T(8,128)S(1)}, f32[6,16,256]{2,1,0:T(8,128)S(1)}, u32[]{:S(2)}, u32[]{:S(2)}) collective-permute-start(f32[6,16,256]{2,1,0:T(8,128)S(1)} %slice_bitcast_fusion), channel_id=1, source_target_pairs={{0,4},{1,3},{4,8},{5,1},{8,12},{9,5},{12,14},{13,9},{14,10},{15,13... | collective-permute-start | bytes 294920 | tf_op jit(solution)/shard_map/ppermute | solution.py:67
  30.9 1.5 %collective-permute-start.16 = (f32[2,6,16,256]{3,2,1,0:T(8,128)S(1)}, f32[2,6,16,256]{3,2,1,0:T(8,128)S(1)}, u32[]{:S(2)}, u32[]{:S(2)}) collective-permute-start(f32[2,6,16,256]{3,2,1,0:T(8,128)S(1)} %collective-permute-done.14.refs_5_), channel_id=1, source_target_pairs={{0,4},{1,3},{4,8},{5,1},{8,12},{9,5},{12,14},{13,9},{14,10},{15,13... | collective-permute-start | bytes 589832 | tf_op jit(solution)/shard_map/ppermute | solution.py:67
  32.4 2.0 %collective-permute-done.25.refs_7_ = f32[6,16,256]{2,1,0:T(8,128)S(1)} collective-permute-done((f32[6,16,256]{2,1,0:T(8,128)S(1)}, f32[6,16,256]{2,1,0:T(8,128)S(1)}, u32[]{:S(2)}, u32[]{:S(2)}) %collective-permute-start.25) | collective-permute-done | bytes 98336 | tf_op jit(solution)/shard_map/ppermute | solution.py:67
  36.6 1.5 %collective-permute-start.5 = (f32[2,6,16,256]{3,2,1,0:T(8,128)S(1)}, f32[2,6,16,256]{3,2,1,0:T(8,128)S(1)}, u32[]{:S(2)}, u32[]{:S(2)}) collective-permute-start(f32[2,6,16,256]{3,2,1,0:T(8,128)S(1)} %collective-permute-done.4.refs_5_), channel_id=1, source_target_pairs={{0,4},{1,3},{4,8},{5,1},{8,12},{9,5},{12,14},{13,9},{14,10},{15,13... | collective-permute-start | bytes 589832 | tf_op jit(solution)/shard_map/ppermute | solution.py:67
  38.4 1.1 %shard_map.41 = (bf16[6,256,256]{2,1,0:T(8,128)(2,1)S(1)}, bf16[6,256,256]{2,1,0:T(8,128)(2,1)S(1)}, f32[4,256,256]{2,1,0:T(8,128)S(1)}, f32[512,256]{1,0:T(8,128)S(1)}) custom-call(f32[2,6,16,256]{3,2,1,0:T(8,128)S(1)} %shard_map.40.refs_0_, f32[2,6,16,256]{3,2,1,0:T(8,128)S(1)} %collective-permute-done.10.refs_1_, ...), custom_call_target="tpu_custom_call" | custom-call | flops 301989888 | bytes 4194304 | tf_op jit(solution)/shard_map/pallas_call | solution.py:41
  39.5 1.0 %shard_map.42 = (bf16[6,256,256]{2,1,0:T(8,128)(2,1)S(1)}, bf16[6,256,256]{2,1,0:T(8,128)(2,1)S(1)}) custom-call(f32[2,6,16,256]{3,2,1,0:T(8,128)S(1)} %shard_map.39.refs_0_, f32[2,6,16,256]{3,2,1,0:T(8,128)S(1)} %collective-permute-done.2.refs_1_, f32[2,6,16,256]{3,2,1,0:T(8,128)S(1)} %collective-permute-done.6.refs_2_, ...), custom_call_target="tpu_custom_call" | custom-call | flops 603979776 | bytes 4194304 | tf_op jit(solution)/shard_map/pallas_call | solution.py:41
  40.5 1.7 %collective-permute-done.5.refs_0_ = f32[2,6,16,256]{3,2,1,0:T(8,128)S(1)} collective-permute-done((f32[2,6,16,256]{3,2,1,0:T(8,128)S(1)}, f32[2,6,16,256]{3,2,1,0:T(8,128)S(1)}, u32[]{:S(2)}, u32[]{:S(2)}) %collective-permute-start.5) | collective-permute-done | bytes 196640 | tf_op jit(solution)/shard_map/ppermute | solution.py:67
  42.2 2.7 %shard_map.45 = (f32[1024,256]{1,0:T(8,128)}, bf16[6,256,256]{2,1,0:T(8,128)(2,1)S(1)}, bf16[6,256,256]{2,1,0:T(8,128)(2,1)S(1)}) custom-call(f32[2,6,16,256]{3,2,1,0:T(8,128)S(1)} %collective-permute-done.5.refs_0_, bf16[6,256,256]{2,1,0:T(8,128)(2,1)S(1)} %get-tuple-element.21.refs_1_, ...), custom_call_target="tpu_custom_call", output_to_operand_aliasing={{1}: (1, {}), {2}: (2, {})} | custom-call | flops 1509949440 | bytes 4194304 | tf_op jit(solution)/shard_map/pallas_call | solution.py:41
  (43 shorter events, 4.4 us)
Async XLA Ops:
  2.6 10.6 %collective-permute-start.19 = (f32[2,6,16,256]{3,2,1,0:T(8,128)S(1)}, f32[2,6,16,256]{3,2,1,0:T(8,128)S(1)}, u32[]{:S(2)}, u32[]{:S(2)}) collective-permute-start(f32[2,6,16,256]{3,2,1,0:T(8,128)S(1)} %shard_map.43.refs_0_), channel_id=1, source_target_pairs={{0,4},{1,3},{4,8},{5,1},{8,12},{9,5},{12,14},{13,9},{14,10},{15,13... | collective-permute-start | bytes 589832 | tf_op jit(solution)/shard_map/ppermute | solution.py:67
  5.6 4.3 %collective-permute-start = (f32[4,16,256]{2,1,0:T(8,128)S(1)}, f32[4,16,256]{2,1,0:T(8,128)S(1)}, u32[]{:S(2)}, u32[]{:S(2)}) collective-permute-start(f32[4,16,256]{2,1,0:T(8,128)S(1)} %get-tuple-element.17.refs_0_), channel_id=1, source_target_pairs={{16,0},{0,16},{17,1},{1,17},{18,2},{2,18},{19,3},{3,19},{20,4},{4,... | collective-permute-start | bytes 196616 | tf_op jit(solution)/shard_map/ppermute | solution.py:323
  7.1 2.8 %collective-permute-start.9 = (f32[6,16,256]{2,1,0:T(8,128)S(1)}, f32[6,16,256]{2,1,0:T(8,128)S(1)}, u32[]{:S(2)}, u32[]{:S(2)}) collective-permute-start(f32[6,16,256]{2,1,0:T(8,128)S(1)} %get-tuple-element.18.own_ref), channel_id=1, source_target_pairs={{0,1},{1,0},{2,3},{3,2},{4,5},{5,4},{6,7},{7,6},{8,9},{9,8},{10,11... | collective-permute-start | bytes 294920 | tf_op jit(solution)/shard_map/ppermute | solution.py:321
  10.0 6.4 %collective-permute-start.10 = (f32[2,6,16,256]{3,2,1,0:T(8,128)S(1)}, f32[2,6,16,256]{3,2,1,0:T(8,128)S(1)}, u32[]{:S(2)}, u32[]{:S(2)}) collective-permute-start(f32[2,6,16,256]{3,2,1,0:T(8,128)S(1)} %shard_map.40.refs_0_), channel_id=1, source_target_pairs={{0,4},{1,3},{4,8},{5,1},{8,12},{9,5},{12,14},{13,9},{14,10},{15,13... | collective-permute-start | bytes 589832 | tf_op jit(solution)/shard_map/ppermute | solution.py:67
  11.6 6.2 %collective-permute-start.2 = (f32[2,6,16,256]{3,2,1,0:T(8,128)S(1)}, f32[2,6,16,256]{3,2,1,0:T(8,128)S(1)}, u32[]{:S(2)}, u32[]{:S(2)}) collective-permute-start(f32[2,6,16,256]{3,2,1,0:T(8,128)S(1)} %shard_map.39.refs_0_), channel_id=1, source_target_pairs={{0,4},{1,3},{4,8},{5,1},{8,12},{9,5},{12,14},{13,9},{14,10},{15,13... | collective-permute-start | bytes 589832 | tf_op jit(solution)/shard_map/ppermute | solution.py:67
  13.3 6.7 %collective-permute-start.21 = (f32[2,6,16,256]{3,2,1,0:T(8,128)S(1)}, f32[2,6,16,256]{3,2,1,0:T(8,128)S(1)}, u32[]{:S(2)}, u32[]{:S(2)}) collective-permute-start(f32[2,6,16,256]{3,2,1,0:T(8,128)S(1)} %collective-permute-done.19.refs_1_), channel_id=1, source_target_pairs={{0,4},{1,3},{4,8},{5,1},{8,12},{9,5},{12,14},{13,9},{14,10},{15,13... | collective-permute-start | bytes 589832 | tf_op jit(solution)/shard_map/ppermute | solution.py:67
  14.8 14.5 %collective-permute-start.17 = (f32[512,256]{1,0:T(8,128)S(1)}, f32[512,256]{1,0:T(8,128)S(1)}, u32[]{:S(2)}, u32[]{:S(2)}) collective-permute-start(f32[512,256]{1,0:T(8,128)S(1)} %slice.6), channel_id=1, source_target_pairs={{16,0},{0,16},{17,1},{1,17},{18,2},{2,18},{19,3},{3,19},{20,4},{4,... | collective-permute-start | bytes 1572872 | tf_op jit(solution)/shard_map/ppermute | solution.py:325
  16.4 5.1 %collective-permute-start.20 = (f32[2,6,16,256]{3,2,1,0:T(8,128)S(1)}, f32[2,6,16,256]{3,2,1,0:T(8,128)S(1)}, u32[]{:S(2)}, u32[]{:S(2)}) collective-permute-start(f32[2,6,16,256]{3,2,1,0:T(8,128)S(1)} %collective-permute-done.19.refs_1_), channel_id=1, source_target_pairs={{0,1},{1,0},{2,3},{3,2},{4,5},{5,4},{6,7},{7,6},{8,9},{9,8},{10,11... | collective-permute-start | bytes 589832 | tf_op jit(solution)/shard_map/ppermute | solution.py:70
  16.4 6.7 %collective-permute-start.12 = (f32[2,6,16,256]{3,2,1,0:T(8,128)S(1)}, f32[2,6,16,256]{3,2,1,0:T(8,128)S(1)}, u32[]{:S(2)}, u32[]{:S(2)}) collective-permute-start(f32[2,6,16,256]{3,2,1,0:T(8,128)S(1)} %collective-permute-done.10.refs_1_), channel_id=1, source_target_pairs={{0,4},{1,3},{4,8},{5,1},{8,12},{9,5},{12,14},{13,9},{14,10},{15,13... | collective-permute-start | bytes 589832 | tf_op jit(solution)/shard_map/ppermute | solution.py:67
  17.8 5.3 %collective-permute-start.11 = (f32[2,6,16,256]{3,2,1,0:T(8,128)S(1)}, f32[2,6,16,256]{3,2,1,0:T(8,128)S(1)}, u32[]{:S(2)}, u32[]{:S(2)}) collective-permute-start(f32[2,6,16,256]{3,2,1,0:T(8,128)S(1)} %collective-permute-done.10.refs_1_), channel_id=1, source_target_pairs={{0,1},{1,0},{2,3},{3,2},{4,5},{5,4},{6,7},{7,6},{8,9},{9,8},{10,11... | collective-permute-start | bytes 589832 | tf_op jit(solution)/shard_map/ppermute | solution.py:70
  19.9 5.7 %collective-permute-start.23 = (f32[2,6,16,256]{3,2,1,0:T(8,128)S(1)}, f32[2,6,16,256]{3,2,1,0:T(8,128)S(1)}, u32[]{:S(2)}, u32[]{:S(2)}) collective-permute-start(f32[2,6,16,256]{3,2,1,0:T(8,128)S(1)} %collective-permute-done.21.refs_3_), channel_id=1, source_target_pairs={{0,4},{1,3},{4,8},{5,1},{8,12},{9,5},{12,14},{13,9},{14,10},{15,13... | collective-permute-start | bytes 589832 | tf_op jit(solution)/shard_map/ppermute | solution.py:67
  21.5 6.2 %collective-permute-start.3 = (f32[2,6,16,256]{3,2,1,0:T(8,128)S(1)}, f32[2,6,16,256]{3,2,1,0:T(8,128)S(1)}, u32[]{:S(2)}, u32[]{:S(2)}) collective-permute-start(f32[2,6,16,256]{3,2,1,0:T(8,128)S(1)} %collective-permute-done.2.refs_1_), channel_id=1, source_target_pairs={{0,4},{1,3},{4,8},{5,1},{8,12},{9,5},{12,14},{13,9},{14,10},{15,13... | collective-permute-start | bytes 589832 | tf_op jit(solution)/shard_map/ppermute | solution.py:67
  23.1 7.8 %collective-permute-start.22 = (f32[2,6,16,256]{3,2,1,0:T(8,128)S(1)}, f32[2,6,16,256]{3,2,1,0:T(8,128)S(1)}, u32[]{:S(2)}, u32[]{:S(2)}) collective-permute-start(f32[2,6,16,256]{3,2,1,0:T(8,128)S(1)} %collective-permute-done.21.refs_3_), channel_id=1, source_target_pairs={{0,1},{1,0},{2,3},{3,2},{4,5},{5,4},{6,7},{7,6},{8,9},{9,8},{10,11... | collective-permute-start | bytes 589832 | tf_op jit(solution)/shard_map/ppermute | solution.py:70
  23.1 7.8 %collective-permute-start.14 = (f32[2,6,16,256]{3,2,1,0:T(8,128)S(1)}, f32[2,6,16,256]{3,2,1,0:T(8,128)S(1)}, u32[]{:S(2)}, u32[]{:S(2)}) collective-permute-start(f32[2,6,16,256]{3,2,1,0:T(8,128)S(1)} %collective-permute-done.12.refs_3_), channel_id=1, source_target_pairs={{0,4},{1,3},{4,8},{5,1},{8,12},{9,5},{12,14},{13,9},{14,10},{15,13... | collective-permute-start | bytes 589832 | tf_op jit(solution)/shard_map/ppermute | solution.py:67
  25.6 8.8 %collective-permute-start.13 = (f32[2,6,16,256]{3,2,1,0:T(8,128)S(1)}, f32[2,6,16,256]{3,2,1,0:T(8,128)S(1)}, u32[]{:S(2)}, u32[]{:S(2)}) collective-permute-start(f32[2,6,16,256]{3,2,1,0:T(8,128)S(1)} %collective-permute-done.12.refs_3_), channel_id=1, source_target_pairs={{0,1},{1,0},{2,3},{3,2},{4,5},{5,4},{6,7},{7,6},{8,9},{9,8},{10,11... | collective-permute-start | bytes 589832 | tf_op jit(solution)/shard_map/ppermute | solution.py:70
  27.7 7.2 %collective-permute-start.4 = (f32[2,6,16,256]{3,2,1,0:T(8,128)S(1)}, f32[2,6,16,256]{3,2,1,0:T(8,128)S(1)}, u32[]{:S(2)}, u32[]{:S(2)}) collective-permute-start(f32[2,6,16,256]{3,2,1,0:T(8,128)S(1)} %collective-permute-done.3.refs_3_), channel_id=1, source_target_pairs={{0,4},{1,3},{4,8},{5,1},{8,12},{9,5},{12,14},{13,9},{14,10},{15,13... | collective-permute-start | bytes 589832 | tf_op jit(solution)/shard_map/ppermute | solution.py:67
  29.3 5.1 %collective-permute-start.25 = (f32[6,16,256]{2,1,0:T(8,128)S(1)}, f32[6,16,256]{2,1,0:T(8,128)S(1)}, u32[]{:S(2)}, u32[]{:S(2)}) collective-permute-start(f32[6,16,256]{2,1,0:T(8,128)S(1)} %slice_bitcast_fusion), channel_id=1, source_target_pairs={{0,4},{1,3},{4,8},{5,1},{8,12},{9,5},{12,14},{13,9},{14,10},{15,13... | collective-permute-start | bytes 294920 | tf_op jit(solution)/shard_map/ppermute | solution.py:67
  30.8 5.0 %collective-permute-start.24 = (f32[2,6,16,256]{3,2,1,0:T(8,128)S(1)}, f32[2,6,16,256]{3,2,1,0:T(8,128)S(1)}, u32[]{:S(2)}, u32[]{:S(2)}) collective-permute-start(f32[2,6,16,256]{3,2,1,0:T(8,128)S(1)} %collective-permute-done.23.refs_5_), channel_id=1, source_target_pairs={{0,1},{1,0},{2,3},{3,2},{4,5},{5,4},{6,7},{7,6},{8,9},{9,8},{10,11... | collective-permute-start | bytes 589832 | tf_op jit(solution)/shard_map/ppermute | solution.py:70
  30.9 5.7 %collective-permute-start.16 = (f32[2,6,16,256]{3,2,1,0:T(8,128)S(1)}, f32[2,6,16,256]{3,2,1,0:T(8,128)S(1)}, u32[]{:S(2)}, u32[]{:S(2)}) collective-permute-start(f32[2,6,16,256]{3,2,1,0:T(8,128)S(1)} %collective-permute-done.14.refs_5_), channel_id=1, source_target_pairs={{0,4},{1,3},{4,8},{5,1},{8,12},{9,5},{12,14},{13,9},{14,10},{15,13... | collective-permute-start | bytes 589832 | tf_op jit(solution)/shard_map/ppermute | solution.py:67
  34.4 4.0 %collective-permute-start.15 = (f32[2,6,16,256]{3,2,1,0:T(8,128)S(1)}, f32[2,6,16,256]{3,2,1,0:T(8,128)S(1)}, u32[]{:S(2)}, u32[]{:S(2)}) collective-permute-start(f32[2,6,16,256]{3,2,1,0:T(8,128)S(1)} %collective-permute-done.14.refs_5_), channel_id=1, source_target_pairs={{0,1},{1,0},{2,3},{3,2},{4,5},{5,4},{6,7},{7,6},{8,9},{9,8},{10,11... | collective-permute-start | bytes 589832 | tf_op jit(solution)/shard_map/ppermute | solution.py:70
  34.9 4.6 %collective-permute-start.6 = (f32[2,6,16,256]{3,2,1,0:T(8,128)S(1)}, f32[2,6,16,256]{3,2,1,0:T(8,128)S(1)}, u32[]{:S(2)}, u32[]{:S(2)}) collective-permute-start(f32[2,6,16,256]{3,2,1,0:T(8,128)S(1)} %collective-permute-done.2.refs_1_), channel_id=1, source_target_pairs={{0,1},{1,0},{2,3},{3,2},{4,5},{5,4},{6,7},{7,6},{8,9},{9,8},{10,11... | collective-permute-start | bytes 589832 | tf_op jit(solution)/shard_map/ppermute | solution.py:70
  35.7 3.8 %collective-permute-start.7 = (f32[2,6,16,256]{3,2,1,0:T(8,128)S(1)}, f32[2,6,16,256]{3,2,1,0:T(8,128)S(1)}, u32[]{:S(2)}, u32[]{:S(2)}) collective-permute-start(f32[2,6,16,256]{3,2,1,0:T(8,128)S(1)} %collective-permute-done.3.refs_3_), channel_id=1, source_target_pairs={{0,1},{1,0},{2,3},{3,2},{4,5},{5,4},{6,7},{7,6},{8,9},{9,8},{10,11... | collective-permute-start | bytes 589832 | tf_op jit(solution)/shard_map/ppermute | solution.py:70
  35.9 3.6 %collective-permute-start.8 = (f32[2,6,16,256]{3,2,1,0:T(8,128)S(1)}, f32[2,6,16,256]{3,2,1,0:T(8,128)S(1)}, u32[]{:S(2)}, u32[]{:S(2)}) collective-permute-start(f32[2,6,16,256]{3,2,1,0:T(8,128)S(1)} %collective-permute-done.4.refs_5_), channel_id=1, source_target_pairs={{0,1},{1,0},{2,3},{3,2},{4,5},{5,4},{6,7},{7,6},{8,9},{9,8},{10,11... | collective-permute-start | bytes 589832 | tf_op jit(solution)/shard_map/ppermute | solution.py:70
  36.6 5.7 %collective-permute-start.5 = (f32[2,6,16,256]{3,2,1,0:T(8,128)S(1)}, f32[2,6,16,256]{3,2,1,0:T(8,128)S(1)}, u32[]{:S(2)}, u32[]{:S(2)}) collective-permute-start(f32[2,6,16,256]{3,2,1,0:T(8,128)S(1)} %collective-permute-done.4.refs_5_), channel_id=1, source_target_pairs={{0,4},{1,3},{4,8},{5,1},{8,12},{9,5},{12,14},{13,9},{14,10},{15,13... | collective-permute-start | bytes 589832 | tf_op jit(solution)/shard_map/ppermute | solution.py:67
  (4 other events, 19.3 us)

commit v12 on v11

--- a/solution.py
+++ b/solution.py
@@ -57,8 +57,9 @@
     nearest = []
     for place in range(chips):
         here = ring_chip(place, chips)
-        nearest.append((2 * here, 2 * ring_chip((place + 1) % chips, chips)))
-        nearest.append((2 * here + 1, 2 * ring_chip((place - 1) % chips, chips) + 1))
+        for up, turn in ((1, 1), (0, -1)):
+            there = ring_chip((place + turn) % chips, chips)
+            nearest.append((2 * here + (here % 2 ^ up), 2 * there + (there % 2 ^ up)))
     swap = [(i, i ^ 1) for i in range(2 * chips)]
     moving = first
     pieces = [first]
@@ -72,13 +73,15 @@
 
 
 def streams(chips):
-    core = lax.axis_index("col") % 2
-    here = ring_place(lax.axis_index("col") // 2, chips)
-    found = [(lax.axis_index("col") // 2, core)]
+    chip, core = lax.axis_index("col") // 2, lax.axis_index("col") % 2
+    here, up = ring_place(chip, chips), (chip + core) % 2
+    found = [(chip, core)]
     for step in range(1, chips // 2 + 1):
-        turn = step * (1 - 2 * core)
-        found.append((ring_chip((here - turn + chips) % chips, chips), core))
-        found.append((ring_chip((here + turn + chips) % chips, chips), 1 - core))
+        turn = step * (2 * up - 1)
+        mine = ring_chip((here - turn + chips) % chips, chips)
+        other = ring_chip((here + turn + chips) % chips, chips)
+        found.append((mine, (mine + up) % 2))
+        found.append((other, (other + 1 - up) % 2))
     return found
 
 
@@ -185,8 +188,9 @@
 
 
 def prep_kernel(plan, *refs):
-    pieces, right_ref = refs[: plan.chips], refs[plan.chips]
-    received = refs[plan.chips + 1 : -5]
+    count = len(refs) - 5 - plan.group_count
+    pieces, right_ref = refs[:count], refs[count]
+    received = refs[count + 1 : -5]
     high_ref, low_ref, start_ref, total_ref, whole_ref = refs[-5:]
     assemble(pieces, high_ref, low_ref, whole_ref, plan.chips)
     mats, nb = [(high_ref, low_ref)], plan.nb
@@ -208,6 +212,11 @@
 def place_kernel(plan, *refs):
     high_ref, low_ref, whole_ref = refs[-3:]
     assemble(refs[:-3], high_ref, low_ref, whole_ref, plan.chips, slice(0, len(refs) - 3))
+
+
+def late_kernel(plan, *refs):
+    *pieces, _, _, high_ref, low_ref = refs
+    assemble(pieces, high_ref, low_ref, None, plan.chips, slice(plan.chips - 1, None))
 
 
 def triangle_kernel(plan, count, *refs):
@@ -334,7 +343,7 @@
             [],
             ((mine, mine_other), (later, later_other), (half, half_other))[chunk],
         )
-        pieces.append(ring(packed, chips, halves=chunk == 1 and depth % 16 == 0))
+        pieces.append(ring(packed, chips, halves=chunk < 2 and depth % 16 == 0))
 
     pairs = [[shape((len(blocks), nb, nb), bf16)] * 2 for blocks in plan.chunks]
     wholes = [whole_scratch(len(blocks), nb, depth) for blocks in plan.chunks]
@@ -359,7 +368,10 @@
         (*early, inv_high, inv_low),
         flops=6 * 6 * nb * nb * nb,
     )
-    below = kernel_call(bound(place_kernel, plan), pairs[1], [wholes[1]], pieces[1])
+    below = kernel_call(bound(place_kernel, plan), pairs[1], [wholes[1]], pieces[1][:count])
+    if count < chips:
+        ends = pieces[1][count:]
+        below = kernel_call(bound(late_kernel, plan), pairs[1], [], (*ends, *below), aliases={2: 0, 3: 1})
     out, _, _ = kernel_call(
         bound(final_kernel, plan, len(late)),
         [shape(right_side.shape, f32), *pairs[2]],

time: 45.1 us -> 47.8 us (1.060)
  waiting for transfers between devices: 13.9 us -> 23.4 us
  starting transfers between devices: 24.7 us -> 17.8 us
    ppermute x12, waiting for transfers between devices: 9.49 us -> 18.3 us  [ring(): lax.ppermute(moving[0] if last and halves else moving, 'col', nearest)]
    ppermute x12, starting transfers between devices: 19.8 us -> 11.7 us  [ring(): lax.ppermute(moving[0] if last and halves else moving, 'col', nearest)]
    ppermute x1, waiting for transfers between devices: 0.01 us -> 1.1 us  [per_device(): mine_other = lax.ppermute(mine, 'col', swap)]
    ppermute x10 -> x11, starting transfers between devices: 1.1 us -> 2.17 us  [ring(): pieces.append(lax.ppermute(moving, 'col', swap))]
    ppermute x10 -> x11, waiting for transfers between devices: 0.74 us -> 0.22 us  [ring(): pieces.append(lax.ppermute(moving, 'col', swap))]
    pallas_call x9 -> x10, Pallas kernels: 6.15 us -> 6.25 us  [kernel_call(): pl.pallas_call(body, out_shape=out_shapes, in_specs=[hbm] * in_hbm + [nea...]
  transfers between devices with their start and end apart: 27 -> 28, of which waited for: 10 -> 13; matrix products, arithmetic and copies ran while one was open for 0% -> 0% of each run, Pallas kernels for 5% -> 5%
where the time goes in v12:
time: 47.8 us; the launch traced here: 47.6 us
  waiting for transfers between devices  23.4 us (49%)
  starting transfers between devices  17.8 us (37%)
  Pallas kernels  6.25 us (13%)
    ppermute x12, waiting for transfers between devices, ring(): lax.ppermute(moving[0] if last and halves else moving, 'col', nearest)  18.3 us
    ppermute x12, starting transfers between devices, ring(): lax.ppermute(moving[0] if last and halves else moving, 'col', nearest)  11.7 us
    pallas_call x10, Pallas kernels, kernel_call(): pl.pallas_call(body, out_shape=out_shapes, in_specs=[hbm] * in_hbm + [nea...  6.25 us
    ppermute x1, waiting for transfers between devices, per_device(): tri = [own] + [lax.ppermute(own, 'row', pairs) for pairs in shifts]  2.75 us
    ppermute x11, starting transfers between devices, ring(): pieces.append(lax.ppermute(moving, 'col', swap))  2.17 us
    ppermute x1, starting transfers between devices, per_device(): received = [lax.ppermute(above, 'row', pairs) for pairs in shifts]  1.58 us
    ppermute x1, starting transfers between devices, per_device(): tri = [own] + [lax.ppermute(own, 'row', pairs) for pairs in shifts]  1.52 us
    ppermute x1, waiting for transfers between devices, per_device(): mine_other = lax.ppermute(mine, 'col', swap)  1.1 us
  transfers between devices with their start and end apart: 28, of which 13 were waited for; matrix products, arithmetic and copies ran while one was open for 0% of the time, Pallas kernels for 5%

profile of v12, /device:TPU:0, one launch (start us, length us, event | category | flops | bytes accessed | tf_op | source)
XLA Modules:
  0.0 47.6 jit_solution(2391535078477070969)
XLA Ops:
  0.0 1.1 %shard_map.37 = (f32[6,16,256]{2,1,0:T(8,128)S(1)}, f32[6,16,256]{2,1,0:T(8,128)S(1)}, f32[4,16,256]{2,1,0:T(8,128)S(1)}) custom-call(f32[4,16,1024]{2,1,0:T(8,128)} %factor_hbm.1, f32[4,16,256]{2,1,0:T(8,128)} %inv_hbm.1), custom_call_target="tpu_custom_call" | custom-call | bytes 4194304 | tf_op jit(solution)/shard_map/pallas_call | solution.py:41
  1.6 0.9 %collective-permute-done.19.other_ref = f32[6,16,256]{2,1,0:T(8,128)S(1)} collective-permute-done((f32[6,16,256]{2,1,0:T(8,128)S(1)}, f32[6,16,256]{2,1,0:T(8,128)S(1)}, u32[]{:S(2)}, u32[]{:S(2)}) %collective-permute-start.19) | collective-permute-done | bytes 98336 | tf_op jit(solution)/shard_map/ppermute | solution.py:331
  2.6 2.6 %collective-permute-start.20 = (f32[2,6,16,256]{3,2,1,0:T(8,128)S(1)}, f32[2,6,16,256]{3,2,1,0:T(8,128)S(1)}, u32[]{:S(2)}, u32[]{:S(2)}) collective-permute-start(f32[2,6,16,256]{3,2,1,0:T(8,128)S(1)} %shard_map.43.refs_0_), channel_id=1, source_target_pairs={{1,5},{0,3},{5,9},{4,0},{9,13},{8,4},{13,14},{12,8},{14,10},{15,12... | collective-permute-start | bytes 589832 | tf_op jit(solution)/shard_map/ppermute | solution.py:68
  5.5 1.1 %collective-permute-done.9.other_ref = f32[6,16,256]{2,1,0:T(8,128)S(1)} collective-permute-done((f32[6,16,256]{2,1,0:T(8,128)S(1)}, f32[6,16,256]{2,1,0:T(8,128)S(1)}, u32[]{:S(2)}, u32[]{:S(2)}) %collective-permute-start.9) | collective-permute-done | bytes 98336 | tf_op jit(solution)/shard_map/ppermute | solution.py:330
  6.6 1.4 %collective-permute-start.10 = (f32[2,6,16,256]{3,2,1,0:T(8,128)S(1)}, f32[2,6,16,256]{3,2,1,0:T(8,128)S(1)}, u32[]{:S(2)}, u32[]{:S(2)}) collective-permute-start(f32[2,6,16,256]{3,2,1,0:T(8,128)S(1)} %shard_map.40.refs_0_), channel_id=1, source_target_pairs={{1,5},{0,3},{5,9},{4,0},{9,13},{8,4},{13,14},{12,8},{14,10},{15,12... | collective-permute-start | bytes 589832 | tf_op jit(solution)/shard_map/ppermute | solution.py:68
  7.9 1.3 %collective-permute-done.20.refs_1_ = f32[2,6,16,256]{3,2,1,0:T(8,128)S(1)} collective-permute-done((f32[2,6,16,256]{3,2,1,0:T(8,128)S(1)}, f32[2,6,16,256]{3,2,1,0:T(8,128)S(1)}, u32[]{:S(2)}, u32[]{:S(2)}) %collective-permute-start.20) | collective-permute-done | bytes 196640 | tf_op jit(solution)/shard_map/ppermute | solution.py:68
  9.2 1.4 %collective-permute-start.21 = (f32[2,6,16,256]{3,2,1,0:T(8,128)S(1)}, f32[2,6,16,256]{3,2,1,0:T(8,128)S(1)}, u32[]{:S(2)}, u32[]{:S(2)}) collective-permute-start(f32[2,6,16,256]{3,2,1,0:T(8,128)S(1)} %collective-permute-done.20.refs_1_), channel_id=1, source_target_pairs={{1,5},{0,3},{5,9},{4,0},{9,13},{8,4},{13,14},{12,8},{14,10},{15,12... | collective-permute-start | bytes 589832 | tf_op jit(solution)/shard_map/ppermute | solution.py:68
  10.6 1.5 %collective-permute-start = (f32[4,16,256]{2,1,0:T(8,128)S(1)}, f32[4,16,256]{2,1,0:T(8,128)S(1)}, u32[]{:S(2)}, u32[]{:S(2)}) collective-permute-start(f32[4,16,256]{2,1,0:T(8,128)S(1)} %get-tuple-element.19.refs_0_), channel_id=1, source_target_pairs={{16,0},{0,16},{17,1},{1,17},{18,2},{2,18},{19,3},{3,19},{20,4},{4,... | collective-permute-start | bytes 196616 | tf_op jit(solution)/shard_map/ppermute | solution.py:332
  12.2 2.7 %collective-permute-done.refs_1_ = f32[4,16,256]{2,1,0:T(8,128)S(1)} collective-permute-done((f32[4,16,256]{2,1,0:T(8,128)S(1)}, f32[4,16,256]{2,1,0:T(8,128)S(1)}, u32[]{:S(2)}, u32[]{:S(2)}) %collective-permute-start) | collective-permute-done | bytes 65568 | tf_op jit(solution)/shard_map/ppermute | solution.py:332
  15.1 1.6 %collective-permute-start.18 = (f32[512,256]{1,0:T(8,128)S(1)}, f32[512,256]{1,0:T(8,128)S(1)}, u32[]{:S(2)}, u32[]{:S(2)}) collective-permute-start(f32[512,256]{1,0:T(8,128)S(1)} %slice.10), channel_id=1, source_target_pairs={{16,0},{0,16},{17,1},{1,17},{18,2},{2,18},{19,3},{3,19},{20,4},{4,... | collective-permute-start | bytes 1572872 | tf_op jit(solution)/shard_map/ppermute | solution.py:334
  17.4 1.4 %collective-permute-start.12 = (f32[2,6,16,256]{3,2,1,0:T(8,128)S(1)}, f32[2,6,16,256]{3,2,1,0:T(8,128)S(1)}, u32[]{:S(2)}, u32[]{:S(2)}) collective-permute-start(f32[2,6,16,256]{3,2,1,0:T(8,128)S(1)} %collective-permute-done.10.refs_1_), channel_id=1, source_target_pairs={{1,5},{0,3},{5,9},{4,0},{9,13},{8,4},{13,14},{12,8},{14,10},{15,12... | collective-permute-start | bytes 589832 | tf_op jit(solution)/shard_map/ppermute | solution.py:68
  18.8 1.3 %collective-permute-start.22 = (f32[2,6,16,256]{3,2,1,0:T(8,128)S(1)}, f32[2,6,16,256]{3,2,1,0:T(8,128)S(1)}, u32[]{:S(2)}, u32[]{:S(2)}) collective-permute-start(f32[2,6,16,256]{3,2,1,0:T(8,128)S(1)} %collective-permute-done.21.refs_3_), channel_id=1, source_target_pairs={{1,5},{0,3},{5,9},{4,0},{9,13},{8,4},{13,14},{12,8},{14,10},{15,12... | collective-permute-start | bytes 589832 | tf_op jit(solution)/shard_map/ppermute | solution.py:68
  20.6 1.8 %collective-permute-done.2.refs_1_ = f32[2,6,16,256]{3,2,1,0:T(8,128)S(1)} collective-permute-done((f32[2,6,16,256]{3,2,1,0:T(8,128)S(1)}, f32[2,6,16,256]{3,2,1,0:T(8,128)S(1)}, u32[]{:S(2)}, u32[]{:S(2)}) %collective-permute-start.2) | collective-permute-done | bytes 196640 | tf_op jit(solution)/shard_map/ppermute | solution.py:68
  22.4 2.1 %collective-permute-done.12.refs_3_ = f32[2,6,16,256]{3,2,1,0:T(8,128)S(1)} collective-permute-done((f32[2,6,16,256]{3,2,1,0:T(8,128)S(1)}, f32[2,6,16,256]{3,2,1,0:T(8,128)S(1)}, u32[]{:S(2)}, u32[]{:S(2)}) %collective-permute-start.12) | collective-permute-done | bytes 196640 | tf_op jit(solution)/shard_map/ppermute | solution.py:68
  24.9 1.7 %collective-permute-done.22.refs_5_ = f32[2,6,16,256]{3,2,1,0:T(8,128)S(1)} collective-permute-done((f32[2,6,16,256]{3,2,1,0:T(8,128)S(1)}, f32[2,6,16,256]{3,2,1,0:T(8,128)S(1)}, u32[]{:S(2)}, u32[]{:S(2)}) %collective-permute-start.22) | collective-permute-done | bytes 196640 | tf_op jit(solution)/shard_map/ppermute | solution.py:68
  27.6 2.6 %collective-permute-done.3.refs_3_ = f32[2,6,16,256]{3,2,1,0:T(8,128)S(1)} collective-permute-done((f32[2,6,16,256]{3,2,1,0:T(8,128)S(1)}, f32[2,6,16,256]{3,2,1,0:T(8,128)S(1)}, u32[]{:S(2)}, u32[]{:S(2)}) %collective-permute-start.3) | collective-permute-done | bytes 196640 | tf_op jit(solution)/shard_map/ppermute | solution.py:68
  30.5 1.7 %collective-permute-done.14.refs_5_ = f32[2,6,16,256]{3,2,1,0:T(8,128)S(1)} collective-permute-done((f32[2,6,16,256]{3,2,1,0:T(8,128)S(1)}, f32[2,6,16,256]{3,2,1,0:T(8,128)S(1)}, u32[]{:S(2)}, u32[]{:S(2)}) %collective-permute-start.14) | collective-permute-done | bytes 196640 | tf_op jit(solution)/shard_map/ppermute | solution.py:68
  32.3 1.0 %collective-permute-start.16 = (f32[6,16,256]{2,1,0:T(8,128)S(1)}, f32[6,16,256]{2,1,0:T(8,128)S(1)}, u32[]{:S(2)}, u32[]{:S(2)}) collective-permute-start(f32[6,16,256]{2,1,0:T(8,128)S(1)} %slice_bitcast_fusion.1), channel_id=1, source_target_pairs={{1,5},{0,3},{5,9},{4,0},{9,13},{8,4},{13,14},{12,8},{14,10},{15,12... | collective-permute-start | bytes 294920 | tf_op jit(solution)/shard_map/ppermute | solution.py:68
  33.3 3.6 %collective-permute-done.23.refs_0_ = f32[6,16,256]{2,1,0:T(8,128)S(1)} collective-permute-done((f32[6,16,256]{2,1,0:T(8,128)S(1)}, f32[6,16,256]{2,1,0:T(8,128)S(1)}, u32[]{:S(2)}, u32[]{:S(2)}) %collective-permute-start.23) | collective-permute-done | bytes 98336 | tf_op jit(solution)/shard_map/ppermute | solution.py:68
  36.9 1.1 %collective-permute-done.16.refs_7_ = f32[6,16,256]{2,1,0:T(8,128)S(1)} collective-permute-done((f32[6,16,256]{2,1,0:T(8,128)S(1)}, f32[6,16,256]{2,1,0:T(8,128)S(1)}, u32[]{:S(2)}, u32[]{:S(2)}) %collective-permute-start.16) | collective-permute-done | bytes 98336 | tf_op jit(solution)/shard_map/ppermute | solution.py:68
  40.3 1.1 %shard_map.41 = (bf16[6,256,256]{2,1,0:T(8,128)(2,1)S(1)}, bf16[6,256,256]{2,1,0:T(8,128)(2,1)S(1)}, f32[4,256,256]{2,1,0:T(8,128)S(1)}, f32[512,256]{1,0:T(8,128)S(1)}) custom-call(f32[2,6,16,256]{3,2,1,0:T(8,128)S(1)} %shard_map.40.refs_0_, f32[2,6,16,256]{3,2,1,0:T(8,128)S(1)} %collective-permute-done.10.refs_1_, ...), custom_call_target="tpu_custom_call" | custom-call | flops 301989888 | bytes 4194304 | tf_op jit(solution)/shard_map/pallas_call | solution.py:41
  41.4 1.0 %shard_map.42 = (bf16[6,256,256]{2,1,0:T(8,128)(2,1)S(1)}, bf16[6,256,256]{2,1,0:T(8,128)(2,1)S(1)}) custom-call(f32[2,6,16,256]{3,2,1,0:T(8,128)S(1)} %shard_map.39.refs_0_, f32[2,6,16,256]{3,2,1,0:T(8,128)S(1)} %collective-permute-done.2.refs_1_, f32[2,6,16,256]{3,2,1,0:T(8,128)S(1)} %collective-permute-done.6.refs_2_, ...), custom_call_target="tpu_custom_call" | custom-call | flops 603979776 | bytes 4194304 | tf_op jit(solution)/shard_map/pallas_call | solution.py:41
  42.4 2.5 %collective-permute-done.5.refs_0_ = f32[2,6,16,256]{3,2,1,0:T(8,128)S(1)} collective-permute-done((f32[2,6,16,256]{3,2,1,0:T(8,128)S(1)}, f32[2,6,16,256]{3,2,1,0:T(8,128)S(1)}, u32[]{:S(2)}, u32[]{:S(2)}) %collective-permute-start.5) | collective-permute-done | bytes 196640 | tf_op jit(solution)/shard_map/ppermute | solution.py:68
  44.9 2.7 %shard_map.46 = (f32[1024,256]{1,0:T(8,128)}, bf16[6,256,256]{2,1,0:T(8,128)(2,1)S(1)}, bf16[6,256,256]{2,1,0:T(8,128)(2,1)S(1)}) custom-call(f32[2,6,16,256]{3,2,1,0:T(8,128)S(1)} %collective-permute-done.5.refs_0_, bf16[6,256,256]{2,1,0:T(8,128)(2,1)S(1)} %get-tuple-element.23.refs_1_, ...), custom_call_target="tpu_custom_call", output_to_operand_aliasing={{1}: (1, {}), {2}: (2, {})} | custom-call | flops 1509949440 | bytes 4194304 | tf_op jit(solution)/shard_map/pallas_call | solution.py:41
  (47 shorter events, 6.2 us)
Async XLA Ops:
  2.6 6.6 %collective-permute-start.20 = (f32[2,6,16,256]{3,2,1,0:T(8,128)S(1)}, f32[2,6,16,256]{3,2,1,0:T(8,128)S(1)}, u32[]{:S(2)}, u32[]{:S(2)}) collective-permute-start(f32[2,6,16,256]{3,2,1,0:T(8,128)S(1)} %shard_map.43.refs_0_), channel_id=1, source_target_pairs={{1,5},{0,3},{5,9},{4,0},{9,13},{8,4},{13,14},{12,8},{14,10},{15,12... | collective-permute-start | bytes 589832 | tf_op jit(solution)/shard_map/ppermute | solution.py:68
  6.6 10.8 %collective-permute-start.10 = (f32[2,6,16,256]{3,2,1,0:T(8,128)S(1)}, f32[2,6,16,256]{3,2,1,0:T(8,128)S(1)}, u32[]{:S(2)}, u32[]{:S(2)}) collective-permute-start(f32[2,6,16,256]{3,2,1,0:T(8,128)S(1)} %shard_map.40.refs_0_), channel_id=1, source_target_pairs={{1,5},{0,3},{5,9},{4,0},{9,13},{8,4},{13,14},{12,8},{14,10},{15,12... | collective-permute-start | bytes 589832 | tf_op jit(solution)/shard_map/ppermute | solution.py:68
  9.2 9.6 %collective-permute-start.21 = (f32[2,6,16,256]{3,2,1,0:T(8,128)S(1)}, f32[2,6,16,256]{3,2,1,0:T(8,128)S(1)}, u32[]{:S(2)}, u32[]{:S(2)}) collective-permute-start(f32[2,6,16,256]{3,2,1,0:T(8,128)S(1)} %collective-permute-done.20.refs_1_), channel_id=1, source_target_pairs={{1,5},{0,3},{5,9},{4,0},{9,13},{8,4},{13,14},{12,8},{14,10},{15,12... | collective-permute-start | bytes 589832 | tf_op jit(solution)/shard_map/ppermute | solution.py:68
  10.6 4.3 %collective-permute-start = (f32[4,16,256]{2,1,0:T(8,128)S(1)}, f32[4,16,256]{2,1,0:T(8,128)S(1)}, u32[]{:S(2)}, u32[]{:S(2)}) collective-permute-start(f32[4,16,256]{2,1,0:T(8,128)S(1)} %get-tuple-element.19.refs_0_), channel_id=1, source_target_pairs={{16,0},{0,16},{17,1},{1,17},{18,2},{2,18},{19,3},{3,19},{20,4},{4,... | collective-permute-start | bytes 196616 | tf_op jit(solution)/shard_map/ppermute | solution.py:332
  14.9 1.7 %collective-permute-start.1 = (f32[6,16,256]{2,1,0:T(8,128)S(1)}, f32[6,16,256]{2,1,0:T(8,128)S(1)}, u32[]{:S(2)}, u32[]{:S(2)}) collective-permute-start(f32[6,16,256]{2,1,0:T(8,128)S(1)} %shard_map.38.own_ref), channel_id=1, source_target_pairs={{0,1},{1,0},{2,3},{3,2},{4,5},{5,4},{6,7},{7,6},{8,9},{9,8},{10,11... | collective-permute-start | bytes 294920 | tf_op jit(solution)/shard_map/ppermute | solution.py:336
  15.1 15.2 %collective-permute-start.18 = (f32[512,256]{1,0:T(8,128)S(1)}, f32[512,256]{1,0:T(8,128)S(1)}, u32[]{:S(2)}, u32[]{:S(2)}) collective-permute-start(f32[512,256]{1,0:T(8,128)S(1)} %slice.10), channel_id=1, source_target_pairs={{16,0},{0,16},{17,1},{1,17},{18,2},{2,18},{19,3},{3,19},{20,4},{4,... | collective-permute-start | bytes 1572872 | tf_op jit(solution)/shard_map/ppermute | solution.py:334
  16.7 5.7 %collective-permute-start.2 = (f32[2,6,16,256]{3,2,1,0:T(8,128)S(1)}, f32[2,6,16,256]{3,2,1,0:T(8,128)S(1)}, u32[]{:S(2)}, u32[]{:S(2)}) collective-permute-start(f32[2,6,16,256]{3,2,1,0:T(8,128)S(1)} %shard_map.39.refs_0_), channel_id=1, source_target_pairs={{1,5},{0,3},{5,9},{4,0},{9,13},{8,4},{13,14},{12,8},{14,10},{15,12... | collective-permute-start | bytes 589832 | tf_op jit(solution)/shard_map/ppermute | solution.py:68
  17.4 7.1 %collective-permute-start.12 = (f32[2,6,16,256]{3,2,1,0:T(8,128)S(1)}, f32[2,6,16,256]{3,2,1,0:T(8,128)S(1)}, u32[]{:S(2)}, u32[]{:S(2)}) collective-permute-start(f32[2,6,16,256]{3,2,1,0:T(8,128)S(1)} %collective-permute-done.10.refs_1_), channel_id=1, source_target_pairs={{1,5},{0,3},{5,9},{4,0},{9,13},{8,4},{13,14},{12,8},{14,10},{15,12... | collective-permute-start | bytes 589832 | tf_op jit(solution)/shard_map/ppermute | solution.py:68
  18.8 7.8 %collective-permute-start.22 = (f32[2,6,16,256]{3,2,1,0:T(8,128)S(1)}, f32[2,6,16,256]{3,2,1,0:T(8,128)S(1)}, u32[]{:S(2)}, u32[]{:S(2)}) collective-permute-start(f32[2,6,16,256]{3,2,1,0:T(8,128)S(1)} %collective-permute-done.21.refs_3_), channel_id=1, source_target_pairs={{1,5},{0,3},{5,9},{4,0},{9,13},{8,4},{13,14},{12,8},{14,10},{15,12... | collective-permute-start | bytes 589832 | tf_op jit(solution)/shard_map/ppermute | solution.py:68
  20.1 6.9 %collective-permute-start.25 = (f32[2,6,16,256]{3,2,1,0:T(8,128)S(1)}, f32[2,6,16,256]{3,2,1,0:T(8,128)S(1)}, u32[]{:S(2)}, u32[]{:S(2)}) collective-permute-start(f32[2,6,16,256]{3,2,1,0:T(8,128)S(1)} %collective-permute-done.20.refs_1_), channel_id=1, source_target_pairs={{0,1},{1,0},{2,3},{3,2},{4,5},{5,4},{6,7},{7,6},{8,9},{9,8},{10,11... | collective-permute-start | bytes 589832 | tf_op jit(solution)/shard_map/ppermute | solution.py:71
  22.4 4.7 %collective-permute-start.11 = (f32[2,6,16,256]{3,2,1,0:T(8,128)S(1)}, f32[2,6,16,256]{3,2,1,0:T(8,128)S(1)}, u32[]{:S(2)}, u32[]{:S(2)}) collective-permute-start(f32[2,6,16,256]{3,2,1,0:T(8,128)S(1)} %collective-permute-done.10.refs_1_), channel_id=1, source_target_pairs={{0,1},{1,0},{2,3},{3,2},{4,5},{5,4},{6,7},{7,6},{8,9},{9,8},{10,11... | collective-permute-start | bytes 589832 | tf_op jit(solution)/shard_map/ppermute | solution.py:71
  24.5 5.7 %collective-permute-start.3 = (f32[2,6,16,256]{3,2,1,0:T(8,128)S(1)}, f32[2,6,16,256]{3,2,1,0:T(8,128)S(1)}, u32[]{:S(2)}, u32[]{:S(2)}) collective-permute-start(f32[2,6,16,256]{3,2,1,0:T(8,128)S(1)} %collective-permute-done.2.refs_1_), channel_id=1, source_target_pairs={{1,5},{0,3},{5,9},{4,0},{9,13},{8,4},{13,14},{12,8},{14,10},{15,12... | collective-permute-start | bytes 589832 | tf_op jit(solution)/shard_map/ppermute | solution.py:68
  26.6 5.7 %collective-permute-start.14 = (f32[2,6,16,256]{3,2,1,0:T(8,128)S(1)}, f32[2,6,16,256]{3,2,1,0:T(8,128)S(1)}, u32[]{:S(2)}, u32[]{:S(2)}) collective-permute-start(f32[2,6,16,256]{3,2,1,0:T(8,128)S(1)} %collective-permute-done.12.refs_3_), channel_id=1, source_target_pairs={{1,5},{0,3},{5,9},{4,0},{9,13},{8,4},{13,14},{12,8},{14,10},{15,12... | collective-permute-start | bytes 589832 | tf_op jit(solution)/shard_map/ppermute | solution.py:68
  27.0 5.3 %collective-permute-start.26 = (f32[2,6,16,256]{3,2,1,0:T(8,128)S(1)}, f32[2,6,16,256]{3,2,1,0:T(8,128)S(1)}, u32[]{:S(2)}, u32[]{:S(2)}) collective-permute-start(f32[2,6,16,256]{3,2,1,0:T(8,128)S(1)} %collective-permute-done.21.refs_3_), channel_id=1, source_target_pairs={{0,1},{1,0},{2,3},{3,2},{4,5},{5,4},{6,7},{7,6},{8,9},{9,8},{10,11... | collective-permute-start | bytes 589832 | tf_op jit(solution)/shard_map/ppermute | solution.py:71
  27.1 10.9 %collective-permute-start.13 = (f32[2,6,16,256]{3,2,1,0:T(8,128)S(1)}, f32[2,6,16,256]{3,2,1,0:T(8,128)S(1)}, u32[]{:S(2)}, u32[]{:S(2)}) collective-permute-start(f32[2,6,16,256]{3,2,1,0:T(8,128)S(1)} %collective-permute-done.12.refs_3_), channel_id=1, source_target_pairs={{0,1},{1,0},{2,3},{3,2},{4,5},{5,4},{6,7},{7,6},{8,9},{9,8},{10,11... | collective-permute-start | bytes 589832 | tf_op jit(solution)/shard_map/ppermute | solution.py:71
  30.2 8.3 %collective-permute-start.4 = (f32[2,6,16,256]{3,2,1,0:T(8,128)S(1)}, f32[2,6,16,256]{3,2,1,0:T(8,128)S(1)}, u32[]{:S(2)}, u32[]{:S(2)}) collective-permute-start(f32[2,6,16,256]{3,2,1,0:T(8,128)S(1)} %collective-permute-done.3.refs_3_), channel_id=1, source_target_pairs={{1,5},{0,3},{5,9},{4,0},{9,13},{8,4},{13,14},{12,8},{14,10},{15,12... | collective-permute-start | bytes 589832 | tf_op jit(solution)/shard_map/ppermute | solution.py:68
  30.3 6.6 %collective-permute-start.23 = (f32[6,16,256]{2,1,0:T(8,128)S(1)}, f32[6,16,256]{2,1,0:T(8,128)S(1)}, u32[]{:S(2)}, u32[]{:S(2)}) collective-permute-start(f32[6,16,256]{2,1,0:T(8,128)S(1)} %slice_bitcast_fusion), channel_id=1, source_target_pairs={{1,5},{0,3},{5,9},{4,0},{9,13},{8,4},{13,14},{12,8},{14,10},{15,12... | collective-permute-start | bytes 294920 | tf_op jit(solution)/shard_map/ppermute | solution.py:68
  32.3 6.7 %collective-permute-start.27 = (f32[2,6,16,256]{3,2,1,0:T(8,128)S(1)}, f32[2,6,16,256]{3,2,1,0:T(8,128)S(1)}, u32[]{:S(2)}, u32[]{:S(2)}) collective-permute-start(f32[2,6,16,256]{3,2,1,0:T(8,128)S(1)} %collective-permute-done.22.refs_5_), channel_id=1, source_target_pairs={{0,1},{1,0},{2,3},{3,2},{4,5},{5,4},{6,7},{7,6},{8,9},{9,8},{10,11... | collective-permute-start | bytes 589832 | tf_op jit(solution)/shard_map/ppermute | solution.py:71
  32.3 5.6 %collective-permute-start.16 = (f32[6,16,256]{2,1,0:T(8,128)S(1)}, f32[6,16,256]{2,1,0:T(8,128)S(1)}, u32[]{:S(2)}, u32[]{:S(2)}) collective-permute-start(f32[6,16,256]{2,1,0:T(8,128)S(1)} %slice_bitcast_fusion.1), channel_id=1, source_target_pairs={{1,5},{0,3},{5,9},{4,0},{9,13},{8,4},{13,14},{12,8},{14,10},{15,12... | collective-permute-start | bytes 294920 | tf_op jit(solution)/shard_map/ppermute | solution.py:68
  38.0 2.3 %collective-permute-start.15 = (f32[2,6,16,256]{3,2,1,0:T(8,128)S(1)}, f32[2,6,16,256]{3,2,1,0:T(8,128)S(1)}, u32[]{:S(2)}, u32[]{:S(2)}) collective-permute-start(f32[2,6,16,256]{3,2,1,0:T(8,128)S(1)} %collective-permute-done.14.refs_5_), channel_id=1, source_target_pairs={{0,1},{1,0},{2,3},{3,2},{4,5},{5,4},{6,7},{7,6},{8,9},{9,8},{10,11... | collective-permute-start | bytes 589832 | tf_op jit(solution)/shard_map/ppermute | solution.py:71
  38.5 3.0 %collective-permute-start.6 = (f32[2,6,16,256]{3,2,1,0:T(8,128)S(1)}, f32[2,6,16,256]{3,2,1,0:T(8,128)S(1)}, u32[]{:S(2)}, u32[]{:S(2)}) collective-permute-start(f32[2,6,16,256]{3,2,1,0:T(8,128)S(1)} %collective-permute-done.2.refs_1_), channel_id=1, source_target_pairs={{0,1},{1,0},{2,3},{3,2},{4,5},{5,4},{6,7},{7,6},{8,9},{9,8},{10,11... | collective-permute-start | bytes 589832 | tf_op jit(solution)/shard_map/ppermute | solution.py:71
  38.5 2.9 %collective-permute-start.7 = (f32[2,6,16,256]{3,2,1,0:T(8,128)S(1)}, f32[2,6,16,256]{3,2,1,0:T(8,128)S(1)}, u32[]{:S(2)}, u32[]{:S(2)}) collective-permute-start(f32[2,6,16,256]{3,2,1,0:T(8,128)S(1)} %collective-permute-done.3.refs_3_), channel_id=1, source_target_pairs={{0,1},{1,0},{2,3},{3,2},{4,5},{5,4},{6,7},{7,6},{8,9},{9,8},{10,11... | collective-permute-start | bytes 589832 | tf_op jit(solution)/shard_map/ppermute | solution.py:71
  39.0 2.5 %collective-permute-start.8 = (f32[2,6,16,256]{3,2,1,0:T(8,128)S(1)}, f32[2,6,16,256]{3,2,1,0:T(8,128)S(1)}, u32[]{:S(2)}, u32[]{:S(2)}) collective-permute-start(f32[2,6,16,256]{3,2,1,0:T(8,128)S(1)} %collective-permute-done.4.refs_5_), channel_id=1, source_target_pairs={{0,1},{1,0},{2,3},{3,2},{4,5},{5,4},{6,7},{7,6},{8,9},{9,8},{10,11... | collective-permute-start | bytes 589832 | tf_op jit(solution)/shard_map/ppermute | solution.py:71
  39.3 5.7 %collective-permute-start.5 = (f32[2,6,16,256]{3,2,1,0:T(8,128)S(1)}, f32[2,6,16,256]{3,2,1,0:T(8,128)S(1)}, u32[]{:S(2)}, u32[]{:S(2)}) collective-permute-start(f32[2,6,16,256]{3,2,1,0:T(8,128)S(1)} %collective-permute-done.4.refs_5_), channel_id=1, source_target_pairs={{1,5},{0,3},{5,9},{4,0},{9,13},{8,4},{13,14},{12,8},{14,10},{15,12... | collective-permute-start | bytes 589832 | tf_op jit(solution)/shard_map/ppermute | solution.py:68
  (5 other events, 20.8 us)

commit v13 on v12

--- a/solution.py
+++ b/solution.py
@@ -164,8 +164,7 @@
     for block in range(plan.wide):
         at = (plan.sure + block) * nb
         copies.append((factor_hbm.at[:1, :, at : at + nb], inv_ref.at[panels + block : panels + block + 1]))
-        to = pl.ds(block * (panels - 1), panels - 1)
-        copies.append((factor_hbm.at[1:, :, at : at + nb], low_ref.at[to]))
+    copies.append((factor_hbm.at[1:, :, plan.sure * nb :], low_ref))
     copies = [pltpu.make_async_copy(*pair, sems.at[n]) for n, pair in enumerate(copies)]
     for copy in copies:
         copy.start()
@@ -174,9 +173,14 @@
 
 
 def pack_kernel(held, chosen, own_ref, other_ref, out_ref):
+    nb = out_ref.shape[3]
     for to, block in enumerate(chosen):
-        out_ref[0, to] = own_ref[held.index(block)]
-        out_ref[1, to] = other_ref[held.index(block)]
+        for side, ref in enumerate((own_ref, other_ref)):
+            if ref.shape[2] == nb:
+                out_ref[side, to] = ref[held.index(block)]
+            else:
+                _, panel, at = block
+                out_ref[side, to] = ref[panel - 1, :, at * nb : (at + 1) * nb]
 
 
 def tri_kernel(plan, *refs):
@@ -188,9 +192,8 @@
 
 
 def prep_kernel(plan, *refs):
-    count = len(refs) - 5 - plan.group_count
-    pieces, right_ref = refs[:count], refs[count]
-    received = refs[count + 1 : -5]
+    pieces, right_ref = refs[: plan.chips], refs[plan.chips]
+    received = refs[plan.chips + 1 : -5]
     high_ref, low_ref, start_ref, total_ref, whole_ref = refs[-5:]
     assemble(pieces, high_ref, low_ref, whole_ref, plan.chips)
     mats, nb = [(high_ref, low_ref)], plan.nb
@@ -212,11 +215,6 @@
 def place_kernel(plan, *refs):
     high_ref, low_ref, whole_ref = refs[-3:]
     assemble(refs[:-3], high_ref, low_ref, whole_ref, plan.chips, slice(0, len(refs) - 3))
-
-
-def late_kernel(plan, *refs):
-    *pieces, _, _, high_ref, low_ref = refs
-    assemble(pieces, high_ref, low_ref, None, plan.chips, slice(plan.chips - 1, None))
 
 
 def triangle_kernel(plan, count, *refs):
@@ -322,8 +320,12 @@
 
     mine, later, own = kernel_call(
         bound(load_kernel, plan),
-        [shape((len(b), depth, nb), f32) for b in (plan.chunks[0], plan.chunks[1], plan.sent)],
-        [pltpu.SemaphoreType.DMA((1 + plan.held + 2 * plan.wide,))],
+        [
+            shape((len(plan.chunks[0]), depth, nb), f32),
+            shape((panels - 1, depth, plan.wide * nb), f32),
+            shape((len(plan.sent), depth, nb), f32),
+        ],
+        [pltpu.SemaphoreType.DMA((2 + plan.held + plan.wide,))],
         [pltpu.with_memory_space_constraint(a, pltpu.HBM) for a in (factor_panels, inverses)],
         in_hbm=2,
     )
@@ -343,7 +345,7 @@
             [],
             ((mine, mine_other), (later, later_other), (half, half_other))[chunk],
         )
-        pieces.append(ring(packed, chips, halves=chunk < 2 and depth % 16 == 0))
+        pieces.append(ring(packed, chips, halves=chunk == 1 and depth % 16 == 0))
 
     pairs = [[shape((len(blocks), nb, nb), bf16)] * 2 for blocks in plan.chunks]
     wholes = [whole_scratch(len(blocks), nb, depth) for blocks in plan.chunks]
@@ -368,10 +370,7 @@
         (*early, inv_high, inv_low),
         flops=6 * 6 * nb * nb * nb,
     )
-    below = kernel_call(bound(place_kernel, plan), pairs[1], [wholes[1]], pieces[1][:count])
-    if count < chips:
-        ends = pieces[1][count:]
-        below = kernel_call(bound(late_kernel, plan), pairs[1], [], (*ends, *below), aliases={2: 0, 3: 1})
+    below = kernel_call(bound(place_kernel, plan), pairs[1], [wholes[1]], pieces[1])
     out, _, _ = kernel_call(
         bound(final_kernel, plan, len(late)),
         [shape(right_side.shape, f32), *pairs[2]],

time: 47.8 us -> 44.8 us (0.937)
  waiting for transfers between devices: 23.4 us -> 21.2 us
  starting transfers between devices: 17.8 us -> 17 us
    ppermute x12, waiting for transfers between devices: 18.3 us -> 16 us  [ring(): lax.ppermute(moving[0] if last and halves else moving, 'col', nearest)]
    ppermute x1, waiting for transfers between devices: 1.1 us -> 0.01 us  [per_device(): mine_other = lax.ppermute(mine, 'col', swap)]
    ppermute x11 -> x10, starting transfers between devices: 2.17 us -> 1.62 us  [ring(): pieces.append(lax.ppermute(moving, 'col', swap))]
    ppermute x11 -> x10, waiting for transfers between devices: 0.22 us -> 0.74 us  [ring(): pieces.append(lax.ppermute(moving, 'col', swap))]
    pallas_call x10 -> x9, Pallas kernels: 6.25 us -> 6.26 us  [kernel_call(): pl.pallas_call(body, out_shape=out_shapes, in_specs=[hbm] * in_hbm + [nea...]
  transfers between devices with their start and end apart: 28 -> 27, of which waited for: 13 -> 14; matrix products, arithmetic and copies ran while one was open for 0% -> 0% of each run, Pallas kernels for 5% -> 5%
where the time goes in v13:
time: 44.8 us; the launch traced here: 44.6 us
  waiting for transfers between devices  21.2 us (47%)
  starting transfers between devices  17 us (38%)
  Pallas kernels  6.26 us (14%)
    ppermute x12, waiting for transfers between devices, ring(): lax.ppermute(moving[0] if last and halves else moving, 'col', nearest)  16 us
    ppermute x12, starting transfers between devices, ring(): lax.ppermute(moving[0] if last and halves else moving, 'col', nearest)  11.7 us
    pallas_call x9, Pallas kernels, kernel_call(): pl.pallas_call(body, out_shape=out_shapes, in_specs=[hbm] * in_hbm + [nea...  6.26 us
    ppermute x1, waiting for transfers between devices, per_device(): tri = [own] + [lax.ppermute(own, 'row', pairs) for pairs in shifts]  2.74 us
    ppermute x10, starting transfers between devices, ring(): pieces.append(lax.ppermute(moving, 'col', swap))  1.62 us
    ppermute x1, starting transfers between devices, per_device(): received = [lax.ppermute(above, 'row', pairs) for pairs in shifts]  1.58 us
    ppermute x1, starting transfers between devices, per_device(): tri = [own] + [lax.ppermute(own, 'row', pairs) for pairs in shifts]  1.52 us
    ppermute x1, waiting for transfers between devices, per_device(): later_other = lax.ppermute(later, 'col', swap)  0.94 us
  transfers between devices with their start and end apart: 27, of which 14 were waited for; matrix products, arithmetic and copies ran while one was open for 0% of the time, Pallas kernels for 5%

profile of v13, /device:TPU:0, one launch (start us, length us, event | category | flops | bytes accessed | tf_op | source)
XLA Modules:
  0.0 44.6 jit_solution(12879010823743848977)
XLA Ops:
  0.0 1.1 %shard_map.37 = (f32[6,16,256]{2,1,0:T(8,128)S(1)}, f32[3,16,512]{2,1,0:T(8,128)S(1)}, f32[4,16,256]{2,1,0:T(8,128)S(1)}) custom-call(f32[4,16,1024]{2,1,0:T(8,128)} %factor_hbm.1, f32[4,16,256]{2,1,0:T(8,128)} %inv_hbm.1), custom_call_target="tpu_custom_call" | custom-call | bytes 4194304 | tf_op jit(solution)/shard_map/pallas_call | solution.py:41
  1.7 0.9 %collective-permute-done.18.other_ref = f32[3,16,512]{2,1,0:T(8,128)S(1)} collective-permute-done((f32[3,16,512]{2,1,0:T(8,128)S(1)}, f32[3,16,512]{2,1,0:T(8,128)S(1)}, u32[]{:S(2)}, u32[]{:S(2)}) %collective-permute-start.18) | collective-permute-done | bytes 98336 | tf_op jit(solution)/shard_map/ppermute | solution.py:333
  2.7 2.6 %collective-permute-start.19 = (f32[2,6,16,256]{3,2,1,0:T(8,128)S(1)}, f32[2,6,16,256]{3,2,1,0:T(8,128)S(1)}, u32[]{:S(2)}, u32[]{:S(2)}) collective-permute-start(f32[2,6,16,256]{3,2,1,0:T(8,128)S(1)} %shard_map.43.refs_0_), channel_id=1, source_target_pairs={{1,5},{0,3},{5,9},{4,0},{9,13},{8,4},{13,14},{12,8},{14,10},{15,12... | collective-permute-start | bytes 589832 | tf_op jit(solution)/shard_map/ppermute | solution.py:68
  5.3 1.5 %collective-permute-start = (f32[4,16,256]{2,1,0:T(8,128)S(1)}, f32[4,16,256]{2,1,0:T(8,128)S(1)}, u32[]{:S(2)}, u32[]{:S(2)}) collective-permute-start(f32[4,16,256]{2,1,0:T(8,128)S(1)} %get-tuple-element.17.refs_0_), channel_id=1, source_target_pairs={{16,0},{0,16},{17,1},{1,17},{18,2},{2,18},{19,3},{3,19},{20,4},{4,... | collective-permute-start | bytes 196616 | tf_op jit(solution)/shard_map/ppermute | solution.py:334
  6.8 2.7 %collective-permute-done.refs_1_ = f32[4,16,256]{2,1,0:T(8,128)S(1)} collective-permute-done((f32[4,16,256]{2,1,0:T(8,128)S(1)}, f32[4,16,256]{2,1,0:T(8,128)S(1)}, u32[]{:S(2)}, u32[]{:S(2)}) %collective-permute-start) | collective-permute-done | bytes 65568 | tf_op jit(solution)/shard_map/ppermute | solution.py:334
  9.7 0.8 %collective-permute-start.10 = (f32[2,6,16,256]{3,2,1,0:T(8,128)S(1)}, f32[2,6,16,256]{3,2,1,0:T(8,128)S(1)}, u32[]{:S(2)}, u32[]{:S(2)}) collective-permute-start(f32[2,6,16,256]{3,2,1,0:T(8,128)S(1)} %shard_map.40.refs_0_), channel_id=1, source_target_pairs={{1,5},{0,3},{5,9},{4,0},{9,13},{8,4},{13,14},{12,8},{14,10},{15,12... | collective-permute-start | bytes 589832 | tf_op jit(solution)/shard_map/ppermute | solution.py:68
  11.0 1.6 %collective-permute-start.2 = (f32[2,6,16,256]{3,2,1,0:T(8,128)S(1)}, f32[2,6,16,256]{3,2,1,0:T(8,128)S(1)}, u32[]{:S(2)}, u32[]{:S(2)}) collective-permute-start(f32[2,6,16,256]{3,2,1,0:T(8,128)S(1)} %shard_map.39.refs_0_), channel_id=1, source_target_pairs={{1,5},{0,3},{5,9},{4,0},{9,13},{8,4},{13,14},{12,8},{14,10},{15,12... | collective-permute-start | bytes 589832 | tf_op jit(solution)/shard_map/ppermute | solution.py:68
  12.6 1.3 %collective-permute-start.21 = (f32[2,6,16,256]{3,2,1,0:T(8,128)S(1)}, f32[2,6,16,256]{3,2,1,0:T(8,128)S(1)}, u32[]{:S(2)}, u32[]{:S(2)}) collective-permute-start(f32[2,6,16,256]{3,2,1,0:T(8,128)S(1)} %collective-permute-done.19.refs_1_), channel_id=1, source_target_pairs={{1,5},{0,3},{5,9},{4,0},{9,13},{8,4},{13,14},{12,8},{14,10},{15,12... | collective-permute-start | bytes 589832 | tf_op jit(solution)/shard_map/ppermute | solution.py:68
  13.9 1.6 %collective-permute-start.17 = (f32[512,256]{1,0:T(8,128)S(1)}, f32[512,256]{1,0:T(8,128)S(1)}, u32[]{:S(2)}, u32[]{:S(2)}) collective-permute-start(f32[512,256]{1,0:T(8,128)S(1)} %slice.6), channel_id=1, source_target_pairs={{16,0},{0,16},{17,1},{1,17},{18,2},{2,18},{19,3},{3,19},{20,4},{4,... | collective-permute-start | bytes 1572872 | tf_op jit(solution)/shard_map/ppermute | solution.py:336
  15.5 0.6 %collective-permute-start.12 = (f32[2,6,16,256]{3,2,1,0:T(8,128)S(1)}, f32[2,6,16,256]{3,2,1,0:T(8,128)S(1)}, u32[]{:S(2)}, u32[]{:S(2)}) collective-permute-start(f32[2,6,16,256]{3,2,1,0:T(8,128)S(1)} %collective-permute-done.10.refs_1_), channel_id=1, source_target_pairs={{1,5},{0,3},{5,9},{4,0},{9,13},{8,4},{13,14},{12,8},{14,10},{15,12... | collective-permute-start | bytes 589832 | tf_op jit(solution)/shard_map/ppermute | solution.py:68
  16.2 1.4 %collective-permute-done.2.refs_1_ = f32[2,6,16,256]{3,2,1,0:T(8,128)S(1)} collective-permute-done((f32[2,6,16,256]{3,2,1,0:T(8,128)S(1)}, f32[2,6,16,256]{3,2,1,0:T(8,128)S(1)}, u32[]{:S(2)}, u32[]{:S(2)}) %collective-permute-start.2) | collective-permute-done | bytes 196640 | tf_op jit(solution)/shard_map/ppermute | solution.py:68
  17.8 1.9 %collective-permute-done.21.refs_3_ = f32[2,6,16,256]{3,2,1,0:T(8,128)S(1)} collective-permute-done((f32[2,6,16,256]{3,2,1,0:T(8,128)S(1)}, f32[2,6,16,256]{3,2,1,0:T(8,128)S(1)}, u32[]{:S(2)}, u32[]{:S(2)}) %collective-permute-start.21) | collective-permute-done | bytes 196640 | tf_op jit(solution)/shard_map/ppermute | solution.py:68
  20.1 1.4 %collective-permute-start.3 = (f32[2,6,16,256]{3,2,1,0:T(8,128)S(1)}, f32[2,6,16,256]{3,2,1,0:T(8,128)S(1)}, u32[]{:S(2)}, u32[]{:S(2)}) collective-permute-start(f32[2,6,16,256]{3,2,1,0:T(8,128)S(1)} %collective-permute-done.2.refs_1_), channel_id=1, source_target_pairs={{1,5},{0,3},{5,9},{4,0},{9,13},{8,4},{13,14},{12,8},{14,10},{15,12... | collective-permute-start | bytes 589832 | tf_op jit(solution)/shard_map/ppermute | solution.py:68
  22.0 1.0 %collective-permute-start.14 = (f32[2,6,16,256]{3,2,1,0:T(8,128)S(1)}, f32[2,6,16,256]{3,2,1,0:T(8,128)S(1)}, u32[]{:S(2)}, u32[]{:S(2)}) collective-permute-start(f32[2,6,16,256]{3,2,1,0:T(8,128)S(1)} %collective-permute-done.12.refs_3_), channel_id=1, source_target_pairs={{1,5},{0,3},{5,9},{4,0},{9,13},{8,4},{13,14},{12,8},{14,10},{15,12... | collective-permute-start | bytes 589832 | tf_op jit(solution)/shard_map/ppermute | solution.py:68
  23.0 2.3 %collective-permute-done.23.refs_5_ = f32[2,6,16,256]{3,2,1,0:T(8,128)S(1)} collective-permute-done((f32[2,6,16,256]{3,2,1,0:T(8,128)S(1)}, f32[2,6,16,256]{3,2,1,0:T(8,128)S(1)}, u32[]{:S(2)}, u32[]{:S(2)}) %collective-permute-start.23) | collective-permute-done | bytes 196640 | tf_op jit(solution)/shard_map/ppermute | solution.py:68
  25.3 2.1 %collective-permute-done.3.refs_3_ = f32[2,6,16,256]{3,2,1,0:T(8,128)S(1)} collective-permute-done((f32[2,6,16,256]{3,2,1,0:T(8,128)S(1)}, f32[2,6,16,256]{3,2,1,0:T(8,128)S(1)}, u32[]{:S(2)}, u32[]{:S(2)}) %collective-permute-start.3) | collective-permute-done | bytes 196640 | tf_op jit(solution)/shard_map/ppermute | solution.py:68
  27.9 0.7 %collective-permute-start.25 = (f32[6,16,256]{2,1,0:T(8,128)S(1)}, f32[6,16,256]{2,1,0:T(8,128)S(1)}, u32[]{:S(2)}, u32[]{:S(2)}) collective-permute-start(f32[6,16,256]{2,1,0:T(8,128)S(1)} %slice_bitcast_fusion), channel_id=1, source_target_pairs={{1,5},{0,3},{5,9},{4,0},{9,13},{8,4},{13,14},{12,8},{14,10},{15,12... | collective-permute-start | bytes 294920 | tf_op jit(solution)/shard_map/ppermute | solution.py:68
  28.7 0.9 %collective-permute-done.14.refs_5_ = f32[2,6,16,256]{3,2,1,0:T(8,128)S(1)} collective-permute-done((f32[2,6,16,256]{3,2,1,0:T(8,128)S(1)}, f32[2,6,16,256]{3,2,1,0:T(8,128)S(1)}, u32[]{:S(2)}, u32[]{:S(2)}) %collective-permute-start.14) | collective-permute-done | bytes 196640 | tf_op jit(solution)/shard_map/ppermute | solution.py:68
  29.8 4.3 %collective-permute-done.25.refs_7_ = f32[6,16,256]{2,1,0:T(8,128)S(1)} collective-permute-done((f32[6,16,256]{2,1,0:T(8,128)S(1)}, f32[6,16,256]{2,1,0:T(8,128)S(1)}, u32[]{:S(2)}, u32[]{:S(2)}) %collective-permute-start.25) | collective-permute-done | bytes 98336 | tf_op jit(solution)/shard_map/ppermute | solution.py:68
  34.7 0.7 %collective-permute-done.26.refs_8_ = f32[6,16,256]{2,1,0:T(8,128)S(1)} collective-permute-done((f32[6,16,256]{2,1,0:T(8,128)S(1)}, f32[6,16,256]{2,1,0:T(8,128)S(1)}, u32[]{:S(2)}, u32[]{:S(2)}) %collective-permute-start.26) | collective-permute-done | bytes 98336 | tf_op jit(solution)/shard_map/ppermute | solution.py:71
  37.2 1.1 %shard_map.41 = (bf16[6,256,256]{2,1,0:T(8,128)(2,1)S(1)}, bf16[6,256,256]{2,1,0:T(8,128)(2,1)S(1)}, f32[4,256,256]{2,1,0:T(8,128)S(1)}, f32[512,256]{1,0:T(8,128)S(1)}) custom-call(f32[2,6,16,256]{3,2,1,0:T(8,128)S(1)} %shard_map.40.refs_0_, f32[2,6,16,256]{3,2,1,0:T(8,128)S(1)} %collective-permute-done.10.refs_1_, ...), custom_call_target="tpu_custom_call" | custom-call | flops 301989888 | bytes 4194304 | tf_op jit(solution)/shard_map/pallas_call | solution.py:41
  38.3 1.0 %shard_map.42 = (bf16[6,256,256]{2,1,0:T(8,128)(2,1)S(1)}, bf16[6,256,256]{2,1,0:T(8,128)(2,1)S(1)}) custom-call(f32[2,6,16,256]{3,2,1,0:T(8,128)S(1)} %shard_map.39.refs_0_, f32[2,6,16,256]{3,2,1,0:T(8,128)S(1)} %collective-permute-done.2.refs_1_, f32[2,6,16,256]{3,2,1,0:T(8,128)S(1)} %collective-permute-done.6.refs_2_, ...), custom_call_target="tpu_custom_call" | custom-call | flops 603979776 | bytes 4194304 | tf_op jit(solution)/shard_map/pallas_call | solution.py:41
  39.3 2.7 %collective-permute-done.5.refs_0_ = f32[2,6,16,256]{3,2,1,0:T(8,128)S(1)} collective-permute-done((f32[2,6,16,256]{3,2,1,0:T(8,128)S(1)}, f32[2,6,16,256]{3,2,1,0:T(8,128)S(1)}, u32[]{:S(2)}, u32[]{:S(2)}) %collective-permute-start.5) | collective-permute-done | bytes 196640 | tf_op jit(solution)/shard_map/ppermute | solution.py:68
  41.9 2.7 %shard_map.45 = (f32[1024,256]{1,0:T(8,128)}, bf16[6,256,256]{2,1,0:T(8,128)(2,1)S(1)}, bf16[6,256,256]{2,1,0:T(8,128)(2,1)S(1)}) custom-call(f32[2,6,16,256]{3,2,1,0:T(8,128)S(1)} %collective-permute-done.5.refs_0_, bf16[6,256,256]{2,1,0:T(8,128)(2,1)S(1)} %get-tuple-element.21.refs_1_, ...), custom_call_target="tpu_custom_call", output_to_operand_aliasing={{1}: (1, {}), {2}: (2, {})} | custom-call | flops 1509949440 | bytes 4194304 | tf_op jit(solution)/shard_map/pallas_call | solution.py:41
  (43 shorter events, 5.4 us)
Async XLA Ops:
  2.7 9.9 %collective-permute-start.19 = (f32[2,6,16,256]{3,2,1,0:T(8,128)S(1)}, f32[2,6,16,256]{3,2,1,0:T(8,128)S(1)}, u32[]{:S(2)}, u32[]{:S(2)}) collective-permute-start(f32[2,6,16,256]{3,2,1,0:T(8,128)S(1)} %shard_map.43.refs_0_), channel_id=1, source_target_pairs={{1,5},{0,3},{5,9},{4,0},{9,13},{8,4},{13,14},{12,8},{14,10},{15,12... | collective-permute-start | bytes 589832 | tf_op jit(solution)/shard_map/ppermute | solution.py:68
  5.3 4.3 %collective-permute-start = (f32[4,16,256]{2,1,0:T(8,128)S(1)}, f32[4,16,256]{2,1,0:T(8,128)S(1)}, u32[]{:S(2)}, u32[]{:S(2)}) collective-permute-start(f32[4,16,256]{2,1,0:T(8,128)S(1)} %get-tuple-element.17.refs_0_), channel_id=1, source_target_pairs={{16,0},{0,16},{17,1},{1,17},{18,2},{2,18},{19,3},{3,19},{20,4},{4,... | collective-permute-start | bytes 196616 | tf_op jit(solution)/shard_map/ppermute | solution.py:334
  6.8 2.8 %collective-permute-start.9 = (f32[6,16,256]{2,1,0:T(8,128)S(1)}, f32[6,16,256]{2,1,0:T(8,128)S(1)}, u32[]{:S(2)}, u32[]{:S(2)}) collective-permute-start(f32[6,16,256]{2,1,0:T(8,128)S(1)} %get-tuple-element.18.own_ref), channel_id=1, source_target_pairs={{0,1},{1,0},{2,3},{3,2},{4,5},{5,4},{6,7},{7,6},{8,9},{9,8},{10,11... | collective-permute-start | bytes 294920 | tf_op jit(solution)/shard_map/ppermute | solution.py:332
  9.7 5.8 %collective-permute-start.10 = (f32[2,6,16,256]{3,2,1,0:T(8,128)S(1)}, f32[2,6,16,256]{3,2,1,0:T(8,128)S(1)}, u32[]{:S(2)}, u32[]{:S(2)}) collective-permute-start(f32[2,6,16,256]{3,2,1,0:T(8,128)S(1)} %shard_map.40.refs_0_), channel_id=1, source_target_pairs={{1,5},{0,3},{5,9},{4,0},{9,13},{8,4},{13,14},{12,8},{14,10},{15,12... | collective-permute-start | bytes 589832 | tf_op jit(solution)/shard_map/ppermute | solution.py:68
  11.0 6.6 %collective-permute-start.2 = (f32[2,6,16,256]{3,2,1,0:T(8,128)S(1)}, f32[2,6,16,256]{3,2,1,0:T(8,128)S(1)}, u32[]{:S(2)}, u32[]{:S(2)}) collective-permute-start(f32[2,6,16,256]{3,2,1,0:T(8,128)S(1)} %shard_map.39.refs_0_), channel_id=1, source_target_pairs={{1,5},{0,3},{5,9},{4,0},{9,13},{8,4},{13,14},{12,8},{14,10},{15,12... | collective-permute-start | bytes 589832 | tf_op jit(solution)/shard_map/ppermute | solution.py:68
  12.6 7.1 %collective-permute-start.21 = (f32[2,6,16,256]{3,2,1,0:T(8,128)S(1)}, f32[2,6,16,256]{3,2,1,0:T(8,128)S(1)}, u32[]{:S(2)}, u32[]{:S(2)}) collective-permute-start(f32[2,6,16,256]{3,2,1,0:T(8,128)S(1)} %collective-permute-done.19.refs_1_), channel_id=1, source_target_pairs={{1,5},{0,3},{5,9},{4,0},{9,13},{8,4},{13,14},{12,8},{14,10},{15,12... | collective-permute-start | bytes 589832 | tf_op jit(solution)/shard_map/ppermute | solution.py:68
  13.9 13.9 %collective-permute-start.17 = (f32[512,256]{1,0:T(8,128)S(1)}, f32[512,256]{1,0:T(8,128)S(1)}, u32[]{:S(2)}, u32[]{:S(2)}) collective-permute-start(f32[512,256]{1,0:T(8,128)S(1)} %slice.6), channel_id=1, source_target_pairs={{16,0},{0,16},{17,1},{1,17},{18,2},{2,18},{19,3},{3,19},{20,4},{4,... | collective-permute-start | bytes 1572872 | tf_op jit(solution)/shard_map/ppermute | solution.py:336
  15.5 4.6 %collective-permute-start.20 = (f32[2,6,16,256]{3,2,1,0:T(8,128)S(1)}, f32[2,6,16,256]{3,2,1,0:T(8,128)S(1)}, u32[]{:S(2)}, u32[]{:S(2)}) collective-permute-start(f32[2,6,16,256]{3,2,1,0:T(8,128)S(1)} %collective-permute-done.19.refs_1_), channel_id=1, source_target_pairs={{0,1},{1,0},{2,3},{3,2},{4,5},{5,4},{6,7},{7,6},{8,9},{9,8},{10,11... | collective-permute-start | bytes 589832 | tf_op jit(solution)/shard_map/ppermute | solution.py:71
  15.5 6.2 %collective-permute-start.12 = (f32[2,6,16,256]{3,2,1,0:T(8,128)S(1)}, f32[2,6,16,256]{3,2,1,0:T(8,128)S(1)}, u32[]{:S(2)}, u32[]{:S(2)}) collective-permute-start(f32[2,6,16,256]{3,2,1,0:T(8,128)S(1)} %collective-permute-done.10.refs_1_), channel_id=1, source_target_pairs={{1,5},{0,3},{5,9},{4,0},{9,13},{8,4},{13,14},{12,8},{14,10},{15,12... | collective-permute-start | bytes 589832 | tf_op jit(solution)/shard_map/ppermute | solution.py:68
  17.5 4.4 %collective-permute-start.11 = (f32[2,6,16,256]{3,2,1,0:T(8,128)S(1)}, f32[2,6,16,256]{3,2,1,0:T(8,128)S(1)}, u32[]{:S(2)}, u32[]{:S(2)}) collective-permute-start(f32[2,6,16,256]{3,2,1,0:T(8,128)S(1)} %collective-permute-done.10.refs_1_), channel_id=1, source_target_pairs={{0,1},{1,0},{2,3},{3,2},{4,5},{5,4},{6,7},{7,6},{8,9},{9,8},{10,11... | collective-permute-start | bytes 589832 | tf_op jit(solution)/shard_map/ppermute | solution.py:71
  19.7 5.7 %collective-permute-start.23 = (f32[2,6,16,256]{3,2,1,0:T(8,128)S(1)}, f32[2,6,16,256]{3,2,1,0:T(8,128)S(1)}, u32[]{:S(2)}, u32[]{:S(2)}) collective-permute-start(f32[2,6,16,256]{3,2,1,0:T(8,128)S(1)} %collective-permute-done.21.refs_3_), channel_id=1, source_target_pairs={{1,5},{0,3},{5,9},{4,0},{9,13},{8,4},{13,14},{12,8},{14,10},{15,12... | collective-permute-start | bytes 589832 | tf_op jit(solution)/shard_map/ppermute | solution.py:68
  20.1 7.3 %collective-permute-start.3 = (f32[2,6,16,256]{3,2,1,0:T(8,128)S(1)}, f32[2,6,16,256]{3,2,1,0:T(8,128)S(1)}, u32[]{:S(2)}, u32[]{:S(2)}) collective-permute-start(f32[2,6,16,256]{3,2,1,0:T(8,128)S(1)} %collective-permute-done.2.refs_1_), channel_id=1, source_target_pairs={{1,5},{0,3},{5,9},{4,0},{9,13},{8,4},{13,14},{12,8},{14,10},{15,12... | collective-permute-start | bytes 589832 | tf_op jit(solution)/shard_map/ppermute | solution.py:68
  21.8 6.8 %collective-permute-start.22 = (f32[2,6,16,256]{3,2,1,0:T(8,128)S(1)}, f32[2,6,16,256]{3,2,1,0:T(8,128)S(1)}, u32[]{:S(2)}, u32[]{:S(2)}) collective-permute-start(f32[2,6,16,256]{3,2,1,0:T(8,128)S(1)} %collective-permute-done.21.refs_3_), channel_id=1, source_target_pairs={{0,1},{1,0},{2,3},{3,2},{4,5},{5,4},{6,7},{7,6},{8,9},{9,8},{10,11... | collective-permute-start | bytes 589832 | tf_op jit(solution)/shard_map/ppermute | solution.py:71
  22.0 7.6 %collective-permute-start.14 = (f32[2,6,16,256]{3,2,1,0:T(8,128)S(1)}, f32[2,6,16,256]{3,2,1,0:T(8,128)S(1)}, u32[]{:S(2)}, u32[]{:S(2)}) collective-permute-start(f32[2,6,16,256]{3,2,1,0:T(8,128)S(1)} %collective-permute-done.12.refs_3_), channel_id=1, source_target_pairs={{1,5},{0,3},{5,9},{4,0},{9,13},{8,4},{13,14},{12,8},{14,10},{15,12... | collective-permute-start | bytes 589832 | tf_op jit(solution)/shard_map/ppermute | solution.py:68
  25.3 8.8 %collective-permute-start.13 = (f32[2,6,16,256]{3,2,1,0:T(8,128)S(1)}, f32[2,6,16,256]{3,2,1,0:T(8,128)S(1)}, u32[]{:S(2)}, u32[]{:S(2)}) collective-permute-start(f32[2,6,16,256]{3,2,1,0:T(8,128)S(1)} %collective-permute-done.12.refs_3_), channel_id=1, source_target_pairs={{0,1},{1,0},{2,3},{3,2},{4,5},{5,4},{6,7},{7,6},{8,9},{9,8},{10,11... | collective-permute-start | bytes 589832 | tf_op jit(solution)/shard_map/ppermute | solution.py:71
  27.4 7.2 %collective-permute-start.4 = (f32[2,6,16,256]{3,2,1,0:T(8,128)S(1)}, f32[2,6,16,256]{3,2,1,0:T(8,128)S(1)}, u32[]{:S(2)}, u32[]{:S(2)}) collective-permute-start(f32[2,6,16,256]{3,2,1,0:T(8,128)S(1)} %collective-permute-done.3.refs_3_), channel_id=1, source_target_pairs={{1,5},{0,3},{5,9},{4,0},{9,13},{8,4},{13,14},{12,8},{14,10},{15,12... | collective-permute-start | bytes 589832 | tf_op jit(solution)/shard_map/ppermute | solution.py:68
  27.9 6.3 %collective-permute-start.25 = (f32[6,16,256]{2,1,0:T(8,128)S(1)}, f32[6,16,256]{2,1,0:T(8,128)S(1)}, u32[]{:S(2)}, u32[]{:S(2)}) collective-permute-start(f32[6,16,256]{2,1,0:T(8,128)S(1)} %slice_bitcast_fusion), channel_id=1, source_target_pairs={{1,5},{0,3},{5,9},{4,0},{9,13},{8,4},{13,14},{12,8},{14,10},{15,12... | collective-permute-start | bytes 294920 | tf_op jit(solution)/shard_map/ppermute | solution.py:68
  28.6 7.1 %collective-permute-start.24 = (f32[2,6,16,256]{3,2,1,0:T(8,128)S(1)}, f32[2,6,16,256]{3,2,1,0:T(8,128)S(1)}, u32[]{:S(2)}, u32[]{:S(2)}) collective-permute-start(f32[2,6,16,256]{3,2,1,0:T(8,128)S(1)} %collective-permute-done.23.refs_5_), channel_id=1, source_target_pairs={{0,1},{1,0},{2,3},{3,2},{4,5},{5,4},{6,7},{7,6},{8,9},{9,8},{10,11... | collective-permute-start | bytes 589832 | tf_op jit(solution)/shard_map/ppermute | solution.py:71
  29.5 6.7 %collective-permute-start.16 = (f32[2,6,16,256]{3,2,1,0:T(8,128)S(1)}, f32[2,6,16,256]{3,2,1,0:T(8,128)S(1)}, u32[]{:S(2)}, u32[]{:S(2)}) collective-permute-start(f32[2,6,16,256]{3,2,1,0:T(8,128)S(1)} %collective-permute-done.14.refs_5_), channel_id=1, source_target_pairs={{1,5},{0,3},{5,9},{4,0},{9,13},{8,4},{13,14},{12,8},{14,10},{15,12... | collective-permute-start | bytes 589832 | tf_op jit(solution)/shard_map/ppermute | solution.py:68
  34.2 3.0 %collective-permute-start.15 = (f32[2,6,16,256]{3,2,1,0:T(8,128)S(1)}, f32[2,6,16,256]{3,2,1,0:T(8,128)S(1)}, u32[]{:S(2)}, u32[]{:S(2)}) collective-permute-start(f32[2,6,16,256]{3,2,1,0:T(8,128)S(1)} %collective-permute-done.14.refs_5_), channel_id=1, source_target_pairs={{0,1},{1,0},{2,3},{3,2},{4,5},{5,4},{6,7},{7,6},{8,9},{9,8},{10,11... | collective-permute-start | bytes 589832 | tf_op jit(solution)/shard_map/ppermute | solution.py:71
  34.7 3.6 %collective-permute-start.6 = (f32[2,6,16,256]{3,2,1,0:T(8,128)S(1)}, f32[2,6,16,256]{3,2,1,0:T(8,128)S(1)}, u32[]{:S(2)}, u32[]{:S(2)}) collective-permute-start(f32[2,6,16,256]{3,2,1,0:T(8,128)S(1)} %collective-permute-done.2.refs_1_), channel_id=1, source_target_pairs={{0,1},{1,0},{2,3},{3,2},{4,5},{5,4},{6,7},{7,6},{8,9},{9,8},{10,11... | collective-permute-start | bytes 589832 | tf_op jit(solution)/shard_map/ppermute | solution.py:71
  35.5 2.8 %collective-permute-start.7 = (f32[2,6,16,256]{3,2,1,0:T(8,128)S(1)}, f32[2,6,16,256]{3,2,1,0:T(8,128)S(1)}, u32[]{:S(2)}, u32[]{:S(2)}) collective-permute-start(f32[2,6,16,256]{3,2,1,0:T(8,128)S(1)} %collective-permute-done.3.refs_3_), channel_id=1, source_target_pairs={{0,1},{1,0},{2,3},{3,2},{4,5},{5,4},{6,7},{7,6},{8,9},{9,8},{10,11... | collective-permute-start | bytes 589832 | tf_op jit(solution)/shard_map/ppermute | solution.py:71
  35.6 2.7 %collective-permute-start.8 = (f32[2,6,16,256]{3,2,1,0:T(8,128)S(1)}, f32[2,6,16,256]{3,2,1,0:T(8,128)S(1)}, u32[]{:S(2)}, u32[]{:S(2)}) collective-permute-start(f32[2,6,16,256]{3,2,1,0:T(8,128)S(1)} %collective-permute-done.4.refs_5_), channel_id=1, source_target_pairs={{0,1},{1,0},{2,3},{3,2},{4,5},{5,4},{6,7},{7,6},{8,9},{9,8},{10,11... | collective-permute-start | bytes 589832 | tf_op jit(solution)/shard_map/ppermute | solution.py:71
  36.3 5.7 %collective-permute-start.5 = (f32[2,6,16,256]{3,2,1,0:T(8,128)S(1)}, f32[2,6,16,256]{3,2,1,0:T(8,128)S(1)}, u32[]{:S(2)}, u32[]{:S(2)}) collective-permute-start(f32[2,6,16,256]{3,2,1,0:T(8,128)S(1)} %collective-permute-done.4.refs_5_), channel_id=1, source_target_pairs={{1,5},{0,3},{5,9},{4,0},{9,13},{8,4},{13,14},{12,8},{14,10},{15,12... | collective-permute-start | bytes 589832 | tf_op jit(solution)/shard_map/ppermute | solution.py:68
  (4 other events, 18.1 us)

commit v14 on v12

--- a/solution.py
+++ b/solution.py
@@ -188,9 +188,8 @@
 
 
 def prep_kernel(plan, *refs):
-    count = len(refs) - 5 - plan.group_count
-    pieces, right_ref = refs[:count], refs[count]
-    received = refs[count + 1 : -5]
+    pieces, right_ref = refs[: plan.chips], refs[plan.chips]
+    received = refs[plan.chips + 1 : -5]
     high_ref, low_ref, start_ref, total_ref, whole_ref = refs[-5:]
     assemble(pieces, high_ref, low_ref, whole_ref, plan.chips)
     mats, nb = [(high_ref, low_ref)], plan.nb
@@ -212,11 +211,6 @@
 def place_kernel(plan, *refs):
     high_ref, low_ref, whole_ref = refs[-3:]
     assemble(refs[:-3], high_ref, low_ref, whole_ref, plan.chips, slice(0, len(refs) - 3))
-
-
-def late_kernel(plan, *refs):
-    *pieces, _, _, high_ref, low_ref = refs
-    assemble(pieces, high_ref, low_ref, None, plan.chips, slice(plan.chips - 1, None))
 
 
 def triangle_kernel(plan, count, *refs):
@@ -343,7 +337,7 @@
             [],
             ((mine, mine_other), (later, later_other), (half, half_other))[chunk],
         )
-        pieces.append(ring(packed, chips, halves=chunk < 2 and depth % 16 == 0))
+        pieces.append(ring(packed, chips, halves=chunk == 1 and depth % 16 == 0))
 
     pairs = [[shape((len(blocks), nb, nb), bf16)] * 2 for blocks in plan.chunks]
     wholes = [whole_scratch(len(blocks), nb, depth) for blocks in plan.chunks]
@@ -368,10 +362,7 @@
         (*early, inv_high, inv_low),
         flops=6 * 6 * nb * nb * nb,
     )
-    below = kernel_call(bound(place_kernel, plan), pairs[1], [wholes[1]], pieces[1][:count])
-    if count < chips:
-        ends = pieces[1][count:]
-        below = kernel_call(bound(late_kernel, plan), pairs[1], [], (*ends, *below), aliases={2: 0, 3: 1})
+    below = kernel_call(bound(place_kernel, plan), pairs[1], [wholes[1]], pieces[1])
     out, _, _ = kernel_call(
         bound(final_kernel, plan, len(late)),
         [shape(right_side.shape, f32), *pairs[2]],

time: 47.8 us -> 44.7 us (0.935)
  waiting for transfers between devices: 23.4 us -> 21.2 us
  starting transfers between devices: 17.8 us -> 17 us
    ppermute x12, waiting for transfers between devices: 18.3 us -> 16 us  [ring(): lax.ppermute(moving[0] if last and halves else moving, 'col', nearest)]
    ppermute x1, waiting for transfers between devices: 1.1 us -> 0.01 us  [per_device(): mine_other = lax.ppermute(mine, 'col', swap)]
    ppermute x11 -> x10, starting transfers between devices: 2.17 us -> 1.62 us  [ring(): pieces.append(lax.ppermute(moving, 'col', swap))]
    ppermute x11 -> x10, waiting for transfers between devices: 0.22 us -> 0.74 us  [ring(): pieces.append(lax.ppermute(moving, 'col', swap))]
    pallas_call x10 -> x9, Pallas kernels: 6.25 us -> 6.2 us  [kernel_call(): pl.pallas_call(body, out_shape=out_shapes, in_specs=[hbm] * in_hbm + [nea...]
  transfers between devices with their start and end apart: 28 -> 27, of which waited for: 13 -> 14; matrix products, arithmetic and copies ran while one was open for 0% -> 0% of each run, Pallas kernels for 5% -> 5%
where the time goes in v14:
time: 44.7 us; the launch traced here: 44.6 us
  waiting for transfers between devices  21.2 us (47%)
  starting transfers between devices  17 us (38%)
  Pallas kernels  6.2 us (14%)
    ppermute x12, waiting for transfers between devices, ring(): lax.ppermute(moving[0] if last and halves else moving, 'col', nearest)  16 us
    ppermute x12, starting transfers between devices, ring(): lax.ppermute(moving[0] if last and halves else moving, 'col', nearest)  11.7 us
    pallas_call x9, Pallas kernels, kernel_call(): pl.pallas_call(body, out_shape=out_shapes, in_specs=[hbm] * in_hbm + [nea...  6.2 us
    ppermute x1, waiting for transfers between devices, per_device(): tri = [own] + [lax.ppermute(own, 'row', pairs) for pairs in shifts]  2.74 us
    ppermute x10, starting transfers between devices, ring(): pieces.append(lax.ppermute(moving, 'col', swap))  1.62 us
    ppermute x1, starting transfers between devices, per_device(): received = [lax.ppermute(above, 'row', pairs) for pairs in shifts]  1.58 us
    ppermute x1, starting transfers between devices, per_device(): tri = [own] + [lax.ppermute(own, 'row', pairs) for pairs in shifts]  1.52 us
    ppermute x1, waiting for transfers between devices, per_device(): later_other = lax.ppermute(later, 'col', swap)  0.94 us
  transfers between devices with their start and end apart: 27, of which 14 were waited for; matrix products, arithmetic and copies ran while one was open for 0% of the time, Pallas kernels for 5%

profile of v14, /device:TPU:0, one launch (start us, length us, event | category | flops | bytes accessed | tf_op | source)
XLA Modules:
  0.0 44.6 jit_solution(367080260342771473)
XLA Ops:
  0.0 1.1 %shard_map.37 = (f32[6,16,256]{2,1,0:T(8,128)S(1)}, f32[6,16,256]{2,1,0:T(8,128)S(1)}, f32[4,16,256]{2,1,0:T(8,128)S(1)}) custom-call(f32[4,16,1024]{2,1,0:T(8,128)} %factor_hbm.1, f32[4,16,256]{2,1,0:T(8,128)} %inv_hbm.1), custom_call_target="tpu_custom_call" | custom-call | bytes 4194304 | tf_op jit(solution)/shard_map/pallas_call | solution.py:41
  1.6 0.9 %collective-permute-done.18.other_ref = f32[6,16,256]{2,1,0:T(8,128)S(1)} collective-permute-done((f32[6,16,256]{2,1,0:T(8,128)S(1)}, f32[6,16,256]{2,1,0:T(8,128)S(1)}, u32[]{:S(2)}, u32[]{:S(2)}) %collective-permute-start.18) | collective-permute-done | bytes 98336 | tf_op jit(solution)/shard_map/ppermute | solution.py:325
  2.6 2.6 %collective-permute-start.19 = (f32[2,6,16,256]{3,2,1,0:T(8,128)S(1)}, f32[2,6,16,256]{3,2,1,0:T(8,128)S(1)}, u32[]{:S(2)}, u32[]{:S(2)}) collective-permute-start(f32[2,6,16,256]{3,2,1,0:T(8,128)S(1)} %shard_map.43.refs_0_), channel_id=1, source_target_pairs={{1,5},{0,3},{5,9},{4,0},{9,13},{8,4},{13,14},{12,8},{14,10},{15,12... | collective-permute-start | bytes 589832 | tf_op jit(solution)/shard_map/ppermute | solution.py:68
  5.3 1.5 %collective-permute-start = (f32[4,16,256]{2,1,0:T(8,128)S(1)}, f32[4,16,256]{2,1,0:T(8,128)S(1)}, u32[]{:S(2)}, u32[]{:S(2)}) collective-permute-start(f32[4,16,256]{2,1,0:T(8,128)S(1)} %get-tuple-element.17.refs_0_), channel_id=1, source_target_pairs={{16,0},{0,16},{17,1},{1,17},{18,2},{2,18},{19,3},{3,19},{20,4},{4,... | collective-permute-start | bytes 196616 | tf_op jit(solution)/shard_map/ppermute | solution.py:326
  6.8 2.7 %collective-permute-done.refs_1_ = f32[4,16,256]{2,1,0:T(8,128)S(1)} collective-permute-done((f32[4,16,256]{2,1,0:T(8,128)S(1)}, f32[4,16,256]{2,1,0:T(8,128)S(1)}, u32[]{:S(2)}, u32[]{:S(2)}) %collective-permute-start) | collective-permute-done | bytes 65568 | tf_op jit(solution)/shard_map/ppermute | solution.py:326
  9.7 0.8 %collective-permute-start.10 = (f32[2,6,16,256]{3,2,1,0:T(8,128)S(1)}, f32[2,6,16,256]{3,2,1,0:T(8,128)S(1)}, u32[]{:S(2)}, u32[]{:S(2)}) collective-permute-start(f32[2,6,16,256]{3,2,1,0:T(8,128)S(1)} %shard_map.40.refs_0_), channel_id=1, source_target_pairs={{1,5},{0,3},{5,9},{4,0},{9,13},{8,4},{13,14},{12,8},{14,10},{15,12... | collective-permute-start | bytes 589832 | tf_op jit(solution)/shard_map/ppermute | solution.py:68
  10.9 1.6 %collective-permute-start.2 = (f32[2,6,16,256]{3,2,1,0:T(8,128)S(1)}, f32[2,6,16,256]{3,2,1,0:T(8,128)S(1)}, u32[]{:S(2)}, u32[]{:S(2)}) collective-permute-start(f32[2,6,16,256]{3,2,1,0:T(8,128)S(1)} %shard_map.39.refs_0_), channel_id=1, source_target_pairs={{1,5},{0,3},{5,9},{4,0},{9,13},{8,4},{13,14},{12,8},{14,10},{15,12... | collective-permute-start | bytes 589832 | tf_op jit(solution)/shard_map/ppermute | solution.py:68
  12.5 1.3 %collective-permute-start.21 = (f32[2,6,16,256]{3,2,1,0:T(8,128)S(1)}, f32[2,6,16,256]{3,2,1,0:T(8,128)S(1)}, u32[]{:S(2)}, u32[]{:S(2)}) collective-permute-start(f32[2,6,16,256]{3,2,1,0:T(8,128)S(1)} %collective-permute-done.19.refs_1_), channel_id=1, source_target_pairs={{1,5},{0,3},{5,9},{4,0},{9,13},{8,4},{13,14},{12,8},{14,10},{15,12... | collective-permute-start | bytes 589832 | tf_op jit(solution)/shard_map/ppermute | solution.py:68
  13.9 1.6 %collective-permute-start.17 = (f32[512,256]{1,0:T(8,128)S(1)}, f32[512,256]{1,0:T(8,128)S(1)}, u32[]{:S(2)}, u32[]{:S(2)}) collective-permute-start(f32[512,256]{1,0:T(8,128)S(1)} %slice.6), channel_id=1, source_target_pairs={{16,0},{0,16},{17,1},{1,17},{18,2},{2,18},{19,3},{3,19},{20,4},{4,... | collective-permute-start | bytes 1572872 | tf_op jit(solution)/shard_map/ppermute | solution.py:328
  15.5 0.6 %collective-permute-start.12 = (f32[2,6,16,256]{3,2,1,0:T(8,128)S(1)}, f32[2,6,16,256]{3,2,1,0:T(8,128)S(1)}, u32[]{:S(2)}, u32[]{:S(2)}) collective-permute-start(f32[2,6,16,256]{3,2,1,0:T(8,128)S(1)} %collective-permute-done.10.refs_1_), channel_id=1, source_target_pairs={{1,5},{0,3},{5,9},{4,0},{9,13},{8,4},{13,14},{12,8},{14,10},{15,12... | collective-permute-start | bytes 589832 | tf_op jit(solution)/shard_map/ppermute | solution.py:68
  16.1 1.4 %collective-permute-done.2.refs_1_ = f32[2,6,16,256]{3,2,1,0:T(8,128)S(1)} collective-permute-done((f32[2,6,16,256]{3,2,1,0:T(8,128)S(1)}, f32[2,6,16,256]{3,2,1,0:T(8,128)S(1)}, u32[]{:S(2)}, u32[]{:S(2)}) %collective-permute-start.2) | collective-permute-done | bytes 196640 | tf_op jit(solution)/shard_map/ppermute | solution.py:68
  17.7 1.9 %collective-permute-done.21.refs_3_ = f32[2,6,16,256]{3,2,1,0:T(8,128)S(1)} collective-permute-done((f32[2,6,16,256]{3,2,1,0:T(8,128)S(1)}, f32[2,6,16,256]{3,2,1,0:T(8,128)S(1)}, u32[]{:S(2)}, u32[]{:S(2)}) %collective-permute-start.21) | collective-permute-done | bytes 196640 | tf_op jit(solution)/shard_map/ppermute | solution.py:68
  20.1 1.4 %collective-permute-start.3 = (f32[2,6,16,256]{3,2,1,0:T(8,128)S(1)}, f32[2,6,16,256]{3,2,1,0:T(8,128)S(1)}, u32[]{:S(2)}, u32[]{:S(2)}) collective-permute-start(f32[2,6,16,256]{3,2,1,0:T(8,128)S(1)} %collective-permute-done.2.refs_1_), channel_id=1, source_target_pairs={{1,5},{0,3},{5,9},{4,0},{9,13},{8,4},{13,14},{12,8},{14,10},{15,12... | collective-permute-start | bytes 589832 | tf_op jit(solution)/shard_map/ppermute | solution.py:68
  21.9 1.0 %collective-permute-start.14 = (f32[2,6,16,256]{3,2,1,0:T(8,128)S(1)}, f32[2,6,16,256]{3,2,1,0:T(8,128)S(1)}, u32[]{:S(2)}, u32[]{:S(2)}) collective-permute-start(f32[2,6,16,256]{3,2,1,0:T(8,128)S(1)} %collective-permute-done.12.refs_3_), channel_id=1, source_target_pairs={{1,5},{0,3},{5,9},{4,0},{9,13},{8,4},{13,14},{12,8},{14,10},{15,12... | collective-permute-start | bytes 589832 | tf_op jit(solution)/shard_map/ppermute | solution.py:68
  22.9 2.3 %collective-permute-done.23.refs_5_ = f32[2,6,16,256]{3,2,1,0:T(8,128)S(1)} collective-permute-done((f32[2,6,16,256]{3,2,1,0:T(8,128)S(1)}, f32[2,6,16,256]{3,2,1,0:T(8,128)S(1)}, u32[]{:S(2)}, u32[]{:S(2)}) %collective-permute-start.23) | collective-permute-done | bytes 196640 | tf_op jit(solution)/shard_map/ppermute | solution.py:68
  25.3 2.1 %collective-permute-done.3.refs_3_ = f32[2,6,16,256]{3,2,1,0:T(8,128)S(1)} collective-permute-done((f32[2,6,16,256]{3,2,1,0:T(8,128)S(1)}, f32[2,6,16,256]{3,2,1,0:T(8,128)S(1)}, u32[]{:S(2)}, u32[]{:S(2)}) %collective-permute-start.3) | collective-permute-done | bytes 196640 | tf_op jit(solution)/shard_map/ppermute | solution.py:68
  27.8 0.7 %collective-permute-start.25 = (f32[6,16,256]{2,1,0:T(8,128)S(1)}, f32[6,16,256]{2,1,0:T(8,128)S(1)}, u32[]{:S(2)}, u32[]{:S(2)}) collective-permute-start(f32[6,16,256]{2,1,0:T(8,128)S(1)} %slice_bitcast_fusion), channel_id=1, source_target_pairs={{1,5},{0,3},{5,9},{4,0},{9,13},{8,4},{13,14},{12,8},{14,10},{15,12... | collective-permute-start | bytes 294920 | tf_op jit(solution)/shard_map/ppermute | solution.py:68
  28.6 0.9 %collective-permute-done.14.refs_5_ = f32[2,6,16,256]{3,2,1,0:T(8,128)S(1)} collective-permute-done((f32[2,6,16,256]{3,2,1,0:T(8,128)S(1)}, f32[2,6,16,256]{3,2,1,0:T(8,128)S(1)}, u32[]{:S(2)}, u32[]{:S(2)}) %collective-permute-start.14) | collective-permute-done | bytes 196640 | tf_op jit(solution)/shard_map/ppermute | solution.py:68
  29.8 4.3 %collective-permute-done.25.refs_7_ = f32[6,16,256]{2,1,0:T(8,128)S(1)} collective-permute-done((f32[6,16,256]{2,1,0:T(8,128)S(1)}, f32[6,16,256]{2,1,0:T(8,128)S(1)}, u32[]{:S(2)}, u32[]{:S(2)}) %collective-permute-start.25) | collective-permute-done | bytes 98336 | tf_op jit(solution)/shard_map/ppermute | solution.py:68
  34.7 0.7 %collective-permute-done.26.refs_8_ = f32[6,16,256]{2,1,0:T(8,128)S(1)} collective-permute-done((f32[6,16,256]{2,1,0:T(8,128)S(1)}, f32[6,16,256]{2,1,0:T(8,128)S(1)}, u32[]{:S(2)}, u32[]{:S(2)}) %collective-permute-start.26) | collective-permute-done | bytes 98336 | tf_op jit(solution)/shard_map/ppermute | solution.py:71
  37.1 1.1 %shard_map.41 = (bf16[6,256,256]{2,1,0:T(8,128)(2,1)S(1)}, bf16[6,256,256]{2,1,0:T(8,128)(2,1)S(1)}, f32[4,256,256]{2,1,0:T(8,128)S(1)}, f32[512,256]{1,0:T(8,128)S(1)}) custom-call(f32[2,6,16,256]{3,2,1,0:T(8,128)S(1)} %shard_map.40.refs_0_, f32[2,6,16,256]{3,2,1,0:T(8,128)S(1)} %collective-permute-done.10.refs_1_, ...), custom_call_target="tpu_custom_call" | custom-call | flops 301989888 | bytes 4194304 | tf_op jit(solution)/shard_map/pallas_call | solution.py:41
  38.2 1.0 %shard_map.42 = (bf16[6,256,256]{2,1,0:T(8,128)(2,1)S(1)}, bf16[6,256,256]{2,1,0:T(8,128)(2,1)S(1)}) custom-call(f32[2,6,16,256]{3,2,1,0:T(8,128)S(1)} %shard_map.39.refs_0_, f32[2,6,16,256]{3,2,1,0:T(8,128)S(1)} %collective-permute-done.2.refs_1_, f32[2,6,16,256]{3,2,1,0:T(8,128)S(1)} %collective-permute-done.6.refs_2_, ...), custom_call_target="tpu_custom_call" | custom-call | flops 603979776 | bytes 4194304 | tf_op jit(solution)/shard_map/pallas_call | solution.py:41
  39.2 2.7 %collective-permute-done.5.refs_0_ = f32[2,6,16,256]{3,2,1,0:T(8,128)S(1)} collective-permute-done((f32[2,6,16,256]{3,2,1,0:T(8,128)S(1)}, f32[2,6,16,256]{3,2,1,0:T(8,128)S(1)}, u32[]{:S(2)}, u32[]{:S(2)}) %collective-permute-start.5) | collective-permute-done | bytes 196640 | tf_op jit(solution)/shard_map/ppermute | solution.py:68
  41.9 2.7 %shard_map.45 = (f32[1024,256]{1,0:T(8,128)}, bf16[6,256,256]{2,1,0:T(8,128)(2,1)S(1)}, bf16[6,256,256]{2,1,0:T(8,128)(2,1)S(1)}) custom-call(f32[2,6,16,256]{3,2,1,0:T(8,128)S(1)} %collective-permute-done.5.refs_0_, bf16[6,256,256]{2,1,0:T(8,128)(2,1)S(1)} %get-tuple-element.21.refs_1_, ...), custom_call_target="tpu_custom_call", output_to_operand_aliasing={{1}: (1, {}), {2}: (2, {})} | custom-call | flops 1509949440 | bytes 4194304 | tf_op jit(solution)/shard_map/pallas_call | solution.py:41
  (43 shorter events, 5.4 us)
Async XLA Ops:
  2.6 9.9 %collective-permute-start.19 = (f32[2,6,16,256]{3,2,1,0:T(8,128)S(1)}, f32[2,6,16,256]{3,2,1,0:T(8,128)S(1)}, u32[]{:S(2)}, u32[]{:S(2)}) collective-permute-start(f32[2,6,16,256]{3,2,1,0:T(8,128)S(1)} %shard_map.43.refs_0_), channel_id=1, source_target_pairs={{1,5},{0,3},{5,9},{4,0},{9,13},{8,4},{13,14},{12,8},{14,10},{15,12... | collective-permute-start | bytes 589832 | tf_op jit(solution)/shard_map/ppermute | solution.py:68
  5.3 4.3 %collective-permute-start = (f32[4,16,256]{2,1,0:T(8,128)S(1)}, f32[4,16,256]{2,1,0:T(8,128)S(1)}, u32[]{:S(2)}, u32[]{:S(2)}) collective-permute-start(f32[4,16,256]{2,1,0:T(8,128)S(1)} %get-tuple-element.17.refs_0_), channel_id=1, source_target_pairs={{16,0},{0,16},{17,1},{1,17},{18,2},{2,18},{19,3},{3,19},{20,4},{4,... | collective-permute-start | bytes 196616 | tf_op jit(solution)/shard_map/ppermute | solution.py:326
  6.8 2.8 %collective-permute-start.9 = (f32[6,16,256]{2,1,0:T(8,128)S(1)}, f32[6,16,256]{2,1,0:T(8,128)S(1)}, u32[]{:S(2)}, u32[]{:S(2)}) collective-permute-start(f32[6,16,256]{2,1,0:T(8,128)S(1)} %get-tuple-element.18.own_ref), channel_id=1, source_target_pairs={{0,1},{1,0},{2,3},{3,2},{4,5},{5,4},{6,7},{7,6},{8,9},{9,8},{10,11... | collective-permute-start | bytes 294920 | tf_op jit(solution)/shard_map/ppermute | solution.py:324
  9.7 5.8 %collective-permute-start.10 = (f32[2,6,16,256]{3,2,1,0:T(8,128)S(1)}, f32[2,6,16,256]{3,2,1,0:T(8,128)S(1)}, u32[]{:S(2)}, u32[]{:S(2)}) collective-permute-start(f32[2,6,16,256]{3,2,1,0:T(8,128)S(1)} %shard_map.40.refs_0_), channel_id=1, source_target_pairs={{1,5},{0,3},{5,9},{4,0},{9,13},{8,4},{13,14},{12,8},{14,10},{15,12... | collective-permute-start | bytes 589832 | tf_op jit(solution)/shard_map/ppermute | solution.py:68
  10.9 6.6 %collective-permute-start.2 = (f32[2,6,16,256]{3,2,1,0:T(8,128)S(1)}, f32[2,6,16,256]{3,2,1,0:T(8,128)S(1)}, u32[]{:S(2)}, u32[]{:S(2)}) collective-permute-start(f32[2,6,16,256]{3,2,1,0:T(8,128)S(1)} %shard_map.39.refs_0_), channel_id=1, source_target_pairs={{1,5},{0,3},{5,9},{4,0},{9,13},{8,4},{13,14},{12,8},{14,10},{15,12... | collective-permute-start | bytes 589832 | tf_op jit(solution)/shard_map/ppermute | solution.py:68
  12.5 7.1 %collective-permute-start.21 = (f32[2,6,16,256]{3,2,1,0:T(8,128)S(1)}, f32[2,6,16,256]{3,2,1,0:T(8,128)S(1)}, u32[]{:S(2)}, u32[]{:S(2)}) collective-permute-start(f32[2,6,16,256]{3,2,1,0:T(8,128)S(1)} %collective-permute-done.19.refs_1_), channel_id=1, source_target_pairs={{1,5},{0,3},{5,9},{4,0},{9,13},{8,4},{13,14},{12,8},{14,10},{15,12... | collective-permute-start | bytes 589832 | tf_op jit(solution)/shard_map/ppermute | solution.py:68
  13.9 13.9 %collective-permute-start.17 = (f32[512,256]{1,0:T(8,128)S(1)}, f32[512,256]{1,0:T(8,128)S(1)}, u32[]{:S(2)}, u32[]{:S(2)}) collective-permute-start(f32[512,256]{1,0:T(8,128)S(1)} %slice.6), channel_id=1, source_target_pairs={{16,0},{0,16},{17,1},{1,17},{18,2},{2,18},{19,3},{3,19},{20,4},{4,... | collective-permute-start | bytes 1572872 | tf_op jit(solution)/shard_map/ppermute | solution.py:328
  15.5 4.6 %collective-permute-start.20 = (f32[2,6,16,256]{3,2,1,0:T(8,128)S(1)}, f32[2,6,16,256]{3,2,1,0:T(8,128)S(1)}, u32[]{:S(2)}, u32[]{:S(2)}) collective-permute-start(f32[2,6,16,256]{3,2,1,0:T(8,128)S(1)} %collective-permute-done.19.refs_1_), channel_id=1, source_target_pairs={{0,1},{1,0},{2,3},{3,2},{4,5},{5,4},{6,7},{7,6},{8,9},{9,8},{10,11... | collective-permute-start | bytes 589832 | tf_op jit(solution)/shard_map/ppermute | solution.py:71
  15.5 6.2 %collective-permute-start.12 = (f32[2,6,16,256]{3,2,1,0:T(8,128)S(1)}, f32[2,6,16,256]{3,2,1,0:T(8,128)S(1)}, u32[]{:S(2)}, u32[]{:S(2)}) collective-permute-start(f32[2,6,16,256]{3,2,1,0:T(8,128)S(1)} %collective-permute-done.10.refs_1_), channel_id=1, source_target_pairs={{1,5},{0,3},{5,9},{4,0},{9,13},{8,4},{13,14},{12,8},{14,10},{15,12... | collective-permute-start | bytes 589832 | tf_op jit(solution)/shard_map/ppermute | solution.py:68
  17.5 4.4 %collective-permute-start.11 = (f32[2,6,16,256]{3,2,1,0:T(8,128)S(1)}, f32[2,6,16,256]{3,2,1,0:T(8,128)S(1)}, u32[]{:S(2)}, u32[]{:S(2)}) collective-permute-start(f32[2,6,16,256]{3,2,1,0:T(8,128)S(1)} %collective-permute-done.10.refs_1_), channel_id=1, source_target_pairs={{0,1},{1,0},{2,3},{3,2},{4,5},{5,4},{6,7},{7,6},{8,9},{9,8},{10,11... | collective-permute-start | bytes 589832 | tf_op jit(solution)/shard_map/ppermute | solution.py:71
  19.6 5.7 %collective-permute-start.23 = (f32[2,6,16,256]{3,2,1,0:T(8,128)S(1)}, f32[2,6,16,256]{3,2,1,0:T(8,128)S(1)}, u32[]{:S(2)}, u32[]{:S(2)}) collective-permute-start(f32[2,6,16,256]{3,2,1,0:T(8,128)S(1)} %collective-permute-done.21.refs_3_), channel_id=1, source_target_pairs={{1,5},{0,3},{5,9},{4,0},{9,13},{8,4},{13,14},{12,8},{14,10},{15,12... | collective-permute-start | bytes 589832 | tf_op jit(solution)/shard_map/ppermute | solution.py:68
  20.1 7.3 %collective-permute-start.3 = (f32[2,6,16,256]{3,2,1,0:T(8,128)S(1)}, f32[2,6,16,256]{3,2,1,0:T(8,128)S(1)}, u32[]{:S(2)}, u32[]{:S(2)}) collective-permute-start(f32[2,6,16,256]{3,2,1,0:T(8,128)S(1)} %collective-permute-done.2.refs_1_), channel_id=1, source_target_pairs={{1,5},{0,3},{5,9},{4,0},{9,13},{8,4},{13,14},{12,8},{14,10},{15,12... | collective-permute-start | bytes 589832 | tf_op jit(solution)/shard_map/ppermute | solution.py:68
  21.7 6.8 %collective-permute-start.22 = (f32[2,6,16,256]{3,2,1,0:T(8,128)S(1)}, f32[2,6,16,256]{3,2,1,0:T(8,128)S(1)}, u32[]{:S(2)}, u32[]{:S(2)}) collective-permute-start(f32[2,6,16,256]{3,2,1,0:T(8,128)S(1)} %collective-permute-done.21.refs_3_), channel_id=1, source_target_pairs={{0,1},{1,0},{2,3},{3,2},{4,5},{5,4},{6,7},{7,6},{8,9},{9,8},{10,11... | collective-permute-start | bytes 589832 | tf_op jit(solution)/shard_map/ppermute | solution.py:71
  21.9 7.6 %collective-permute-start.14 = (f32[2,6,16,256]{3,2,1,0:T(8,128)S(1)}, f32[2,6,16,256]{3,2,1,0:T(8,128)S(1)}, u32[]{:S(2)}, u32[]{:S(2)}) collective-permute-start(f32[2,6,16,256]{3,2,1,0:T(8,128)S(1)} %collective-permute-done.12.refs_3_), channel_id=1, source_target_pairs={{1,5},{0,3},{5,9},{4,0},{9,13},{8,4},{13,14},{12,8},{14,10},{15,12... | collective-permute-start | bytes 589832 | tf_op jit(solution)/shard_map/ppermute | solution.py:68
  25.3 8.8 %collective-permute-start.13 = (f32[2,6,16,256]{3,2,1,0:T(8,128)S(1)}, f32[2,6,16,256]{3,2,1,0:T(8,128)S(1)}, u32[]{:S(2)}, u32[]{:S(2)}) collective-permute-start(f32[2,6,16,256]{3,2,1,0:T(8,128)S(1)} %collective-permute-done.12.refs_3_), channel_id=1, source_target_pairs={{0,1},{1,0},{2,3},{3,2},{4,5},{5,4},{6,7},{7,6},{8,9},{9,8},{10,11... | collective-permute-start | bytes 589832 | tf_op jit(solution)/shard_map/ppermute | solution.py:71
  27.4 7.2 %collective-permute-start.4 = (f32[2,6,16,256]{3,2,1,0:T(8,128)S(1)}, f32[2,6,16,256]{3,2,1,0:T(8,128)S(1)}, u32[]{:S(2)}, u32[]{:S(2)}) collective-permute-start(f32[2,6,16,256]{3,2,1,0:T(8,128)S(1)} %collective-permute-done.3.refs_3_), channel_id=1, source_target_pairs={{1,5},{0,3},{5,9},{4,0},{9,13},{8,4},{13,14},{12,8},{14,10},{15,12... | collective-permute-start | bytes 589832 | tf_op jit(solution)/shard_map/ppermute | solution.py:68
  27.8 6.3 %collective-permute-start.25 = (f32[6,16,256]{2,1,0:T(8,128)S(1)}, f32[6,16,256]{2,1,0:T(8,128)S(1)}, u32[]{:S(2)}, u32[]{:S(2)}) collective-permute-start(f32[6,16,256]{2,1,0:T(8,128)S(1)} %slice_bitcast_fusion), channel_id=1, source_target_pairs={{1,5},{0,3},{5,9},{4,0},{9,13},{8,4},{13,14},{12,8},{14,10},{15,12... | collective-permute-start | bytes 294920 | tf_op jit(solution)/shard_map/ppermute | solution.py:68
  28.5 7.1 %collective-permute-start.24 = (f32[2,6,16,256]{3,2,1,0:T(8,128)S(1)}, f32[2,6,16,256]{3,2,1,0:T(8,128)S(1)}, u32[]{:S(2)}, u32[]{:S(2)}) collective-permute-start(f32[2,6,16,256]{3,2,1,0:T(8,128)S(1)} %collective-permute-done.23.refs_5_), channel_id=1, source_target_pairs={{0,1},{1,0},{2,3},{3,2},{4,5},{5,4},{6,7},{7,6},{8,9},{9,8},{10,11... | collective-permute-start | bytes 589832 | tf_op jit(solution)/shard_map/ppermute | solution.py:71
  29.5 6.7 %collective-permute-start.16 = (f32[2,6,16,256]{3,2,1,0:T(8,128)S(1)}, f32[2,6,16,256]{3,2,1,0:T(8,128)S(1)}, u32[]{:S(2)}, u32[]{:S(2)}) collective-permute-start(f32[2,6,16,256]{3,2,1,0:T(8,128)S(1)} %collective-permute-done.14.refs_5_), channel_id=1, source_target_pairs={{1,5},{0,3},{5,9},{4,0},{9,13},{8,4},{13,14},{12,8},{14,10},{15,12... | collective-permute-start | bytes 589832 | tf_op jit(solution)/shard_map/ppermute | solution.py:68
  34.1 3.0 %collective-permute-start.15 = (f32[2,6,16,256]{3,2,1,0:T(8,128)S(1)}, f32[2,6,16,256]{3,2,1,0:T(8,128)S(1)}, u32[]{:S(2)}, u32[]{:S(2)}) collective-permute-start(f32[2,6,16,256]{3,2,1,0:T(8,128)S(1)} %collective-permute-done.14.refs_5_), channel_id=1, source_target_pairs={{0,1},{1,0},{2,3},{3,2},{4,5},{5,4},{6,7},{7,6},{8,9},{9,8},{10,11... | collective-permute-start | bytes 589832 | tf_op jit(solution)/shard_map/ppermute | solution.py:71
  34.6 3.6 %collective-permute-start.6 = (f32[2,6,16,256]{3,2,1,0:T(8,128)S(1)}, f32[2,6,16,256]{3,2,1,0:T(8,128)S(1)}, u32[]{:S(2)}, u32[]{:S(2)}) collective-permute-start(f32[2,6,16,256]{3,2,1,0:T(8,128)S(1)} %collective-permute-done.2.refs_1_), channel_id=1, source_target_pairs={{0,1},{1,0},{2,3},{3,2},{4,5},{5,4},{6,7},{7,6},{8,9},{9,8},{10,11... | collective-permute-start | bytes 589832 | tf_op jit(solution)/shard_map/ppermute | solution.py:71
  35.4 2.8 %collective-permute-start.7 = (f32[2,6,16,256]{3,2,1,0:T(8,128)S(1)}, f32[2,6,16,256]{3,2,1,0:T(8,128)S(1)}, u32[]{:S(2)}, u32[]{:S(2)}) collective-permute-start(f32[2,6,16,256]{3,2,1,0:T(8,128)S(1)} %collective-permute-done.3.refs_3_), channel_id=1, source_target_pairs={{0,1},{1,0},{2,3},{3,2},{4,5},{5,4},{6,7},{7,6},{8,9},{9,8},{10,11... | collective-permute-start | bytes 589832 | tf_op jit(solution)/shard_map/ppermute | solution.py:71
  35.6 2.7 %collective-permute-start.8 = (f32[2,6,16,256]{3,2,1,0:T(8,128)S(1)}, f32[2,6,16,256]{3,2,1,0:T(8,128)S(1)}, u32[]{:S(2)}, u32[]{:S(2)}) collective-permute-start(f32[2,6,16,256]{3,2,1,0:T(8,128)S(1)} %collective-permute-done.4.refs_5_), channel_id=1, source_target_pairs={{0,1},{1,0},{2,3},{3,2},{4,5},{5,4},{6,7},{7,6},{8,9},{9,8},{10,11... | collective-permute-start | bytes 589832 | tf_op jit(solution)/shard_map/ppermute | solution.py:71
  36.2 5.7 %collective-permute-start.5 = (f32[2,6,16,256]{3,2,1,0:T(8,128)S(1)}, f32[2,6,16,256]{3,2,1,0:T(8,128)S(1)}, u32[]{:S(2)}, u32[]{:S(2)}) collective-permute-start(f32[2,6,16,256]{3,2,1,0:T(8,128)S(1)} %collective-permute-done.4.refs_5_), channel_id=1, source_target_pairs={{1,5},{0,3},{5,9},{4,0},{9,13},{8,4},{13,14},{12,8},{14,10},{15,12... | collective-permute-start | bytes 589832 | tf_op jit(solution)/shard_map/ppermute | solution.py:68
  (4 other events, 18.0 us)
